TPU v7x, 32 devices: a whole 2x2x4 slice. The times are simulated.
32 devices in a mesh: section: 2 (over y), group: 4 (over x, core), expert: 4 (over z).
Axes of the slice: x: 2, y: 2, z: 4, core: 2. Of those that a mesh axis runs over, the one named last changes fastest.
Arguments:
- inputs: bfloat16 [2, 16, 128, 1536], P(None, ('group', 'expert')), may hold values from -6 to 6
- cotangent: bfloat16 [2, 16, 128, 1536], P(None, ('group', 'expert')), may hold values from -6 to 6
- segment_ids: int32 [2, 16, 128], P(None, ('group', 'expert')), may hold values from 0 to 63, as said below
- live_first: int32 [2, 16, 2], P(None, ('group', 'expert')), may hold values from 0 to 1, as said below
- routes: int32 [2, 2, 16, 128, 8], P('section', None, ('group', 'expert')), may hold values from 0 to 19, all different within a row; in each aligned block of 128 rows (0 to 127, 128 to 255, ..., all dimensions but the last counted through in order) at most 64 rows name the same one
- gain_attn: bfloat16 [2, 1536], P('section', ('group', 'expert')), may hold values from 0.5 to 1.5
- gain_moe: bfloat16 [2, 1536], P('section', ('group', 'expert')), may hold values from 0.5 to 1.5
- w_query: bfloat16 [2, 1536, 1536], P('section', ('group', 'expert')), may hold values from -0.15625 to 0.15625
- key_weight: bfloat16 [2, 1536, 512], P('section', ('group', 'expert')), may hold values from -0.15625 to 0.15625
- value_weight: bfloat16 [2, 1536, 512], P('section', ('group', 'expert')), may hold values from -0.15625 to 0.15625
- w_out: bfloat16 [2, 1536, 1536], P('section', None, ('group', 'expert')), may hold values from -0.625 to 0.625
- w_router: bfloat16 [2, 1536, 20], P('section', ('group', 'expert')), may hold values from -0.076171875 to 0.076171875
- w_gate: bfloat16 [2, 20, 1536, 512], P('section', 'expert'), may hold values from -0.15625 to 0.15625
- w_up: bfloat16 [2, 20, 1536, 512], P('section', 'expert'), may hold values from -0.15625 to 0.15625
- w_down: bfloat16 [2, 20, 512, 1536], P('section', 'expert'), may hold values from -1 to 1
Outputs:
- layer_out: bfloat16 [2, 2, 16, 128, 1536], P('section', None, ('group', 'expert'))
- input_grad: float32 [2, 2, 16, 128, 1536], P('section', None, ('group', 'expert'))
- gain_attn_grad: float32 [2, 1536], P('section', ('group', 'expert'))
- gain_moe_grad: float32 [2, 1536], P('section', ('group', 'expert'))
- w_query_grad: float32 [2, 1536, 1536], P('section', ('group', 'expert'))
- w_key_grad: float32 [2, 1536, 512], P('section', ('group', 'expert'))
- w_value_grad: float32 [2, 1536, 512], P('section', ('group', 'expert'))
- w_out_grad: float32 [2, 1536, 1536], P('section', None, ('group', 'expert'))
- w_router_grad: float32 [2, 1536, 20], P('section', ('group', 'expert'))
- w_gate_grad: float32 [2, 20, 1536, 512], P('section', 'expert', 'group')
- w_up_grad: float32 [2, 20, 1536, 512], P('section', 'expert', 'group')
- w_down_grad: float32 [2, 20, 512, 1536], P('section', 'expert', None, 'group')
Inputs may be any that keep to these rules, and one draw needn't show every extreme that they name: `segment_ids`: within each sequence the numbers start at 0 at its first position, never fall, and rise by one where a new document starts; in each micro-batch some sequence reaches 63, and document lengths run from a few positions to the whole sequence. `live_first`: for each query block of 64 positions: the index of the block that holds the start of the document of the query block's first position. `routes`: in the 128 tokens of one sequence of one micro-batch and layer, no expert is named more than 64 times, a bound that some block reaches; a token names 8 different experts.
All inputs are finite; a program needn't handle non-finite values.
Results may differ from a plain program's by a relative error of at most 0.023.
Values may be sent and summed in bfloat16 or wider, within the bound.
A program may use at most 320 MiB of HBM per device.

v0:
```python
import jax
import jax.numpy as jnp
from jax import lax
from jax.sharding import PartitionSpec as P

QUERY_HEADS = 24
KEY_VALUE_HEADS = 8
HEAD_SIZE = 64
BLK = 64


EPS = 1e-06
THETA = 10000.0
NEG_FILL = -1e30


def passed_along(value, axis, steps):
    count = lax.axis_size(axis)
    first, last = (max(0, -steps), min(count, count - steps))
    return lax.ppermute(value, axis, [(source, source + steps) for source in range(first, last)])


def rotate_halves(values, direction):
    sequence_length = values.shape[-3]
    half_size = values.shape[-1] // 2
    frequency = THETA ** (-jnp.arange(half_size, dtype=jnp.float32) * 2.0 / values.shape[-1])
    angles = jnp.arange(sequence_length, dtype=jnp.float32)[:, None] * frequency[None, :]
    cosine = jnp.cos(angles)[:, None, :]
    sine_val = direction * jnp.sin(angles)[:, None, :]
    first_half = values[..., :half_size]
    second_half = values[..., half_size:]
    return jnp.concatenate(
        [
            first_half * cosine - second_half * sine_val,
            second_half * cosine + first_half * sine_val,
        ],
        axis=-1,
    )


def normalize(values, gain_vec):
    factor = lax.rsqrt(jnp.mean(values * values, axis=-1, keepdims=True) + EPS)
    return (factor, values * factor * gain_vec.astype(jnp.float32))


def norm_back(grad_out, values, factor, gain_vec):
    gain_wide = gain_vec.astype(jnp.float32)
    gain_grad = jnp.sum(grad_out * values * factor, axis=0)
    scaled = grad_out * gain_wide
    grad_in = factor * scaled - values * factor**3 * jnp.mean(
        scaled * values, axis=-1, keepdims=True
    )
    return (gain_grad, grad_in)


def build_mask(seg_now, live_now):
    position = jnp.arange(seg_now.shape[0], dtype=jnp.int32)
    causal = position[None, :] <= position[:, None]
    same_doc = seg_now[:, None] == seg_now[None, :]
    first_block = jnp.repeat(live_now, BLK)[:, None]
    reaches = position[None, :] // BLK >= first_block
    return causal & same_doc & reaches


def score_block(grouped_heads, key_heads_split, allowed):
    scores = jnp.einsum(
        "qhgd,khd->hgqk", grouped_heads, key_heads_split, preferred_element_type=jnp.float32
    ) * HEAD_SIZE ** (-0.5)
    return jnp.where(allowed[None, None], scores, NEG_FILL)


def route_layout(route_now, experts_total, per_dev, expert_count, slot_cap):
    sequence_length, top_count = route_now.shape
    choose = route_now[:, :, None] == jnp.arange(experts_total, dtype=jnp.int32)[None, None, :]
    flat_hot = choose.reshape(sequence_length * top_count, experts_total).astype(jnp.int32)
    before = jnp.cumsum(flat_hot, axis=0) - flat_hot
    slot_num = jnp.sum(before * flat_hot, axis=-1)
    flat_route = route_now.reshape(-1)
    slot_place = (flat_route % per_dev * expert_count + flat_route // per_dev) * slot_cap + slot_num
    return (choose, slot_place)


def pack_rows(row_data, slot_place, per_dev, expert_count, slot_cap):
    features = row_data.shape[1]
    buffer = (
        jnp.zeros((per_dev * expert_count * slot_cap, features), row_data.dtype)
        .at[slot_place]
        .set(row_data)
    )
    return buffer.reshape(per_dev, expert_count, slot_cap, features)


def layer_forward(layer_in, dense_set, expert_set, seg_now, live_now, route_now, expert_count):
    query_mat, key_matrix, value_matrix, out_mat, router_mat, attn_gain, moe_gain = dense_set
    gate_mat, up_mat, down_mat = expert_set
    sequence_length, features = layer_in.shape
    per_dev = gate_mat.shape[0]
    experts_total = router_mat.shape[1]
    top_count = route_now.shape[1]
    slot_cap = sequence_length * top_count * 5 // (4 * experts_total)
    resid_in = layer_in.astype(jnp.float32)
    scale_one, normed_one = normalize(resid_in, attn_gain)
    normed_input = normed_one.astype(jnp.bfloat16)
    query_rows = rotate_halves(
        jnp.dot(normed_input, query_mat, preferred_element_type=jnp.float32).reshape(
            sequence_length, QUERY_HEADS, HEAD_SIZE
        ),
        1.0,
    ).astype(jnp.bfloat16)
    key_heads_split = rotate_halves(
        jnp.dot(normed_input, key_matrix, preferred_element_type=jnp.float32).reshape(
            sequence_length, KEY_VALUE_HEADS, HEAD_SIZE
        ),
        1.0,
    ).astype(jnp.bfloat16)
    value_heads_split = (
        jnp.dot(normed_input, value_matrix, preferred_element_type=jnp.float32)
        .reshape(sequence_length, KEY_VALUE_HEADS, HEAD_SIZE)
        .astype(jnp.bfloat16)
    )
    grouped_heads = query_rows.reshape(
        sequence_length, KEY_VALUE_HEADS, QUERY_HEADS // KEY_VALUE_HEADS, HEAD_SIZE
    )
    allowed = build_mask(seg_now, live_now)
    scores = score_block(grouped_heads, key_heads_split, allowed)
    top_score = jnp.max(scores, axis=-1, keepdims=True)
    exp_scores = jnp.exp(scores - top_score)
    row_total = jnp.sum(exp_scores, axis=-1, keepdims=True)
    probs = exp_scores / row_total
    logsum = top_score + jnp.log(row_total)
    mixed_heads = jnp.einsum(
        "hgqk,khd->qhgd",
        probs.astype(jnp.bfloat16),
        value_heads_split,
        preferred_element_type=jnp.float32,
    )
    mixed_heads = mixed_heads.reshape(sequence_length, QUERY_HEADS * HEAD_SIZE).astype(jnp.bfloat16)
    hidden = resid_in + jnp.dot(mixed_heads, out_mat, preferred_element_type=jnp.float32)
    scale_two, normed_two = normalize(hidden, moe_gain)
    moe_in = normed_two.astype(jnp.bfloat16)
    logits = jnp.dot(moe_in, router_mat, preferred_element_type=jnp.float32)
    choose, slot_place = route_layout(route_now, experts_total, per_dev, expert_count, slot_cap)
    picked = jnp.sum(jnp.where(choose, logits[:, None, :], 0.0), axis=-1)
    gate_probs = jax.nn.softmax(picked, axis=-1)
    send_rows = pack_rows(
        jnp.repeat(moe_in, top_count, axis=0), slot_place, per_dev, expert_count, slot_cap
    )
    received = lax.all_to_all(send_rows, "expert", split_axis=1, concat_axis=1, tiled=True)
    flat_recv = received.reshape(per_dev, expert_count * slot_cap, features)
    gate_pre = jnp.einsum("erd,edf->erf", flat_recv, gate_mat, preferred_element_type=jnp.float32)
    up_pre = jnp.einsum("erd,edf->erf", flat_recv, up_mat, preferred_element_type=jnp.float32)
    inner_act = (jax.nn.silu(gate_pre) * up_pre).astype(jnp.bfloat16)
    produced = jnp.einsum(
        "erf,efd->erd", inner_act, down_mat, preferred_element_type=jnp.float32
    ).astype(jnp.bfloat16)
    produced = produced.reshape(per_dev, expert_count, slot_cap, features)
    returned = lax.all_to_all(produced, "expert", split_axis=1, concat_axis=1, tiled=True)
    back_rows = returned.reshape(-1, features)[slot_place].reshape(
        sequence_length, top_count, features
    )
    moe_out = jnp.sum(gate_probs[:, :, None] * back_rows.astype(jnp.float32), axis=1)
    kept_vals = (
        resid_in,
        scale_one,
        normed_input,
        query_rows,
        key_heads_split,
        value_heads_split,
        logsum,
        mixed_heads,
        hidden,
        scale_two,
        moe_in,
        gate_probs,
        choose,
        slot_place,
        flat_recv,
        gate_pre,
        up_pre,
        back_rows,
        allowed,
    )
    return (hidden + moe_out, kept_vals)


def layer_backward(grad_y, kept_vals, dense_set, expert_set, expert_count):
    (
        resid_in,
        scale_one,
        normed_input,
        query_rows,
        key_heads_split,
        value_heads_split,
        logsum,
        mixed_heads,
        hidden,
        scale_two,
        moe_in,
        gate_probs,
        choose,
        slot_place,
        flat_recv,
        gate_pre,
        up_pre,
        back_rows,
        allowed,
    ) = kept_vals
    query_mat, key_matrix, value_matrix, out_mat, router_mat, attn_gain, moe_gain = dense_set
    gate_mat, up_mat, down_mat = expert_set
    sequence_length, features = resid_in.shape
    top_count = gate_probs.shape[1]
    per_dev = gate_mat.shape[0]
    slot_cap = flat_recv.shape[1] // expert_count
    grad_rows = (
        (gate_probs[:, :, None] * grad_y[:, None, :])
        .reshape(sequence_length * top_count, features)
        .astype(jnp.bfloat16)
    )
    grad_gate = jnp.sum(back_rows.astype(jnp.float32) * grad_y[:, None, :], axis=-1)
    grad_send = pack_rows(grad_rows, slot_place, per_dev, expert_count, slot_cap)
    grad_recv = lax.all_to_all(
        grad_send, "expert", split_axis=1, concat_axis=1, tiled=True
    ).reshape(per_dev, expert_count * slot_cap, features)
    sigma = jax.nn.sigmoid(gate_pre)
    silu_val = gate_pre * sigma
    inner_act = (silu_val * up_pre).astype(jnp.bfloat16)
    grad_inner = jnp.einsum("erd,efd->erf", grad_recv, down_mat, preferred_element_type=jnp.float32)
    down_grad = jnp.einsum("erf,erd->efd", inner_act, grad_recv, preferred_element_type=jnp.float32)
    grad_gate_pre = (grad_inner * up_pre * sigma * (1.0 + gate_pre * (1.0 - sigma))).astype(
        jnp.bfloat16
    )
    grad_up_pre = (grad_inner * silu_val).astype(jnp.bfloat16)
    gate_grad = jnp.einsum(
        "erd,erf->edf", flat_recv, grad_gate_pre, preferred_element_type=jnp.float32
    )
    up_grad = jnp.einsum("erd,erf->edf", flat_recv, grad_up_pre, preferred_element_type=jnp.float32)
    grad_rows_in = jnp.einsum(
        "erf,edf->erd", grad_gate_pre, gate_mat, preferred_element_type=jnp.float32
    )
    grad_rows_in = grad_rows_in + jnp.einsum(
        "erf,edf->erd", grad_up_pre, up_mat, preferred_element_type=jnp.float32
    )
    grad_rows_in = grad_rows_in.astype(jnp.bfloat16).reshape(
        per_dev, expert_count, slot_cap, features
    )
    grad_back = lax.all_to_all(grad_rows_in, "expert", split_axis=1, concat_axis=1, tiled=True)
    grad_moe_in = jnp.sum(
        grad_back.reshape(-1, features)[slot_place]
        .reshape(sequence_length, top_count, features)
        .astype(jnp.float32),
        axis=1,
    )
    grad_picked = gate_probs * (grad_gate - jnp.sum(gate_probs * grad_gate, axis=-1, keepdims=True))
    grad_logits = jnp.sum(jnp.where(choose, grad_picked[:, :, None], 0.0), axis=1).astype(
        jnp.bfloat16
    )
    grad_moe_in = grad_moe_in + jnp.einsum(
        "te,de->td", grad_logits, router_mat, preferred_element_type=jnp.float32
    )
    router_grad = jnp.einsum("td,te->de", moe_in, grad_logits, preferred_element_type=jnp.float32)
    moe_gain_grad, grad_norm_two = norm_back(grad_moe_in, hidden, scale_two, moe_gain)
    grad_hidden = grad_y + grad_norm_two
    grad_hid_low = grad_hidden.astype(jnp.bfloat16)
    out_grad = jnp.einsum(
        "tc,td->cd", mixed_heads, grad_hid_low, preferred_element_type=jnp.float32
    )
    mixed_heads_gradient = jnp.einsum(
        "td,cd->tc", grad_hid_low, out_mat, preferred_element_type=jnp.float32
    ).astype(jnp.bfloat16)
    mixed_heads_gradient = mixed_heads_gradient.reshape(
        sequence_length, KEY_VALUE_HEADS, QUERY_HEADS // KEY_VALUE_HEADS, HEAD_SIZE
    )
    grouped_heads = query_rows.reshape(
        sequence_length, KEY_VALUE_HEADS, QUERY_HEADS // KEY_VALUE_HEADS, HEAD_SIZE
    )
    probs = jnp.exp(score_block(grouped_heads, key_heads_split, allowed) - logsum)
    grad_probs = jnp.einsum(
        "qhgd,khd->hgqk",
        mixed_heads_gradient,
        value_heads_split,
        preferred_element_type=jnp.float32,
    )
    value_rows_gradient = jnp.einsum(
        "hgqk,qhgd->khd",
        probs.astype(jnp.bfloat16),
        mixed_heads_gradient,
        preferred_element_type=jnp.float32,
    )
    value_rows_gradient = value_rows_gradient.reshape(
        sequence_length, KEY_VALUE_HEADS * HEAD_SIZE
    ).astype(jnp.bfloat16)
    delta = jnp.sum(probs * grad_probs, axis=-1, keepdims=True)
    grad_scores = (probs * (grad_probs - delta) * HEAD_SIZE ** (-0.5)).astype(jnp.bfloat16)
    grad_queries = jnp.einsum(
        "hgqk,khd->qhgd", grad_scores, key_heads_split, preferred_element_type=jnp.float32
    ).reshape(sequence_length, QUERY_HEADS, HEAD_SIZE)
    key_rows_gradient = jnp.einsum(
        "hgqk,qhgd->khd", grad_scores, grouped_heads, preferred_element_type=jnp.float32
    )
    grad_qpre = (
        rotate_halves(grad_queries, -1.0)
        .reshape(sequence_length, QUERY_HEADS * HEAD_SIZE)
        .astype(jnp.bfloat16)
    )
    key_prerotate_gradient = (
        rotate_halves(key_rows_gradient, -1.0)
        .reshape(sequence_length, KEY_VALUE_HEADS * HEAD_SIZE)
        .astype(jnp.bfloat16)
    )
    query_grad = jnp.einsum(
        "td,tc->dc", normed_input, grad_qpre, preferred_element_type=jnp.float32
    )
    key_grad = jnp.einsum(
        "td,tc->dc", normed_input, key_prerotate_gradient, preferred_element_type=jnp.float32
    )
    value_grad = jnp.einsum(
        "td,tc->dc", normed_input, value_rows_gradient, preferred_element_type=jnp.float32
    )
    grad_normed = jnp.einsum("tc,dc->td", grad_qpre, query_mat, preferred_element_type=jnp.float32)
    grad_normed = grad_normed + jnp.einsum(
        "tc,dc->td", key_prerotate_gradient, key_matrix, preferred_element_type=jnp.float32
    )
    grad_normed = grad_normed + jnp.einsum(
        "tc,dc->td", value_rows_gradient, value_matrix, preferred_element_type=jnp.float32
    )
    attn_gain_grad, grad_norm_one = norm_back(grad_normed, resid_in, scale_one, attn_gain)
    grad_in = grad_hidden + grad_norm_one
    dense_terms = (
        query_grad,
        key_grad,
        value_grad,
        out_grad,
        router_grad,
        attn_gain_grad,
        moe_gain_grad,
    )
    expert_terms = (gate_grad, up_grad, down_grad)
    return (grad_in, dense_terms, expert_terms)


def add_terms(total_sum, new_terms):
    if total_sum is None:
        return new_terms
    return jax.tree.map(jnp.add, total_sum, new_terms)


def local(
    inputs,
    cotangent,
    segment_ids,
    live_first,
    routes,
    gain_attn,
    gain_moe,
    w_query,
    key_weight,
    value_weight,
    w_out,
    w_router,
    w_gate,
    w_up,
    w_down,
):
    expert_count = lax.axis_size("expert")
    section_idx = lax.axis_index("section")
    micro_count = inputs.shape[0]
    sequence_length = inputs.shape[2]
    features = inputs.shape[3]
    dense_set = (
        lax.all_gather(w_query[0], ("group", "expert"), axis=0, tiled=True),
        lax.all_gather(key_weight[0], ("group", "expert"), axis=0, tiled=True),
        lax.all_gather(value_weight[0], ("group", "expert"), axis=0, tiled=True),
        lax.all_gather(w_out[0], ("group", "expert"), axis=1, tiled=True),
        lax.all_gather(w_router[0], ("group", "expert"), axis=0, tiled=True),
        lax.all_gather(gain_attn[0], ("group", "expert"), axis=0, tiled=True),
        lax.all_gather(gain_moe[0], ("group", "expert"), axis=0, tiled=True),
    )
    expert_set = (w_gate[0], w_up[0], w_down[0])
    carried = jnp.zeros((sequence_length, features), jnp.bfloat16)
    outputs = []
    keeps = []
    for tick_num in range(micro_count + 1):
        batch_idx = jnp.clip(tick_num - section_idx, 0, micro_count - 1)
        own_in = inputs[min(tick_num, micro_count - 1), 0]
        layer_in = jnp.where(section_idx == 0, own_in, carried)
        seg_now = lax.dynamic_index_in_dim(segment_ids[:, 0], batch_idx, 0, keepdims=False)
        live_now = lax.dynamic_index_in_dim(live_first[:, 0], batch_idx, 0, keepdims=False)
        route_now = lax.dynamic_index_in_dim(routes[0, :, 0], batch_idx, 0, keepdims=False)
        layer_y, kept_vals = layer_forward(
            layer_in, dense_set, expert_set, seg_now, live_now, route_now, expert_count
        )
        sent_out = layer_y.astype(jnp.bfloat16)
        outputs.append(sent_out)
        keeps.append(kept_vals)
        if tick_num < micro_count:
            carried = passed_along(sent_out, "section", 1)
    incoming = jnp.zeros((sequence_length, features), jnp.bfloat16)
    grads_in = []
    dense_sums = None
    expert_sums = None
    for tick_num in range(micro_count + 1):
        batch_num = micro_count - tick_num - section_idx
        is_valid = (batch_num >= 0) & (batch_num < micro_count)
        own_cot = cotangent[max(micro_count - 1 - tick_num, 0), 0]
        grad_y = jnp.where(section_idx == 1, own_cot, incoming).astype(jnp.float32)
        grad_y = jnp.where(is_valid, grad_y, 0.0)
        grad_in, dense_terms, expert_terms = layer_backward(
            grad_y, keeps[micro_count - tick_num], dense_set, expert_set, expert_count
        )
        grads_in.append(grad_in)
        if tick_num < micro_count:
            incoming = passed_along(grad_in.astype(jnp.bfloat16), "section", -1)
        dense_sums = add_terms(dense_sums, tuple(dense_terms))
        expert_sums = add_terms(expert_sums, tuple(expert_terms))
    query_total, key_total, value_total, out_total, router_total, attn_total, moe_total = dense_sums
    gate_total, up_total, down_total = expert_sums
    dense_final = (
        lax.psum_scatter(query_total, ("group", "expert"), scatter_dimension=0, tiled=True),
        lax.psum_scatter(key_total, ("group", "expert"), scatter_dimension=0, tiled=True),
        lax.psum_scatter(value_total, ("group", "expert"), scatter_dimension=0, tiled=True),
        lax.psum_scatter(out_total, ("group", "expert"), scatter_dimension=1, tiled=True),
        lax.psum_scatter(router_total, ("group", "expert"), scatter_dimension=0, tiled=True),
        lax.psum_scatter(attn_total, ("group", "expert"), scatter_dimension=0, tiled=True),
        lax.psum_scatter(moe_total, ("group", "expert"), scatter_dimension=0, tiled=True),
    )
    expert_final = (
        lax.psum_scatter(
            gate_total.astype(jnp.bfloat16), "group", scatter_dimension=1, tiled=True
        ).astype(jnp.float32),
        lax.psum_scatter(
            up_total.astype(jnp.bfloat16), "group", scatter_dimension=1, tiled=True
        ).astype(jnp.float32),
        lax.psum_scatter(
            down_total.astype(jnp.bfloat16), "group", scatter_dimension=2, tiled=True
        ).astype(jnp.float32),
    )
    query_grad, key_grad, value_grad, out_grad, router_grad, attn_gain_grad, moe_gain_grad = (
        dense_final
    )
    gate_grad, up_grad, down_grad = expert_final
    layer_stack = jnp.stack(
        [
            jnp.where(section_idx == 0, outputs[index_num], outputs[index_num + 1])
            for index_num in range(micro_count)
        ]
    )
    grad_stack = jnp.stack(
        [
            jnp.where(
                section_idx == 0,
                grads_in[micro_count - index_num],
                grads_in[micro_count - 1 - index_num],
            )
            for index_num in range(micro_count)
        ]
    )
    return (
        layer_stack[None, :, None],
        grad_stack[None, :, None],
        attn_gain_grad[None],
        moe_gain_grad[None],
        query_grad[None],
        key_grad[None],
        value_grad[None],
        out_grad[None],
        router_grad[None],
        gate_grad[None],
        up_grad[None],
        down_grad[None],
    )


def solution(mesh):
    return jax.shard_map(
        local,
        mesh=mesh,
        in_specs=(
            P(None, ("group", "expert"), None, None),
            P(None, ("group", "expert"), None, None),
            P(None, ("group", "expert"), None),
            P(None, ("group", "expert"), None),
            P("section", None, ("group", "expert"), None, None),
            P("section", ("group", "expert")),
            P("section", ("group", "expert")),
            P("section", ("group", "expert"), None),
            P("section", ("group", "expert"), None),
            P("section", ("group", "expert"), None),
            P("section", None, ("group", "expert")),
            P("section", ("group", "expert"), None),
            P("section", "expert", None, None),
            P("section", "expert", None, None),
            P("section", "expert", None, None),
        ),
        out_specs=(
            P("section", None, ("group", "expert"), None, None),
            P("section", None, ("group", "expert"), None, None),
            P("section", ("group", "expert")),
            P("section", ("group", "expert")),
            P("section", ("group", "expert"), None),
            P("section", ("group", "expert"), None),
            P("section", ("group", "expert"), None),
            P("section", None, ("group", "expert")),
            P("section", ("group", "expert"), None),
            P("section", "expert", "group", None),
            P("section", "expert", "group", None),
            P("section", "expert", None, "group"),
        ),
        check_vma=False,
    )
```

profile of v0, /device:TPU:0, one launch (start us, length us, event | category | flops | bytes accessed | tf_op | source)
XLA Modules:
  0.0 2277.6 jit_solution(14642610668785040874)
XLA Ops:
  15.4 36.5 %all-reduce.5 = (bf16[1536]{0:T(1024)(128)(2,1)S(1)}, bf16[1536]{0:T(1024)(128)(2,1)S(1)}) all-reduce(bf16[1536]{0:T(1024)(128)(2,1)S(1)} %dynamic-update-slice, bf16[1536]{0:T(1024)(128)(2,1)S(1)} %dynamic-update-slice.1), channel_id=2, replica_groups=mesh['section'=2,'group'=4,'expert'=4] {'group','expert'}, use_global_device_ids=true, to_apply=%add | all-reduce | flops 3072 | bytes 12288
  65.8 28.2 %all-gather.14.cloned.1.call-done = bf16[1,1536,512]{2,1,0:T(8,128)(2,1)} async-done(((bf16[1,96,512]{2,1,0:T(8,128)(2,1)}), bf16[1,1536,512]{2,1,0:T(8,128)(2,1)}) %all-gather.14.cloned.1.call-update) | async-done | bytes 1572880 | tf_op jit(solution)/shard_map/all_gather | solution.py:371
  99.4 49.2 %all-gather.16.cloned.1.call-done = bf16[1,1536,1536]{2,1,0:T(8,128)(2,1)} async-done(((bf16[1,96,1536]{2,1,0:T(8,128)(2,1)}), bf16[1,1536,1536]{2,1,0:T(8,128)(2,1)}) %all-gather.16.cloned.1.call-update) | async-done | bytes 4718608 | tf_op jit(solution)/shard_map/all_gather | solution.py:370
  162.2 40.6 %all-gather.18.cloned.1.call-done = bf16[1,1536,1536]{1,2,0:T(8,128)(2,1)} async-done(((bf16[1,1536,96]{1,2,0:T(8,128)(2,1)}), bf16[1,1536,1536]{1,2,0:T(8,128)(2,1)}) %all-gather.18.cloned.1.call-update) | async-done | bytes 4718608 | tf_op jit(solution)/shard_map/all_gather | solution.py:373
  218.7 91.2 %all_to_all.60 = bf16[5,4,64,1536]{3,2,0,1:T(8,128)(2,1)S(1)} all-to-all(bf16[5,4,64,1536]{3,2,0,1:T(8,128)(2,1)S(1)} %copy.408), channel_id=1, replica_groups=mesh['section'=2,'group'=4,'expert'=4] {'expert'}, dimensions={1} | all-to-all | bytes 7864320 | tf_op jit(solution)/shard_map/all_to_all | solution.py:148
  328.9 118.7 %all-gather.6 = bf16[1,1536,20]{2,0,1:T(2,128)(2,1)S(1)} all-gather(bf16[1,96,20]{2,0,1:T(2,128)(2,1)S(1)} %copy.398), channel_id=8, replica_groups=mesh['section'=2,'group'=4,'expert'=4] {'group','expert'}, dimensions={1}, use_global_device_ids=true | all-gather | bytes 65280 | tf_op jit(solution)/shard_map/all_gather | solution.py:374
  514.3 91.8 %all_to_all.61 = bf16[5,4,64,1536]{3,2,0,1:T(8,128)(2,1)S(1)} all-to-all(bf16[5,4,64,1536]{3,2,0,1:T(8,128)(2,1)S(1)} %copy.424), channel_id=1, replica_groups=mesh['section'=2,'group'=4,'expert'=4] {'expert'}, dimensions={1} | all-to-all | bytes 7864320 | tf_op jit(solution)/shard_map/all_to_all | solution.py:148
  625.6 85.6 %all-to-all-done.3 = bf16[5,4,64,1536]{3,2,0,1:T(8,128)(2,1)} async-done(((bf16[5,4,64,1536]{3,2,0,1:T(8,128)(2,1)}), bf16[5,4,64,1536]{3,2,0,1:T(8,128)(2,1)}, u32[]{:S(2)}, u32[]{:S(2)}) %all-to-all-start.3) | async-done | bytes 3932192 | tf_op jit(solution)/shard_map/all_to_all | solution.py:157
  715.6 9.9 gather_fusion.1
  797.8 73.5 %all-to-all-done.6 = bf16[5,4,64,1536]{3,2,0,1:T(8,128)(2,1)} async-done(((bf16[5,4,64,1536]{3,2,0,1:T(8,128)(2,1)}), bf16[5,4,64,1536]{3,2,0,1:T(8,128)(2,1)}, u32[]{:S(2)}, u32[]{:S(2)}) %all-to-all-start.6) | async-done | bytes 3932192 | tf_op jit(solution)/shard_map/all_to_all | solution.py:221
  887.4 75.8 %all-to-all-done.4 = bf16[5,4,64,1536]{3,2,0,1:T(8,128)(2,1)} async-done(((bf16[5,4,64,1536]{3,2,0,1:T(8,128)(2,1)}), bf16[5,4,64,1536]{3,2,0,1:T(8,128)(2,1)}, u32[]{:S(2)}, u32[]{:S(2)}) %all-to-all-start.4) | async-done | bytes 3932192 | tf_op jit(solution)/shard_map/all_to_all | solution.py:148
  1010.3 67.7 %all-to-all-done.5 = bf16[5,4,64,1536]{3,2,0,1:T(8,128)(2,1)} async-done(((bf16[5,4,64,1536]{3,2,0,1:T(8,128)(2,1)}), bf16[5,4,64,1536]{3,2,0,1:T(8,128)(2,1)}, u32[]{:S(2)}, u32[]{:S(2)}) %all-to-all-start.5) | async-done | bytes 3932192 | tf_op jit(solution)/shard_map/all_to_all | solution.py:157
  1089.9 10.0 gather_fusion.2
  1104.9 65.1 %all-to-all-done.7 = bf16[5,4,64,1536]{3,2,0,1:T(8,128)(2,1)} async-done(((bf16[5,4,64,1536]{3,2,0,1:T(8,128)(2,1)}), bf16[5,4,64,1536]{3,2,0,1:T(8,128)(2,1)}, u32[]{:S(2)}, u32[]{:S(2)}) %all-to-all-start.7) | async-done | bytes 3932192 | tf_op jit(solution)/shard_map/all_to_all | solution.py:246
  1174.4 10.2 gather_fusion.3
  1252.9 88.8 %all_to_all.62 = bf16[5,4,64,1536]{3,2,0,1:T(8,128)(2,1)S(1)} all-to-all(bf16[5,4,64,1536]{3,2,0,1:T(8,128)(2,1)S(1)} %copy.456), channel_id=1, replica_groups=mesh['section'=2,'group'=4,'expert'=4] {'expert'}, dimensions={1} | all-to-all | bytes 7864320 | tf_op jit(solution)/shard_map/all_to_all | solution.py:221
  1378.3 82.8 %all-to-all-done.9 = bf16[5,4,64,1536]{3,2,0,1:T(8,128)(2,1)} async-done(((bf16[5,4,64,1536]{3,2,0,1:T(8,128)(2,1)}), bf16[5,4,64,1536]{3,2,0,1:T(8,128)(2,1)}, u32[]{:S(2)}, u32[]{:S(2)}) %all-to-all-start.9) | async-done | bytes 3932192 | tf_op jit(solution)/shard_map/all_to_all | solution.py:246
  1510.9 10.6 collective-permute-done.3
  1539.6 10.4 fusion.366
  1560.6 68.3 %all-to-all-done.10 = bf16[5,4,64,1536]{3,2,0,1:T(8,128)(2,1)} async-done(((bf16[5,4,64,1536]{3,2,0,1:T(8,128)(2,1)}), bf16[5,4,64,1536]{3,2,0,1:T(8,128)(2,1)}, u32[]{:S(2)}, u32[]{:S(2)}) %all-to-all-start.10) | async-done | bytes 3932192 | tf_op jit(solution)/shard_map/all_to_all | solution.py:221
  1633.3 16.2 add_convert_fusion
  1649.5 15.7 copy.528
  1665.2 12.9 copy.533
  1679.4 12.3 fusion.362
  1707.8 16.4 add_convert_fusion.2
  1725.6 10.0 fusion.364
  1743.2 17.5 add_convert_fusion.1
  1789.9 82.8 %all-to-all-done.11 = bf16[5,4,64,1536]{3,2,0,1:T(8,128)(2,1)} async-done(((bf16[5,4,64,1536]{3,2,0,1:T(8,128)(2,1)}), bf16[5,4,64,1536]{3,2,0,1:T(8,128)(2,1)}, u32[]{:S(2)}, u32[]{:S(2)}) %all-to-all-start.11) | async-done | bytes 3932192 | tf_op jit(solution)/shard_map/all_to_all | solution.py:246
  1877.2 9.9 gather_fusion.5
  1956.7 58.8 %all-reduce.4 = (f32[1536]{0:T(1024)S(1)}, f32[1536]{0:T(1024)S(1)}) all-reduce(f32[1536]{0:T(1024)S(1)} %add_add_fusion.1, f32[1536]{0:T(1024)S(1)} %add_add_fusion), channel_id=9, replica_groups=mesh['section'=2,'group'=4,'expert'=4] {'group','expert'}, use_global_device_ids=true, to_apply=%region_63.64.clone | all-reduce | flops 3072 | bytes 24576
  2039.2 115.1 %reduce-scatter.13.cloned.1.call-done = f32[96,1536]{1,0:T(8,128)} async-done(((f32[1536,1536]{1,0:T(8,128)}), f32[96,1536]{1,0:T(8,128)}) %reduce-scatter.13.cloned.1.call-update) | async-done | bytes 589840 | tf_op jit(solution)/shard_map/reduce_scatter | solution.py:418
  2154.3 116.2 %reduce-scatter.19.cloned.1.call-done = f32[1536,96]{0,1:T(8,128)} async-done(((f32[1536,1536]{0,1:T(8,128)}), f32[1536,96]{0,1:T(8,128)}) %reduce-scatter.19.cloned.1.call-update) | async-done | bytes 589840 | tf_op jit(solution)/shard_map/reduce_scatter | solution.py:421
  (831 shorter events, 660.1 us)
Async XLA Ops:
  7.2 56.9 %all-gather.12.cloned.1.call-start = ((), (), s32[]{:S(2)}) async-start(), calls=%async_computation.26 | async-start | bytes 1671168 | tf_op jit(solution)/shard_map/all_gather | solution.py:372
  7.9 86.1 %all-gather.14.cloned.1.call-start = ((), (), s32[]{:S(2)}) async-start(), calls=%async_computation.27 | async-start | bytes 1671168 | tf_op jit(solution)/shard_map/all_gather | solution.py:371
  8.7 140.0 %all-gather.16.cloned.1.call-start = ((), (), s32[]{:S(2)}) async-start(), calls=%async_computation.28 | async-start | bytes 5013504 | tf_op jit(solution)/shard_map/all_gather | solution.py:370
  9.4 193.4 %all-gather.18.cloned.1.call-start = ((), (), s32[]{:S(2)}) async-start(), calls=%async_computation.29 | async-start | bytes 5013504 | tf_op jit(solution)/shard_map/all_gather | solution.py:373
  11.4 450.2 %copy-start.119 = (s32[1,1,1,128,8]{3,4,2,1,0:T(8,128)}, s32[1,1,1,128,8]{3,4,2,1,0:T(8,128)S(1)}, u32[]{:S(2)}) copy-start(s32[1,1,1,128,8]{3,4,2,1,0:T(8,128)S(1)} %get-tuple-element.109) | copy-start | bytes 12292
  11.4 451.1 %copy-start.121 = (s32[1,1,1,128,8]{3,4,2,1,0:T(8,128)}, s32[1,1,1,128,8]{3,4,2,1,0:T(8,128)S(1)}, u32[]{:S(2)}) copy-start(s32[1,1,1,128,8]{3,4,2,1,0:T(8,128)S(1)} %get-tuple-element.152) | copy-start | bytes 12292
  11.4 612.9 %copy-start.123 = (s32[1,1,1,128,8]{3,4,2,1,0:T(8,128)}, s32[1,1,1,128,8]{3,4,2,1,0:T(8,128)S(1)}, u32[]{:S(2)}) copy-start(s32[1,1,1,128,8]{3,4,2,1,0:T(8,128)S(1)} %get-tuple-element.154) | copy-start | bytes 12292
  59.9 1420.7 %copy-start.99 = (f32[1536]{0:T(1024)}, f32[1536]{0:T(1024)S(1)}, u32[]{:S(2)}) copy-start(f32[1536]{0:T(1024)S(1)} %convert_element_type.528) | copy-start | bytes 18436
  63.3 435.1 %copy-start.80 = (f32[128,32]{0,1:T(8,128)}, f32[128,32]{0,1:T(8,128)S(1)}, u32[]{:S(2)}) copy-start(f32[128,32]{0,1:T(8,128)S(1)} %get-tuple-element.175) | copy-start | bytes 49156
  63.3 435.1 %copy-start.104 = (f32[128,32]{0,1:T(8,128)}, f32[128,32]{0,1:T(8,128)S(1)}, u32[]{:S(2)}) copy-start(f32[128,32]{0,1:T(8,128)S(1)} %get-tuple-element.174) | copy-start | bytes 49156
  322.9 139.8 %all-to-all-start.1 = ((bf16[5,4,64,1536]{3,2,0,1:T(8,128)(2,1)}), bf16[5,4,64,1536]{3,2,0,1:T(8,128)(2,1)}, u32[]{:S(2)}, u32[]{:S(2)}) async-start(bf16[5,4,64,1536]{3,2,0,1:T(8,128)(2,1)} %copy.410), calls=%async_computation.1 | async-start | bytes 7864320 | tf_op jit(solution)/shard_map/all_to_all | solution.py:157
  480.2 9.0 collective-permute-start
  619.2 92.0 %all-to-all-start.3 = ((bf16[5,4,64,1536]{3,2,0,1:T(8,128)(2,1)}), bf16[5,4,64,1536]{3,2,0,1:T(8,128)(2,1)}, u32[]{:S(2)}, u32[]{:S(2)}) async-start(bf16[5,4,64,1536]{3,2,0,1:T(8,128)(2,1)} %copy.426), calls=%async_computation.3 | async-start | bytes 7864320 | tf_op jit(solution)/shard_map/all_to_all | solution.py:157
  732.4 10.8 collective-permute-start.1
  743.4 481.8 %copy-start.7 = (bf16[128,1536]{1,0:T(8,128)(2,1)}, bf16[128,1536]{1,0:T(8,128)(2,1)S(1)}, u32[]{:S(2)}) copy-start(bf16[128,1536]{1,0:T(8,128)(2,1)S(1)} %get-tuple-element.111) | copy-start | bytes 1179652
  779.9 91.4 %all-to-all-start.6 = ((bf16[5,4,64,1536]{3,2,0,1:T(8,128)(2,1)}), bf16[5,4,64,1536]{3,2,0,1:T(8,128)(2,1)}, u32[]{:S(2)}, u32[]{:S(2)}) async-start(bf16[5,4,64,1536]{3,2,0,1:T(8,128)(2,1)} %copy.445), calls=%async_computation.6 | async-start | bytes 7864320 | tf_op jit(solution)/shard_map/all_to_all | solution.py:221
  871.3 91.9 %all-to-all-start.4 = ((bf16[5,4,64,1536]{3,2,0,1:T(8,128)(2,1)}), bf16[5,4,64,1536]{3,2,0,1:T(8,128)(2,1)}, u32[]{:S(2)}, u32[]{:S(2)}) async-start(bf16[5,4,64,1536]{3,2,0,1:T(8,128)(2,1)} %copy.440), calls=%async_computation.4 | async-start | bytes 7864320 | tf_op jit(solution)/shard_map/all_to_all | solution.py:148
  986.0 92.1 %all-to-all-start.5 = ((bf16[5,4,64,1536]{3,2,0,1:T(8,128)(2,1)}), bf16[5,4,64,1536]{3,2,0,1:T(8,128)(2,1)}, u32[]{:S(2)}, u32[]{:S(2)}) async-start(bf16[5,4,64,1536]{3,2,0,1:T(8,128)(2,1)} %copy.442), calls=%async_computation.5 | async-start | bytes 7864320 | tf_op jit(solution)/shard_map/all_to_all | solution.py:157
  1078.1 91.9 %all-to-all-start.7 = ((bf16[5,4,64,1536]{3,2,0,1:T(8,128)(2,1)}), bf16[5,4,64,1536]{3,2,0,1:T(8,128)(2,1)}, u32[]{:S(2)}, u32[]{:S(2)}) async-start(bf16[5,4,64,1536]{3,2,0,1:T(8,128)(2,1)} %copy.447), calls=%async_computation.7 | async-start | bytes 7864320 | tf_op jit(solution)/shard_map/all_to_all | solution.py:246
  1226.7 12.3 collective-permute-start.2
  1369.6 91.6 %all-to-all-start.9 = ((bf16[5,4,64,1536]{3,2,0,1:T(8,128)(2,1)}), bf16[5,4,64,1536]{3,2,0,1:T(8,128)(2,1)}, u32[]{:S(2)}, u32[]{:S(2)}) async-start(bf16[5,4,64,1536]{3,2,0,1:T(8,128)(2,1)} %copy.458), calls=%async_computation.9 | async-start | bytes 7864320 | tf_op jit(solution)/shard_map/all_to_all | solution.py:246
  1509.5 12.0 collective-permute-start.3
  1534.7 94.2 %all-to-all-start.10 = ((bf16[5,4,64,1536]{3,2,0,1:T(8,128)(2,1)}), bf16[5,4,64,1536]{3,2,0,1:T(8,128)(2,1)}, u32[]{:S(2)}, u32[]{:S(2)}) async-start(bf16[5,4,64,1536]{3,2,0,1:T(8,128)(2,1)} %copy.467), calls=%async_computation.10 | async-start | bytes 7864320 | tf_op jit(solution)/shard_map/all_to_all | solution.py:221
  1539.5 407.6 %reduce-scatter.25.cloned.1.call-start = ((), (), s32[]{:S(2)}) async-start(), calls=%async_computation.30 | async-start | bytes 835584
  1560.5 459.0 %reduce-scatter.27.cloned.1.call-start = ((), (), s32[]{:S(2)}) async-start(), calls=%async_computation.31 | async-start | bytes 9830400
  1678.1 352.5 %reduce-scatter.21.cloned.1.call-start = ((), (), s32[]{:S(2)}) async-start(), calls=%async_computation.24 | async-start | bytes 9830400 | tf_op jit(solution)/shard_map/reduce_scatter | solution.py:427
  1724.3 310.3 %reduce-scatter.23.cloned.1.call-start = ((), (), s32[]{:S(2)}) async-start(), calls=%async_computation.25 | async-start | bytes 9830400 | tf_op jit(solution)/shard_map/reduce_scatter | solution.py:430
  1781.4 91.4 %all-to-all-start.11 = ((bf16[5,4,64,1536]{3,2,0,1:T(8,128)(2,1)}), bf16[5,4,64,1536]{3,2,0,1:T(8,128)(2,1)}, u32[]{:S(2)}, u32[]{:S(2)}) async-start(bf16[5,4,64,1536]{3,2,0,1:T(8,128)(2,1)} %copy.469), calls=%async_computation.11 | async-start | bytes 7864320 | tf_op jit(solution)/shard_map/all_to_all | solution.py:246
  1786.4 252.3 %reduce-scatter.15.cloned.1.call-start = ((), (), s32[]{:S(2)}) async-start(), calls=%async_computation.21 | async-start | bytes 3342336 | tf_op jit(solution)/shard_map/reduce_scatter | solution.py:419
  1905.9 133.3 %reduce-scatter.17.cloned.1.call-start = ((), (), s32[]{:S(2)}) async-start(), calls=%async_computation.22 | async-start | bytes 3342336 | tf_op jit(solution)/shard_map/reduce_scatter | solution.py:420
  1912.0 242.3 %reduce-scatter.13.cloned.1.call-start = ((), (), s32[]{:S(2)}) async-start(), calls=%async_computation.20 | async-start | bytes 10027008 | tf_op jit(solution)/shard_map/reduce_scatter | solution.py:418
  1932.3 338.2 %reduce-scatter.19.cloned.1.call-start = ((), (), s32[]{:S(2)}) async-start(), calls=%async_computation.23 | async-start | bytes 10027008 | tf_op jit(solution)/shard_map/reduce_scatter | solution.py:421
  (217 other events, 3657.3 us)
Sparse Core Ops, SparseCore 0:
  10.3 42.7 all-gather.11
  55.4 38.5 all-gather.13
  96.3 52.2 all-gather.15
  150.8 51.9 all-gather.17
  1560.6 84.1 reduce-scatter.24
  1678.2 66.2 reduce-scatter.26
  1747.0 68.9 reduce-scatter.20
  1818.8 68.9 reduce-scatter.22
  1906.0 63.4 reduce-scatter.14
  1973.8 65.4 reduce-scatter.16
  2043.9 110.3 reduce-scatter.12
  2159.4 111.1 reduce-scatter.18
where the time goes:
time: 2290 us; the launch traced here: 2280 us
  waiting for transfers between devices  981 us (43%)
  blocking collectives  486 us (21%)
  matrix products  348 us (15%)
  local copies, waits for them, and re-layouts  259 us (11%)
  other arithmetic  128 us (6%)
  starting transfers between devices  56.3 us (2%)
    all_to_all x3, waiting for transfers between devices, layer_backward(): lax.all_to_all(grad_rows_in, 'expert', split_axis=1, concat_axis=1, tiled...  231 us
    all_to_all x2, blocking collectives, layer_forward(): lax.all_to_all(send_rows, 'expert', split_axis=1, concat_axis=1, tiled=True)  183 us
    all_to_all x3, waiting for transfers between devices, layer_forward(): lax.all_to_all(produced, 'expert', split_axis=1, concat_axis=1, tiled=True)  153 us
    all_to_all x2, waiting for transfers between devices, layer_backward(): lax.all_to_all(grad_send, 'expert', split_axis=1, concat_axis=1, tiled=True)  142 us
    all_gather x1, blocking collectives, local(): lax.all_gather(w_router[0], ('group', 'expert'), axis=0, tiled=True)  119 us
    reduce_scatter x1, waiting for transfers between devices, local(): lax.psum_scatter(out_total, ('group', 'expert'), scatter_dimension=1, til...  116 us
    reduce_scatter x1, waiting for transfers between devices, local(): lax.psum_scatter(query_total, ('group', 'expert'), scatter_dimension=0, t...  115 us
    unnamed x2, blocking collectives  95.3 us
  transfers between devices with their start and end apart: 25, of which 18 were waited for; matrix products, arithmetic and copies ran while one was open for 17% of the time, Pallas kernels for 0%

commit v1 on v0

v1 whole, which is shorter than its diff:
```python
import functools

import jax
import jax.numpy as jnp
from jax import lax
from jax.experimental import pallas as pl
from jax.experimental.pallas import tpu as pltpu
from jax.sharding import PartitionSpec as P

QUERY_HEADS = 24
KEY_VALUE_HEADS = 8
HEAD_SIZE = 64
BLK = 64
EPS = 1e-06
THETA = 10000.0
NEG_FILL = -1e30
BF = jnp.bfloat16
F32 = jnp.float32
MESH = pl.DeviceIdType.MESH
LANES = 128
TILE = 512
QW = QUERY_HEADS * HEAD_SIZE
KW = KEY_VALUE_HEADS * HEAD_SIZE
QKV = QW + 2 * KW
GAIN_MOE_ROW = 126
GAIN_ATTN_ROW = 127
VMEM_LIMIT = 60 * 1024 * 1024
HEAD_PAIRS = KEY_VALUE_HEADS // 2
TILES_PER_PAIR = QUERY_HEADS // KEY_VALUE_HEADS


def dot(a, b, ca=1, cb=0):
    return lax.dot_general(a, b, (((ca,), (cb,)), ((), ())), preferred_element_type=F32)


def iota(shape, axis):
    return lax.broadcasted_iota(jnp.int32, shape, axis)


def rope(z, cos, sin, direction):
    width = z.shape[1]
    half = HEAD_SIZE // 2
    first = iota(z.shape, 1) % HEAD_SIZE < half
    partner = jnp.where(first, pltpu.roll(z, width - half, 1), pltpu.roll(z, half, 1))
    signed = jnp.where(first, -direction, direction) * partner
    reps = width // LANES
    return z * jnp.concatenate([cos] * reps, axis=1) + signed * jnp.concatenate([sin] * reps, axis=1)


def lane_masks(t):
    low = iota((t, LANES), 1) < HEAD_SIZE
    return low, jnp.logical_not(low)


def swapped(z):
    return pltpu.roll(z.astype(F32), HEAD_SIZE, 1).astype(BF)


def head_plan():
    return [(r, half, (2 * r + half) // TILES_PER_PAIR != half) for r in range(TILES_PER_PAIR) for half in range(2)]


def pick(z, half, masks):
    return jnp.where(masks[half], z, jnp.zeros_like(z))


def attn_fwd_kernel(x_ref, w_ref, cos_ref, sin_ref, meta_ref, segr_ref, qkv_ref, p_ref, o_ref, h_ref, b_ref, wrt_ref):
    t, d = x_ref.shape
    aux = jnp.transpose(w_ref[:, QKV + QW :].astype(F32))
    wrt_ref[...] = aux.astype(BF)
    gain_attn = aux[GAIN_ATTN_ROW : GAIN_ATTN_ROW + 1]
    gain_moe = aux[GAIN_MOE_ROW : GAIN_MOE_ROW + 1]
    x = x_ref[...].astype(F32)
    r1 = lax.rsqrt(jnp.mean(x * x, axis=1, keepdims=True) + EPS)
    a = (x * r1 * gain_attn).astype(BF)
    cos, sin = cos_ref[...], sin_ref[...]
    for n in range(QKV // TILE):
        cols = slice(n * TILE, (n + 1) * TILE)
        y = dot(a, w_ref[:, cols])
        if n * TILE < QW + KW:
            y = rope(y, cos, sin, 1.0)
        qkv_ref[:, cols] = y.astype(BF)
    i, j = iota((t, t), 0), iota((t, t), 1)
    allowed = (j <= i) & (meta_ref[:, 0:1] == segr_ref[0:1, :]) & (j // BLK >= meta_ref[:, 1:2])
    masks = lane_masks(t)

    def pair(m, carry):
        def lanes(base):
            return pl.ds(pl.multiple_of(base, LANES), LANES)

        kp = qkv_ref[:, lanes(QW + m * LANES)]
        vp = qkv_ref[:, lanes(QW + KW + m * LANES)]
        ks, vs = swapped(kp), swapped(vp)
        parts = {}
        for r, half, swap in head_plan():
            q = pick(qkv_ref[:, lanes((m * TILES_PER_PAIR + r) * LANES)], half, masks)
            s = dot(q, ks if swap else kp, 1, 1) * HEAD_SIZE ** (-0.5)
            s = jnp.where(allowed, s, NEG_FILL)
            e = jnp.exp(s - jnp.max(s, axis=1, keepdims=True))
            p = e / jnp.sum(e, axis=1, keepdims=True)
            p_ref[m * 2 * TILES_PER_PAIR + 2 * r + half] = p
            part = dot(p.astype(BF), pick(vs if swap else vp, half, masks))
            parts[half] = part
            if half == 1:
                o_ref[:, lanes((m * TILES_PER_PAIR + r) * LANES)] = (parts[0] + parts[1]).astype(BF)
        return carry

    lax.fori_loop(0, HEAD_PAIRS, pair, 0)
    o = o_ref[...]
    for n in range(d // TILE):
        rows = slice(n * TILE, (n + 1) * TILE)
        h_ref[:, rows] = x_ref[:, rows].astype(F32) + dot(o, w_ref[rows, QKV : QKV + QW], 1, 1)
    h = h_ref[...]
    r2 = lax.rsqrt(jnp.mean(h * h, axis=1, keepdims=True) + EPS)
    b_ref[...] = (h * r2 * gain_moe).astype(BF)


def vmem(n):
    return [pl.BlockSpec(memory_space=pltpu.VMEM)] * n


def attn_fwd(x, w, cos, sin, meta, segr):
    t, d = x.shape
    sds = jax.ShapeDtypeStruct
    return pl.pallas_call(
        attn_fwd_kernel,
        out_shape=(
            sds((t, QKV), BF),
            sds((QUERY_HEADS, t, t), F32),
            sds((t, QW), BF),
            sds((t, d), F32),
            sds((t, d), BF),
            sds((LANES, d), BF),
        ),
        in_specs=vmem(6),
        out_specs=tuple(vmem(6)),
        compiler_params=pltpu.CompilerParams(vmem_limit_bytes=VMEM_LIMIT),
        cost_estimate=pl.CostEstimate(flops=2 * t * d * 4096, bytes_accessed=w.size * 2, transcendentals=QUERY_HEADS * t * t),
    )(x, w, cos, sin, meta, segr)


def gates_of(rt, wrt, b, e_pad):
    t = rt.shape[1]
    experts = iota((e_pad, t), 0)
    chosen = experts == rt[0:1]
    for k in range(1, rt.shape[0]):
        chosen = chosen | (experts == rt[k : k + 1])
    logits = jnp.where(chosen, dot(wrt[0:e_pad], b, 1, 1), NEG_FILL)
    e = jnp.where(chosen, jnp.exp(logits - jnp.max(logits, axis=0, keepdims=True)), 0.0)
    return e / jnp.sum(e, axis=0, keepdims=True)


def attn_bwd_kernel(
    e_pad, gy_ref, h_ref, x_ref, w_ref, qkv_ref, p_ref, o_ref, b_ref, wrt_ref, back_ref, dg_ref, rt_ref, cos_ref, sin_ref,
    dx_ref, dd_ref, do_ref, dqkv_ref, dh_ref, lt_ref,
):
    t, d = x_ref.shape
    gain_attn = wrt_ref[GAIN_ATTN_ROW - 7 :, :].astype(F32)[7:8]
    gain_moe = wrt_ref[GAIN_ATTN_ROW - 7 :, :].astype(F32)[6:7]
    b = b_ref[...]
    gates = gates_of(rt_ref[...], wrt_ref, b, e_pad)
    dg = dg_ref[...]
    dl = (gates * (dg - jnp.sum(gates * dg, axis=0, keepdims=True)))
    dlb = dl.astype(BF)
    db = dot(dlb, wrt_ref[0:e_pad, :], 0, 0)
    for z in range(back_ref.shape[0]):
        db = db + back_ref[z].astype(F32)
    h = h_ref[...]
    r2 = lax.rsqrt(jnp.mean(h * h, axis=1, keepdims=True) + EPS)
    grad_moe = jnp.sum(db * h * r2, axis=0, keepdims=True)
    dn = db * gain_moe
    dh = gy_ref[...].astype(F32) + r2 * dn - h * (r2 * r2 * r2) * jnp.mean(dn * h, axis=1, keepdims=True)
    dh_ref[...] = dh
    dhb = dh.astype(BF)
    for n in range(QW // TILE):
        cols = slice(n * TILE, (n + 1) * TILE)
        do_ref[:, cols] = dot(dhb, w_ref[:, QKV + n * TILE : QKV + (n + 1) * TILE]).astype(BF)
    masks = lane_masks(t)
    cos, sin = cos_ref[...], sin_ref[...]

    def pair(m, carry):
        def lanes(base):
            return pl.ds(pl.multiple_of(base, LANES), LANES)

        kp = qkv_ref[:, lanes(QW + m * LANES)]
        vp = qkv_ref[:, lanes(QW + KW + m * LANES)]
        ks, vs = swapped(kp), swapped(vp)
        zero = jnp.zeros((t, LANES), F32)
        dk = {False: zero, True: zero}
        dv = {False: zero, True: zero}
        dq = zero
        for r, half, swap in head_plan():
            tile = lanes((m * TILES_PER_PAIR + r) * LANES)
            q = pick(qkv_ref[:, tile], half, masks)
            do = pick(do_ref[:, tile], half, masks)
            p = p_ref[m * 2 * TILES_PER_PAIR + 2 * r + half]
            dp = dot(do, vs if swap else vp, 1, 1)
            dv[swap] = dv[swap] + dot(p.astype(BF), do, 0, 0)
            dt = p * (dp - jnp.sum(p * dp, axis=1, keepdims=True)) * HEAD_SIZE ** (-0.5)
            dt = dt.astype(BF)
            dk[swap] = dk[swap] + dot(dt, q, 0, 0)
            part = dot(dt, pick(ks if swap else kp, half, masks))
            dq = part if half == 0 else dq + part
            if half == 1:
                dqkv_ref[:, tile] = rope(dq, cos, sin, -1.0).astype(BF)
        dk_all = dk[False] + pltpu.roll(dk[True], HEAD_SIZE, 1)
        dv_all = dv[False] + pltpu.roll(dv[True], HEAD_SIZE, 1)
        dqkv_ref[:, lanes(QW + m * LANES)] = rope(dk_all, cos, sin, -1.0).astype(BF)
        dqkv_ref[:, lanes(QW + KW + m * LANES)] = dv_all.astype(BF)
        return carry

    lax.fori_loop(0, HEAD_PAIRS, pair, 0)
    x = x_ref[...].astype(F32)
    r1 = lax.rsqrt(jnp.mean(x * x, axis=1, keepdims=True) + EPS)
    dqkv = dqkv_ref[...]
    for n in range(d // TILE):
        rows = slice(n * TILE, (n + 1) * TILE)
        dx_ref[:, rows] = dot(dqkv, w_ref[rows, 0:QKV], 1, 1)
    da = dx_ref[...]
    grad_attn = jnp.sum(da * x * r1, axis=0, keepdims=True)
    dag = da * gain_attn
    dx_ref[...] = dh_ref[...] + r1 * dag - x * (r1 * r1 * r1) * jnp.mean(dag * x, axis=1, keepdims=True)
    lt_ref[...] = jnp.transpose(x * r1 * gain_attn).astype(BF)
    for n in range(QKV // TILE):
        cols = slice(n * TILE, (n + 1) * TILE)
        dd_ref[:, cols] = dot(lt_ref[...], dqkv_ref[:, cols]).astype(BF)
    lt_ref[...] = jnp.transpose(dh_ref[...]).astype(BF)
    for n in range(QW // TILE):
        cols = slice(n * TILE, (n + 1) * TILE)
        dd_ref[:, QKV + n * TILE : QKV + (n + 1) * TILE] = dot(lt_ref[...], o_ref[:, cols]).astype(BF)
    lt_ref[...] = jnp.transpose(b_ref[...].astype(F32)).astype(BF)
    row = iota((LANES, d), 0)
    grads = jnp.where(row == GAIN_MOE_ROW, grad_moe, jnp.where(row == GAIN_ATTN_ROW, grad_attn, 0.0))
    dl_full = jnp.concatenate([dl, jnp.zeros((LANES - e_pad, t), F32)], axis=0)
    dl_rows = jnp.transpose(dl_full).astype(BF)
    dd_ref[:, QKV + QW :] = (dot(lt_ref[...], dl_rows) + jnp.transpose(grads)).astype(BF)


def attn_bwd(gy, h, x, w, qkv, p, o, b, wrt, back, dg, rt, cos, sin):
    t, d = x.shape
    sds = jax.ShapeDtypeStruct
    return pl.pallas_call(
        functools.partial(attn_bwd_kernel, dg.shape[0]),
        out_shape=(sds((t, d), F32), sds(w.shape, BF)),
        in_specs=vmem(14),
        out_specs=tuple(vmem(2)),
        scratch_shapes=[
            pltpu.VMEM((t, QW), BF),
            pltpu.VMEM((t, QKV), BF),
            pltpu.VMEM((t, d), F32),
            pltpu.VMEM((d, t), BF),
        ],
        compiler_params=pltpu.CompilerParams(vmem_limit_bytes=VMEM_LIMIT),
        cost_estimate=pl.CostEstimate(flops=4 * t * d * 4096, bytes_accessed=w.size * 4, transcendentals=0),
    )(gy, h, x, w, qkv, p, o, b, wrt, back, dg, rt, cos, sin)


def one_hot(pos_row, cap):
    return jnp.where(iota((cap, pos_row.shape[1]), 0) == pos_row, 1.0, 0.0)


def all_hots(pos, per, cap):
    return jnp.concatenate([one_hot(pos[j : j + 1], cap) for j in range(per)], axis=0)


def slots_of(rt, first, per):
    t = rt.shape[1]
    experts = iota((16, t), 0)
    mine = jnp.where(experts < per, experts + first, -1)
    chosen = mine == rt[0:1]
    for k in range(1, rt.shape[0]):
        chosen = chosen | (mine == rt[k : k + 1])
    earlier = jnp.where(iota((t, t), 0) < iota((t, t), 1), 1.0, 0.0).astype(BF)
    before = dot(jnp.where(chosen, 1.0, 0.0).astype(BF), earlier)
    return jnp.where(chosen, before.astype(jnp.int32), -1)[0:8]


def streamed(count, copies, body):
    for c in copies(0, 0):
        c.start()

    def step(b, carry):
        slot = lax.rem(b, 2)

        @pl.when(b + 1 < count)
        def _():
            for c in copies(b + 1, lax.rem(b + 1, 2)):
                c.start()

        for c in copies(b, slot):
            c.wait()
        body(b, slot)
        return carry

    lax.fori_loop(0, count, step, 0)


def combine(count, per, cap, pos_ref, rows_ref, out_hbm, obuf, osem):
    def copy(b, slot):
        return pltpu.make_async_copy(obuf.at[slot], out_hbm.at[b], osem.at[slot])

    def step(b, carry):
        slot = lax.rem(b, 2)

        @pl.when(b >= 2)
        def _():
            copy(b - 2, slot).wait()

        back = jnp.transpose(all_hots(pos_ref[b], per, cap)).astype(BF)
        at = pl.ds(pl.multiple_of(b * cap, cap), cap)
        rows = jnp.concatenate([rows_ref[j, at, :] for j in range(per)], axis=0)
        obuf[slot] = dot(back, rows).astype(BF)
        copy(b, slot).start()
        return carry

    lax.fori_loop(0, count, step, 0)
    copy(count - 2, (count - 2) % 2).wait()
    copy(count - 1, (count - 1) % 2).wait()


def chunk_gates(c, j, chunk, cap, pos_ref, gate_ref):
    hots, gates = [], []
    for bb in range(chunk // cap):
        b = c * (chunk // cap) + bb
        hot = one_hot(pos_ref[b, pl.ds(j, 1), :], cap)
        hots.append(hot)
        gates.append(jnp.sum(hot * gate_ref[b, pl.ds(j, 1), :], axis=1, keepdims=True))
    return hots, jnp.concatenate(gates, axis=0)


def experts_fwd_kernel(
    layer, e_pad, cap, rt_ref, wrt_ref, wg_ref, wu_ref, wd_ref, b_hbm,
    gp_ref, up_ref, pos_ref, gate_ref, out_hbm, x_scr, y_scr, all_gates, bbuf, obuf, bsem, osem,
):
    per, rows, d = x_scr.shape
    count = rt_ref.shape[0]
    chunk = 256
    j = pl.program_id(0)
    first = lax.axis_index("expert") * per

    @pl.when(lax.axis_index("section") == layer)
    def _():
        @pl.when(j == 0)
        def _():
            def prepare(b, slot):
                rt = rt_ref[b]
                block = bbuf[slot]
                pos = slots_of(rt, first, per)
                pos_ref[b] = pos
                all_gates[...] = gates_of(rt, wrt_ref, block, e_pad)
                gate_ref[b] = jnp.concatenate(
                    [all_gates[pl.ds(first + k, 1), :] for k in range(per)] + [jnp.zeros((8 - per, rt.shape[1]), F32)], axis=0
                )
                x = dot(all_hots(pos, per, cap).astype(BF), block).astype(BF)
                at = pl.ds(pl.multiple_of(b * cap, cap), cap)
                for k in range(per):
                    x_scr[k, at, :] = x[k * cap : (k + 1) * cap]

            streamed(count, lambda b, slot: [pltpu.make_async_copy(b_hbm.at[b], bbuf.at[slot], bsem.at[slot])], prepare)

        def part(c, carry):
            at = pl.ds(pl.multiple_of(c * chunk, chunk), chunk)
            x = x_scr[j, at, :]
            gp = dot(x, wg_ref[0])
            up = dot(x, wu_ref[0])
            gp_ref[0, at, :] = gp
            up_ref[0, at, :] = up
            hid = (gp / (1.0 + jnp.exp(-gp)) * up).astype(BF)
            _, gate = chunk_gates(c, j, chunk, cap, pos_ref, gate_ref)
            y_scr[j, at, :] = (dot(hid, wd_ref[0]) * gate).astype(BF)
            return carry

        lax.fori_loop(0, rows // chunk, part, 0)

        @pl.when(j == per - 1)
        def _():
            combine(count, per, cap, pos_ref, y_scr, out_hbm, obuf, osem)


def any_spec():
    return pl.BlockSpec(memory_space=pl.ANY)


def fixed(shape):
    return pl.BlockSpec(shape, lambda j: (0,) * len(shape))


def experts_fwd(layer, e_pad, cap, rt, wrt, wg, wu, wd, blocks):
    count, t, d = blocks.shape
    per, _, f = wg.shape
    rows = count * cap
    sds = jax.ShapeDtypeStruct
    return pl.pallas_call(
        functools.partial(experts_fwd_kernel, layer, e_pad, cap),
        grid=(per,),
        out_shape=(
            sds((per, rows, f), F32),
            sds((per, rows, f), F32),
            sds((count, 8, t), jnp.int32),
            sds((count, 8, t), F32),
            sds((count, t, d), BF),
        ),
        in_specs=[
            fixed(rt.shape),
            fixed(wrt.shape),
            pl.BlockSpec((1, d, f), lambda j: (j, 0, 0)),
            pl.BlockSpec((1, d, f), lambda j: (j, 0, 0)),
            pl.BlockSpec((1, f, d), lambda j: (j, 0, 0)),
            any_spec(),
        ],
        out_specs=(
            pl.BlockSpec((1, rows, f), lambda j: (j, 0, 0)),
            pl.BlockSpec((1, rows, f), lambda j: (j, 0, 0)),
            fixed((count, 8, t)),
            fixed((count, 8, t)),
            any_spec(),
        ),
        scratch_shapes=[
            pltpu.VMEM((per, rows, d), BF),
            pltpu.VMEM((per, rows, d), BF),
            pltpu.VMEM((e_pad, t), F32),
            pltpu.VMEM((2, t, d), BF),
            pltpu.VMEM((2, t, d), BF),
            pltpu.SemaphoreType.DMA((2,)),
            pltpu.SemaphoreType.DMA((2,)),
        ],
        compiler_params=pltpu.CompilerParams(vmem_limit_bytes=VMEM_LIMIT),
        cost_estimate=pl.CostEstimate(flops=6 * per * rows * d * f, bytes_accessed=6 * per * d * f, transcendentals=per * rows * f),
    )(rt, wrt, wg, wu, wd, blocks)


def experts_bwd_kernel(
    layer, cap, pos_ref, gate_ref, wg_ref, wu_ref, wd_ref, gp_ref, up_ref, b_hbm, gy_hbm,
    dw_ref, dg_ref, out_hbm, x_scr, y_scr, dgp_scr, dup_scr, hid_scr, bbuf, gbuf, obuf, bsem, gsem, osem,
):
    per, rows, d = x_scr.shape
    count = pos_ref.shape[0]
    parts = dw_ref.shape[0]
    piece = d // parts
    chunk = 256
    j = pl.program_id(0)

    @pl.when(lax.axis_index("section") == layer)
    def _():
        @pl.when(j == 0)
        def _():
            def prepare(b, slot):
                hots = all_hots(pos_ref[b], per, cap).astype(BF)
                x = dot(hots, bbuf[slot]).astype(BF)
                y = dot(hots, gbuf[slot]).astype(BF)
                at = pl.ds(pl.multiple_of(b * cap, cap), cap)
                for k in range(per):
                    x_scr[k, at, :] = x[k * cap : (k + 1) * cap]
                    y_scr[k, at, :] = y[k * cap : (k + 1) * cap]

            streamed(
                count,
                lambda b, slot: [
                    pltpu.make_async_copy(b_hbm.at[b], bbuf.at[slot], bsem.at[slot]),
                    pltpu.make_async_copy(gy_hbm.at[b], gbuf.at[slot], gsem.at[slot]),
                ],
                prepare,
            )
            dg_ref[...] = jnp.zeros_like(dg_ref)

        def part(c, carry):
            at = pl.ds(pl.multiple_of(c * chunk, chunk), chunk)
            raw = dot(y_scr[j, at, :], wd_ref[0], 1, 1)
            gp, up = gp_ref[0, at, :], up_ref[0, at, :]
            sg = 1.0 / (1.0 + jnp.exp(-gp))
            silu = gp * sg
            hid = silu * up
            hots, gate = chunk_gates(c, j, chunk, cap, pos_ref, gate_ref)
            dgate = jnp.sum(hid.astype(BF).astype(F32) * raw, axis=1, keepdims=True)
            for bb in range(chunk // cap):
                b = c * (chunk // cap) + bb
                dg_ref[b, pl.ds(j, 1), :] = jnp.sum(hots[bb] * dgate[bb * cap : (bb + 1) * cap], axis=0, keepdims=True)
            dh = raw * gate
            dgp_scr[at, :] = (dh * up * sg * (1.0 + gp * (1.0 - sg))).astype(BF)
            dup_scr[at, :] = (dh * silu).astype(BF)
            hid_scr[at, :] = (hid * gate).astype(BF)
            return carry

        lax.fori_loop(0, rows // chunk, part, 0)

        def weights(g, carry):
            cols = pl.ds(pl.multiple_of(g * piece, LANES), piece)
            x = x_scr[j, :, cols]
            dw_ref[g, 0, 0] = dot(x, dgp_scr[...], 0, 0).astype(BF)
            dw_ref[g, 0, 1] = dot(x, dup_scr[...], 0, 0).astype(BF)
            dw_ref[g, 0, 2] = dot(y_scr[j, :, cols], hid_scr[...], 0, 0).astype(BF)
            return carry

        if piece % LANES == 0:
            lax.fori_loop(0, parts, weights, 0)
        else:
            wide = LANES
            while wide % piece:
                wide += LANES
            for g0 in range(0, d, wide):
                x = x_scr[j, :, g0 : g0 + wide]
                y = y_scr[j, :, g0 : g0 + wide]
                for n, (left, right) in enumerate(((x, dgp_scr), (x, dup_scr), (y, hid_scr))):
                    full = dot(left, right[...], 0, 0).astype(BF)
                    for i in range(wide // piece):
                        dw_ref[g0 // piece + i, 0, n] = full[i * piece : (i + 1) * piece]

        def rows_back(c, carry):
            at = pl.ds(pl.multiple_of(c * chunk, chunk), chunk)
            y_scr[j, at, :] = (dot(dgp_scr[at, :], wg_ref[0], 1, 1) + dot(dup_scr[at, :], wu_ref[0], 1, 1)).astype(BF)
            return carry

        lax.fori_loop(0, rows // chunk, rows_back, 0)

        @pl.when(j == per - 1)
        def _():
            combine(count, per, cap, pos_ref, y_scr, out_hbm, obuf, osem)


def experts_bwd(layer, cap, groups, pos, gate, wg, wu, wd, gp, up, blocks, grads):
    count, t, d = blocks.shape
    per, _, f = wg.shape
    rows = count * cap
    sds = jax.ShapeDtypeStruct
    return pl.pallas_call(
        functools.partial(experts_bwd_kernel, layer, cap),
        grid=(per,),
        out_shape=(
            sds((groups, per, 3, d // groups, f), BF),
            sds((count, 8, t), F32),
            sds((count, t, d), BF),
        ),
        in_specs=[
            fixed(pos.shape),
            fixed(gate.shape),
            pl.BlockSpec((1, d, f), lambda j: (j, 0, 0)),
            pl.BlockSpec((1, d, f), lambda j: (j, 0, 0)),
            pl.BlockSpec((1, f, d), lambda j: (j, 0, 0)),
            pl.BlockSpec((1, rows, f), lambda j: (j, 0, 0)),
            pl.BlockSpec((1, rows, f), lambda j: (j, 0, 0)),
            any_spec(),
            any_spec(),
        ],
        out_specs=(
            pl.BlockSpec((groups, 1, 3, d // groups, f), lambda j: (0, j, 0, 0, 0)),
            fixed((count, 8, t)),
            any_spec(),
        ),
        scratch_shapes=[
            pltpu.VMEM((per, rows, d), BF),
            pltpu.VMEM((per, rows, d), BF),
            pltpu.VMEM((rows, f), BF),
            pltpu.VMEM((rows, f), BF),
            pltpu.VMEM((rows, f), BF),
            pltpu.VMEM((2, t, d), BF),
            pltpu.VMEM((2, t, d), BF),
            pltpu.VMEM((2, t, d), BF),
            pltpu.SemaphoreType.DMA((2,)),
            pltpu.SemaphoreType.DMA((2,)),
            pltpu.SemaphoreType.DMA((2,)),
        ],
        compiler_params=pltpu.CompilerParams(vmem_limit_bytes=VMEM_LIMIT),
        cost_estimate=pl.CostEstimate(flops=12 * per * rows * d * f, bytes_accessed=12 * per * d * f, transcendentals=per * rows * f),
    )(pos, gate, wg, wu, wd, gp, up, blocks, grads)


def meet(n, with_cross):
    s, z = lax.axis_index("section"), lax.axis_index("expert")
    barrier = pltpu.get_barrier_semaphore()
    for k in range(1, n):
        pl.semaphore_signal(barrier, inc=1, device_id={"expert": lax.rem(z + k, n)}, device_id_type=MESH)
    for k in range(n if with_cross else 1):
        pl.semaphore_signal(
            barrier, inc=1, device_id={"section": 1 - s, "expert": lax.rem(z + k, n)}, device_id_type=MESH
        )
    pl.semaphore_wait(barrier, 2 * n - 1 if with_cross else n)


def spread_kernel(layer, n, x_ref, o_ref, send_sem, recv_sem, local_sem):
    s, z = lax.axis_index("section"), lax.axis_index("expert")
    meet(n, True)

    def copy(k, source_section):
        return pltpu.make_async_remote_copy(
            src_ref=x_ref,
            dst_ref=o_ref.at[source_section, z],
            send_sem=send_sem.at[k],
            recv_sem=recv_sem.at[source_section, k],
            device_id={"section": layer, "expert": lax.rem(z + k, n)},
            device_id_type=MESH,
        )

    order = sorted(range(n), key=lambda k: (k == 0, abs(k - n // 2)))

    @pl.when(s == layer)
    def _():
        own = pltpu.make_async_copy(x_ref, o_ref.at[layer, z], local_sem)
        own.start()
        sends = [copy(k, layer) for k in order if k]
        for c in sends:
            c.start()
        own.wait()
        for c in sends:
            c.wait()
        for k in range(n):
            copy(k, 1 - layer).wait_recv()

    @pl.when(s != layer)
    def _():
        sends = [copy(k, 1 - layer) for k in order]
        for c in sends:
            c.start()
        for c in sends:
            c.wait_send()


def spread(layer, cid, x):
    n = lax.axis_size("expert")
    return pl.pallas_call(
        functools.partial(spread_kernel, layer, n),
        out_shape=jax.ShapeDtypeStruct((2, n) + x.shape, x.dtype),
        in_specs=[any_spec()],
        out_specs=any_spec(),
        scratch_shapes=[
            pltpu.SemaphoreType.DMA((n,)),
            pltpu.SemaphoreType.DMA((2, n)),
            pltpu.SemaphoreType.DMA,
        ],
        compiler_params=pltpu.CompilerParams(collective_id=cid, has_side_effects=True),
    )(x)


def collect_kernel(layer, n, arrays, *refs):
    srcs, outs, relays = refs[:arrays], refs[arrays : 2 * arrays], refs[2 * arrays : 3 * arrays]
    relay_send, relay_recv, send_sem, recv_sem, local_sem = refs[3 * arrays :]
    s, z = lax.axis_index("section"), lax.axis_index("expert")
    meet(n, False)

    def hop(a, to):
        return pltpu.make_async_remote_copy(
            src_ref=srcs[a].at[1 - layer, to],
            dst_ref=relays[a].at[to],
            send_sem=relay_send.at[a, to],
            recv_sem=relay_recv.at[a, to],
            device_id={"section": 1 - s},
            device_id_type=MESH,
        )

    def give(a, source, k):
        return pltpu.make_async_remote_copy(
            src_ref=source,
            dst_ref=outs[a].at[z],
            send_sem=send_sem.at[a, k],
            recv_sem=recv_sem.at[a, k],
            device_id={"expert": lax.rem(z + k, n)},
            device_id_type=MESH,
        )

    order = sorted(range(n), key=lambda k: (k == 0, abs(k - n // 2)))

    @pl.when(s == layer)
    def _():
        for k in order:
            for a in range(arrays):
                hop(a, lax.rem(z + k, n)).start()
        for k in order:
            for a in range(arrays):
                if k:
                    give(a, srcs[a].at[layer, lax.rem(z + k, n)], k).start()
                else:
                    pltpu.make_async_copy(srcs[a].at[layer, z], outs[a].at[z], local_sem.at[a]).start()
        for k in order:
            for a in range(arrays):
                hop(a, lax.rem(z + k, n)).wait_send()

    @pl.when(s != layer)
    def _():
        for k in order:
            to = lax.rem(z + k, n)
            for a in range(arrays):
                hop(a, to).wait_recv()
                if k:
                    give(a, relays[a].at[to], k).start()
                else:
                    pltpu.make_async_copy(relays[a].at[z], outs[a].at[z], local_sem.at[a]).start()

    for a in range(arrays):
        for k in order:
            if k:
                give(a, relays[a].at[lax.rem(z + k, n)], k).wait()
            else:
                pltpu.make_async_copy(relays[a].at[z], outs[a].at[z], local_sem.at[a]).wait()


def collect(layer, cid, *arrays):
    n = lax.axis_size("expert")
    count = len(arrays)
    return pl.pallas_call(
        functools.partial(collect_kernel, layer, n, count),
        out_shape=tuple(jax.ShapeDtypeStruct(a.shape[1:], a.dtype) for a in arrays),
        in_specs=[any_spec()] * count,
        out_specs=tuple([any_spec()] * count),
        scratch_shapes=[pltpu.VMEM(a.shape[1:], a.dtype) for a in arrays]
        + [
            pltpu.SemaphoreType.DMA((count, n)),
            pltpu.SemaphoreType.DMA((count, n)),
            pltpu.SemaphoreType.DMA((count, n)),
            pltpu.SemaphoreType.DMA((count, n)),
            pltpu.SemaphoreType.DMA((count,)),
        ],
        compiler_params=pltpu.CompilerParams(collective_id=cid, has_side_effects=True),
    )(*arrays)


def swap_sections(value):
    return lax.ppermute(value, "section", [(0, 1), (1, 0)])


def rope_tables(t):
    half = HEAD_SIZE // 2
    frequency = THETA ** (-jnp.arange(half, dtype=F32) * 2.0 / HEAD_SIZE)
    angles = jnp.arange(t, dtype=F32)[:, None] * frequency[None, :]
    reps = LANES // half
    return jnp.tile(jnp.cos(angles), (1, reps)), jnp.tile(jnp.sin(angles), (1, reps))


def local(
    inputs, cotangent, segment_ids, live_first, routes, gain_attn, gain_moe,
    w_query, key_weight, value_weight, w_out, w_router, w_gate, w_up, w_down,
):
    s = lax.axis_index("section")
    n = lax.axis_size("expert")
    groups = lax.axis_size("group")
    t, d = inputs.shape[2:]
    top = routes.shape[-1]
    per = w_gate.shape[1]
    experts = per * n
    e_pad = -(-experts // 16) * 16
    cap = t * top * 5 // (4 * experts)
    wg, wu, wd = w_gate[0], w_up[0], w_down[0]
    at_zero = s == 0

    shard = w_query.shape[1]
    aux = jnp.concatenate(
        [
            w_router[0],
            jnp.zeros((shard, GAIN_MOE_ROW - experts), BF),
            gain_moe[0][:, None],
            gain_attn[0][:, None],
        ],
        axis=1,
    )
    packed = jnp.concatenate([w_query[0], key_weight[0], value_weight[0], w_out[0].T, aux], axis=1)
    other = swap_sections(packed)
    shards = (jnp.where(at_zero, packed, other), jnp.where(at_zero, other, packed))
    first_weights = lax.all_gather(shards[0], ("group", "expert"), axis=0, tiled=True)

    x0 = lax.dynamic_index_in_dim(inputs[:, 0], s, 0, keepdims=False)
    cot = lax.dynamic_index_in_dim(cotangent[:, 0], s, 0, keepdims=False)
    seg = lax.dynamic_index_in_dim(segment_ids[:, 0], s, 0, keepdims=False)
    live = lax.dynamic_index_in_dim(live_first[:, 0], s, 0, keepdims=False)
    meta = jnp.stack([seg, jnp.repeat(live, BLK)], axis=1)
    meta = jnp.pad(meta, ((0, 0), (0, LANES - 2)))
    segr = jnp.broadcast_to(seg[None, :], (8, t))
    cos, sin = rope_tables(t)

    rt = jnp.swapaxes(routes[0, :, 0], 1, 2)
    rt_mine = lax.dynamic_index_in_dim(rt, s, 0, keepdims=False)
    rt_theirs = swap_sections(lax.dynamic_index_in_dim(rt, 1 - s, 0, keepdims=False))
    rt_tokens = (jnp.where(at_zero, rt_mine, rt_theirs), jnp.where(at_zero, rt_theirs, rt_mine))
    rt_all = lax.all_gather(rt, "expert", axis=1, tiled=False).reshape(2 * n, top, t)

    def flat(z):
        return z.reshape((2 * n,) + z.shape[2:])

    def paired(z):
        return z.reshape((2, n) + z.shape[1:])

    gy1 = flat(spread(1, 1, cot))

    qkv0, p0, o0, h0, b0, wrt0 = attn_fwd(x0, first_weights, cos, sin, meta, segr)
    second_weights = lax.all_gather(shards[1], ("group", "expert"), axis=0, tiled=True)
    b0_all = flat(spread(0, 2, b0))
    gp0, up0, pos0, gate0, part0 = experts_fwd(0, e_pad, cap, rt_all, wrt0, wg, wu, wd, b0_all)
    (back0,) = collect(0, 3, paired(part0))
    x1 = (h0 + jnp.sum(back0.astype(F32), axis=0)).astype(BF)

    qkv1, p1, o1, h1, b1, wrt1 = attn_fwd(x1, second_weights, cos, sin, meta, segr)
    b1_all = flat(spread(1, 4, b1))
    gp1, up1, pos1, gate1, part1 = experts_fwd(1, e_pad, cap, rt_all, wrt1, wg, wu, wd, b1_all)
    dw1, dg1, dpart1 = experts_bwd(1, cap, groups, pos1, gate1, wg, wu, wd, gp1, up1, b1_all, gy1)
    dback1, dgate1 = collect(1, 5, paired(dpart1), paired(dg1))

    def gates_back(dg):
        dg = dg[:, :per].reshape(experts, t)
        return jnp.pad(dg, ((0, e_pad - experts), (0, 0)))

    dx1, dd1 = attn_bwd(cot, h1, x1, second_weights, qkv1, p1, o1, b1, wrt1, dback1, gates_back(dgate1), rt_tokens[1], cos, sin)
    gy0 = dx1.astype(BF)

    gy0_all = flat(spread(0, 6, gy0))
    dw0, dg0, dpart0 = experts_bwd(0, cap, groups, pos0, gate0, wg, wu, wd, gp0, up0, b0_all, gy0_all)
    dback0, dgate0 = collect(0, 7, paired(dpart0), paired(dg0))
    dw = jnp.where(at_zero, dw0, dw1)
    dw = lax.psum_scatter(dw, "group", scatter_dimension=0, tiled=True)[0].astype(F32)
    dx0, dd0 = attn_bwd(gy0, h0, x0, first_weights, qkv0, p0, o0, b0, wrt0, dback0, gates_back(dgate0), rt_tokens[0], cos, sin)

    part1, _ = lax.optimization_barrier((part1, dback0))
    (back1,) = collect(1, 8, paired(part1))
    y1 = (h1 + jnp.sum(back1.astype(F32), axis=0)).astype(BF)

    ds1 = lax.psum_scatter(dd1, ("group", "expert"), scatter_dimension=0, tiled=True)
    ds0 = lax.psum_scatter(dd0, ("group", "expert"), scatter_dimension=0, tiled=True)
    kept = jnp.where(at_zero, ds0, ds1)
    dense = kept.astype(F32) + swap_sections(jnp.where(at_zero, ds1, ds0)).astype(F32)

    kept_out = jnp.where(at_zero, x1, y1)
    swapped_out = swap_sections(jnp.where(at_zero, y1, x1))
    layer_out = jnp.where(at_zero, jnp.stack([kept_out, swapped_out]), jnp.stack([swapped_out, kept_out]))
    kept_in = jnp.where(at_zero, dx0, dx1)
    swapped_in = swap_sections(jnp.where(at_zero, dx1, dx0))
    input_grad = jnp.where(at_zero, jnp.stack([kept_in, swapped_in]), jnp.stack([swapped_in, kept_in]))

    return (
        layer_out[None, :, None],
        input_grad[None, :, None],
        dense[:, QKV + QW + GAIN_ATTN_ROW][None],
        dense[:, QKV + QW + GAIN_MOE_ROW][None],
        dense[None, :, 0:QW],
        dense[None, :, QW : QW + KW],
        dense[None, :, QW + KW : QKV],
        dense[:, QKV : QKV + QW].T[None],
        dense[None, :, QKV + QW : QKV + QW + experts],
        dw[None, :, 0],
        dw[None, :, 1],
        jnp.swapaxes(dw[:, 2], 1, 2)[None],
    )


def solution(mesh):
    return jax.shard_map(
        local,
        mesh=mesh,
        in_specs=(
            P(None, ("group", "expert"), None, None),
            P(None, ("group", "expert"), None, None),
            P(None, ("group", "expert"), None),
            P(None, ("group", "expert"), None),
            P("section", None, ("group", "expert"), None, None),
            P("section", ("group", "expert")),
            P("section", ("group", "expert")),
            P("section", ("group", "expert"), None),
            P("section", ("group", "expert"), None),
            P("section", ("group", "expert"), None),
            P("section", None, ("group", "expert")),
            P("section", ("group", "expert"), None),
            P("section", "expert", None, None),
            P("section", "expert", None, None),
            P("section", "expert", None, None),
        ),
        out_specs=(
            P("section", None, ("group", "expert"), None, None),
            P("section", None, ("group", "expert"), None, None),
            P("section", ("group", "expert")),
            P("section", ("group", "expert")),
            P("section", ("group", "expert"), None),
            P("section", ("group", "expert"), None),
            P("section", ("group", "expert"), None),
            P("section", None, ("group", "expert")),
            P("section", ("group", "expert"), None),
            P("section", "expert", "group", None),
            P("section", "expert", "group", None),
            P("section", "expert", None, "group"),
        ),
        check_vma=False,
    )
```

time: 2290 us -> 1130 us (0.49)
  Pallas kernels: 0 us -> 687 us
  waiting for transfers between devices: 981 us -> 324 us
  blocking collectives: 486 us -> 14.2 us
  matrix products: 348 us -> 0 us
  local copies, waits for them, and re-layouts: 259 us -> 29.9 us
  other arithmetic: 128 us -> 43.3 us
  starting transfers between devices: 56.3 us -> 8.6 us
    pallas_call x0 -> x16, Pallas kernels: none -> 687 us  [the longest x4 315 us: collect(): pl.pallas_call(functools.partial(collect_kernel, layer, n, count), out_sh...]
    all_to_all x9 -> x0, waiting for transfers between devices: 602 us -> none  [the longest x3 231 us: layer_backward(): lax.all_to_all(grad_rows_in, 'expert', split_axis=1, concat_axis=1, tiled...]
    dot_general x90 -> x0, matrix products: 348 us -> none  [the longest x3 37.5 us: layer_backward(): jnp.einsum('erd,erf->edf', flat_recv, grad_gate_pre, preferred_element_ty...]
    all_to_all x3 -> x0, blocking collectives: 272 us -> none  [the longest x2 183 us: layer_forward(): lax.all_to_all(send_rows, 'expert', split_axis=1, concat_axis=1, tiled=True)]
    all_gather x1, blocking collectives: 119 us -> 14.2 us  [local(): lax.all_gather(rt, 'expert', axis=1, tiled=False).reshape(2 * n, top, t)]
    unnamed x2 -> x0, blocking collectives: 95.3 us -> none
    unnamed x467 -> x29, local copies, waits for them, and re-layouts: 69.1 us -> 8.07 us
    gather x6 -> x0, local copies, waits for them, and re-layouts: 59.1 us -> none  [the longest x3 30 us: layer_backward(): grad_back.reshape(-1, features)[slot_place]]
  transfers between devices with their start and end apart: 25 -> 10, of which waited for: 18 -> 6; matrix products, arithmetic and copies ran while one was open for 17% -> 4% of each run, Pallas kernels for 0% -> 42%
where the time goes in v1:
time: 1130 us; the launch traced here: 1120 us
  Pallas kernels  687 us (61%)
  waiting for transfers between devices  324 us (29%)
  other arithmetic  43.3 us (4%)
  local copies, waits for them, and re-layouts  29.9 us (3%)
  between operations  14.4 us (1%)
  blocking collectives  14.2 us (1%)
    pallas_call x4, Pallas kernels, collect(): pl.pallas_call(functools.partial(collect_kernel, layer, n, count), out_sh...  315 us
    pallas_call x4, Pallas kernels, spread(): pl.pallas_call(functools.partial(spread_kernel, layer, n), out_shape=jax....  175 us
    reduce_scatter x1, waiting for transfers between devices, local(): lax.psum_scatter(dw, 'group', scatter_dimension=0, tiled=True)[0]  148 us
    pallas_call x2, Pallas kernels, experts_bwd(): pl.pallas_call(functools.partial(experts_bwd_kernel, layer, cap), grid=(p...  75.7 us
    reduce_scatter x1, waiting for transfers between devices, local(): lax.psum_scatter(dd0, ('group', 'expert'), scatter_dimension=0, tiled=True)  75 us
    all_gather x1, waiting for transfers between devices, local(): lax.all_gather(shards[0], ('group', 'expert'), axis=0, tiled=True)  67.5 us
    pallas_call x2, Pallas kernels, attn_bwd(): pl.pallas_call(functools.partial(attn_bwd_kernel, dg.shape[0]), out_shape...  48.8 us
    pallas_call x2, Pallas kernels, experts_fwd(): pl.pallas_call(functools.partial(experts_fwd_kernel, layer, e_pad, cap),...  44.6 us
  transfers between devices with their start and end apart: 10, of which 6 were waited for; matrix products, arithmetic and copies ran while one was open for 4% of the time, Pallas kernels for 42%

profile of v1, /device:TPU:0, one launch (start us, length us, event | category | flops | bytes accessed | tf_op | source)
XLA Modules:
  0.0 1121.2 jit_solution(11709810076601093207)
XLA Ops:
  11.1 3.0 collective-permute-start
  14.1 18.1 %collective-permute-done = bf16[96,4224]{1,0:T(8,128)(2,1)S(1)} collective-permute-done((bf16[96,4224]{1,0:T(8,128)(2,1)S(1)}, bf16[96,4224]{1,0:T(8,128)(2,1)S(1)}, u32[]{:S(2)}, u32[]{:S(2)}) %collective-permute-start) | collective-permute-done | bytes 811040 | tf_op jit(solution)/shard_map/ppermute | solution.py:716
  34.4 1.8 collective-permute-start.1
  37.5 14.2 %all-gather = s32[2,32,128]{2,1,0:T(8,128)} all-gather(s32[2,8,128]{2,1,0:T(8,128)S(1)} %bitcast.106), channel_id=2, replica_groups=mesh['section'=2,'group'=4,'expert'=4] {'expert'}, dimensions={1}, use_global_device_ids=true | all-gather | bytes 40960 | tf_op jit(solution)/shard_map/all_gather | solution.py:771
  53.9 42.3 %shard_map.245 = bf16[2,4,128,1536]{3,2,1,0:T(8,128)(2,1)} custom-call(bf16[128,1536]{1,0:T(8,128)(2,1)} %get-tuple-element.143.x_ref.gy_ref), custom_call_target="tpu_custom_call" | custom-call | tf_op jit(solution)/shard_map/pallas_call | solution.py:619
  96.8 67.5 %all-gather.4.cloned.1.call-done.w_ref = bf16[1536,4224]{1,0:T(8,128)(2,1)} async-done(((bf16[96,4224]{1,0:T(8,128)(2,1)}), bf16[1536,4224]{1,0:T(8,128)(2,1)}) %all-gather.4.cloned.1.call-update) | async-done | bytes 12976144 | tf_op jit(solution)/shard_map/all_gather | solution.py:756
  164.9 14.1 %shard_map.238 = (bf16[128,2560]{1,0:T(8,128)(2,1)}, f32[24,128,128]{2,1,0:T(8,128)}, bf16[128,1536]{1,0:T(8,128)(2,1)}, f32[128,1536]{1,0:T(8,128)}, bf16[128,1...) custom-call(bf16[128,1536]{1,0:T(8,128)(2,1)} %get-tuple-element.144.x_ref, ...), custom_call_target="tpu_custom_call" | custom-call | flops 1610612736 | bytes 12976128 | tf_op jit(solution)/shard_map/pallas_call | solution.py:125
  178.9 49.7 %shard_map.239 = bf16[2,4,128,1536]{3,2,1,0:T(8,128)(2,1)} custom-call(bf16[128,1536]{1,0:T(8,128)(2,1)} %get-tuple-element.51.x_ref.b_ref), custom_call_target="tpu_custom_call" | custom-call | tf_op jit(solution)/shard_map/pallas_call | solution.py:619
  228.7 32.0 %shard_map.240 = (f32[5,512,512]{2,1,0:T(8,128)}, f32[5,512,512]{2,1,0:T(8,128)}, s32[8,8,128]{2,1,0:T(8,128)}, f32[8,8,128]{2,1,0:T(8,128)}, bf16[8,128,1536]{2,1,0:T(8,128)(2,1)}) custom-call(s32[8,8,128]{2,1,0:T(8,128)} %bitcast.107, bf16[128,1536]{1,0:T(8,128)(2,1)} %get-tuple-element.50.wrt_ref, bf16[5,1536,512]{2,1,0:T(8,128)(2,1)} %bitcast.115, ...), custom_call_target="tpu_custom_call" | custom-call | flops 12079595520 | bytes 23592960 | tf_op jit(solution)/shard_map/pallas_call | solution.py:393
  260.7 55.9 %shard_map.241 = bf16[4,128,1536]{2,1,0:T(8,128)(2,1)} custom-call(bf16[2,4,128,1536]{3,2,1,0:T(8,128)(2,1)} %bitcast.95), custom_call_target="tpu_custom_call" | custom-call | tf_op jit(solution)/shard_map/pallas_call | solution.py:698
  316.6 1.7 convert_reduce_fusion.1
  320.4 14.1 %shard_map.242 = (bf16[128,2560]{1,0:T(8,128)(2,1)}, f32[24,128,128]{2,1,0:T(8,128)}, bf16[128,1536]{1,0:T(8,128)(2,1)}, f32[128,1536]{1,0:T(8,128)}, bf16[128,1...) custom-call(bf16[128,1536]{1,0:T(8,128)(2,1)} %add_convert_fusion.1.x_ref, ...), custom_call_target="tpu_custom_call" | custom-call | flops 1610612736 | bytes 12976128 | tf_op jit(solution)/shard_map/pallas_call | solution.py:125
  334.4 45.9 %shard_map.243 = bf16[2,4,128,1536]{3,2,1,0:T(8,128)(2,1)} custom-call(bf16[128,1536]{1,0:T(8,128)(2,1)} %get-tuple-element.55.x_ref.b_ref), custom_call_target="tpu_custom_call" | custom-call | tf_op jit(solution)/shard_map/pallas_call | solution.py:619
  380.4 12.6 %shard_map.244 = (f32[5,512,512]{2,1,0:T(8,128)}, f32[5,512,512]{2,1,0:T(8,128)}, s32[8,8,128]{2,1,0:T(8,128)}, f32[8,8,128]{2,1,0:T(8,128)}, bf16[8,128,1536]{2,1,0:T(8,128)(2,1)}) custom-call(s32[8,8,128]{2,1,0:T(8,128)} %bitcast.108, bf16[128,1536]{1,0:T(8,128)(2,1)} %get-tuple-element.54.wrt_ref, bf16[5,1536,512]{2,1,0:T(8,128)(2,1)} %bitcast.116, ...), custom_call_target="tpu_custom_call" | custom-call | flops 12079595520 | bytes 23592960 | tf_op jit(solution)/shard_map/pallas_call | solution.py:393
  392.9 20.1 %shard_map.246 = (bf16[4,5,3,384,512]{4,3,2,1,0:T(8,128)(2,1)}, f32[8,8,128]{2,1,0:T(8,128)}, bf16[8,128,1536]{2,1,0:T(8,128)(2,1)}) custom-call(s32[8,8,128]{2,1,0:T(8,128)} %get-tuple-element.64.pos_ref, f32[8,8,128]{2,1,0:T(8,128)} %get-tuple-element.65.gate_ref, bf16[5,1536,512]{2,1,0:T(8,128)(2,1)} %bitcast.117, bf16[5,1536,512]{2,1,0:T(8,128)(2,1)} %bitcast.121, ...), custom_call_target="tpu_custom_call" | custom-call | flops 24159191040 | bytes 47185920 | tf_op jit(solution)/shard_map/pallas_call | solution.py:525
  413.0 104.1 %shard_map.247 = (bf16[4,128,1536]{2,1,0:T(8,128)(2,1)}, f32[4,8,128]{2,1,0:T(8,128)}) custom-call(bf16[2,4,128,1536]{3,2,1,0:T(8,128)(2,1)} %bitcast.92, f32[2,4,8,128]{3,2,1,0:T(8,128)} %bitcast.104), custom_call_target="tpu_custom_call" | custom-call | tf_op jit(solution)/shard_map/pallas_call | solution.py:698
  518.5 24.4 %shard_map.248 = (f32[128,1536]{1,0:T(8,128)}, bf16[1536,4224]{1,0:T(8,128)(2,1)}) custom-call(bf16[128,1536]{1,0:T(8,128)(2,1)} %get-tuple-element.143.x_ref.gy_ref, f32[128,1536]{1,0:T(8,128)} %get-tuple-element.53.h_ref, bf16[128,1536]{1,0:T(8,128)(2,1)} %add_convert_fusion.1.x_ref, bf16[1536,4224]{1,0:T(8,128)(2,1)} %all-gather.6.cloned.1.call-done.w_ref, ...), custom_call_target="tpu_custom_call" | custom-call | flops 3221225472 | bytes 25952256 | tf_op jit(solution)/shard_map/pallas_call | solution.py:242
  544.8 36.9 %shard_map.249 = bf16[2,4,128,1536]{3,2,1,0:T(8,128)(2,1)} custom-call(bf16[128,1536]{1,0:T(8,128)(2,1)} %convert_element_type.32.x_ref.gy_ref), custom_call_target="tpu_custom_call" | custom-call | tf_op jit(solution)/shard_map/pallas_call | solution.py:619
  581.6 55.6 %shard_map.250 = (bf16[4,5,3,384,512]{4,3,2,1,0:T(8,128)(2,1)}, f32[8,8,128]{2,1,0:T(8,128)}, bf16[8,128,1536]{2,1,0:T(8,128)(2,1)}) custom-call(s32[8,8,128]{2,1,0:T(8,128)} %get-tuple-element.57.pos_ref, f32[8,8,128]{2,1,0:T(8,128)} %get-tuple-element.58.gate_ref, bf16[5,1536,512]{2,1,0:T(8,128)(2,1)} %bitcast.118, bf16[5,1536,512]{2,1,0:T(8,128)(2,1)} %bitcast.122, ...), custom_call_target="tpu_custom_call" | custom-call | flops 24159191040 | bytes 47185920 | tf_op jit(solution)/shard_map/pallas_call | solution.py:525
  637.3 64.6 %shard_map.251 = (bf16[4,128,1536]{2,1,0:T(8,128)(2,1)}, f32[4,8,128]{2,1,0:T(8,128)}) custom-call(bf16[2,4,128,1536]{3,2,1,0:T(8,128)(2,1)} %bitcast.93, f32[2,4,8,128]{3,2,1,0:T(8,128)} %bitcast.105), custom_call_target="tpu_custom_call" | custom-call | tf_op jit(solution)/shard_map/pallas_call | solution.py:698
  703.2 24.5 %shard_map.253 = (f32[128,1536]{1,0:T(8,128)}, bf16[1536,4224]{1,0:T(8,128)(2,1)}) custom-call(bf16[128,1536]{1,0:T(8,128)(2,1)} %convert_element_type.32.x_ref.gy_ref, f32[128,1536]{1,0:T(8,128)} %get-tuple-element.49.h_ref, bf16[128,1536]{1,0:T(8,128)(2,1)} %get-tuple-element.144.x_ref, bf16[1536,4224]{1,0:T(8,128)(2,1)} %all-gather.4.cloned.1.call-done.w_ref, ...), custom_call_target="tpu_custom_call" | custom-call | flops 3221225472 | bytes 25952256 | tf_op jit(solution)/shard_map/pallas_call | solution.py:242
  727.8 20.0 %broadcast_select_fusion = bf16[4,5,3,384,512]{4,3,2,1,0:T(8,128)(2,1)} fusion(bf16[4,5,3,384,512]{4,3,2,1,0:T(8,128)(2,1)} %get-tuple-element.84, bf16[4,5,3,384,512]{4,3,2,1,0:T(8,128)(2,1)} %get-tuple-element.85, pred[]{:T(512)S(6)} %eq.3), kind=kLoop, calls=%fused_computation | loop fusion | flops 11796480 | bytes 70778880 | tf_op jit(solution)/shard_map/jit(_where)/select_n | solution.py:804
  747.8 90.2 %shard_map.252 = bf16[4,128,1536]{2,1,0:T(8,128)(2,1)} custom-call(bf16[2,4,128,1536]{3,2,1,0:T(8,128)(2,1)} %bitcast.86), custom_call_target="tpu_custom_call" | custom-call | tf_op jit(solution)/shard_map/pallas_call | solution.py:698
  838.1 1.8 convert_reduce_fusion
  841.9 2.0 collective-permute-start.3
  843.9 75.0 %reduce-scatter.4.cloned.1.call-done = bf16[96,4224]{1,0:T(8,128)(2,1)} async-done(((bf16[1536,4224]{1,0:T(8,128)(2,1)}), bf16[96,4224]{1,0:T(8,128)(2,1)}) %reduce-scatter.4.cloned.1.call-update) | async-done | bytes 811024 | tf_op jit(solution)/shard_map/reduce_scatter | solution.py:813
  922.8 2.9 maximum_select_fusion
  925.7 13.6 %collective-permute-done.4 = bf16[96,4224]{1,0:T(8,128)(2,1)S(1)} collective-permute-done((bf16[96,4224]{1,0:T(8,128)(2,1)S(1)}, bf16[96,4224]{1,0:T(8,128)(2,1)S(1)}, u32[]{:S(2)}, u32[]{:S(2)}) %collective-permute-start.4) | collective-permute-done | bytes 811040 | tf_op jit(solution)/shard_map/ppermute | solution.py:716
  942.9 147.8 %reduce-scatter.8.cloned.1.call-done = bf16[1,5,3,384,512]{4,3,2,1,0:T(8,128)(2,1)} async-done(((bf16[4,5,3,384,512]{4,3,2,1,0:T(8,128)(2,1)}), bf16[1,5,3,384,512]{4,3,2,1,0:T(8,128)(2,1)}) %reduce-scatter.8.cloned.1.call-update) | async-done | bytes 5898256 | tf_op jit(solution)/shard_map/reduce_scatter | solution.py:805
  1090.7 8.6 bitcast_convert_fusion
  1099.3 9.6 slice_bitcast_fusion
  1108.9 5.5 copy.62
  (83 shorter events, 26.8 us)
Async XLA Ops:
  7.2 29.0 %copy-start = (s32[2,1,2]{2,1,0:T(1,128)S(1)}, s32[2,1,2]{2,1,0:T(1,128)}, u32[]{:S(2)}) copy-start(s32[2,1,2]{2,1,0:T(1,128)} %param.18) | copy-start | bytes 52
  7.2 157.1 %all-gather.4.cloned.1.call-start = ((), (), s32[]{:S(2)}) async-start(), calls=%async_computation.3 | async-start | bytes 13787136 | tf_op jit(solution)/shard_map/all_gather | solution.py:756
  9.6 24.7 %copy-start.11 = (s32[1,2,1,128,8]{3,4,2,1,0:T(8,128)S(1)}, s32[1,2,1,128,8]{3,4,2,1,0:T(8,128)}, u32[]{:S(2)}) copy-start(s32[1,2,1,128,8]{3,4,2,1,0:T(8,128)} %param.19) | copy-start | bytes 24580
  9.6 26.7 %copy-start.12 = (s32[2,1,128]{2,1,0:T(1,128)S(1)}, s32[2,1,128]{2,1,0:T(1,128)}, u32[]{:S(2)}) copy-start(s32[2,1,128]{2,1,0:T(1,128)} %param.17) | copy-start | bytes 3076
  9.6 26.9 %copy-start.9 = (bf16[2,1,128,1536]{3,2,1,0:T(8,128)(2,1)S(1)}, bf16[2,1,128,1536]{3,2,1,0:T(8,128)(2,1)}, u32[]{:S(2)}) copy-start(bf16[2,1,128,1536]{3,2,1,0:T(8,128)(2,1)} %param.16) | copy-start | bytes 2359300
  9.6 26.9 %copy-start.10 = (bf16[2,1,128,1536]{3,2,1,0:T(8,128)(2,1)S(1)}, bf16[2,1,128,1536]{3,2,1,0:T(8,128)(2,1)}, u32[]{:S(2)}) copy-start(bf16[2,1,128,1536]{3,2,1,0:T(8,128)(2,1)} %param.15) | copy-start | bytes 2359300
  11.1 21.1 %collective-permute-start = (bf16[96,4224]{1,0:T(8,128)(2,1)S(1)}, bf16[96,4224]{1,0:T(8,128)(2,1)S(1)}, u32[]{:S(2)}, u32[]{:S(2)}) collective-permute-start(bf16[96,4224]{1,0:T(8,128)(2,1)S(1)} %concatenate.31), channel_id=1, source_target_pairs={{0,16},{16,0},{1,17},{17,1},{2,18},{18,2},{3,19},{19,3},{4,20},{20... | collective-permute-start | bytes 2433032 | tf_op jit(solution)/shard_map/ppermute | solution.py:716
  33.5 286.8 %all-gather.6.cloned.1.call-start = ((), (), s32[]{:S(2)}) async-start(), calls=%async_computation.4 | async-start | bytes 13787136 | tf_op jit(solution)/shard_map/all_gather | solution.py:782
  34.3 809.6 %reduce-scatter.6.cloned.1.call-start = ((), (), s32[]{:S(2)}) async-start(), calls=%async_computation.6 | async-start | bytes 13787136 | tf_op jit(solution)/shard_map/reduce_scatter | solution.py:812
  34.4 61.8 %collective-permute-start.1 = (s32[8,128]{1,0:T(8,128)S(1)}, s32[8,128]{1,0:T(8,128)S(1)}, u32[]{:S(2)}, u32[]{:S(2)}) collective-permute-start(s32[8,128]{1,0:T(8,128)S(1)} %dynamic-slice_bitcast_fusion.2), channel_id=1, source_target_pairs={{0,16},{16,0},{1,17},{17,1},{2,18},{18,2},{3,19},{19,3},{4,20},{20... | collective-permute-start | bytes 12296 | tf_op jit(solution)/shard_map/ppermute | solution.py:716
  260.7 57.6 %copy-start.6 = (f32[128,1536]{1,0:T(8,128)S(1)}, f32[128,1536]{1,0:T(8,128)}, u32[]{:S(2)}) copy-start(f32[128,1536]{1,0:T(8,128)} %get-tuple-element.49.h_ref) | copy-start | bytes 2359300
  542.8 1.1 copy-start.7
  542.9 376.1 %reduce-scatter.4.cloned.1.call-start = ((), (), s32[]{:S(2)}) async-start(), calls=%async_computation.5 | async-start | bytes 13787136 | tf_op jit(solution)/shard_map/reduce_scatter | solution.py:813
  727.7 363.0 %reduce-scatter.8.cloned.1.call-start = ((), (), s32[]{:S(2)}) async-start(), calls=%async_computation.7 | async-start | bytes 29491200 | tf_op jit(solution)/shard_map/reduce_scatter | solution.py:805
  747.8 92.0 %copy-start.2 = (bf16[128,1536]{1,0:T(8,128)(2,1)S(1)}, bf16[128,1536]{1,0:T(8,128)(2,1)}, u32[]{:S(2)}) copy-start(bf16[128,1536]{1,0:T(8,128)(2,1)} %add_convert_fusion.1.x_ref) | copy-start | bytes 1179652
  747.8 92.0 %copy-start.5 = (f32[128,1536]{1,0:T(8,128)S(1)}, f32[128,1536]{1,0:T(8,128)}, u32[]{:S(2)}) copy-start(f32[128,1536]{1,0:T(8,128)} %get-tuple-element.53.h_ref) | copy-start | bytes 2359300
  838.1 2.8 copy-start.8
  840.8 80.9 %collective-permute-start.2 = (bf16[128,1536]{1,0:T(8,128)(2,1)}, bf16[128,1536]{1,0:T(8,128)(2,1)S(1)}, u32[]{:S(2)}, u32[]{:S(2)}) collective-permute-start(bf16[128,1536]{1,0:T(8,128)(2,1)} %broadcast_select_fusion.5), channel_id=1, source_target_pairs={{0,16},{16,0},{1,17},{17,1},{2,18},{18,2},{3,19},{19,3},{4,20},{20... | collective-permute-start | bytes 1179656 | tf_op jit(solution)/shard_map/ppermute | solution.py:716
  841.9 80.9 %collective-permute-start.3 = (f32[128,1536]{1,0:T(8,128)}, f32[128,1536]{1,0:T(8,128)}, u32[]{:S(2)}, u32[]{:S(2)}) collective-permute-start(f32[128,1536]{1,0:T(8,128)} %get-tuple-element.136), channel_id=1, source_target_pairs={{0,16},{16,0},{1,17},{17,1},{2,18},{18,2},{3,19},{19,3},{4,20},{20... | collective-permute-start | bytes 2359304 | tf_op jit(solution)/shard_map/ppermute | solution.py:716
  843.9 95.4 %copy-start.3 = (bf16[96,4224]{1,0:T(8,128)(2,1)S(1)}, bf16[96,4224]{1,0:T(8,128)(2,1)}, u32[]{:S(2)}) copy-start(bf16[96,4224]{1,0:T(8,128)(2,1)} %reduce-scatter.6.cloned.1.call-done) | copy-start | bytes 2433028
  918.9 20.4 %copy-start.4 = (bf16[96,4224]{1,0:T(8,128)(2,1)S(1)}, bf16[96,4224]{1,0:T(8,128)(2,1)}, u32[]{:S(2)}) copy-start(bf16[96,4224]{1,0:T(8,128)(2,1)} %reduce-scatter.4.cloned.1.call-done) | copy-start | bytes 2433028
  920.2 19.0 %collective-permute-start.4 = (bf16[96,4224]{1,0:T(8,128)(2,1)S(1)}, bf16[96,4224]{1,0:T(8,128)(2,1)S(1)}, u32[]{:S(2)}, u32[]{:S(2)}) collective-permute-start(bf16[96,4224]{1,0:T(8,128)(2,1)S(1)} %broadcast_select_fusion.1), channel_id=1, source_target_pairs={{0,16},{16,0},{1,17},{17,1},{2,18},{18,2},{3,19},{19,3},{4,20},{20... | collective-permute-start | bytes 2433032 | tf_op jit(solution)/shard_map/ppermute | solution.py:716
  1108.9 5.5 copy-start.1
Sparse Core Ops, SparseCore 0:
  33.7 130.5 all-gather.3
  167.1 153.1 all-gather.5
  543.0 172.4 reduce-scatter.5
  727.8 191.0 reduce-scatter.3
  921.4 169.2 reduce-scatter.7

commit v2 on v1

--- a/solution.py
+++ b/solution.py
@@ -431,12 +431,12 @@
 
 def experts_bwd_kernel(
     layer, cap, pos_ref, gate_ref, wg_ref, wu_ref, wd_ref, gp_ref, up_ref, b_hbm, gy_hbm,
-    dw_ref, dg_ref, out_hbm, x_scr, y_scr, dgp_scr, dup_scr, hid_scr, bbuf, gbuf, obuf, bsem, gsem, osem,
+    even_ref, odd_ref, evend_ref, oddd_ref, dg_ref, out_hbm, x_scr, y_scr, dgp_scr, dup_scr, hid_scr, bbuf, gbuf, obuf, bsem, gsem, osem,
 ):
     per, rows, d = x_scr.shape
     count = pos_ref.shape[0]
-    parts = dw_ref.shape[0]
-    piece = d // parts
+    parts = even_ref.shape[0]
+    piece = even_ref.shape[3]
     chunk = 256
     j = pl.program_id(0)
 
@@ -483,27 +483,27 @@
 
         lax.fori_loop(0, rows // chunk, part, 0)
 
-        def weights(g, carry):
-            cols = pl.ds(pl.multiple_of(g * piece, LANES), piece)
-            x = x_scr[j, :, cols]
-            dw_ref[g, 0, 0] = dot(x, dgp_scr[...], 0, 0).astype(BF)
-            dw_ref[g, 0, 1] = dot(x, dup_scr[...], 0, 0).astype(BF)
-            dw_ref[g, 0, 2] = dot(y_scr[j, :, cols], hid_scr[...], 0, 0).astype(BF)
-            return carry
-
-        if piece % LANES == 0:
-            lax.fori_loop(0, parts, weights, 0)
-        else:
-            wide = LANES
-            while wide % piece:
-                wide += LANES
-            for g0 in range(0, d, wide):
-                x = x_scr[j, :, g0 : g0 + wide]
-                y = y_scr[j, :, g0 : g0 + wide]
-                for n, (left, right) in enumerate(((x, dgp_scr), (x, dup_scr), (y, hid_scr))):
-                    full = dot(left, right[...], 0, 0).astype(BF)
-                    for i in range(wide // piece):
-                        dw_ref[g0 // piece + i, 0, n] = full[i * piece : (i + 1) * piece]
+        odd = lax.rem(lax.axis_index("group"), 2)
+        place = lax.axis_index("group") // 2
+        for q in range(parts):
+            cols = slice(2 * q * piece, 2 * (q + 1) * piece)
+            at = lax.bitwise_xor(place, q)
+            for n, right in ((0, dgp_scr), (1, dup_scr)):
+                full = dot(x_scr[j, :, cols], right[...], 0, 0).astype(BF)
+                for parity, (low, high) in ((0, (even_ref, odd_ref)), (1, (odd_ref, even_ref))):
+
+                    @pl.when(odd == parity)
+                    def _(low=low, high=high):
+                        low[at, n, 0] = full[:piece]
+                        high[at, n, 0] = full[piece:]
+
+            full = dot(hid_scr[...], y_scr[j, :, cols], 0, 0).astype(BF)
+            for parity, (low, high) in ((0, (evend_ref, oddd_ref)), (1, (oddd_ref, evend_ref))):
+
+                @pl.when(odd == parity)
+                def _(low=low, high=high):
+                    low[at, 0] = full[:, :piece]
+                    high[at, 0] = full[:, piece:]
 
         def rows_back(c, carry):
             at = pl.ds(pl.multiple_of(c * chunk, chunk), chunk)
@@ -526,7 +526,10 @@
         functools.partial(experts_bwd_kernel, layer, cap),
         grid=(per,),
         out_shape=(
-            sds((groups, per, 3, d // groups, f), BF),
+            sds((groups // 2, 2, per, d // groups, f), BF),
+            sds((groups // 2, 2, per, d // groups, f), BF),
+            sds((groups // 2, per, f, d // groups), BF),
+            sds((groups // 2, per, f, d // groups), BF),
             sds((count, 8, t), F32),
             sds((count, t, d), BF),
         ),
@@ -542,7 +545,10 @@
             any_spec(),
         ],
         out_specs=(
-            pl.BlockSpec((groups, 1, 3, d // groups, f), lambda j: (0, j, 0, 0, 0)),
+            pl.BlockSpec((groups // 2, 2, 1, d // groups, f), lambda j: (0, 0, j, 0, 0)),
+            pl.BlockSpec((groups // 2, 2, 1, d // groups, f), lambda j: (0, 0, j, 0, 0)),
+            pl.BlockSpec((groups // 2, 1, f, d // groups), lambda j: (0, j, 0, 0)),
+            pl.BlockSpec((groups // 2, 1, f, d // groups), lambda j: (0, j, 0, 0)),
             fixed((count, 8, t)),
             any_spec(),
         ),
@@ -712,6 +718,396 @@
     )(*arrays)
 
 
+def top_bit(q):
+    return q.bit_length() - 1
+
+
+def finish_kernel(
+    n, dd0, dd1, egu0, ogu0, ed0, od0, egu1, ogu1, ed1, od1,
+    dense_out, gate_out, up_out, down_out,
+    core_gu, core_dn, hop_gu, hop_dn, core_dd, hop_y, hop_z, hop_x, dd_buf, gu_buf, dn_buf, gu_f32, dn_f32,
+    s_core_gu, r_core_gu, s_core_dn, r_core_dn, s_hop_gu, r_hop_gu, s_hop_dn, r_hop_dn,
+    s_core_dd, r_core_dd, s_y, r_y, s_z, r_z, s_x, r_x, l_dd, l_gu, l_dn, o_gu, o_dn,
+):
+    s, g, z = lax.axis_index("section"), lax.axis_index("group"), lax.axis_index("expert")
+    pairs, cgu = core_gu.shape[:2]
+    cdn = core_dn.shape[1]
+    levels = top_bit(pairs)
+    units = pairs * n
+    remote = functools.partial(pltpu.make_async_remote_copy, device_id_type=MESH)
+    twin = {"group": lax.bitwise_xor(g, 1)}
+    other = {"section": 1 - s}
+
+    def across(k):
+        return {"group": lax.bitwise_xor(g, 2 << k)}
+
+    barrier = pltpu.get_barrier_semaphore()
+    peers = [twin, other] + [across(k) for k in range(levels)] + [{"expert": lax.rem(z + k, n)} for k in range(1, n)]
+    for peer in peers:
+        pl.semaphore_signal(barrier, inc=1, device_id=peer, device_id_type=MESH)
+    pl.semaphore_wait(barrier, len(peers))
+
+    def by_section(action):
+        @pl.when(s == 0)
+        def _():
+            action(dd0, dd1, egu0, ogu0, ed0, od0)
+
+        @pl.when(s != 0)
+        def _():
+            action(dd1, dd0, egu1, ogu1, ed1, od1)
+
+    def unit(i):
+        return pairs - 1 - i // n, lax.rem(z + 1 + lax.rem(i, n), n)
+
+    def shard(i, core):
+        q, place = unit(i)
+        return (lax.bitwise_xor(g // 2, q) * 2 + core) * n + place
+
+    core = lax.rem(g, 2)
+
+    def core_dd_copy(kind, i, source):
+        return remote(
+            src_ref=source.at[shard(i, 1 - core)],
+            dst_ref=core_dd.at[kind, i],
+            send_sem=s_core_dd.at[kind, i],
+            recv_sem=r_core_dd.at[kind, i],
+            device_id=twin,
+        )
+
+    def core_chunk(source, dest, ssem, rsem, q, c):
+        return remote(
+            src_ref=source.at[q, c], dst_ref=dest.at[q, c], send_sem=ssem.at[q, c], recv_sem=rsem.at[q, c], device_id=twin
+        )
+
+    def core_gu_copy(source, q, c):
+        return core_chunk(source, core_gu, s_core_gu, r_core_gu, q, c)
+
+    def core_dn_copy(source, q, c):
+        return core_chunk(source, core_dn, s_core_dn, r_core_dn, q, c)
+
+    def send_all(own, away, egu, ogu, ed, od):
+        @pl.loop(0, units)
+        def _(i):
+            core_dd_copy(0, i, away).start()
+
+            @pl.when(i < cgu)
+            def _():
+                core_gu_copy(ogu, pairs - 1, i).start()
+
+            @pl.when(i < cdn)
+            def _():
+                core_dn_copy(od, pairs - 1, i).start()
+
+        for i in range(units, max(cgu, cdn)):
+            if i < cgu:
+                core_gu_copy(ogu, pairs - 1, i).start()
+            if i < cdn:
+                core_dn_copy(od, pairs - 1, i).start()
+
+        @pl.loop(0, units)
+        def _(i):
+            core_dd_copy(1, i, own).start()
+
+        for q in reversed(range(pairs - 1)):
+
+            @pl.loop(0, cgu)
+            def _(c):
+                core_gu_copy(ogu, q, c).start()
+
+            @pl.loop(0, cdn)
+            def _(c):
+                core_dn_copy(od, q, c).start()
+
+    by_section(send_all)
+
+    def load(buf, sem, slot, source):
+        return pltpu.make_async_copy(source, buf.at[slot], sem.at[slot])
+
+    def dd_load(i, slot, source):
+        return load(dd_buf, l_dd, slot, source.at[shard(i, core)])
+
+    def hop(dest, ssem, rsem, source, k, q, c):
+        return remote(
+            src_ref=source.at[q, c],
+            dst_ref=dest.at[k, q - (1 << k), c],
+            send_sem=ssem.at[k, q - (1 << k), c],
+            recv_sem=rsem.at[k, q - (1 << k), c],
+            device_id=across(k),
+        )
+
+    def gu_hop(k, q, c):
+        return hop(hop_gu, s_hop_gu, r_hop_gu, core_gu, k, q, c)
+
+    def dn_hop(k, q, c):
+        return hop(hop_dn, s_hop_dn, r_hop_dn, core_dn, k, q, c)
+
+    def y_copy(i):
+        return remote(src_ref=core_dd.at[0, i], dst_ref=hop_y.at[i], send_sem=s_y.at[i], recv_sem=r_y.at[i], device_id=other)
+
+    def z_copy(q, k, i):
+        return remote(
+            src_ref=core_dd.at[1, i],
+            dst_ref=hop_z.at[k - 1, q],
+            send_sem=s_z.at[k - 1, q],
+            recv_sem=r_z.at[k - 1, q],
+            device_id={"expert": lax.rem(z + k, n)},
+        )
+
+    def x_copy(k, q, i):
+        return remote(
+            src_ref=core_dd.at[1, i],
+            dst_ref=hop_x.at[k, q - (1 << k)],
+            send_sem=s_x.at[k, q - (1 << k)],
+            recv_sem=r_x.at[k, q - (1 << k)],
+            device_id=across(k),
+        )
+
+    def chunk_start(i, slot, q, egu, ed):
+        @pl.when(i < cgu)
+        def _():
+            load(gu_buf, l_gu, slot, egu.at[q, i]).start()
+
+        @pl.when(i < cdn)
+        def _():
+            load(dn_buf, l_dn, slot, ed.at[q, i]).start()
+
+    def expert_sum(hops, rsem, dest, core_r, buf, sem, slot, even, q, c, hop_copy):
+        load(buf, sem, slot, even.at[q, c]).wait()
+        core_r(q, c).wait_recv()
+        total = buf[slot].astype(F32) + dest[q, c].astype(F32)
+        for k in range(top_bit(q) + 1 if q else 0, levels):
+            hop_copy(k, q + (1 << k), c).wait_recv()
+            total = total + hops[k, q, c].astype(F32)
+        return total
+
+    def gu_sum(slot, q, c):
+        return expert_sum(hop_gu, r_hop_gu, core_gu, functools.partial(core_gu_copy, ogu0), gu_buf, l_gu, slot, egu0, q, c, gu_hop)
+
+    def dn_sum(slot, q, c):
+        return expert_sum(hop_dn, r_hop_dn, core_dn, functools.partial(core_dn_copy, od0), dn_buf, l_dn, slot, ed0, q, c, dn_hop)
+
+    def stepped(count, start, body):
+        start(0, 0)
+
+        def step(i, carry):
+            @pl.when(i + 1 < count)
+            def _():
+                start(i + 1, lax.rem(i + 1, 2))
+
+            body(i, lax.rem(i, 2))
+            return carry
+
+        lax.fori_loop(0, count, step, 0)
+
+    for q in reversed(range(1, pairs)):
+        dense_too = q == pairs - 1
+        steps = max(units, cgu, cdn) if dense_too else max(cgu, cdn)
+
+        def start(i, slot):
+            def go(own, away, egu, ogu, ed, od):
+                if dense_too:
+
+                    @pl.when(i < units)
+                    def _():
+                        dd_load(i, slot, away).start()
+
+                chunk_start(i, slot, q, egu, ed)
+
+            by_section(go)
+
+        def body(i, slot):
+            if dense_too:
+
+                @pl.when(i < units)
+                def _():
+                    dd_load(i, slot, dd0).wait()
+                    core_dd_copy(0, i, dd0).wait_recv()
+                    core_dd[0, i] = core_dd[0, i] + dd_buf[slot]
+                    y_copy(i).start()
+
+            @pl.when(i < cgu)
+            def _():
+                core_gu[q, i] = gu_sum(slot, q, i).astype(BF)
+                gu_hop(top_bit(q), q, i).start()
+
+            @pl.when(i < cdn)
+            def _():
+                core_dn[q, i] = dn_sum(slot, q, i).astype(BF)
+                dn_hop(top_bit(q), q, i).start()
+
+        stepped(steps, start, body)
+
+    def gu_out_copy(c, slot, to=gate_out):
+        return pltpu.make_async_copy(gu_f32.at[slot], to.at[lax.rem(c, cgu // 2)], o_gu.at[slot])
+
+    def dn_out_copy(c, slot):
+        return pltpu.make_async_copy(dn_f32.at[slot], down_out.at[c], o_dn.at[slot])
+
+    def dense_sum(q):
+        i = (pairs - 1 - q) * n + n - 1
+        total = core_dd[1, i].astype(F32)
+        for k in range(1, n):
+            z_copy(q, k, i).wait_recv()
+            total = total + hop_z[k - 1, q].astype(F32)
+        for k in range(top_bit(q) + 1 if q else 0, levels):
+            x_copy(k, q + (1 << k), i).wait_recv()
+            total = total + hop_x[k, q].astype(F32)
+        return i, total
+
+    def pass_on(q):
+        i, total = dense_sum(q)
+        core_dd[1, i] = total.astype(BF)
+        x_copy(top_bit(q), q, i).start()
+
+    steps = max(units, cgu, cdn)
+
+    def start(i, slot):
+        def go(own, away, egu, ogu, ed, od):
+            @pl.when(i < units)
+            def _():
+                dd_load(i, slot, own).start()
+
+            chunk_start(i, slot, 0, egu, ed)
+
+        by_section(go)
+
+    def body(i, slot):
+        @pl.when(i < units)
+        def _():
+            dd_load(i, slot, dd0).wait()
+            core_dd_copy(1, i, dd0).wait_recv()
+            y_copy(i).wait_recv()
+            core_dd[1, i] = (core_dd[1, i].astype(F32) + dd_buf[slot].astype(F32) + hop_y[i].astype(F32)).astype(BF)
+            q, _ = unit(i)
+            k = lax.rem(i, n) + 1
+
+            @pl.when(k < n)
+            def _():
+                z_copy(q, k, i).start()
+
+        for q in range(1, pairs):
+
+            @pl.when(i == (pairs - q) * n + min(2, n - 1))
+            def _():
+                pass_on(q)
+
+        @pl.when(i < cgu)
+        def _():
+            @pl.when(i >= 2)
+            def _():
+                gu_out_copy(i - 2, slot).wait()
+
+            gu_f32[slot] = gu_sum(slot, 0, i)
+
+            @pl.when(i < cgu // 2)
+            def _():
+                gu_out_copy(i, slot).start()
+
+            @pl.when(i >= cgu // 2)
+            def _():
+                gu_out_copy(i, slot, up_out).start()
+
+        @pl.when(i < cdn)
+        def _():
+            @pl.when(i >= 2)
+            def _():
+                dn_out_copy(i - 2, slot).wait()
+
+            dn_f32[slot] = dn_sum(slot, 0, i)
+            dn_out_copy(i, slot).start()
+
+    stepped(steps, start, body)
+    _, total = dense_sum(0)
+    dense_out[...] = total
+    for c in (cgu - 2, cgu - 1):
+        gu_out_copy(c, c % 2).wait()
+    for c in (cdn - 2, cdn - 1):
+        dn_out_copy(c, c % 2).wait()
+
+    @pl.loop(0, units)
+    def _(i):
+        core_dd_copy(0, i, dd0).wait_send()
+        core_dd_copy(1, i, dd0).wait_send()
+        y_copy(i).wait_send()
+        q, _ = unit(i)
+        k = lax.rem(i, n) + 1
+
+        @pl.when(k < n)
+        def _():
+            z_copy(q, k, i).wait_send()
+
+    for q in range(pairs):
+        if q:
+            x_copy(top_bit(q), q, (pairs - 1 - q) * n + n - 1).wait_send()
+
+        @pl.loop(0, cgu)
+        def _(c):
+            core_gu_copy(ogu0, q, c).wait_send()
+            if q:
+                gu_hop(top_bit(q), q, c).wait_send()
+
+        @pl.loop(0, cdn)
+        def _(c):
+            core_dn_copy(od0, q, c).wait_send()
+            if q:
+                dn_hop(top_bit(q), q, c).wait_send()
+
+
+def finish(cid, dd0, dd1, experts0, experts1):
+    n, groups = lax.axis_size("expert"), lax.axis_size("group")
+    pairs, levels = groups // 2, top_bit(groups // 2)
+    width = dd0.shape[1]
+    rows = dd0.shape[0] // (groups * n)
+    dd0, dd1 = (v.reshape(groups * n, rows, width) for v in (dd0, dd1))
+
+    def chunked(arrays):
+        gu_even, gu_odd, dn_even, dn_odd = arrays
+        flat = (pairs, -1) + gu_even.shape[3:]
+        return gu_even.reshape(flat), gu_odd.reshape(flat), dn_even, dn_odd
+
+    experts0, experts1 = chunked(experts0), chunked(experts1)
+    gu, dn = experts0[0].shape[1:], experts0[2].shape[1:]
+    units = pairs * n
+    dma = pltpu.SemaphoreType.DMA
+    sds = jax.ShapeDtypeStruct
+    half = max(1, pairs // 2)
+
+    def both(shape):
+        return [dma(shape), dma(shape)]
+
+    return pl.pallas_call(
+        functools.partial(finish_kernel, n),
+        out_shape=(sds((rows, width), F32), sds((gu[0] // 2,) + gu[1:], F32), sds((gu[0] // 2,) + gu[1:], F32), sds(dn, F32)),
+        in_specs=[any_spec()] * 10,
+        out_specs=(pl.BlockSpec(memory_space=pltpu.VMEM), any_spec(), any_spec(), any_spec()),
+        scratch_shapes=[
+            pltpu.VMEM((pairs,) + gu, BF),
+            pltpu.VMEM((pairs,) + dn, BF),
+            pltpu.VMEM((levels, half) + gu, BF),
+            pltpu.VMEM((levels, half) + dn, BF),
+            pltpu.VMEM((2, units, rows, width), BF),
+            pltpu.VMEM((units, rows, width), BF),
+            pltpu.VMEM((n - 1, pairs, rows, width), BF),
+            pltpu.VMEM((levels, half, rows, width), BF),
+            pltpu.VMEM((2, rows, width), BF),
+            pltpu.VMEM((2,) + gu[1:], BF),
+            pltpu.VMEM((2,) + dn[1:], BF),
+            pltpu.VMEM((2,) + gu[1:], F32),
+            pltpu.VMEM((2,) + dn[1:], F32),
+        ]
+        + both((pairs, gu[0]))
+        + both((pairs, dn[0]))
+        + both((levels, half, gu[0]))
+        + both((levels, half, dn[0]))
+        + both((2, units))
+        + both((units,))
+        + both((n - 1, pairs))
+        + both((levels, half))
+        + [dma((2,))] * 5,
+        compiler_params=pltpu.CompilerParams(collective_id=cid, has_side_effects=True, vmem_limit_bytes=VMEM_LIMIT),
+    )(dd0, dd1, *experts0, *experts1)
+
+
 def swap_sections(value):
     return lax.ppermute(value, "section", [(0, 1), (1, 0)])
 
@@ -788,7 +1184,7 @@
     qkv1, p1, o1, h1, b1, wrt1 = attn_fwd(x1, second_weights, cos, sin, meta, segr)
     b1_all = flat(spread(1, 4, b1))
     gp1, up1, pos1, gate1, part1 = experts_fwd(1, e_pad, cap, rt_all, wrt1, wg, wu, wd, b1_all)
-    dw1, dg1, dpart1 = experts_bwd(1, cap, groups, pos1, gate1, wg, wu, wd, gp1, up1, b1_all, gy1)
+    ge1, go1, de1, do1, dg1, dpart1 = experts_bwd(1, cap, groups, pos1, gate1, wg, wu, wd, gp1, up1, b1_all, gy1)
     dback1, dgate1 = collect(1, 5, paired(dpart1), paired(dg1))
 
     def gates_back(dg):
@@ -799,20 +1195,16 @@
     gy0 = dx1.astype(BF)
 
     gy0_all = flat(spread(0, 6, gy0))
-    dw0, dg0, dpart0 = experts_bwd(0, cap, groups, pos0, gate0, wg, wu, wd, gp0, up0, b0_all, gy0_all)
+    gy0_all, part1 = lax.optimization_barrier((gy0_all, part1))
+    crossed = lax.ppermute(paired(part1)[0], "section", [(1, 0)])
+    ge0, go0, de0, do0, dg0, dpart0 = experts_bwd(0, cap, groups, pos0, gate0, wg, wu, wd, gp0, up0, b0_all, gy0_all)
     dback0, dgate0 = collect(0, 7, paired(dpart0), paired(dg0))
-    dw = jnp.where(at_zero, dw0, dw1)
-    dw = lax.psum_scatter(dw, "group", scatter_dimension=0, tiled=True)[0].astype(F32)
+    dback0, part1, crossed = lax.optimization_barrier((dback0, part1, crossed))
+    back1 = lax.all_to_all(jnp.where(at_zero, crossed, paired(part1)[1]), "expert", split_axis=0, concat_axis=0, tiled=True)
+    y1 = (h1 + jnp.sum(back1.astype(F32), axis=0)).astype(BF)
     dx0, dd0 = attn_bwd(gy0, h0, x0, first_weights, qkv0, p0, o0, b0, wrt0, dback0, gates_back(dgate0), rt_tokens[0], cos, sin)
 
-    part1, _ = lax.optimization_barrier((part1, dback0))
-    (back1,) = collect(1, 8, paired(part1))
-    y1 = (h1 + jnp.sum(back1.astype(F32), axis=0)).astype(BF)
-
-    ds1 = lax.psum_scatter(dd1, ("group", "expert"), scatter_dimension=0, tiled=True)
-    ds0 = lax.psum_scatter(dd0, ("group", "expert"), scatter_dimension=0, tiled=True)
-    kept = jnp.where(at_zero, ds0, ds1)
-    dense = kept.astype(F32) + swap_sections(jnp.where(at_zero, ds1, ds0)).astype(F32)
+    dense, gate_grad, up_grad, down = finish(9, dd0, dd1, (ge0, go0, de0, do0), (ge1, go1, de1, do1))
 
     kept_out = jnp.where(at_zero, x1, y1)
     swapped_out = swap_sections(jnp.where(at_zero, y1, x1))
@@ -831,9 +1223,9 @@
         dense[None, :, QW + KW : QKV],
         dense[:, QKV : QKV + QW].T[None],
         dense[None, :, QKV + QW : QKV + QW + experts],
-        dw[None, :, 0],
-        dw[None, :, 1],
-        jnp.swapaxes(dw[:, 2], 1, 2)[None],
+        gate_grad[None],
+        up_grad[None],
+        down[None],
     )
 
 

time: 1130 us -> 952 us (0.84)
  waiting for transfers between devices: 324 us -> 88.9 us
  Pallas kernels: 687 us -> 761 us
  other arithmetic: 43.3 us -> 16 us
  starting transfers between devices: 8.6 us -> 21.9 us
    reduce_scatter x3 -> x0, waiting for transfers between devices: 223 us -> none  [the longest x1 148 us: local(): lax.psum_scatter(dw, 'group', scatter_dimension=0, tiled=True)[0]]
    pallas_call x0 -> x1, Pallas kernels: none -> 180 us  [finish(): pl.pallas_call(functools.partial(finish_kernel, n), out_shape=(sds((rows,...]
    pallas_call x4 -> x3, Pallas kernels: 315 us -> 204 us  [collect(): pl.pallas_call(functools.partial(collect_kernel, layer, n, count), out_sh...]
    select_n x2 -> x1, other arithmetic: 21.3 us -> 2.78 us  [local(): jnp.where(at_zero, crossed, paired(part1)[1])]
    ppermute x5 -> x4, waiting for transfers between devices: 31.7 us -> 19.8 us  [swap_sections(): return lax.ppermute(value, 'section', [(0, 1), (1, 0)])]
  transfers between devices with their start and end apart: 10 -> 8, of which waited for: 6 -> 4; matrix products, arithmetic and copies ran while one was open for 4% -> 2% of each run, Pallas kernels for 42% -> 53%
where the time goes in v2:
time: 952 us; the launch traced here: 944 us
  Pallas kernels  761 us (80%)
  waiting for transfers between devices  88.9 us (9%)
  local copies, waits for them, and re-layouts  27.3 us (3%)
  starting transfers between devices  21.9 us (2%)
  other arithmetic  16 us (2%)
  between operations  14.6 us (2%)
  blocking collectives  14.2 us (1%)
    pallas_call x3, Pallas kernels, collect(): pl.pallas_call(functools.partial(collect_kernel, layer, n, count), out_sh...  204 us
    pallas_call x1, Pallas kernels, finish(): pl.pallas_call(functools.partial(finish_kernel, n), out_shape=(sds((rows,...  180 us
    pallas_call x4, Pallas kernels, spread(): pl.pallas_call(functools.partial(spread_kernel, layer, n), out_shape=jax....  175 us
    pallas_call x2, Pallas kernels, experts_bwd(): pl.pallas_call(functools.partial(experts_bwd_kernel, layer, cap), grid=(p...  81.3 us
    all_gather x1, waiting for transfers between devices, local(): lax.all_gather(shards[0], ('group', 'expert'), axis=0, tiled=True)  67.3 us
    pallas_call x2, Pallas kernels, attn_bwd(): pl.pallas_call(functools.partial(attn_bwd_kernel, dg.shape[0]), out_shape...  48.8 us
    pallas_call x2, Pallas kernels, experts_fwd(): pl.pallas_call(functools.partial(experts_fwd_kernel, layer, e_pad, cap),...  44.7 us
    pallas_call x2, Pallas kernels, attn_fwd(): pl.pallas_call(attn_fwd_kernel, out_shape=(sds((t, QKV), BF), sds((QUERY_...  28.1 us
  transfers between devices with their start and end apart: 8, of which 4 were waited for; matrix products, arithmetic and copies ran while one was open for 2% of the time, Pallas kernels for 53%

profile of v2, /device:TPU:0, one launch (start us, length us, event | category | flops | bytes accessed | tf_op | source)
XLA Modules:
  0.0 944.3 jit_solution(2778505984213034818)
XLA Ops:
  11.1 3.0 collective-permute-start
  14.1 18.1 %collective-permute-done = bf16[96,4224]{1,0:T(8,128)(2,1)S(1)} collective-permute-done((bf16[96,4224]{1,0:T(8,128)(2,1)S(1)}, bf16[96,4224]{1,0:T(8,128)(2,1)S(1)}, u32[]{:S(2)}, u32[]{:S(2)}) %collective-permute-start) | collective-permute-done | bytes 811040 | tf_op jit(solution)/shard_map/ppermute | solution.py:1112
  34.3 1.8 collective-permute-start.1
  37.4 14.2 %all-gather = s32[2,32,128]{2,1,0:T(8,128)} all-gather(s32[2,8,128]{2,1,0:T(8,128)S(1)} %bitcast.109), channel_id=2, replica_groups=mesh['section'=2,'group'=4,'expert'=4] {'expert'}, dimensions={1}, use_global_device_ids=true | all-gather | bytes 40960 | tf_op jit(solution)/shard_map/all_gather | solution.py:1167
  53.9 42.4 %shard_map.245 = bf16[2,4,128,1536]{3,2,1,0:T(8,128)(2,1)} custom-call(bf16[128,1536]{1,0:T(8,128)(2,1)} %get-tuple-element.168.x_ref.gy_ref), custom_call_target="tpu_custom_call" | custom-call | tf_op jit(solution)/shard_map/pallas_call | solution.py:625
  96.9 67.3 %all-gather.4.cloned.1.call-done.w_ref = bf16[1536,4224]{1,0:T(8,128)(2,1)} async-done(((bf16[96,4224]{1,0:T(8,128)(2,1)}), bf16[1536,4224]{1,0:T(8,128)(2,1)}) %all-gather.4.cloned.1.call-update) | async-done | bytes 12976144 | tf_op jit(solution)/shard_map/all_gather | solution.py:1152
  164.8 14.0 %shard_map.238 = (bf16[128,2560]{1,0:T(8,128)(2,1)}, f32[24,128,128]{2,1,0:T(8,128)}, bf16[128,1536]{1,0:T(8,128)(2,1)}, f32[128,1536]{1,0:T(8,128)}, bf16[128,1...) custom-call(bf16[128,1536]{1,0:T(8,128)(2,1)} %get-tuple-element.169.x_ref, ...), custom_call_target="tpu_custom_call" | custom-call | flops 1610612736 | bytes 12976128 | tf_op jit(solution)/shard_map/pallas_call | solution.py:125
  178.9 49.7 %shard_map.239 = bf16[2,4,128,1536]{3,2,1,0:T(8,128)(2,1)} custom-call(bf16[128,1536]{1,0:T(8,128)(2,1)} %get-tuple-element.65.x_ref.b_ref), custom_call_target="tpu_custom_call" | custom-call | tf_op jit(solution)/shard_map/pallas_call | solution.py:625
  228.6 32.1 %shard_map.240 = (f32[5,512,512]{2,1,0:T(8,128)}, f32[5,512,512]{2,1,0:T(8,128)}, s32[8,8,128]{2,1,0:T(8,128)}, f32[8,8,128]{2,1,0:T(8,128)}, bf16[8,128,1536]{2,1,0:T(8,128)(2,1)}) custom-call(s32[8,8,128]{2,1,0:T(8,128)} %bitcast.110, bf16[128,1536]{1,0:T(8,128)(2,1)} %get-tuple-element.64.wrt_ref, bf16[5,1536,512]{2,1,0:T(8,128)(2,1)} %bitcast.118, ...), custom_call_target="tpu_custom_call" | custom-call | flops 12079595520 | bytes 23592960 | tf_op jit(solution)/shard_map/pallas_call | solution.py:393
  260.7 55.8 %shard_map.241 = bf16[4,128,1536]{2,1,0:T(8,128)(2,1)} custom-call(bf16[2,4,128,1536]{3,2,1,0:T(8,128)(2,1)} %bitcast.98), custom_call_target="tpu_custom_call" | custom-call | tf_op jit(solution)/shard_map/pallas_call | solution.py:704
  320.3 14.0 %shard_map.242 = (bf16[128,2560]{1,0:T(8,128)(2,1)}, f32[24,128,128]{2,1,0:T(8,128)}, bf16[128,1536]{1,0:T(8,128)(2,1)}, f32[128,1536]{1,0:T(8,128)}, bf16[128,1...) custom-call(bf16[128,1536]{1,0:T(8,128)(2,1)} %add_convert_fusion.1.x_ref, ...), custom_call_target="tpu_custom_call" | custom-call | flops 1610612736 | bytes 12976128 | tf_op jit(solution)/shard_map/pallas_call | solution.py:125
  334.3 46.0 %shard_map.243 = bf16[2,4,128,1536]{3,2,1,0:T(8,128)(2,1)} custom-call(bf16[128,1536]{1,0:T(8,128)(2,1)} %get-tuple-element.75.x_ref.b_ref), custom_call_target="tpu_custom_call" | custom-call | tf_op jit(solution)/shard_map/pallas_call | solution.py:625
  380.3 12.5 %shard_map.244 = (f32[5,512,512]{2,1,0:T(8,128)}, f32[5,512,512]{2,1,0:T(8,128)}, s32[8,8,128]{2,1,0:T(8,128)}, f32[8,8,128]{2,1,0:T(8,128)}, bf16[8,128,1536]{2,1,0:T(8,128)(2,1)}) custom-call(s32[8,8,128]{2,1,0:T(8,128)} %bitcast.111, bf16[128,1536]{1,0:T(8,128)(2,1)} %get-tuple-element.76.wrt_ref, bf16[5,1536,512]{2,1,0:T(8,128)(2,1)} %bitcast.119, ...), custom_call_target="tpu_custom_call" | custom-call | flops 12079595520 | bytes 23592960 | tf_op jit(solution)/shard_map/pallas_call | solution.py:393
  392.9 20.0 %shard_map.246 = (bf16[2,2,5,384,512]{4,3,2,1,0:T(8,128)(2,1)}, bf16[2,2,5,384,512]{4,3,2,1,0:T(8,128)(2,1)}, bf16[2,5,512,384]{3,2,1,0:T(8,128)(2,1)}, bf16[2,5...) custom-call(s32[8,8,128]{2,1,0:T(8,128)} %get-tuple-element.77.pos_ref, ...), custom_call_target="tpu_custom_call" | custom-call | flops 24159191040 | bytes 47185920 | tf_op jit(solution)/shard_map/pallas_call | solution.py:525
  412.8 109.9 %shard_map.247 = (bf16[4,128,1536]{2,1,0:T(8,128)(2,1)}, f32[4,8,128]{2,1,0:T(8,128)}) custom-call(bf16[2,4,128,1536]{3,2,1,0:T(8,128)(2,1)} %bitcast.96, f32[2,4,8,128]{3,2,1,0:T(8,128)} %bitcast.107), custom_call_target="tpu_custom_call" | custom-call | tf_op jit(solution)/shard_map/pallas_call | solution.py:704
  524.1 24.4 %shard_map.248 = (f32[128,1536]{1,0:T(8,128)}, bf16[1536,4224]{1,0:T(8,128)(2,1)}) custom-call(bf16[128,1536]{1,0:T(8,128)(2,1)} %get-tuple-element.168.x_ref.gy_ref, f32[128,1536]{1,0:T(8,128)} %get-tuple-element.67.h_ref, bf16[128,1536]{1,0:T(8,128)(2,1)} %add_convert_fusion.1.x_ref, bf16[1536,4224]{1,0:T(8,128)(2,1)} %all-gather.6.cloned.1.call-done.w_ref, ...), custom_call_target="tpu_custom_call" | custom-call | flops 3221225472 | bytes 25952256 | tf_op jit(solution)/shard_map/pallas_call | solution.py:242
  548.5 2.1 convert_element_type.20.x_ref.gy_ref
  550.6 36.9 %shard_map.249 = bf16[2,4,128,1536]{3,2,1,0:T(8,128)(2,1)} custom-call(bf16[128,1536]{1,0:T(8,128)(2,1)} %convert_element_type.20.x_ref.gy_ref), custom_call_target="tpu_custom_call" | custom-call | tf_op jit(solution)/shard_map/pallas_call | solution.py:625
  590.3 61.4 %shard_map.250 = (bf16[2,2,5,384,512]{4,3,2,1,0:T(8,128)(2,1)}, bf16[2,2,5,384,512]{4,3,2,1,0:T(8,128)(2,1)}, bf16[2,5,512,384]{3,2,1,0:T(8,128)(2,1)}, bf16[2,5...) custom-call(s32[8,8,128]{2,1,0:T(8,128)} %get-tuple-element.68.pos_ref, ...), custom_call_target="tpu_custom_call" | custom-call | flops 24159191040 | bytes 47185920 | tf_op jit(solution)/shard_map/pallas_call | solution.py:525
  651.7 38.0 %shard_map.251 = (bf16[4,128,1536]{2,1,0:T(8,128)(2,1)}, f32[4,8,128]{2,1,0:T(8,128)}) custom-call(bf16[2,4,128,1536]{3,2,1,0:T(8,128)(2,1)} %bitcast.97, f32[2,4,8,128]{3,2,1,0:T(8,128)} %bitcast.108), custom_call_target="tpu_custom_call" | custom-call | tf_op jit(solution)/shard_map/pallas_call | solution.py:704
  689.6 2.8 slice_select_fusion
  692.4 4.3 all-to-all-start
  697.3 24.4 %shard_map.252 = (f32[128,1536]{1,0:T(8,128)}, bf16[1536,4224]{1,0:T(8,128)(2,1)}) custom-call(bf16[128,1536]{1,0:T(8,128)(2,1)} %convert_element_type.20.x_ref.gy_ref, f32[128,1536]{1,0:T(8,128)} %get-tuple-element.63.h_ref, bf16[128,1536]{1,0:T(8,128)(2,1)} %get-tuple-element.169.x_ref, bf16[1536,4224]{1,0:T(8,128)(2,1)} %all-gather.4.cloned.1.call-done.w_ref, ...), custom_call_target="tpu_custom_call" | custom-call | flops 3221225472 | bytes 25952256 | tf_op jit(solution)/shard_map/pallas_call | solution.py:242
  721.7 2.2 select_bitcast_fusion
  723.9 9.7 %collective-permute-start.4 = (f32[128,1536]{1,0:T(8,128)}, f32[128,1536]{1,0:T(8,128)}, u32[]{:S(2)}, u32[]{:S(2)}) collective-permute-start(f32[128,1536]{1,0:T(8,128)} %get-tuple-element.161), channel_id=1, source_target_pairs={{0,16},{16,0},{1,17},{17,1},{2,18},{18,2},{3,19},{19,3},{4,20},{20... | collective-permute-start | bytes 2359304 | tf_op jit(solution)/shard_map/ppermute | solution.py:1112
  733.7 179.8 %shard_map.253 = (f32[96,4224]{1,0:T(8,128)}, f32[5,384,512]{2,1,0:T(8,128)}, f32[5,384,512]{2,1,0:T(8,128)}, f32[5,512,384]{2,1,0:T(8,128)}) custom-call(bf16[16,96,4224]{2,1,0:T(8,128)(2,1)} %bitcast.82, bf16[16,96,4224]{2,1,0:T(8,128)(2,1)} %bitcast.81, bf16[2,10,384,512]{3,2,1,0:T(8,128)(2,1)} %bitcast.85, bf16[2,10,384,512]{3,2,1,0:T(8,128)(2,1)} %bitcast.86, ...), custom_call_target="tpu_custom_call" | custom-call | tf_op jit(solution)/shard_map/pallas_call | solution.py:1078
  913.5 1.9 slice_bitcast_fusion.2
  915.4 2.3 slice_bitcast_fusion
  922.8 2.8 maximum_select_fusion
  928.3 2.0 copy.63
  931.8 2.0 copy.64
  935.4 1.9 copy.65
  (79 shorter events, 30.0 us)
Async XLA Ops:
  7.2 29.0 %copy-start = (s32[2,1,2]{2,1,0:T(1,128)S(1)}, s32[2,1,2]{2,1,0:T(1,128)}, u32[]{:S(2)}) copy-start(s32[2,1,2]{2,1,0:T(1,128)} %param.18) | copy-start | bytes 52
  7.2 157.0 %all-gather.4.cloned.1.call-start = ((), (), s32[]{:S(2)}) async-start(), calls=%async_computation.1 | async-start | bytes 13787136 | tf_op jit(solution)/shard_map/all_gather | solution.py:1152
  9.6 24.7 %copy-start.12 = (s32[1,2,1,128,8]{3,4,2,1,0:T(8,128)S(1)}, s32[1,2,1,128,8]{3,4,2,1,0:T(8,128)}, u32[]{:S(2)}) copy-start(s32[1,2,1,128,8]{3,4,2,1,0:T(8,128)} %param.19) | copy-start | bytes 24580
  9.6 26.7 %copy-start.14 = (s32[2,1,128]{2,1,0:T(1,128)S(1)}, s32[2,1,128]{2,1,0:T(1,128)}, u32[]{:S(2)}) copy-start(s32[2,1,128]{2,1,0:T(1,128)} %param.17) | copy-start | bytes 3076
  9.6 26.9 %copy-start.10 = (bf16[2,1,128,1536]{3,2,1,0:T(8,128)(2,1)S(1)}, bf16[2,1,128,1536]{3,2,1,0:T(8,128)(2,1)}, u32[]{:S(2)}) copy-start(bf16[2,1,128,1536]{3,2,1,0:T(8,128)(2,1)} %param.16) | copy-start | bytes 2359300
  9.6 26.9 %copy-start.11 = (bf16[2,1,128,1536]{3,2,1,0:T(8,128)(2,1)S(1)}, bf16[2,1,128,1536]{3,2,1,0:T(8,128)(2,1)}, u32[]{:S(2)}) copy-start(bf16[2,1,128,1536]{3,2,1,0:T(8,128)(2,1)} %param.15) | copy-start | bytes 2359300
  11.1 21.1 %collective-permute-start = (bf16[96,4224]{1,0:T(8,128)(2,1)S(1)}, bf16[96,4224]{1,0:T(8,128)(2,1)S(1)}, u32[]{:S(2)}, u32[]{:S(2)}) collective-permute-start(bf16[96,4224]{1,0:T(8,128)(2,1)S(1)} %concatenate.31), channel_id=1, source_target_pairs={{0,16},{16,0},{1,17},{17,1},{2,18},{18,2},{3,19},{19,3},{4,20},{20... | collective-permute-start | bytes 2433032 | tf_op jit(solution)/shard_map/ppermute | solution.py:1112
  33.5 286.8 %all-gather.6.cloned.1.call-start = ((), (), s32[]{:S(2)}) async-start(), calls=%async_computation.2 | async-start | bytes 13787136 | tf_op jit(solution)/shard_map/all_gather | solution.py:1178
  34.3 62.0 %collective-permute-start.1 = (s32[8,128]{1,0:T(8,128)S(1)}, s32[8,128]{1,0:T(8,128)S(1)}, u32[]{:S(2)}, u32[]{:S(2)}) collective-permute-start(s32[8,128]{1,0:T(8,128)S(1)} %dynamic-slice_bitcast_fusion.2), channel_id=1, source_target_pairs={{0,16},{16,0},{1,17},{17,1},{2,18},{18,2},{3,19},{19,3},{4,20},{20... | collective-permute-start | bytes 12296 | tf_op jit(solution)/shard_map/ppermute | solution.py:1112
  260.7 57.6 %copy-start.7 = (f32[128,1536]{1,0:T(8,128)S(1)}, f32[128,1536]{1,0:T(8,128)}, u32[]{:S(2)}) copy-start(f32[128,1536]{1,0:T(8,128)} %get-tuple-element.63.h_ref) | copy-start | bytes 2359300
  548.5 39.0 %copy-start.8 = (bf16[8,128,1536]{2,1,0:T(8,128)(2,1)S(1)}, bf16[8,128,1536]{2,1,0:T(8,128)(2,1)}, u32[]{:S(2)}) copy-start(bf16[8,128,1536]{2,1,0:T(8,128)(2,1)} %get-tuple-element.93) | copy-start | bytes 9437188
  588.8 100.9 %collective-permute-start.2 = (bf16[4,128,1536]{2,1,0:T(8,128)(2,1)}, bf16[4,128,1536]{2,1,0:T(8,128)(2,1)}, u32[]{:S(2)}, u32[]{:S(2)}) collective-permute-start(bf16[4,128,1536]{2,1,0:T(8,128)(2,1)} %slice.36), channel_id=1, source_target_pairs={{16,0},{17,1},{18,2},{19,3},{20,4},{21,5},{22,6},{23,7},{24,8},{25... | collective-permute-start | bytes 4718600 | tf_op jit(solution)/shard_map/ppermute | solution.py:1199
  689.6 7.1 copy-start.13
  692.4 225.3 %all-to-all-start = ((bf16[4,128,1536]{2,1,0:T(8,128)(2,1)}), bf16[4,128,1536]{2,1,0:T(8,128)(2,1)S(1)}, u32[]{:S(2)}, u32[]{:S(2)}) async-start(bf16[4,128,1536]{2,1,0:T(8,128)(2,1)} %slice_select_fusion), calls=%async_computation | async-start | bytes 3145728 | tf_op jit(solution)/shard_map/all_to_all | solution.py:1203
  697.3 24.4 %copy-start.9 = (f32[128,1536]{1,0:T(8,128)S(1)}, f32[128,1536]{1,0:T(8,128)}, u32[]{:S(2)}) copy-start(f32[128,1536]{1,0:T(8,128)} %get-tuple-element.85) | copy-start | bytes 2359300
  723.9 198.9 %collective-permute-start.4 = (f32[128,1536]{1,0:T(8,128)}, f32[128,1536]{1,0:T(8,128)}, u32[]{:S(2)}, u32[]{:S(2)}) collective-permute-start(f32[128,1536]{1,0:T(8,128)} %get-tuple-element.161), channel_id=1, source_target_pairs={{0,16},{16,0},{1,17},{17,1},{2,18},{18,2},{3,19},{19,3},{4,20},{20... | collective-permute-start | bytes 2359304 | tf_op jit(solution)/shard_map/ppermute | solution.py:1112
  913.5 4.5 copy-start.2
  913.5 4.5 copy-start.6
  918.2 9.1 collective-permute-start.3
  921.1 7.2 copy-start.5
  928.3 3.5 copy-start.4
  931.8 3.5 copy-start.3
  931.8 5.5 copy-start.1
Sparse Core Ops, SparseCore 0:
  33.7 130.4 all-gather.3
  167.1 153.1 all-gather.5

commit v3 on v2

--- a/solution.py
+++ b/solution.py
@@ -263,6 +263,14 @@
     return jnp.concatenate([one_hot(pos[j : j + 1], cap) for j in range(per)], axis=0)
 
 
+def all_hots_back(pos, per, cap):
+    width = per * cap
+    expert = jnp.where(iota((8, width), 1) // cap == iota((8, width), 0), 1.0, 0.0).astype(BF)
+    wide = dot(pos.astype(F32).astype(BF), expert, 0, 0)
+    slot = (iota((1, width), 1) % cap).astype(F32)
+    return jnp.where(wide == slot, 1.0, 0.0).astype(BF)
+
+
 def slots_of(rt, first, per):
     t = rt.shape[1]
     experts = iota((16, t), 0)
@@ -306,7 +314,7 @@
         def _():
             copy(b - 2, slot).wait()
 
-        back = jnp.transpose(all_hots(pos_ref[b], per, cap)).astype(BF)
+        back = all_hots_back(pos_ref[b], per, cap)
         at = pl.ds(pl.multiple_of(b * cap, cap), cap)
         rows = jnp.concatenate([rows_ref[j, at, :] for j in range(per)], axis=0)
         obuf[slot] = dot(back, rows).astype(BF)
@@ -363,8 +371,8 @@
             x = x_scr[j, at, :]
             gp = dot(x, wg_ref[0])
             up = dot(x, wu_ref[0])
-            gp_ref[0, at, :] = gp
-            up_ref[0, at, :] = up
+            gp_ref[0, at, :] = gp.astype(BF)
+            up_ref[0, at, :] = up.astype(BF)
             hid = (gp / (1.0 + jnp.exp(-gp)) * up).astype(BF)
             _, gate = chunk_gates(c, j, chunk, cap, pos_ref, gate_ref)
             y_scr[j, at, :] = (dot(hid, wd_ref[0]) * gate).astype(BF)
@@ -394,8 +402,8 @@
         functools.partial(experts_fwd_kernel, layer, e_pad, cap),
         grid=(per,),
         out_shape=(
-            sds((per, rows, f), F32),
-            sds((per, rows, f), F32),
+            sds((per, rows, f), BF),
+            sds((per, rows, f), BF),
             sds((count, 8, t), jnp.int32),
             sds((count, 8, t), F32),
             sds((count, t, d), BF),
@@ -429,14 +437,31 @@
     )(rt, wrt, wg, wu, wd, blocks)
 
 
+def gather_rows(count, per, cap, pos_ref, b_hbm, gy_hbm, x_scr, y_scr, bbuf, gbuf, bsem, gsem):
+    def prepare(b, slot):
+        hots = all_hots(pos_ref[b], per, cap).astype(BF)
+        at = pl.ds(pl.multiple_of(b * cap, cap), cap)
+        for source, dest in ((bbuf, x_scr), (gbuf, y_scr)):
+            if dest is not None:
+                rows = dot(hots, source[slot]).astype(BF)
+                for k in range(per):
+                    dest[k, at, :] = rows[k * cap : (k + 1) * cap]
+
+    def copies(b, slot):
+        both = [pltpu.make_async_copy(gy_hbm.at[b], gbuf.at[slot], gsem.at[slot])]
+        if x_scr is not None:
+            both.append(pltpu.make_async_copy(b_hbm.at[b], bbuf.at[slot], bsem.at[slot]))
+        return both
+
+    streamed(count, copies, prepare)
+
+
 def experts_bwd_kernel(
-    layer, cap, pos_ref, gate_ref, wg_ref, wu_ref, wd_ref, gp_ref, up_ref, b_hbm, gy_hbm,
-    even_ref, odd_ref, evend_ref, oddd_ref, dg_ref, out_hbm, x_scr, y_scr, dgp_scr, dup_scr, hid_scr, bbuf, gbuf, obuf, bsem, gsem, osem,
+    layer, cap, pos_ref, gate_ref, wg_ref, wu_ref, wd_ref, gp_ref, up_ref, gy_hbm,
+    dgp_ref, dup_ref, hid_ref, dg_ref, out_hbm, y_scr, gbuf, obuf, gsem, osem,
 ):
-    per, rows, d = x_scr.shape
+    per, rows, d = y_scr.shape
     count = pos_ref.shape[0]
-    parts = even_ref.shape[0]
-    piece = even_ref.shape[3]
     chunk = 256
     j = pl.program_id(0)
 
@@ -444,29 +469,13 @@
     def _():
         @pl.when(j == 0)
         def _():
-            def prepare(b, slot):
-                hots = all_hots(pos_ref[b], per, cap).astype(BF)
-                x = dot(hots, bbuf[slot]).astype(BF)
-                y = dot(hots, gbuf[slot]).astype(BF)
-                at = pl.ds(pl.multiple_of(b * cap, cap), cap)
-                for k in range(per):
-                    x_scr[k, at, :] = x[k * cap : (k + 1) * cap]
-                    y_scr[k, at, :] = y[k * cap : (k + 1) * cap]
-
-            streamed(
-                count,
-                lambda b, slot: [
-                    pltpu.make_async_copy(b_hbm.at[b], bbuf.at[slot], bsem.at[slot]),
-                    pltpu.make_async_copy(gy_hbm.at[b], gbuf.at[slot], gsem.at[slot]),
-                ],
-                prepare,
-            )
+            gather_rows(count, per, cap, pos_ref, None, gy_hbm, None, y_scr, None, gbuf, None, gsem)
             dg_ref[...] = jnp.zeros_like(dg_ref)
 
         def part(c, carry):
             at = pl.ds(pl.multiple_of(c * chunk, chunk), chunk)
             raw = dot(y_scr[j, at, :], wd_ref[0], 1, 1)
-            gp, up = gp_ref[0, at, :], up_ref[0, at, :]
+            gp, up = gp_ref[0, at, :].astype(F32), up_ref[0, at, :].astype(F32)
             sg = 1.0 / (1.0 + jnp.exp(-gp))
             silu = gp * sg
             hid = silu * up
@@ -476,98 +485,105 @@
                 b = c * (chunk // cap) + bb
                 dg_ref[b, pl.ds(j, 1), :] = jnp.sum(hots[bb] * dgate[bb * cap : (bb + 1) * cap], axis=0, keepdims=True)
             dh = raw * gate
-            dgp_scr[at, :] = (dh * up * sg * (1.0 + gp * (1.0 - sg))).astype(BF)
-            dup_scr[at, :] = (dh * silu).astype(BF)
-            hid_scr[at, :] = (hid * gate).astype(BF)
+            dgp = (dh * up * sg * (1.0 + gp * (1.0 - sg))).astype(BF)
+            dup = (dh * silu).astype(BF)
+            dgp_ref[0, at, :] = dgp
+            dup_ref[0, at, :] = dup
+            hid_ref[0, at, :] = (hid * gate).astype(BF)
+            y_scr[j, at, :] = (dot(dgp, wg_ref[0], 1, 1) + dot(dup, wu_ref[0], 1, 1)).astype(BF)
             return carry
 
         lax.fori_loop(0, rows // chunk, part, 0)
-
-        odd = lax.rem(lax.axis_index("group"), 2)
-        place = lax.axis_index("group") // 2
-        for q in range(parts):
-            cols = slice(2 * q * piece, 2 * (q + 1) * piece)
-            at = lax.bitwise_xor(place, q)
-            for n, right in ((0, dgp_scr), (1, dup_scr)):
-                full = dot(x_scr[j, :, cols], right[...], 0, 0).astype(BF)
-                for parity, (low, high) in ((0, (even_ref, odd_ref)), (1, (odd_ref, even_ref))):
-
-                    @pl.when(odd == parity)
-                    def _(low=low, high=high):
-                        low[at, n, 0] = full[:piece]
-                        high[at, n, 0] = full[piece:]
-
-            full = dot(hid_scr[...], y_scr[j, :, cols], 0, 0).astype(BF)
-            for parity, (low, high) in ((0, (evend_ref, oddd_ref)), (1, (oddd_ref, evend_ref))):
-
-                @pl.when(odd == parity)
-                def _(low=low, high=high):
-                    low[at, 0] = full[:, :piece]
-                    high[at, 0] = full[:, piece:]
-
-        def rows_back(c, carry):
-            at = pl.ds(pl.multiple_of(c * chunk, chunk), chunk)
-            y_scr[j, at, :] = (dot(dgp_scr[at, :], wg_ref[0], 1, 1) + dot(dup_scr[at, :], wu_ref[0], 1, 1)).astype(BF)
-            return carry
-
-        lax.fori_loop(0, rows // chunk, rows_back, 0)
 
         @pl.when(j == per - 1)
         def _():
             combine(count, per, cap, pos_ref, y_scr, out_hbm, obuf, osem)
 
 
-def experts_bwd(layer, cap, groups, pos, gate, wg, wu, wd, gp, up, blocks, grads):
-    count, t, d = blocks.shape
+def experts_bwd(layer, cap, pos, gate, wg, wu, wd, gp, up, grads):
+    count, t, d = grads.shape
     per, _, f = wg.shape
     rows = count * cap
     sds = jax.ShapeDtypeStruct
+    by_expert = pl.BlockSpec((1, rows, f), lambda j: (j, 0, 0))
     return pl.pallas_call(
         functools.partial(experts_bwd_kernel, layer, cap),
         grid=(per,),
-        out_shape=(
-            sds((groups // 2, 2, per, d // groups, f), BF),
-            sds((groups // 2, 2, per, d // groups, f), BF),
-            sds((groups // 2, per, f, d // groups), BF),
-            sds((groups // 2, per, f, d // groups), BF),
-            sds((count, 8, t), F32),
-            sds((count, t, d), BF),
-        ),
+        out_shape=(sds((per, rows, f), BF),) * 3 + (sds((count, 8, t), F32), sds((count, t, d), BF)),
         in_specs=[
             fixed(pos.shape),
             fixed(gate.shape),
             pl.BlockSpec((1, d, f), lambda j: (j, 0, 0)),
             pl.BlockSpec((1, d, f), lambda j: (j, 0, 0)),
             pl.BlockSpec((1, f, d), lambda j: (j, 0, 0)),
-            pl.BlockSpec((1, rows, f), lambda j: (j, 0, 0)),
-            pl.BlockSpec((1, rows, f), lambda j: (j, 0, 0)),
-            any_spec(),
+            by_expert,
+            by_expert,
             any_spec(),
         ],
-        out_specs=(
-            pl.BlockSpec((groups // 2, 2, 1, d // groups, f), lambda j: (0, 0, j, 0, 0)),
-            pl.BlockSpec((groups // 2, 2, 1, d // groups, f), lambda j: (0, 0, j, 0, 0)),
-            pl.BlockSpec((groups // 2, 1, f, d // groups), lambda j: (0, j, 0, 0)),
-            pl.BlockSpec((groups // 2, 1, f, d // groups), lambda j: (0, j, 0, 0)),
-            fixed((count, 8, t)),
-            any_spec(),
-        ),
+        out_specs=(by_expert, by_expert, by_expert, fixed((count, 8, t)), any_spec()),
         scratch_shapes=[
             pltpu.VMEM((per, rows, d), BF),
-            pltpu.VMEM((per, rows, d), BF),
-            pltpu.VMEM((rows, f), BF),
-            pltpu.VMEM((rows, f), BF),
-            pltpu.VMEM((rows, f), BF),
-            pltpu.VMEM((2, t, d), BF),
             pltpu.VMEM((2, t, d), BF),
             pltpu.VMEM((2, t, d), BF),
             pltpu.SemaphoreType.DMA((2,)),
             pltpu.SemaphoreType.DMA((2,)),
-            pltpu.SemaphoreType.DMA((2,)),
         ],
         compiler_params=pltpu.CompilerParams(vmem_limit_bytes=VMEM_LIMIT),
-        cost_estimate=pl.CostEstimate(flops=12 * per * rows * d * f, bytes_accessed=12 * per * d * f, transcendentals=per * rows * f),
-    )(pos, gate, wg, wu, wd, gp, up, blocks, grads)
+        cost_estimate=pl.CostEstimate(flops=6 * per * rows * d * f, bytes_accessed=8 * per * d * f, transcendentals=per * rows * f),
+    )(pos, gate, wg, wu, wd, gp, up, grads)
+
+
+def weight_grads(
+    cap, pos_ref, b_hbm, gy_hbm, dgp_hbm, dup_hbm, hid_hbm, outs, x_scr, y_scr, bbuf, gbuf, act_buf, gu_buf, dn_buf,
+    bsem, gsem, act_sem, gu_sem, dn_sem,
+):
+    even, odd, even_dn, odd_dn = outs
+    per, rows, d = x_scr.shape
+    count = pos_ref.shape[0]
+    parts, piece = gu_buf.shape[1] // 2, gu_buf.shape[3]
+    g = lax.axis_index("group")
+    parity, place = lax.rem(g, 2), g // 2
+    gather_rows(count, per, cap, pos_ref, b_hbm, gy_hbm, x_scr, y_scr, bbuf, gbuf, bsem, gsem)
+
+    def acts(j, slot):
+        return [
+            pltpu.make_async_copy(source.at[j], act_buf.at[slot, n], act_sem.at[slot, n])
+            for n, source in enumerate((dgp_hbm, dup_hbm, hid_hbm))
+        ]
+
+    def outgoing(j, slot):
+        half = pl.ds(0, parts), pl.ds(parts, parts)
+        return [
+            pltpu.make_async_copy(gu_buf.at[slot, half[0]], even.at[:, :, j], gu_sem.at[slot, 0]),
+            pltpu.make_async_copy(gu_buf.at[slot, half[1]], odd.at[:, :, j], gu_sem.at[slot, 1]),
+            pltpu.make_async_copy(dn_buf.at[slot, half[0]], even_dn.at[:, j], dn_sem.at[slot, 0]),
+            pltpu.make_async_copy(dn_buf.at[slot, half[1]], odd_dn.at[:, j], dn_sem.at[slot, 1]),
+        ]
+
+    def body(j, slot):
+        @pl.when(j >= 2)
+        def _():
+            for c in outgoing(j - 2, slot):
+                c.wait()
+
+        for q in range(parts):
+            cols = slice(2 * q * piece, 2 * (q + 1) * piece)
+            at = lax.bitwise_xor(place, q)
+            low, high = parity * parts + at, (1 - parity) * parts + at
+            for n in range(2):
+                full = dot(x_scr[j, :, cols], act_buf[slot, n], 0, 0).astype(BF)
+                gu_buf[slot, low, n] = full[:piece]
+                gu_buf[slot, high, n] = full[piece:]
+            full = dot(act_buf[slot, 2], y_scr[j, :, cols], 0, 0).astype(BF)
+            dn_buf[slot, low] = full[:, :piece]
+            dn_buf[slot, high] = full[:, piece:]
+        for c in outgoing(j, slot):
+            c.start()
+
+    streamed(per, acts, body)
+    for j in (per - 2, per - 1):
+        for c in outgoing(j, j % 2):
+            c.wait()
 
 
 def meet(n, with_cross):
@@ -625,7 +641,7 @@
     return pl.pallas_call(
         functools.partial(spread_kernel, layer, n),
         out_shape=jax.ShapeDtypeStruct((2, n) + x.shape, x.dtype),
-        in_specs=[any_spec()],
+        in_specs=vmem(1),
         out_specs=any_spec(),
         scratch_shapes=[
             pltpu.SemaphoreType.DMA((n,)),
@@ -636,9 +652,13 @@
     )(x)
 
 
-def collect_kernel(layer, n, arrays, *refs):
-    srcs, outs, relays = refs[:arrays], refs[arrays : 2 * arrays], refs[2 * arrays : 3 * arrays]
-    relay_send, relay_recv, send_sem, recv_sem, local_sem = refs[3 * arrays :]
+def collect_kernel(layer, n, arrays, cap, *refs):
+    srcs, refs = refs[:arrays], refs[arrays:]
+    work_in, refs = (refs[:6], refs[6:]) if cap else ((), refs)
+    outs, refs = refs[:arrays], refs[arrays:]
+    work_out, refs = (refs[:4], refs[4:]) if cap else ((), refs)
+    relays, refs = refs[:arrays], refs[arrays:]
+    relay_send, relay_recv, send_sem, recv_sem, local_sem = refs[:5]
     s, z = lax.axis_index("section"), lax.axis_index("expert")
     meet(n, False)
 
@@ -675,6 +695,8 @@
                     give(a, srcs[a].at[layer, lax.rem(z + k, n)], k).start()
                 else:
                     pltpu.make_async_copy(srcs[a].at[layer, z], outs[a].at[z], local_sem.at[a]).start()
+        if cap:
+            weight_grads(cap, *work_in, work_out, *refs[5:])
         for k in order:
             for a in range(arrays):
                 hop(a, lax.rem(z + k, n)).wait_send()
@@ -698,24 +720,48 @@
                 pltpu.make_async_copy(relays[a].at[z], outs[a].at[z], local_sem.at[a]).wait()
 
 
-def collect(layer, cid, *arrays):
-    n = lax.axis_size("expert")
+def collect(layer, cid, arrays, work=None):
+    n, groups = lax.axis_size("expert"), lax.axis_size("group")
     count = len(arrays)
+    sds = jax.ShapeDtypeStruct
+    dma = pltpu.SemaphoreType.DMA
+    outs = [sds(a.shape[1:], a.dtype) for a in arrays]
+    scratch = [pltpu.VMEM(a.shape[1:], a.dtype) for a in arrays]
+    scratch += [dma((count, n)), dma((count, n)), dma((count, n)), dma((count, n)), dma((count,))]
+    in_specs = [any_spec()] * count
+    extra = ()
+    if work:
+        extra = work[1:]
+        pos, blocks, _, dgp = extra[:4]
+        t, d = blocks.shape[1:]
+        per, rows, f = dgp.shape
+        piece = d // groups
+        outs += [sds((groups // 2, 2, per, piece, f), BF)] * 2 + [sds((groups // 2, per, f, piece), BF)] * 2
+        in_specs += vmem(1) + [any_spec()] * 5
+        scratch += [
+            pltpu.VMEM((per, rows, d), BF),
+            pltpu.VMEM((per, rows, d), BF),
+            pltpu.VMEM((2, t, d), BF),
+            pltpu.VMEM((2, t, d), BF),
+            pltpu.VMEM((2, 3, rows, f), BF),
+            pltpu.VMEM((2, groups, 2, piece, f), BF),
+            pltpu.VMEM((2, groups, f, piece), BF),
+            dma((2,)),
+            dma((2,)),
+            dma((2, 3)),
+            dma((2, 2)),
+            dma((2, 2)),
+        ]
     return pl.pallas_call(
-        functools.partial(collect_kernel, layer, n, count),
-        out_shape=tuple(jax.ShapeDtypeStruct(a.shape[1:], a.dtype) for a in arrays),
-        in_specs=[any_spec()] * count,
-        out_specs=tuple([any_spec()] * count),
-        scratch_shapes=[pltpu.VMEM(a.shape[1:], a.dtype) for a in arrays]
-        + [
-            pltpu.SemaphoreType.DMA((count, n)),
-            pltpu.SemaphoreType.DMA((count, n)),
-            pltpu.SemaphoreType.DMA((count, n)),
-            pltpu.SemaphoreType.DMA((count, n)),
-            pltpu.SemaphoreType.DMA((count,)),
-        ],
-        compiler_params=pltpu.CompilerParams(collective_id=cid, has_side_effects=True),
-    )(*arrays)
+        functools.partial(collect_kernel, layer, n, count, work[0] if work else 0),
+        out_shape=tuple(outs),
+        in_specs=in_specs,
+        out_specs=tuple([any_spec()] * len(outs)),
+        scratch_shapes=scratch,
+        compiler_params=pltpu.CompilerParams(
+            collective_id=cid, has_side_effects=True, vmem_limit_bytes=VMEM_LIMIT if work else 16 * 1024 * 1024
+        ),
+    )(*arrays, *extra)
 
 
 def top_bit(q):
@@ -1108,6 +1154,198 @@
     )(dd0, dd1, *experts0, *experts1)
 
 
+def low_bit(q):
+    return top_bit(q & -q)
+
+
+def open_kernel(
+    n, groups, pieces, w_ref, cot_ref, rt_ref, w_out, gy_out, rt_out, rt_side,
+    s_right, r_right, s_left, r_left, s_group, r_group, s_y, r_y, s_cross, r_cross, s_rt, r_rt, s_side, r_side, local_sem,
+):
+    s, g, z = lax.axis_index("section"), lax.axis_index("group"), lax.axis_index("expert")
+    remote = functools.partial(pltpu.make_async_remote_copy, device_id_type=MESH)
+    rows = w_ref.shape[0] // pieces
+    bits = top_bit(groups)
+    other = {"section": 1 - s}
+    barrier = pltpu.get_barrier_semaphore()
+    peers = [other] + [{"group": lax.bitwise_xor(g, 1 << b)} for b in range(bits)] + [{"expert": lax.rem(z + k, n)} for k in range(1, n)]
+    for peer in peers:
+        pl.semaphore_signal(barrier, inc=1, device_id=peer, device_id_type=MESH)
+    pl.semaphore_wait(barrier, len(peers))
+    sent = []
+
+    def launch(cond, make):
+        sent.append((cond, make))
+        if cond is None:
+            make().start()
+        else:
+
+            @pl.when(cond)
+            def _():
+                make().start()
+
+    def part(q, zz, c):
+        return w_out.at[lax.bitwise_xor(g, q) * n + zz, pl.ds(c * rows, rows)] if c < pieces else gy_out.at[s, zz]
+
+    def chain(to, zz, t, c, ssem, rsem):
+        return remote(src_ref=part(0, zz, c), dst_ref=part(0, zz, c), send_sem=ssem.at[t, c], recv_sem=rsem.at[t, c], device_id={"expert": to})
+
+    def right(t, c):
+        return chain(z + 1, z - t, t, c, s_right, r_right)
+
+    def left(t, c):
+        return chain(z - 1, z + t, t, c, s_left, r_left)
+
+    def over(q, b, zz, c):
+        at = q | (1 << b)
+        return remote(
+            src_ref=part(q, zz, c), dst_ref=part(q, zz, c), send_sem=s_group.at[at, zz, c], recv_sem=r_group.at[at, zz, c],
+            device_id={"group": lax.bitwise_xor(g, 1 << b)},
+        )
+
+    def hop(c):
+        at = pl.ds(c * rows, rows)
+        return remote(
+            src_ref=w_ref.at[at], dst_ref=w_out.at[g * n + z, at], send_sem=s_y.at[c], recv_sem=r_y.at[c], device_id=other
+        )
+
+    def cross(zz):
+        return remote(src_ref=gy_out.at[0, zz], dst_ref=gy_out.at[0, zz], send_sem=s_cross.at[zz], recv_sem=r_cross.at[zz], device_id=other)
+
+    def route(m, k):
+        return remote(
+            src_ref=rt_ref.at[m], dst_ref=rt_out.at[m, z], send_sem=s_rt.at[m, k], recv_sem=r_rt.at[m, k],
+            device_id={"expert": lax.rem(z + k, n)},
+        )
+
+    def side():
+        return remote(src_ref=rt_ref.at[1 - s], dst_ref=rt_side, send_sem=s_side, recv_sem=r_side, device_id=other)
+
+    launch(s == 0, functools.partial(hop, 0))
+    launch(None, side)
+    own = [pltpu.make_async_copy(cot_ref, gy_out.at[s, z], local_sem.at[0])]
+    own += [pltpu.make_async_copy(rt_ref.at[m], rt_out.at[m, z], local_sem.at[1 + m]) for m in range(2)]
+
+    def keep():
+        return pltpu.make_async_copy(w_ref, w_out.at[g * n + z], local_sem.at[3])
+
+    for copy in own:
+        copy.start()
+
+    @pl.when(s == 0)
+    def _():
+        keep().start()
+        keep().wait()
+
+    def spread_out(cond, zz, c):
+        if c < pieces:
+            for b in reversed(range(bits)):
+                launch(cond, functools.partial(over, 0, b, zz, c))
+        else:
+            launch((s == 0) if cond is None else ((s == 0) & cond), functools.partial(cross, zz))
+
+    def pass_along(t, c):
+        if t == 0:
+            if c < pieces:
+
+                @pl.when(s != 0)
+                def _():
+                    hop(c).wait_recv()
+            else:
+                own[0].wait()
+            launch(z < n - 1, functools.partial(right, t, c))
+            launch(z > 0, functools.partial(left, t, c))
+            spread_out(None, z, c)
+            if c + 1 < pieces:
+
+                @pl.when(s == 0)
+                def _():
+                    hop(c).wait_send()
+                    hop(c + 1).start()
+        else:
+            from_left, from_right = z >= t, z + t < n
+
+            @pl.when(from_left)
+            def _():
+                right(t - 1, c).wait_recv()
+
+            launch(from_left & (z < n - 1), functools.partial(right, t, c))
+            spread_out(from_left, z - t, c)
+
+            @pl.when(from_right)
+            def _():
+                left(t - 1, c).wait_recv()
+
+            launch(from_right & (z > 0), functools.partial(left, t, c))
+            spread_out(from_right, z + t, c)
+
+    def forward(q, k):
+        zz = lax.rem(z + k, n)
+        for c in range(pieces):
+            over(q & (q - 1), low_bit(q), zz, c).wait_recv()
+            for b in reversed(range(low_bit(q))):
+                launch(None, functools.partial(over, q, b, zz, c))
+
+    for t in range(n):
+        for c in range(pieces):
+            pass_along(t, c)
+        if t == 0:
+            for m in range(2):
+                for k in range(1, n):
+                    launch(None, functools.partial(route, m, k))
+    pending = [(q, k) for q in sorted(range(1, groups), key=lambda q: -low_bit(q)) for k in range(n)]
+    for t in range(n):
+        pass_along(t, pieces)
+        forward(*pending.pop(0))
+    for q, k in pending:
+        forward(q, k)
+
+    @pl.when(s != 0)
+    def _():
+        for zz in range(n):
+            cross(zz).wait_recv()
+
+    side().wait_recv()
+    for m in range(2):
+        own[1 + m].wait()
+        for k in range(1, n):
+            route(m, k).wait_recv()
+    @pl.when(s == 0)
+    def _():
+        if pieces > 1:
+            hop(pieces - 1).wait_send()
+
+    for cond, make in sent[(1 if pieces > 1 else 0) :]:
+        if cond is None:
+            make().wait_send()
+        else:
+
+            @pl.when(cond)
+            def _(make=make):
+                make().wait_send()
+
+
+def open_up(cid, packed, cot, rt):
+    n, groups = lax.axis_size("expert"), lax.axis_size("group")
+    sh = packed.shape[0]
+    pieces = 3 if sh % 48 == 0 else 1
+    dma = pltpu.SemaphoreType.DMA
+    sds = jax.ShapeDtypeStruct
+
+    def both(shape):
+        return [dma(shape), dma(shape)]
+
+    w, gy, rt_all, rt_side = pl.pallas_call(
+        functools.partial(open_kernel, n, groups, pieces),
+        out_shape=(sds((groups * n,) + packed.shape, BF), sds((2, n) + cot.shape, BF), sds((2, n) + rt.shape[1:], rt.dtype), sds(rt.shape[1:], rt.dtype)),
+        in_specs=vmem(3),
+        out_specs=(any_spec(), any_spec(), any_spec(), any_spec()),
+        scratch_shapes=both((n, pieces + 1)) + both((n, pieces + 1)) + both((groups, n, pieces)) + both((pieces,)) + both((n,)) + both((2, n)) + [dma, dma] + [dma((4,))],
+        compiler_params=pltpu.CompilerParams(collective_id=cid, has_side_effects=True),
+    )(packed, cot, rt)
+    return w.reshape(groups * n * sh, -1), gy, rt_all, rt_side
+
+
 def swap_sections(value):
     return lax.ppermute(value, "section", [(0, 1), (1, 0)])
 
@@ -1147,9 +1385,8 @@
         axis=1,
     )
     packed = jnp.concatenate([w_query[0], key_weight[0], value_weight[0], w_out[0].T, aux], axis=1)
-    other = swap_sections(packed)
-    shards = (jnp.where(at_zero, packed, other), jnp.where(at_zero, other, packed))
-    first_weights = lax.all_gather(shards[0], ("group", "expert"), axis=0, tiled=True)
+    other = lax.ppermute(packed, "section", [(1, 0)])
+    second_shard = jnp.where(at_zero, other, packed)
 
     x0 = lax.dynamic_index_in_dim(inputs[:, 0], s, 0, keepdims=False)
     cot = lax.dynamic_index_in_dim(cotangent[:, 0], s, 0, keepdims=False)
@@ -1162,9 +1399,6 @@
 
     rt = jnp.swapaxes(routes[0, :, 0], 1, 2)
     rt_mine = lax.dynamic_index_in_dim(rt, s, 0, keepdims=False)
-    rt_theirs = swap_sections(lax.dynamic_index_in_dim(rt, 1 - s, 0, keepdims=False))
-    rt_tokens = (jnp.where(at_zero, rt_mine, rt_theirs), jnp.where(at_zero, rt_theirs, rt_mine))
-    rt_all = lax.all_gather(rt, "expert", axis=1, tiled=False).reshape(2 * n, top, t)
 
     def flat(z):
         return z.reshape((2 * n,) + z.shape[2:])
@@ -1172,20 +1406,23 @@
     def paired(z):
         return z.reshape((2, n) + z.shape[1:])
 
-    gy1 = flat(spread(1, 1, cot))
+    first_weights, gy1, rt_all, rt_theirs = open_up(1, packed, cot, rt)
+    rt_tokens = (jnp.where(at_zero, rt_mine, rt_theirs), jnp.where(at_zero, rt_theirs, rt_mine))
+    gy1, rt_all = flat(gy1), flat(rt_all)
 
     qkv0, p0, o0, h0, b0, wrt0 = attn_fwd(x0, first_weights, cos, sin, meta, segr)
-    second_weights = lax.all_gather(shards[1], ("group", "expert"), axis=0, tiled=True)
+    second_shard, b0 = lax.optimization_barrier((second_shard, b0))
+    second_weights = lax.all_gather(second_shard, ("group", "expert"), axis=0, tiled=True)
     b0_all = flat(spread(0, 2, b0))
     gp0, up0, pos0, gate0, part0 = experts_fwd(0, e_pad, cap, rt_all, wrt0, wg, wu, wd, b0_all)
-    (back0,) = collect(0, 3, paired(part0))
+    (back0,) = collect(0, 3, (paired(part0),))
     x1 = (h0 + jnp.sum(back0.astype(F32), axis=0)).astype(BF)
 
     qkv1, p1, o1, h1, b1, wrt1 = attn_fwd(x1, second_weights, cos, sin, meta, segr)
     b1_all = flat(spread(1, 4, b1))
     gp1, up1, pos1, gate1, part1 = experts_fwd(1, e_pad, cap, rt_all, wrt1, wg, wu, wd, b1_all)
-    ge1, go1, de1, do1, dg1, dpart1 = experts_bwd(1, cap, groups, pos1, gate1, wg, wu, wd, gp1, up1, b1_all, gy1)
-    dback1, dgate1 = collect(1, 5, paired(dpart1), paired(dg1))
+    dgp1, dup1, hid1, dg1, dpart1 = experts_bwd(1, cap, pos1, gate1, wg, wu, wd, gp1, up1, gy1)
+    dback1, dgate1, *dw1 = collect(1, 5, (paired(dpart1), paired(dg1)), (cap, pos1, b1_all, gy1, dgp1, dup1, hid1))
 
     def gates_back(dg):
         dg = dg[:, :per].reshape(experts, t)
@@ -1197,14 +1434,14 @@
     gy0_all = flat(spread(0, 6, gy0))
     gy0_all, part1 = lax.optimization_barrier((gy0_all, part1))
     crossed = lax.ppermute(paired(part1)[0], "section", [(1, 0)])
-    ge0, go0, de0, do0, dg0, dpart0 = experts_bwd(0, cap, groups, pos0, gate0, wg, wu, wd, gp0, up0, b0_all, gy0_all)
-    dback0, dgate0 = collect(0, 7, paired(dpart0), paired(dg0))
+    dgp0, dup0, hid0, dg0, dpart0 = experts_bwd(0, cap, pos0, gate0, wg, wu, wd, gp0, up0, gy0_all)
+    dback0, dgate0, *dw0 = collect(0, 7, (paired(dpart0), paired(dg0)), (cap, pos0, b0_all, gy0_all, dgp0, dup0, hid0))
     dback0, part1, crossed = lax.optimization_barrier((dback0, part1, crossed))
     back1 = lax.all_to_all(jnp.where(at_zero, crossed, paired(part1)[1]), "expert", split_axis=0, concat_axis=0, tiled=True)
     y1 = (h1 + jnp.sum(back1.astype(F32), axis=0)).astype(BF)
     dx0, dd0 = attn_bwd(gy0, h0, x0, first_weights, qkv0, p0, o0, b0, wrt0, dback0, gates_back(dgate0), rt_tokens[0], cos, sin)
 
-    dense, gate_grad, up_grad, down = finish(9, dd0, dd1, (ge0, go0, de0, do0), (ge1, go1, de1, do1))
+    dense, gate_grad, up_grad, down = finish(9, dd0, dd1, dw0, dw1)
 
     kept_out = jnp.where(at_zero, x1, y1)
     swapped_out = swap_sections(jnp.where(at_zero, y1, x1))

time: 952 us -> 864 us (0.908)
  waiting for transfers between devices: 88.9 us -> 6.33 us
  blocking collectives: 14.2 us -> 0 us
  Pallas kernels: 761 us -> 772 us
    pallas_call x3 -> x4, Pallas kernels: 204 us -> 288 us  [the longest x3 192 us: collect(): pl.pallas_call(functools.partial(collect_kernel, layer, n, count, work[0]...]
    all_gather x2 -> x1, waiting for transfers between devices: 68.4 us -> 4.64 us  [local(): lax.all_gather(second_shard, ('group', 'expert'), axis=0, tiled=True)]
    pallas_call x4 -> x3, Pallas kernels: 175 us -> 135 us  [spread(): pl.pallas_call(functools.partial(spread_kernel, layer, n), out_shape=jax....]
    pallas_call x2, Pallas kernels: 81.3 us -> 48.3 us  [experts_bwd(): pl.pallas_call(functools.partial(experts_bwd_kernel, layer, cap), grid=(p...]
    ppermute x4 -> x2, waiting for transfers between devices: 19.8 us -> 1.66 us  [swap_sections(): return lax.ppermute(value, 'section', [(0, 1), (1, 0)])]
    all_gather x1 -> x0, blocking collectives: 14.2 us -> none  [local(): lax.all_gather(rt, 'expert', axis=1, tiled=False).reshape(2 * n, top, t)]
  transfers between devices with their start and end apart: 8 -> 6, of which waited for: 4 -> 2; matrix products, arithmetic and copies ran while one was open for 2% -> 2% of each run, Pallas kernels for 53% -> 63%
where the time goes in v3:
time: 864 us; the launch traced here: 855 us
  Pallas kernels  772 us (89%)
  local copies, waits for them, and re-layouts  30.6 us (4%)
  starting transfers between devices  17.9 us (2%)
  between operations  14.5 us (2%)
  other arithmetic  14.1 us (2%)
    pallas_call x3, Pallas kernels, collect(): pl.pallas_call(functools.partial(collect_kernel, layer, n, count, work[0]...  192 us
    pallas_call x1, Pallas kernels, finish(): pl.pallas_call(functools.partial(finish_kernel, n), out_shape=(sds((rows,...  180 us
    pallas_call x3, Pallas kernels, spread(): pl.pallas_call(functools.partial(spread_kernel, layer, n), out_shape=jax....  135 us
    pallas_call x1, Pallas kernels, open_up(): pl.pallas_call(functools.partial(open_kernel, n, groups, pieces), out_sha...  96.5 us
    pallas_call x2, Pallas kernels, attn_bwd(): pl.pallas_call(functools.partial(attn_bwd_kernel, dg.shape[0]), out_shape...  48.8 us
    pallas_call x2, Pallas kernels, experts_bwd(): pl.pallas_call(functools.partial(experts_bwd_kernel, layer, cap), grid=(p...  48.3 us
    pallas_call x2, Pallas kernels, experts_fwd(): pl.pallas_call(functools.partial(experts_fwd_kernel, layer, e_pad, cap),...  43.6 us
    pallas_call x2, Pallas kernels, attn_fwd(): pl.pallas_call(attn_fwd_kernel, out_shape=(sds((t, QKV), BF), sds((QUERY_...  28.1 us
  transfers between devices with their start and end apart: 6, of which 2 were waited for; matrix products, arithmetic and copies ran while one was open for 2% of the time, Pallas kernels for 63%

profile of v3, /device:TPU:0, one launch (start us, length us, event | category | flops | bytes accessed | tf_op | source)
XLA Modules:
  0.0 855.3 jit_solution(9951637379424600538)
XLA Ops:
  9.7 2.1 concatenate.31.w_ref
  17.3 96.5 %shard_map.238 = (bf16[16,96,4224]{2,1,0:T(8,128)(2,1)}, bf16[2,4,128,1536]{3,2,1,0:T(8,128)(2,1)}, s32[2,4,8,128]{3,2,1,0:T(8,128)}, s32[8,128]{1,0:T(8,128)}) custom-call(bf16[96,4224]{1,0:T(8,128)(2,1)} %concatenate.31.w_ref, bf16[128,1536]{1,0:T(8,128)(2,1)} %get-tuple-element.190.cot_ref.gy_ref, s32[2,8,128]{2,1,0:T(8,128)} %bitcast.108), custom_call_target="tpu_custom_call" | custom-call | tf_op jit(solution)/shard_map/pallas_call | solution.py:1338
  114.3 14.0 %shard_map.239 = (bf16[128,2560]{1,0:T(8,128)(2,1)}, f32[24,128,128]{2,1,0:T(8,128)}, bf16[128,1536]{1,0:T(8,128)(2,1)}, f32[128,1536]{1,0:T(8,128)}, bf16[128,1...) custom-call(bf16[128,1536]{1,0:T(8,128)(2,1)} %get-tuple-element.191.x_ref, bf16[1536,4224]{1,0:T(8,128)(2,1)} %bitcast.77, ...), custom_call_target="tpu_custom_call" | custom-call | flops 1610612736 | bytes 12976128 | tf_op jit(solution)/shard_map/pallas_call | solution.py:125
  130.1 54.1 %shard_map.240 = bf16[2,4,128,1536]{3,2,1,0:T(8,128)(2,1)} custom-call(bf16[128,1536]{1,0:T(8,128)(2,1)} %get-tuple-element.80.x_ref.b_ref), custom_call_target="tpu_custom_call" | custom-call | tf_op jit(solution)/shard_map/pallas_call | solution.py:641
  184.2 32.8 %shard_map.241 = (bf16[5,512,512]{2,1,0:T(8,128)(2,1)}, bf16[5,512,512]{2,1,0:T(8,128)(2,1)}, s32[8,8,128]{2,1,0:T(8,128)}, f32[8,8,128]{2,1,0:T(8,128)}, bf16[8,128,1536]{2,1,0:T(8,128)(2,1)}) custom-call(s32[8,8,128]{2,1,0:T(8,128)} %bitcast.127, bf16[128,1536]{1,0:T(8,128)(2,1)} %get-tuple-element.78.wrt_ref, bf16[5,1536,512]{2,1,0:T(8,128)(2,1)} %bitcast.115, ...), custom_call_target="tpu_custom_call" | custom-call | flops 12079595520 | bytes 23592960 | tf_op jit(solution)/shard_map/pallas_call | solution.py:401
  217.0 1.9 copy-done.2
  218.9 59.2 %shard_map.242 = bf16[4,128,1536]{2,1,0:T(8,128)(2,1)S(1)} custom-call(bf16[2,4,128,1536]{3,2,1,0:T(8,128)(2,1)S(1)} %bitcast.76), custom_call_target="tpu_custom_call" | custom-call | tf_op jit(solution)/shard_map/pallas_call | solution.py:755
  279.2 4.6 all-gather.2.cloned.1.call-done.w_ref
  283.8 14.0 %shard_map.243 = (bf16[128,2560]{1,0:T(8,128)(2,1)}, f32[24,128,128]{2,1,0:T(8,128)}, bf16[128,1536]{1,0:T(8,128)(2,1)}, f32[128,1536]{1,0:T(8,128)}, bf16[128,1...) custom-call(bf16[128,1536]{1,0:T(8,128)(2,1)} %add_convert_fusion.1.x_ref, ...), custom_call_target="tpu_custom_call" | custom-call | flops 1610612736 | bytes 12976128 | tf_op jit(solution)/shard_map/pallas_call | solution.py:125
  297.8 43.5 %shard_map.244 = bf16[2,4,128,1536]{3,2,1,0:T(8,128)(2,1)} custom-call(bf16[128,1536]{1,0:T(8,128)(2,1)} %get-tuple-element.91.x_ref.b_ref), custom_call_target="tpu_custom_call" | custom-call | tf_op jit(solution)/shard_map/pallas_call | solution.py:641
  341.3 10.7 %shard_map.245 = (bf16[5,512,512]{2,1,0:T(8,128)(2,1)}, bf16[5,512,512]{2,1,0:T(8,128)(2,1)}, s32[8,8,128]{2,1,0:T(8,128)}, f32[8,8,128]{2,1,0:T(8,128)}, bf16[8,128,1536]{2,1,0:T(8,128)(2,1)}) custom-call(s32[8,8,128]{2,1,0:T(8,128)} %bitcast.128, bf16[128,1536]{1,0:T(8,128)(2,1)} %get-tuple-element.92.wrt_ref, bf16[5,1536,512]{2,1,0:T(8,128)(2,1)} %bitcast.116, ...), custom_call_target="tpu_custom_call" | custom-call | flops 12079595520 | bytes 23592960 | tf_op jit(solution)/shard_map/pallas_call | solution.py:401
  352.1 13.1 %shard_map.246 = (bf16[5,512,512]{2,1,0:T(8,128)(2,1)}, bf16[5,512,512]{2,1,0:T(8,128)(2,1)}, bf16[5,512,512]{2,1,0:T(8,128)(2,1)}, f32[8,8,128]{2,1,0:T(8,128)}, bf16[8,128,1536]{2,1,0:T(8,128)(2,1)}) custom-call(s32[8,8,128]{2,1,0:T(8,128)} %get-tuple-element.93.pos_ref.refs_2_, f32[8,8,128]{2,1,0:T(8,128)} %get-tuple-element.94.gate_ref, ...), custom_call_target="tpu_custom_call" | custom-call | flops 12079595520 | bytes 31457280 | tf_op jit(solution)/shard_map/pallas_call | solution.py:509
  365.2 93.3 %shard_map.247 = (bf16[4,128,1536]{2,1,0:T(8,128)(2,1)}, f32[4,8,128]{2,1,0:T(8,128)}, bf16[2,2,5,384,512]{4,3,2,1,0:T(8,128)(2,1)}, bf16[2,2,5,384,512]{4,3,2,1...) custom-call(bf16[2,4,128,1536]{3,2,1,0:T(8,128)(2,1)} %bitcast.96, ...), custom_call_target="tpu_custom_call" | custom-call | tf_op jit(solution)/shard_map/pallas_call | solution.py:755
  459.9 24.4 %shard_map.248 = (f32[128,1536]{1,0:T(8,128)}, bf16[1536,4224]{1,0:T(8,128)(2,1)}) custom-call(bf16[128,1536]{1,0:T(8,128)(2,1)} %get-tuple-element.190.cot_ref.gy_ref, f32[128,1536]{1,0:T(8,128)} %get-tuple-element.83.h_ref, bf16[128,1536]{1,0:T(8,128)(2,1)} %add_convert_fusion.1.x_ref, bf16[1536,4224]{1,0:T(8,128)(2,1)} %all-gather.2.cloned.1.call-done.w_ref, ...), custom_call_target="tpu_custom_call" | custom-call | flops 3221225472 | bytes 25952256 | tf_op jit(solution)/shard_map/pallas_call | solution.py:242
  484.3 2.1 convert_element_type.20.x_ref.gy_ref
  486.4 37.5 %shard_map.249 = bf16[2,4,128,1536]{3,2,1,0:T(8,128)(2,1)} custom-call(bf16[128,1536]{1,0:T(8,128)(2,1)} %convert_element_type.20.x_ref.gy_ref), custom_call_target="tpu_custom_call" | custom-call | tf_op jit(solution)/shard_map/pallas_call | solution.py:641
  526.5 35.1 %shard_map.250 = (bf16[5,512,512]{2,1,0:T(8,128)(2,1)}, bf16[5,512,512]{2,1,0:T(8,128)(2,1)}, bf16[5,512,512]{2,1,0:T(8,128)(2,1)}, f32[8,8,128]{2,1,0:T(8,128)}, bf16[8,128,1536]{2,1,0:T(8,128)(2,1)}) custom-call(s32[8,8,128]{2,1,0:T(8,128)} %get-tuple-element.84.pos_ref.refs_2_, f32[8,8,128]{2,1,0:T(8,128)} %get-tuple-element.85.gate_ref, ...), custom_call_target="tpu_custom_call" | custom-call | flops 12079595520 | bytes 31457280 | tf_op jit(solution)/shard_map/pallas_call | solution.py:509
  561.6 39.4 %shard_map.251 = (bf16[4,128,1536]{2,1,0:T(8,128)(2,1)}, f32[4,8,128]{2,1,0:T(8,128)}, bf16[2,2,5,384,512]{4,3,2,1,0:T(8,128)(2,1)}, bf16[2,2,5,384,512]{4,3,2,1...) custom-call(bf16[2,4,128,1536]{3,2,1,0:T(8,128)(2,1)} %bitcast.97, ...), custom_call_target="tpu_custom_call" | custom-call | tf_op jit(solution)/shard_map/pallas_call | solution.py:755
  601.0 2.7 slice_select_fusion
  603.8 4.0 all-to-all-start
  608.3 24.4 %shard_map.252 = (f32[128,1536]{1,0:T(8,128)}, bf16[1536,4224]{1,0:T(8,128)(2,1)}) custom-call(bf16[128,1536]{1,0:T(8,128)(2,1)} %convert_element_type.20.x_ref.gy_ref, f32[128,1536]{1,0:T(8,128)} %get-tuple-element.76.h_ref, bf16[128,1536]{1,0:T(8,128)(2,1)} %get-tuple-element.191.x_ref, bf16[1536,4224]{1,0:T(8,128)(2,1)} %bitcast.78, ...), custom_call_target="tpu_custom_call" | custom-call | flops 3221225472 | bytes 25952256 | tf_op jit(solution)/shard_map/pallas_call | solution.py:242
  632.8 2.2 select_bitcast_fusion
  635.0 9.8 %collective-permute-start.3 = (f32[128,1536]{1,0:T(8,128)}, f32[128,1536]{1,0:T(8,128)}, u32[]{:S(2)}, u32[]{:S(2)}) collective-permute-start(f32[128,1536]{1,0:T(8,128)} %get-tuple-element.183), channel_id=1, source_target_pairs={{0,16},{16,0},{1,17},{17,1},{2,18},{18,2},{3,19},{19,3},{4,20},{20... | collective-permute-start | bytes 2359304 | tf_op jit(solution)/shard_map/ppermute | solution.py:1350
  644.8 179.7 %shard_map.253 = (f32[96,4224]{1,0:T(8,128)}, f32[5,384,512]{2,1,0:T(8,128)}, f32[5,384,512]{2,1,0:T(8,128)}, f32[5,512,384]{2,1,0:T(8,128)}) custom-call(bf16[16,96,4224]{2,1,0:T(8,128)(2,1)} %bitcast.80, bf16[16,96,4224]{2,1,0:T(8,128)(2,1)} %bitcast.79, bf16[2,10,384,512]{3,2,1,0:T(8,128)(2,1)} %bitcast.89, bf16[2,10,384,512]{3,2,1,0:T(8,128)(2,1)} %bitcast.90, ...), custom_call_target="tpu_custom_call" | custom-call | tf_op jit(solution)/shard_map/pallas_call | solution.py:1124
  824.5 1.9 slice_bitcast_fusion.2
  826.4 2.3 slice_bitcast_fusion
  832.1 1.7 slice_reduce_fusion
  833.8 2.8 maximum_select_fusion
  836.6 1.7 collective-permute-done.2
  839.3 2.0 copy.63
  842.8 2.0 copy.64
  846.4 1.9 copy.65
  (74 shorter events, 23.2 us)
Async XLA Ops:
  7.2 6.6 copy-start
  7.2 9.1 %copy-start.12 = (bf16[2,1,128,1536]{3,2,1,0:T(8,128)(2,1)S(1)}, bf16[2,1,128,1536]{3,2,1,0:T(8,128)(2,1)}, u32[]{:S(2)}) copy-start(bf16[2,1,128,1536]{3,2,1,0:T(8,128)(2,1)} %param.15) | copy-start | bytes 2359300
  7.2 9.1 %copy-start.11 = (bf16[2,1,128,1536]{3,2,1,0:T(8,128)(2,1)S(1)}, bf16[2,1,128,1536]{3,2,1,0:T(8,128)(2,1)}, u32[]{:S(2)}) copy-start(bf16[2,1,128,1536]{3,2,1,0:T(8,128)(2,1)} %param.16) | copy-start | bytes 2359300
  7.2 276.6 %all-gather.2.cloned.1.call-start = ((), (), s32[]{:S(2)}) async-start(), calls=%async_computation.1 | async-start | bytes 13787136 | tf_op jit(solution)/shard_map/all_gather | solution.py:1415
  11.8 116.6 %collective-permute-start = (bf16[96,4224]{1,0:T(8,128)(2,1)}, bf16[96,4224]{1,0:T(8,128)(2,1)S(1)}, u32[]{:S(2)}, u32[]{:S(2)}) collective-permute-start(bf16[96,4224]{1,0:T(8,128)(2,1)} %concatenate.31.w_ref), channel_id=1, source_target_pairs={{16,0},{17,1},{18,2},{19,3},{20,4},{21,5},{22,6},{23,7},{24,8},{25... | collective-permute-start | bytes 2433032 | tf_op jit(solution)/shard_map/ppermute | solution.py:1388
  128.4 1.1 copy-start.13
  128.4 1.1 copy-start.15
  217.0 1.9 copy-start.2
  218.9 59.4 %copy-start.8 = (f32[128,1536]{1,0:T(8,128)S(1)}, f32[128,1536]{1,0:T(8,128)}, u32[]{:S(2)}) copy-start(f32[128,1536]{1,0:T(8,128)} %get-tuple-element.76.h_ref) | copy-start | bytes 2359300
  484.3 39.6 %copy-start.9 = (bf16[8,128,1536]{2,1,0:T(8,128)(2,1)S(1)}, bf16[8,128,1536]{2,1,0:T(8,128)(2,1)}, u32[]{:S(2)}) copy-start(bf16[8,128,1536]{2,1,0:T(8,128)(2,1)} %get-tuple-element.117) | copy-start | bytes 9437188
  525.2 75.8 %collective-permute-start.1 = (bf16[4,128,1536]{2,1,0:T(8,128)(2,1)}, bf16[4,128,1536]{2,1,0:T(8,128)(2,1)}, u32[]{:S(2)}, u32[]{:S(2)}) collective-permute-start(bf16[4,128,1536]{2,1,0:T(8,128)(2,1)} %slice.36), channel_id=1, source_target_pairs={{16,0},{17,1},{18,2},{19,3},{20,4},{21,5},{22,6},{23,7},{24,8},{25... | collective-permute-start | bytes 4718600 | tf_op jit(solution)/shard_map/ppermute | solution.py:1436
  603.8 4.0 copy-start.14
  603.8 224.9 %all-to-all-start = ((bf16[4,128,1536]{2,1,0:T(8,128)(2,1)}), bf16[4,128,1536]{2,1,0:T(8,128)(2,1)S(1)}, u32[]{:S(2)}, u32[]{:S(2)}) async-start(bf16[4,128,1536]{2,1,0:T(8,128)(2,1)} %slice_select_fusion), calls=%async_computation | async-start | bytes 3145728 | tf_op jit(solution)/shard_map/all_to_all | solution.py:1440
  608.3 24.4 %copy-start.10 = (f32[128,1536]{1,0:T(8,128)S(1)}, f32[128,1536]{1,0:T(8,128)}, u32[]{:S(2)}) copy-start(f32[128,1536]{1,0:T(8,128)} %get-tuple-element.106) | copy-start | bytes 2359300
  635.0 198.9 %collective-permute-start.3 = (f32[128,1536]{1,0:T(8,128)}, f32[128,1536]{1,0:T(8,128)}, u32[]{:S(2)}, u32[]{:S(2)}) collective-permute-start(f32[128,1536]{1,0:T(8,128)} %get-tuple-element.183), channel_id=1, source_target_pairs={{0,16},{16,0},{1,17},{17,1},{2,18},{18,2},{3,19},{19,3},{4,20},{20... | collective-permute-start | bytes 2359304 | tf_op jit(solution)/shard_map/ppermute | solution.py:1350
  824.5 4.5 copy-start.3
  824.5 4.5 copy-start.7
  829.2 9.1 %collective-permute-start.2 = (bf16[128,1536]{1,0:T(8,128)(2,1)S(1)}, bf16[128,1536]{1,0:T(8,128)(2,1)S(1)}, u32[]{:S(2)}, u32[]{:S(2)}) collective-permute-start(bf16[128,1536]{1,0:T(8,128)(2,1)S(1)} %broadcast_select_fusion.2), channel_id=1, source_target_pairs={{0,16},{16,0},{1,17},{17,1},{2,18},{18,2},{3,19},{19,3},{4,20},{20... | collective-permute-start | bytes 1179656 | tf_op jit(solution)/shard_map/ppermute | solution.py:1350
  832.1 7.2 copy-start.6
  839.3 3.5 copy-start.5
  842.8 3.5 copy-start.4
  842.8 5.5 copy-start.1
Sparse Core Ops, SparseCore 0:
  129.6 154.1 all-gather.1

commit v4 on v3

--- a/solution.py
+++ b/solution.py
@@ -1,4 +1,5 @@
 import functools
+import types
 
 import jax
 import jax.numpy as jnp
@@ -283,9 +284,10 @@
     return jnp.where(chosen, before.astype(jnp.int32), -1)[0:8]
 
 
-def streamed(count, copies, body):
-    for c in copies(0, 0):
-        c.start()
+def streamed(count, copies, body, primed=False):
+    if not primed:
+        for c in copies(0, 0):
+            c.start()
 
     def step(b, carry):
         slot = lax.rem(b, 2)
@@ -303,7 +305,7 @@
     lax.fori_loop(0, count, step, 0)
 
 
-def combine(count, per, cap, pos_ref, rows_ref, out_hbm, obuf, osem):
+def combine(base, count, per, cap, pos_ref, rows_ref, out_hbm, obuf, osem):
     def copy(b, slot):
         return pltpu.make_async_copy(obuf.at[slot], out_hbm.at[b], osem.at[slot])
 
@@ -314,8 +316,8 @@
         def _():
             copy(b - 2, slot).wait()
 
-        back = all_hots_back(pos_ref[b], per, cap)
-        at = pl.ds(pl.multiple_of(b * cap, cap), cap)
+        back = all_hots_back(pos_ref[base + b], per, cap)
+        at = pl.ds(pl.multiple_of((base + b) * cap, cap), cap)
         rows = jnp.concatenate([rows_ref[j, at, :] for j in range(per)], axis=0)
         obuf[slot] = dot(back, rows).astype(BF)
         copy(b, slot).start()
@@ -336,254 +338,67 @@
     return hots, jnp.concatenate(gates, axis=0)
 
 
-def experts_fwd_kernel(
-    layer, e_pad, cap, rt_ref, wrt_ref, wg_ref, wu_ref, wd_ref, b_hbm,
-    gp_ref, up_ref, pos_ref, gate_ref, out_hbm, x_scr, y_scr, all_gates, bbuf, obuf, bsem, osem,
-):
-    per, rows, d = x_scr.shape
-    count = rt_ref.shape[0]
-    chunk = 256
-    j = pl.program_id(0)
-    first = lax.axis_index("expert") * per
-
-    @pl.when(lax.axis_index("section") == layer)
-    def _():
-        @pl.when(j == 0)
-        def _():
-            def prepare(b, slot):
-                rt = rt_ref[b]
-                block = bbuf[slot]
-                pos = slots_of(rt, first, per)
-                pos_ref[b] = pos
-                all_gates[...] = gates_of(rt, wrt_ref, block, e_pad)
-                gate_ref[b] = jnp.concatenate(
-                    [all_gates[pl.ds(first + k, 1), :] for k in range(per)] + [jnp.zeros((8 - per, rt.shape[1]), F32)], axis=0
-                )
-                x = dot(all_hots(pos, per, cap).astype(BF), block).astype(BF)
-                at = pl.ds(pl.multiple_of(b * cap, cap), cap)
-                for k in range(per):
-                    x_scr[k, at, :] = x[k * cap : (k + 1) * cap]
-
-            streamed(count, lambda b, slot: [pltpu.make_async_copy(b_hbm.at[b], bbuf.at[slot], bsem.at[slot])], prepare)
-
-        def part(c, carry):
-            at = pl.ds(pl.multiple_of(c * chunk, chunk), chunk)
-            x = x_scr[j, at, :]
-            gp = dot(x, wg_ref[0])
-            up = dot(x, wu_ref[0])
-            gp_ref[0, at, :] = gp.astype(BF)
-            up_ref[0, at, :] = up.astype(BF)
-            hid = (gp / (1.0 + jnp.exp(-gp)) * up).astype(BF)
-            _, gate = chunk_gates(c, j, chunk, cap, pos_ref, gate_ref)
-            y_scr[j, at, :] = (dot(hid, wd_ref[0]) * gate).astype(BF)
-            return carry
-
-        lax.fori_loop(0, rows // chunk, part, 0)
-
-        @pl.when(j == per - 1)
-        def _():
-            combine(count, per, cap, pos_ref, y_scr, out_hbm, obuf, osem)
-
-
 def any_spec():
     return pl.BlockSpec(memory_space=pl.ANY)
 
 
-def fixed(shape):
-    return pl.BlockSpec(shape, lambda j: (0,) * len(shape))
-
-
-def experts_fwd(layer, e_pad, cap, rt, wrt, wg, wu, wd, blocks):
-    count, t, d = blocks.shape
-    per, _, f = wg.shape
-    rows = count * cap
-    sds = jax.ShapeDtypeStruct
-    return pl.pallas_call(
-        functools.partial(experts_fwd_kernel, layer, e_pad, cap),
-        grid=(per,),
-        out_shape=(
-            sds((per, rows, f), BF),
-            sds((per, rows, f), BF),
-            sds((count, 8, t), jnp.int32),
-            sds((count, 8, t), F32),
-            sds((count, t, d), BF),
-        ),
-        in_specs=[
-            fixed(rt.shape),
-            fixed(wrt.shape),
-            pl.BlockSpec((1, d, f), lambda j: (j, 0, 0)),
-            pl.BlockSpec((1, d, f), lambda j: (j, 0, 0)),
-            pl.BlockSpec((1, f, d), lambda j: (j, 0, 0)),
-            any_spec(),
-        ],
-        out_specs=(
-            pl.BlockSpec((1, rows, f), lambda j: (j, 0, 0)),
-            pl.BlockSpec((1, rows, f), lambda j: (j, 0, 0)),
-            fixed((count, 8, t)),
-            fixed((count, 8, t)),
-            any_spec(),
-        ),
-        scratch_shapes=[
-            pltpu.VMEM((per, rows, d), BF),
-            pltpu.VMEM((per, rows, d), BF),
-            pltpu.VMEM((e_pad, t), F32),
-            pltpu.VMEM((2, t, d), BF),
-            pltpu.VMEM((2, t, d), BF),
-            pltpu.SemaphoreType.DMA((2,)),
-            pltpu.SemaphoreType.DMA((2,)),
-        ],
-        compiler_params=pltpu.CompilerParams(vmem_limit_bytes=VMEM_LIMIT),
-        cost_estimate=pl.CostEstimate(flops=6 * per * rows * d * f, bytes_accessed=6 * per * d * f, transcendentals=per * rows * f),
-    )(rt, wrt, wg, wu, wd, blocks)
-
-
-def gather_rows(count, per, cap, pos_ref, b_hbm, gy_hbm, x_scr, y_scr, bbuf, gbuf, bsem, gsem):
-    def prepare(b, slot):
-        hots = all_hots(pos_ref[b], per, cap).astype(BF)
-        at = pl.ds(pl.multiple_of(b * cap, cap), cap)
-        for source, dest in ((bbuf, x_scr), (gbuf, y_scr)):
-            if dest is not None:
-                rows = dot(hots, source[slot]).astype(BF)
-                for k in range(per):
-                    dest[k, at, :] = rows[k * cap : (k + 1) * cap]
-
-    def copies(b, slot):
-        both = [pltpu.make_async_copy(gy_hbm.at[b], gbuf.at[slot], gsem.at[slot])]
-        if x_scr is not None:
-            both.append(pltpu.make_async_copy(b_hbm.at[b], bbuf.at[slot], bsem.at[slot]))
-        return both
-
-    streamed(count, copies, prepare)
-
-
-def experts_bwd_kernel(
-    layer, cap, pos_ref, gate_ref, wg_ref, wu_ref, wd_ref, gp_ref, up_ref, gy_hbm,
-    dgp_ref, dup_ref, hid_ref, dg_ref, out_hbm, y_scr, gbuf, obuf, gsem, osem,
-):
-    per, rows, d = y_scr.shape
-    count = pos_ref.shape[0]
-    chunk = 256
-    j = pl.program_id(0)
-
-    @pl.when(lax.axis_index("section") == layer)
-    def _():
-        @pl.when(j == 0)
-        def _():
-            gather_rows(count, per, cap, pos_ref, None, gy_hbm, None, y_scr, None, gbuf, None, gsem)
-            dg_ref[...] = jnp.zeros_like(dg_ref)
-
-        def part(c, carry):
-            at = pl.ds(pl.multiple_of(c * chunk, chunk), chunk)
-            raw = dot(y_scr[j, at, :], wd_ref[0], 1, 1)
-            gp, up = gp_ref[0, at, :].astype(F32), up_ref[0, at, :].astype(F32)
-            sg = 1.0 / (1.0 + jnp.exp(-gp))
-            silu = gp * sg
-            hid = silu * up
-            hots, gate = chunk_gates(c, j, chunk, cap, pos_ref, gate_ref)
-            dgate = jnp.sum(hid.astype(BF).astype(F32) * raw, axis=1, keepdims=True)
-            for bb in range(chunk // cap):
-                b = c * (chunk // cap) + bb
-                dg_ref[b, pl.ds(j, 1), :] = jnp.sum(hots[bb] * dgate[bb * cap : (bb + 1) * cap], axis=0, keepdims=True)
-            dh = raw * gate
-            dgp = (dh * up * sg * (1.0 + gp * (1.0 - sg))).astype(BF)
-            dup = (dh * silu).astype(BF)
-            dgp_ref[0, at, :] = dgp
-            dup_ref[0, at, :] = dup
-            hid_ref[0, at, :] = (hid * gate).astype(BF)
-            y_scr[j, at, :] = (dot(dgp, wg_ref[0], 1, 1) + dot(dup, wu_ref[0], 1, 1)).astype(BF)
-            return carry
-
-        lax.fori_loop(0, rows // chunk, part, 0)
-
-        @pl.when(j == per - 1)
-        def _():
-            combine(count, per, cap, pos_ref, y_scr, out_hbm, obuf, osem)
-
-
-def experts_bwd(layer, cap, pos, gate, wg, wu, wd, gp, up, grads):
-    count, t, d = grads.shape
-    per, _, f = wg.shape
-    rows = count * cap
-    sds = jax.ShapeDtypeStruct
-    by_expert = pl.BlockSpec((1, rows, f), lambda j: (j, 0, 0))
-    return pl.pallas_call(
-        functools.partial(experts_bwd_kernel, layer, cap),
-        grid=(per,),
-        out_shape=(sds((per, rows, f), BF),) * 3 + (sds((count, 8, t), F32), sds((count, t, d), BF)),
-        in_specs=[
-            fixed(pos.shape),
-            fixed(gate.shape),
-            pl.BlockSpec((1, d, f), lambda j: (j, 0, 0)),
-            pl.BlockSpec((1, d, f), lambda j: (j, 0, 0)),
-            pl.BlockSpec((1, f, d), lambda j: (j, 0, 0)),
-            by_expert,
-            by_expert,
-            any_spec(),
-        ],
-        out_specs=(by_expert, by_expert, by_expert, fixed((count, 8, t)), any_spec()),
-        scratch_shapes=[
-            pltpu.VMEM((per, rows, d), BF),
-            pltpu.VMEM((2, t, d), BF),
-            pltpu.VMEM((2, t, d), BF),
-            pltpu.SemaphoreType.DMA((2,)),
-            pltpu.SemaphoreType.DMA((2,)),
-        ],
-        compiler_params=pltpu.CompilerParams(vmem_limit_bytes=VMEM_LIMIT),
-        cost_estimate=pl.CostEstimate(flops=6 * per * rows * d * f, bytes_accessed=8 * per * d * f, transcendentals=per * rows * f),
-    )(pos, gate, wg, wu, wd, gp, up, grads)
-
-
-def weight_grads(
-    cap, pos_ref, b_hbm, gy_hbm, dgp_hbm, dup_hbm, hid_hbm, outs, x_scr, y_scr, bbuf, gbuf, act_buf, gu_buf, dn_buf,
-    bsem, gsem, act_sem, gu_sem, dn_sem,
-):
-    even, odd, even_dn, odd_dn = outs
-    per, rows, d = x_scr.shape
-    count = pos_ref.shape[0]
-    parts, piece = gu_buf.shape[1] // 2, gu_buf.shape[3]
+def put_rows(hots, block, b, per, cap, dest):
+    at = pl.ds(pl.multiple_of(b * cap, cap), cap)
+    rows = dot(hots, block).astype(BF)
+    for k in range(per):
+        dest[k, at, :] = rows[k * cap : (k + 1) * cap]
+
+
+def gather_from(count, per, cap, pos, source, dest, buf, sem):
+    def body(b, slot):
+        put_rows(all_hots(pos[b], per, cap).astype(BF), buf[slot], b, per, cap, dest)
+
+    streamed(count, lambda b, slot: [pltpu.make_async_copy(source.at[b], buf.at[slot], sem.at[slot])], body)
+
+
+def weight_grads(r, per):
+    parts, piece = r.even.shape[0], r.even.shape[3]
     g = lax.axis_index("group")
     parity, place = lax.rem(g, 2), g // 2
-    gather_rows(count, per, cap, pos_ref, b_hbm, gy_hbm, x_scr, y_scr, bbuf, gbuf, bsem, gsem)
-
-    def acts(j, slot):
+
+    def outgoing(j, at, slot):
         return [
-            pltpu.make_async_copy(source.at[j], act_buf.at[slot, n], act_sem.at[slot, n])
-            for n, source in enumerate((dgp_hbm, dup_hbm, hid_hbm))
+            pltpu.make_async_copy(r.gu_buf.at[slot, 0], r.even.at[at, :, j], r.gu_sem.at[slot, 0]),
+            pltpu.make_async_copy(r.gu_buf.at[slot, 1], r.odd.at[at, :, j], r.gu_sem.at[slot, 1]),
+            pltpu.make_async_copy(r.dn_buf.at[slot, 0], r.even_dn.at[at, j], r.dn_sem.at[slot, 0]),
+            pltpu.make_async_copy(r.dn_buf.at[slot, 1], r.odd_dn.at[at, j], r.dn_sem.at[slot, 1]),
         ]
 
-    def outgoing(j, slot):
-        half = pl.ds(0, parts), pl.ds(parts, parts)
-        return [
-            pltpu.make_async_copy(gu_buf.at[slot, half[0]], even.at[:, :, j], gu_sem.at[slot, 0]),
-            pltpu.make_async_copy(gu_buf.at[slot, half[1]], odd.at[:, :, j], gu_sem.at[slot, 1]),
-            pltpu.make_async_copy(dn_buf.at[slot, half[0]], even_dn.at[:, j], dn_sem.at[slot, 0]),
-            pltpu.make_async_copy(dn_buf.at[slot, half[1]], odd_dn.at[:, j], dn_sem.at[slot, 1]),
-        ]
-
-    def body(j, slot):
-        @pl.when(j >= 2)
-        def _():
-            for c in outgoing(j - 2, slot):
-                c.wait()
-
+    def finished(slot):
+        for c in outgoing(0, 0, slot):
+            c.wait()
+
+    def body(j, carry):
         for q in range(parts):
+            slot = q % 2
+            if q >= 2:
+                finished(slot)
+            else:
+
+                @pl.when(j > 0)
+                def _():
+                    finished(slot)
+
             cols = slice(2 * q * piece, 2 * (q + 1) * piece)
-            at = lax.bitwise_xor(place, q)
-            low, high = parity * parts + at, (1 - parity) * parts + at
-            for n in range(2):
-                full = dot(x_scr[j, :, cols], act_buf[slot, n], 0, 0).astype(BF)
-                gu_buf[slot, low, n] = full[:piece]
-                gu_buf[slot, high, n] = full[piece:]
-            full = dot(act_buf[slot, 2], y_scr[j, :, cols], 0, 0).astype(BF)
-            dn_buf[slot, low] = full[:, :piece]
-            dn_buf[slot, high] = full[:, piece:]
-        for c in outgoing(j, slot):
-            c.start()
-
-    streamed(per, acts, body)
-    for j in (per - 2, per - 1):
-        for c in outgoing(j, j % 2):
-            c.wait()
+            for m in range(2):
+                full = dot(r.x_scr[j, :, cols], r.act[m, j], 0, 0).astype(BF)
+                r.gu_buf[slot, parity, m] = full[:piece]
+                r.gu_buf[slot, 1 - parity, m] = full[piece:]
+            full = dot(r.act[2, j], r.y_scr[j, :, cols], 0, 0).astype(BF)
+            r.dn_buf[slot, parity] = full[:, :piece]
+            r.dn_buf[slot, 1 - parity] = full[:, piece:]
+            for c in outgoing(j, lax.bitwise_xor(place, q), slot):
+                c.start()
+        return carry
+
+    lax.fori_loop(0, per, body, 0)
+    for slot in range(2):
+        finished(slot)
 
 
 def meet(n, with_cross):
@@ -598,170 +413,375 @@
     pl.semaphore_wait(barrier, 2 * n - 1 if with_cross else n)
 
 
-def spread_kernel(layer, n, x_ref, o_ref, send_sem, recv_sem, local_sem):
+def moe_kernel(layer, mode, n, e_pad, cap, names, *refs):
+    r = types.SimpleNamespace(**dict(zip(names, refs)))
+    forward, backward = mode != "bwd", mode != "fwd"
     s, z = lax.axis_index("section"), lax.axis_index("expert")
-    meet(n, True)
-
-    def copy(k, source_section):
-        return pltpu.make_async_remote_copy(
-            src_ref=x_ref,
-            dst_ref=o_ref.at[source_section, z],
-            send_sem=send_sem.at[k],
-            recv_sem=recv_sem.at[source_section, k],
-            device_id={"section": layer, "expert": lax.rem(z + k, n)},
-            device_id_type=MESH,
+    here = s == layer
+    count = 2 * n
+    per, rows, d = r.y_scr.shape
+    first = z * per
+    chunk = 256
+    remote = functools.partial(pltpu.make_async_remote_copy, device_id_type=MESH)
+    other = {"section": 1 - s}
+    meet(n, False)
+    r.blk[s, z] = r.own[...]
+
+    def weights(j, slot):
+        both = [
+            pltpu.make_async_copy(r.wg.at[j], r.wg_buf.at[slot], r.w_sem.at[slot, 0]),
+            pltpu.make_async_copy(r.wu.at[j], r.wu_buf.at[slot], r.w_sem.at[slot, 1]),
+            pltpu.make_async_copy(r.wd.at[j], r.wd_buf.at[slot], r.w_sem.at[slot, 2]),
+        ]
+        if mode == "bwd":
+            both.append(pltpu.make_async_copy(r.gp.at[j], r.gp_buf.at[slot], r.gp_sem.at[slot, 0]))
+            both.append(pltpu.make_async_copy(r.up.at[j], r.gp_buf.at[2 + slot], r.gp_sem.at[slot, 1]))
+        return both
+
+    def chain(to, zz, t, ssem, rsem):
+        return remote(
+            src_ref=r.blk.at[s, zz], dst_ref=r.blk.at[s, zz], send_sem=ssem.at[t], recv_sem=rsem.at[t], device_id={"expert": to}
         )
 
-    order = sorted(range(n), key=lambda k: (k == 0, abs(k - n // 2)))
-
-    @pl.when(s == layer)
+    def right(t):
+        return chain(z + 1, z - t, t, r.s_right, r.r_right)
+
+    def left(t):
+        return chain(z - 1, z + t, t, r.s_left, r.r_left)
+
+    def cross(zz):
+        return remote(
+            src_ref=r.blk.at[s, zz], dst_ref=r.blk.at[s, zz], send_sem=r.s_cross.at[zz], recv_sem=r.r_cross.at[zz], device_id=other
+        )
+
+    def prepare(section, zz):
+        b = section * n + zz
+        block = r.blk[section, zz]
+        if forward:
+            rt = r.rt[b]
+            pos = slots_of(rt, first, per)
+            r.pos[b] = pos
+            r.gates[...] = gates_of(rt, r.wrt, block, e_pad)
+            r.gate[b] = jnp.concatenate(
+                [r.gates[pl.ds(first + k, 1), :] for k in range(per)] + [jnp.zeros((8 - per, rt.shape[1]), F32)], axis=0
+            )
+            put_rows(all_hots(pos, per, cap).astype(BF), block, b, per, cap, r.x_scr)
+        else:
+            put_rows(all_hots(r.pos[b], per, cap).astype(BF), block, b, per, cap, r.y_scr)
+
+    @pl.when(here)
     def _():
-        own = pltpu.make_async_copy(x_ref, o_ref.at[layer, z], local_sem)
-        own.start()
-        sends = [copy(k, layer) for k in order if k]
-        for c in sends:
+        for c in weights(0, 0):
             c.start()
-        own.wait()
-        for c in sends:
-            c.wait()
-        for k in range(n):
-            copy(k, 1 - layer).wait_recv()
-
-    @pl.when(s != layer)
-    def _():
-        sends = [copy(k, 1 - layer) for k in order]
-        for c in sends:
-            c.start()
-        for c in sends:
-            c.wait_send()
-
-
-def spread(layer, cid, x):
-    n = lax.axis_size("expert")
-    return pl.pallas_call(
-        functools.partial(spread_kernel, layer, n),
-        out_shape=jax.ShapeDtypeStruct((2, n) + x.shape, x.dtype),
-        in_specs=vmem(1),
-        out_specs=any_spec(),
-        scratch_shapes=[
-            pltpu.SemaphoreType.DMA((n,)),
-            pltpu.SemaphoreType.DMA((2, n)),
-            pltpu.SemaphoreType.DMA,
-        ],
-        compiler_params=pltpu.CompilerParams(collective_id=cid, has_side_effects=True),
-    )(x)
-
-
-def collect_kernel(layer, n, arrays, cap, *refs):
-    srcs, refs = refs[:arrays], refs[arrays:]
-    work_in, refs = (refs[:6], refs[6:]) if cap else ((), refs)
-    outs, refs = refs[:arrays], refs[arrays:]
-    work_out, refs = (refs[:4], refs[4:]) if cap else ((), refs)
-    relays, refs = refs[:arrays], refs[arrays:]
-    relay_send, relay_recv, send_sem, recv_sem, local_sem = refs[:5]
-    s, z = lax.axis_index("section"), lax.axis_index("expert")
-    meet(n, False)
+
+    @pl.loop(0, n + 1)
+    def _(t):
+        from_left = (t < n) & (z >= t)
+        from_right = (t < n) & (z + t < n)
+
+        @pl.when(from_left & (t > 0))
+        def _():
+            right(t - 1).wait_recv()
+
+        @pl.when(from_left & (z < n - 1))
+        def _():
+            right(t).start()
+
+        @pl.when(from_left & jnp.logical_not(here))
+        def _():
+            cross(z - t).start()
+
+        @pl.when(from_right & (t > 0))
+        def _():
+            left(t - 1).wait_recv()
+
+        @pl.when(from_right & (z > 0))
+        def _():
+            left(t).start()
+
+        @pl.when(from_right & (t > 0) & jnp.logical_not(here))
+        def _():
+            cross(z + t).start()
+
+        @pl.when(here)
+        def _():
+            if mode == "both":
+
+                @pl.when(t == 0)
+                def _():
+                    @pl.loop(0, count)
+                    def _(b):
+                        r.pos[b] = slots_of(r.rt[b], first, per)
+
+                    gather_from(count, per, cap, r.pos, r.gy, r.y_scr, r.row_buf, r.row_sem)
+
+            u = t - 1
+
+            @pl.when((u >= 0) & (z >= u))
+            def _():
+                cross(z - u).wait_recv()
+
+            @pl.when((u > 0) & (z + u < n))
+            def _():
+                cross(z + u).wait_recv()
+
+            def candidate(m, carry):
+                on_left = lax.rem(m, 2) == 0
+                far = t - m // 2
+                zz = jnp.where(on_left, z - far, z + far)
+                valid = (far >= 0) & (far < n) & (zz >= 0) & (zz < n) & (on_left | (far > 0))
+
+                @pl.when(valid)
+                def _():
+                    prepare(jnp.where(m >= 2, 1 - layer, layer), zz)
+
+                return carry
+
+            lax.fori_loop(0, 4, candidate, 0)
+
+    srcs = (r.pbuf, r.dg) if backward else (r.pbuf,)
+    outs = (r.back, r.dgate) if backward else (r.back,)
+    relays = (r.relay, r.dg_relay) if backward else (r.relay,)
+    arrays = range(len(srcs))
 
     def hop(a, to):
-        return pltpu.make_async_remote_copy(
+        return remote(
             src_ref=srcs[a].at[1 - layer, to],
             dst_ref=relays[a].at[to],
-            send_sem=relay_send.at[a, to],
-            recv_sem=relay_recv.at[a, to],
-            device_id={"section": 1 - s},
-            device_id_type=MESH,
+            send_sem=r.s_hop.at[a, to],
+            recv_sem=r.r_hop.at[a, to],
+            device_id=other,
         )
 
     def give(a, source, k):
-        return pltpu.make_async_remote_copy(
+        return remote(
             src_ref=source,
             dst_ref=outs[a].at[z],
-            send_sem=send_sem.at[a, k],
-            recv_sem=recv_sem.at[a, k],
+            send_sem=r.s_give.at[a, k],
+            recv_sem=r.r_give.at[a, k],
             device_id={"expert": lax.rem(z + k, n)},
-            device_id_type=MESH,
         )
 
-    order = sorted(range(n), key=lambda k: (k == 0, abs(k - n // 2)))
-
-    @pl.when(s == layer)
+    def keep(a, source):
+        return pltpu.make_async_copy(source, outs[a].at[z], r.keep_sem.at[a])
+
+    def saved(j, slot):
+        return [
+            pltpu.make_async_copy(r.gp_buf.at[slot], r.gp.at[j], r.gp_sem.at[slot, 0]),
+            pltpu.make_async_copy(r.gp_buf.at[2 + slot], r.up.at[j], r.gp_sem.at[slot, 1]),
+        ]
+
+    def expert(j, slot):
+        if mode == "fwd":
+
+            @pl.when(j >= 2)
+            def _():
+                for c in saved(j - 2, slot):
+                    c.wait()
+
+        def part(c, carry):
+            at = pl.ds(pl.multiple_of(c * chunk, chunk), chunk)
+            if forward:
+                x = r.x_scr[j, at, :]
+                gp = dot(x, r.wg_buf[slot])
+                up = dot(x, r.wu_buf[slot])
+            else:
+                gp, up = r.gp_buf[slot, at, :].astype(F32), r.gp_buf[2 + slot, at, :].astype(F32)
+            sg = 1.0 / (1.0 + jnp.exp(-gp))
+            silu = gp * sg
+            hid = silu * up
+            hots, gate = chunk_gates(c, j, chunk, cap, r.pos, r.gate)
+            if not backward:
+                r.gp_buf[slot, at, :] = gp.astype(BF)
+                r.gp_buf[2 + slot, at, :] = up.astype(BF)
+                r.y_scr[j, at, :] = (dot(hid.astype(BF), r.wd_buf[slot]) * gate).astype(BF)
+                return carry
+            raw = dot(r.y_scr[j, at, :], r.wd_buf[slot], 1, 1)
+            dgate = jnp.sum(hid.astype(BF).astype(F32) * raw, axis=1, keepdims=True)
+            for bb in range(chunk // cap):
+                b = c * (chunk // cap) + bb
+                r.dg[b // n, lax.rem(b, n), pl.ds(j, 1), :] = jnp.sum(
+                    hots[bb] * dgate[bb * cap : (bb + 1) * cap], axis=0, keepdims=True
+                )
+            dh = raw * gate
+            dgp = (dh * up * sg * (1.0 + gp * (1.0 - sg))).astype(BF)
+            dup = (dh * silu).astype(BF)
+            r.act[0, j, at, :] = dgp
+            r.act[1, j, at, :] = dup
+            r.act[2, j, at, :] = (hid * gate).astype(BF)
+            r.y_scr[j, at, :] = (dot(dgp, r.wg_buf[slot], 1, 1) + dot(dup, r.wu_buf[slot], 1, 1)).astype(BF)
+            return carry
+
+        lax.fori_loop(0, rows // chunk, part, 0)
+        if mode == "fwd":
+            for c in saved(j, slot):
+                c.start()
+
+    def summed(b, source):
+        at = pl.ds(pl.multiple_of(b * cap, cap), cap)
+        stacked = jnp.concatenate([source[j, at, :] for j in range(per)], axis=0)
+        return dot(all_hots_back(r.pos[b], per, cap), stacked).astype(BF)
+
+    @pl.when(here)
     def _():
-        for k in order:
-            for a in range(arrays):
-                hop(a, lax.rem(z + k, n)).start()
-        for k in order:
-            for a in range(arrays):
-                if k:
-                    give(a, srcs[a].at[layer, lax.rem(z + k, n)], k).start()
-                else:
-                    pltpu.make_async_copy(srcs[a].at[layer, z], outs[a].at[z], local_sem.at[a]).start()
-        if cap:
-            weight_grads(cap, *work_in, work_out, *refs[5:])
-        for k in order:
-            for a in range(arrays):
-                hop(a, lax.rem(z + k, n)).wait_send()
-
-    @pl.when(s != layer)
+        if backward:
+            r.dg[...] = jnp.zeros_like(r.dg)
+        if mode == "fwd":
+            keep_blocks = pltpu.make_async_copy(r.blk, r.blocks, r.row_sem.at[0])
+            keep_blocks.start()
+        streamed(per, weights, expert, primed=True)
+
+        def emit(i, carry):
+            to = lax.rem(z + i + 1, n)
+            section = jnp.where(i < n, 1 - layer, layer)
+            r.pbuf[section, to] = summed(section * n + to, r.y_scr)
+
+            @pl.when(i < n)
+            def _():
+                for a in arrays:
+                    hop(a, to).start()
+
+            @pl.when((i >= n) & (to != z))
+            def _():
+                for a in arrays:
+                    give(a, srcs[a].at[layer, to], i + 1 - n).start()
+
+            return carry
+
+        lax.fori_loop(0, 2 * n, emit, 0)
+        for a in arrays:
+            keep(a, srcs[a].at[layer, z]).start()
+        if mode == "fwd":
+            for j in (per - 2, per - 1):
+                for c in saved(j, j % 2):
+                    c.wait()
+            keep_blocks.wait()
+        if mode == "bwd":
+
+            @pl.loop(0, count)
+            def _(b):
+                put_rows(all_hots(r.pos[b], per, cap).astype(BF), r.blk[b // n, lax.rem(b, n)], b, per, cap, r.y_scr)
+
+            gather_from(count, per, cap, r.pos, r.blocks, r.x_scr, r.row_buf, r.row_sem)
+        if mode == "both":
+            gather_from(count, per, cap, r.pos, r.gy, r.y_scr, r.row_buf, r.row_sem)
+        if backward:
+            weight_grads(r, per)
+        if mode == "both":
+            def output(j, slot):
+                @pl.loop(0, rows // chunk)
+                def _(c):
+                    at = pl.ds(pl.multiple_of(c * chunk, chunk), chunk)
+                    r.x_scr[j, at, :] = dot(r.act[2, j, at, :], r.wd_buf[slot]).astype(BF)
+
+            streamed(per, lambda j, slot: weights(j, slot)[2:], output)
+            combine(0, n, per, cap, r.pos, r.x_scr, r.part0, r.row_buf, r.row_sem)
+            combine(n, n, per, cap, r.pos, r.x_scr, r.part1, r.row_buf, r.row_sem)
+        for to in range(n):
+            for a in arrays:
+                hop(a, to).wait_send()
+
+    @pl.when(jnp.logical_not(here))
     def _():
-        for k in order:
-            to = lax.rem(z + k, n)
-            for a in range(arrays):
+        @pl.loop(1, n + 1)
+        def _(k):
+            to = lax.rem(lax.rem(k, n) + z, n)
+            for a in arrays:
                 hop(a, to).wait_recv()
-                if k:
+
+            @pl.when(k < n)
+            def _():
+                for a in arrays:
                     give(a, relays[a].at[to], k).start()
-                else:
-                    pltpu.make_async_copy(relays[a].at[z], outs[a].at[z], local_sem.at[a]).start()
-
-    for a in range(arrays):
-        for k in order:
-            if k:
-                give(a, relays[a].at[lax.rem(z + k, n)], k).wait()
-            else:
-                pltpu.make_async_copy(relays[a].at[z], outs[a].at[z], local_sem.at[a]).wait()
-
-
-def collect(layer, cid, arrays, work=None):
+
+        for a in arrays:
+            keep(a, relays[a].at[z]).start()
+        for zz in range(n):
+            cross(zz).wait_send()
+
+    for a in arrays:
+        keep(a, relays[a].at[z]).wait()
+        for k in range(1, n):
+            give(a, relays[a].at[lax.rem(z + k, n)], k).wait()
+    for t in range(n):
+
+        @pl.when((z >= t) & (z < n - 1))
+        def _():
+            right(t).wait_send()
+
+        @pl.when((z + t < n) & (z > 0))
+        def _():
+            left(t).wait_send()
+
+
+def moe(layer, mode, cid, e_pad, cap, own, wg, wu, wd, **given):
     n, groups = lax.axis_size("expert"), lax.axis_size("group")
-    count = len(arrays)
+    count = 2 * n
+    t, d = own.shape
+    per, _, f = wg.shape
+    rows = count * cap
+    piece = d // groups
     sds = jax.ShapeDtypeStruct
     dma = pltpu.SemaphoreType.DMA
-    outs = [sds(a.shape[1:], a.dtype) for a in arrays]
-    scratch = [pltpu.VMEM(a.shape[1:], a.dtype) for a in arrays]
-    scratch += [dma((count, n)), dma((count, n)), dma((count, n)), dma((count, n)), dma((count,))]
-    in_specs = [any_spec()] * count
-    extra = ()
-    if work:
-        extra = work[1:]
-        pos, blocks, _, dgp = extra[:4]
-        t, d = blocks.shape[1:]
-        per, rows, f = dgp.shape
-        piece = d // groups
-        outs += [sds((groups // 2, 2, per, piece, f), BF)] * 2 + [sds((groups // 2, per, f, piece), BF)] * 2
-        in_specs += vmem(1) + [any_spec()] * 5
-        scratch += [
-            pltpu.VMEM((per, rows, d), BF),
-            pltpu.VMEM((per, rows, d), BF),
-            pltpu.VMEM((2, t, d), BF),
-            pltpu.VMEM((2, t, d), BF),
-            pltpu.VMEM((2, 3, rows, f), BF),
-            pltpu.VMEM((2, groups, 2, piece, f), BF),
-            pltpu.VMEM((2, groups, f, piece), BF),
-            dma((2,)),
-            dma((2,)),
-            dma((2, 3)),
-            dma((2, 2)),
-            dma((2, 2)),
-        ]
-    return pl.pallas_call(
-        functools.partial(collect_kernel, layer, n, count, work[0] if work else 0),
-        out_shape=tuple(outs),
-        in_specs=in_specs,
-        out_specs=tuple([any_spec()] * len(outs)),
-        scratch_shapes=scratch,
-        compiler_params=pltpu.CompilerParams(
-            collective_id=cid, has_side_effects=True, vmem_limit_bytes=VMEM_LIMIT if work else 16 * 1024 * 1024
-        ),
-    )(*arrays, *extra)
+    vm, hbm = pl.BlockSpec(memory_space=pltpu.VMEM), any_spec()
+    on_chip = ("own", "rt", "wrt", "pos", "gate")
+    ins = dict(own=own, wg=wg, wu=wu, wd=wd, **given)
+    outs = dict(back=sds((n, t, d), BF))
+    scratch = dict(
+        blk=pltpu.VMEM((2, n, t, d), BF),
+        y_scr=pltpu.VMEM((per, rows, d), BF),
+        wg_buf=pltpu.VMEM((2, d, f), BF),
+        wu_buf=pltpu.VMEM((2, d, f), BF),
+        wd_buf=pltpu.VMEM((2, f, d), BF),
+        pbuf=pltpu.VMEM((2, n, t, d), BF),
+        relay=pltpu.VMEM((n, t, d), BF),
+        x_scr=pltpu.VMEM((per, rows, d), BF),
+        row_buf=pltpu.VMEM((2, t, d), BF),
+        row_sem=dma((2,)),
+        w_sem=dma((2, 3)),
+        keep_sem=dma((2,)),
+    )
+    for name in ("right", "left", "cross"):
+        scratch["s_" + name] = dma((n,))
+        scratch["r_" + name] = dma((n,))
+    for name in ("hop", "give"):
+        scratch["s_" + name] = dma((2, n))
+        scratch["r_" + name] = dma((2, n))
+    if mode != "both":
+        scratch["gp_buf"] = pltpu.VMEM((4, rows, f), BF)
+        scratch["gp_sem"] = dma((2, 2))
+    if mode != "bwd":
+        scratch["gates"] = pltpu.VMEM((e_pad, t), F32)
+    if mode == "fwd":
+        del scratch["row_buf"]
+        outs.update(pos=sds((count, 8, t), jnp.int32), gate=sds((count, 8, t), F32))
+        outs.update(gp=sds((per, rows, f), BF), up=sds((per, rows, f), BF), blocks=sds((2, n, t, d), BF))
+    else:
+        outs["dgate"] = sds((n, 8, t), F32)
+        outs["even"] = outs["odd"] = sds((groups // 2, 2, per, piece, f), BF)
+        outs["even_dn"] = outs["odd_dn"] = sds((groups // 2, per, f, piece), BF)
+        scratch.update(
+            dg=pltpu.VMEM((2, n, 8, t), F32),
+            dg_relay=pltpu.VMEM((n, 8, t), F32),
+            act=pltpu.VMEM((3, per, rows, f), BF),
+            gu_buf=pltpu.VMEM((2, 2, 2, piece, f), BF),
+            dn_buf=pltpu.VMEM((2, 2, f, piece), BF),
+            gu_sem=dma((2, 2)),
+            dn_sem=dma((2, 2)),
+        )
+    if mode == "both":
+        outs["part0"] = outs["part1"] = sds((n, t, d), BF)
+        scratch.update(pos=pltpu.VMEM((count, 8, t), jnp.int32), gate=pltpu.VMEM((count, 8, t), F32))
+    names = tuple(ins) + tuple(outs) + tuple(scratch)
+    results = pl.pallas_call(
+        functools.partial(moe_kernel, layer, mode, n, e_pad, cap, names),
+        out_shape=tuple(outs.values()),
+        in_specs=[vm if name in on_chip else hbm for name in ins],
+        out_specs=tuple(vm if name in on_chip else hbm for name in outs),
+        scratch_shapes=list(scratch.values()),
+        compiler_params=pltpu.CompilerParams(collective_id=cid, has_side_effects=True, vmem_limit_bytes=VMEM_LIMIT),
+    )(*ins.values())
+    return types.SimpleNamespace(**dict(zip(outs, results)))
 
 
 def top_bit(q):
@@ -1413,35 +1433,28 @@
     qkv0, p0, o0, h0, b0, wrt0 = attn_fwd(x0, first_weights, cos, sin, meta, segr)
     second_shard, b0 = lax.optimization_barrier((second_shard, b0))
     second_weights = lax.all_gather(second_shard, ("group", "expert"), axis=0, tiled=True)
-    b0_all = flat(spread(0, 2, b0))
-    gp0, up0, pos0, gate0, part0 = experts_fwd(0, e_pad, cap, rt_all, wrt0, wg, wu, wd, b0_all)
-    (back0,) = collect(0, 3, (paired(part0),))
-    x1 = (h0 + jnp.sum(back0.astype(F32), axis=0)).astype(BF)
+    m0 = moe(0, "fwd", 2, e_pad, cap, b0, wg, wu, wd, rt=rt_all, wrt=wrt0)
+    x1 = (h0 + jnp.sum(m0.back.astype(F32), axis=0)).astype(BF)
 
     qkv1, p1, o1, h1, b1, wrt1 = attn_fwd(x1, second_weights, cos, sin, meta, segr)
-    b1_all = flat(spread(1, 4, b1))
-    gp1, up1, pos1, gate1, part1 = experts_fwd(1, e_pad, cap, rt_all, wrt1, wg, wu, wd, b1_all)
-    dgp1, dup1, hid1, dg1, dpart1 = experts_bwd(1, cap, pos1, gate1, wg, wu, wd, gp1, up1, gy1)
-    dback1, dgate1, *dw1 = collect(1, 5, (paired(dpart1), paired(dg1)), (cap, pos1, b1_all, gy1, dgp1, dup1, hid1))
+    m1 = moe(1, "both", 3, e_pad, cap, b1, wg, wu, wd, rt=rt_all, wrt=wrt1, gy=gy1)
+
+    crossed = lax.ppermute(m1.part0, "section", [(1, 0)])
 
     def gates_back(dg):
         dg = dg[:, :per].reshape(experts, t)
         return jnp.pad(dg, ((0, e_pad - experts), (0, 0)))
 
-    dx1, dd1 = attn_bwd(cot, h1, x1, second_weights, qkv1, p1, o1, b1, wrt1, dback1, gates_back(dgate1), rt_tokens[1], cos, sin)
+    dx1, dd1 = attn_bwd(cot, h1, x1, second_weights, qkv1, p1, o1, b1, wrt1, m1.back, gates_back(m1.dgate), rt_tokens[1], cos, sin)
     gy0 = dx1.astype(BF)
 
-    gy0_all = flat(spread(0, 6, gy0))
-    gy0_all, part1 = lax.optimization_barrier((gy0_all, part1))
-    crossed = lax.ppermute(paired(part1)[0], "section", [(1, 0)])
-    dgp0, dup0, hid0, dg0, dpart0 = experts_bwd(0, cap, pos0, gate0, wg, wu, wd, gp0, up0, gy0_all)
-    dback0, dgate0, *dw0 = collect(0, 7, (paired(dpart0), paired(dg0)), (cap, pos0, b0_all, gy0_all, dgp0, dup0, hid0))
-    dback0, part1, crossed = lax.optimization_barrier((dback0, part1, crossed))
-    back1 = lax.all_to_all(jnp.where(at_zero, crossed, paired(part1)[1]), "expert", split_axis=0, concat_axis=0, tiled=True)
+    n0 = moe(0, "bwd", 4, e_pad, cap, gy0, wg, wu, wd, pos=m0.pos, gate=m0.gate, gp=m0.gp, up=m0.up, blocks=flat(m0.blocks))
+    dback0, crossed, straight = lax.optimization_barrier((n0.back, crossed, m1.part1))
+    back1 = lax.all_to_all(jnp.where(at_zero, crossed, straight), "expert", split_axis=0, concat_axis=0, tiled=True)
     y1 = (h1 + jnp.sum(back1.astype(F32), axis=0)).astype(BF)
-    dx0, dd0 = attn_bwd(gy0, h0, x0, first_weights, qkv0, p0, o0, b0, wrt0, dback0, gates_back(dgate0), rt_tokens[0], cos, sin)
-
-    dense, gate_grad, up_grad, down = finish(9, dd0, dd1, dw0, dw1)
+    dx0, dd0 = attn_bwd(gy0, h0, x0, first_weights, qkv0, p0, o0, b0, wrt0, dback0, gates_back(n0.dgate), rt_tokens[0], cos, sin)
+
+    dense, gate_grad, up_grad, down = finish(5, dd0, dd1, (n0.even, n0.odd, n0.even_dn, n0.odd_dn), (m1.even, m1.odd, m1.even_dn, m1.odd_dn))
 
     kept_out = jnp.where(at_zero, x1, y1)
     swapped_out = swap_sections(jnp.where(at_zero, y1, x1))

time: 864 us -> 784 us (0.907)
  Pallas kernels: 772 us -> 683 us
    pallas_call x10 -> x3, Pallas kernels: 419 us -> 335 us  [moe(): pl.pallas_call(functools.partial(moe_kernel, layer, mode, n, e_pad, cap,...]
    all_to_all x1, starting transfers between devices: 3.96 us -> 12.7 us  [local(): lax.all_to_all(jnp.where(at_zero, crossed, straight), 'expert', split_axi...]
  transfers between devices with their start and end apart: 6 -> 6, of which waited for: 2 -> 2; matrix products, arithmetic and copies ran while one was open for 2% -> 3% of each run, Pallas kernels for 63% -> 72%
where the time goes in v4:
time: 784 us; the launch traced here: 776 us
  Pallas kernels  683 us (87%)
  local copies, waits for them, and re-layouts  27.6 us (4%)
  starting transfers between devices  24.9 us (3%)
  between operations  14.5 us (2%)
  other arithmetic  14.4 us (2%)
  waiting for transfers between devices  11.5 us (1%)
    pallas_call x3, Pallas kernels, moe(): pl.pallas_call(functools.partial(moe_kernel, layer, mode, n, e_pad, cap,...  335 us
    pallas_call x1, Pallas kernels, finish(): pl.pallas_call(functools.partial(finish_kernel, n), out_shape=(sds((rows,...  175 us
    pallas_call x1, Pallas kernels, open_up(): pl.pallas_call(functools.partial(open_kernel, n, groups, pieces), out_sha...  96.4 us
    pallas_call x2, Pallas kernels, attn_bwd(): pl.pallas_call(functools.partial(attn_bwd_kernel, dg.shape[0]), out_shape...  48.9 us
    pallas_call x2, Pallas kernels, attn_fwd(): pl.pallas_call(attn_fwd_kernel, out_shape=(sds((t, QKV), BF), sds((QUERY_...  28.1 us
  transfers between devices with their start and end apart: 6, of which 2 were waited for; matrix products, arithmetic and copies ran while one was open for 3% of the time, Pallas kernels for 72%

profile of v4, /device:TPU:0, one launch (start us, length us, event | category | flops | bytes accessed | tf_op | source)
XLA Modules:
  0.0 775.6 jit_solution(8222904723988945635)
XLA Ops:
  9.7 2.1 concatenate.31.w_ref
  11.8 1.3 collective-permute-start
  16.6 96.4 %shard_map.238 = (bf16[16,96,4224]{2,1,0:T(8,128)(2,1)}, bf16[2,4,128,1536]{3,2,1,0:T(8,128)(2,1)}, s32[2,4,8,128]{3,2,1,0:T(8,128)}, s32[8,128]{1,0:T(8,128)}) custom-call(bf16[96,4224]{1,0:T(8,128)(2,1)} %concatenate.31.w_ref, bf16[128,1536]{1,0:T(8,128)(2,1)} %get-tuple-element.162.cot_ref.gy_ref, s32[2,8,128]{2,1,0:T(8,128)} %bitcast.101), custom_call_target="tpu_custom_call" | custom-call | tf_op jit(solution)/shard_map/pallas_call | solution.py:1358
  113.6 14.0 %shard_map.239 = (bf16[128,2560]{1,0:T(8,128)(2,1)}, f32[24,128,128]{2,1,0:T(8,128)}, bf16[128,1536]{1,0:T(8,128)(2,1)}, f32[128,1536]{1,0:T(8,128)}, bf16[128,1...) custom-call(bf16[128,1536]{1,0:T(8,128)(2,1)} %get-tuple-element.163.x_ref, bf16[1536,4224]{1,0:T(8,128)(2,1)} %bitcast.78, ...), custom_call_target="tpu_custom_call" | custom-call | flops 1610612736 | bytes 12976128 | tf_op jit(solution)/shard_map/pallas_call | solution.py:126
  127.7 1.0 broadcast_select_fusion.1
  128.7 133.4 %shard_map.240 = (bf16[4,128,1536]{2,1,0:T(8,128)(2,1)}, s32[8,8,128]{2,1,0:T(8,128)}, f32[8,8,128]{2,1,0:T(8,128)}, bf16[5,512,512]{2,1,0:T(8,128)(2,1)}, bf16[...) custom-call(bf16[128,1536]{1,0:T(8,128)(2,1)} %get-tuple-element.64.refs_0_.b_ref, ...), custom_call_target="tpu_custom_call" | custom-call | tf_op jit(solution)/shard_map/pallas_call | solution.py:776
  262.1 1.9 convert_reduce_fusion.1
  264.9 9.9 %all-gather.2.cloned.1.call-done.w_ref = bf16[1536,4224]{1,0:T(8,128)(2,1)} async-done(((bf16[96,4224]{1,0:T(8,128)(2,1)}), bf16[1536,4224]{1,0:T(8,128)(2,1)}) %all-gather.2.cloned.1.call-update) | async-done | bytes 12976144 | tf_op jit(solution)/shard_map/all_gather | solution.py:1435
  274.8 14.1 %shard_map.241 = (bf16[128,2560]{1,0:T(8,128)(2,1)}, f32[24,128,128]{2,1,0:T(8,128)}, bf16[128,1536]{1,0:T(8,128)(2,1)}, f32[128,1536]{1,0:T(8,128)}, bf16[128,1...) custom-call(bf16[128,1536]{1,0:T(8,128)(2,1)} %add_convert_fusion.1.x_ref, ...), custom_call_target="tpu_custom_call" | custom-call | flops 1610612736 | bytes 12976128 | tf_op jit(solution)/shard_map/pallas_call | solution.py:126
  288.9 106.8 %shard_map.242 = (bf16[4,128,1536]{2,1,0:T(8,128)(2,1)}, f32[4,8,128]{2,1,0:T(8,128)}, bf16[2,2,5,384,512]{4,3,2,1,0:T(8,128)(2,1)}, bf16[2,2,5,384,512]{4,3,2,1...) custom-call(bf16[128,1536]{1,0:T(8,128)(2,1)} %get-tuple-element.73., ...), custom_call_target="tpu_custom_call" | custom-call | tf_op jit(solution)/shard_map/pallas_call | solution.py:776
  395.7 1.5 collective-permute-start.1
  399.2 24.4 %shard_map.243 = (f32[128,1536]{1,0:T(8,128)}, bf16[1536,4224]{1,0:T(8,128)(2,1)}) custom-call(bf16[128,1536]{1,0:T(8,128)(2,1)} %get-tuple-element.162.cot_ref.gy_ref, f32[128,1536]{1,0:T(8,128)} %get-tuple-element.69.h_ref, bf16[128,1536]{1,0:T(8,128)(2,1)} %add_convert_fusion.1.x_ref, bf16[1536,4224]{1,0:T(8,128)(2,1)} %all-gather.2.cloned.1.call-done.w_ref, ...), custom_call_target="tpu_custom_call" | custom-call | flops 3221225472 | bytes 25952256 | tf_op jit(solution)/shard_map/pallas_call | solution.py:243
  423.6 1.9 convert_element_type.20.refs_0_.gy_ref
  425.5 94.4 %shard_map.244 = (bf16[4,128,1536]{2,1,0:T(8,128)(2,1)}, f32[4,8,128]{2,1,0:T(8,128)}, bf16[2,2,5,384,512]{4,3,2,1,0:T(8,128)(2,1)}, bf16[2,2,5,384,512]{4,3,2,1...) custom-call(bf16[128,1536]{1,0:T(8,128)(2,1)} %convert_element_type.20.refs_0_.gy_ref, ...), custom_call_target="tpu_custom_call" | custom-call | tf_op jit(solution)/shard_map/pallas_call | solution.py:776
  519.9 1.3 broadcast_select_fusion
  521.2 12.7 %all-to-all-start = ((bf16[4,128,1536]{2,1,0:T(8,128)(2,1)}), bf16[4,128,1536]{2,1,0:T(8,128)(2,1)S(1)}, u32[]{:S(2)}, u32[]{:S(2)}) async-start(bf16[4,128,1536]{2,1,0:T(8,128)(2,1)} %broadcast_select_fusion), calls=%async_computation | async-start | bytes 3145728 | tf_op jit(solution)/shard_map/all_to_all | solution.py:1453
  534.6 24.5 %shard_map.245 = (f32[128,1536]{1,0:T(8,128)}, bf16[1536,4224]{1,0:T(8,128)(2,1)}) custom-call(bf16[128,1536]{1,0:T(8,128)(2,1)} %convert_element_type.20.refs_0_.gy_ref, f32[128,1536]{1,0:T(8,128)} %get-tuple-element.62.h_ref, bf16[128,1536]{1,0:T(8,128)(2,1)} %get-tuple-element.163.x_ref, bf16[1536,4224]{1,0:T(8,128)(2,1)} %bitcast.79, ...), custom_call_target="tpu_custom_call" | custom-call | flops 3221225472 | bytes 25952256 | tf_op jit(solution)/shard_map/pallas_call | solution.py:243
  559.1 2.2 select_bitcast_fusion
  561.3 7.8 %collective-permute-start.3 = (f32[128,1536]{1,0:T(8,128)}, f32[128,1536]{1,0:T(8,128)}, u32[]{:S(2)}, u32[]{:S(2)}) collective-permute-start(f32[128,1536]{1,0:T(8,128)} %get-tuple-element.155), channel_id=1, source_target_pairs={{0,16},{16,0},{1,17},{17,1},{2,18},{18,2},{3,19},{19,3},{4,20},{20... | collective-permute-start | bytes 2359304 | tf_op jit(solution)/shard_map/ppermute | solution.py:1370
  569.0 174.9 %shard_map.246 = (f32[96,4224]{1,0:T(8,128)}, f32[5,384,512]{2,1,0:T(8,128)}, f32[5,384,512]{2,1,0:T(8,128)}, f32[5,512,384]{2,1,0:T(8,128)}) custom-call(bf16[16,96,4224]{2,1,0:T(8,128)(2,1)} %bitcast.81, bf16[16,96,4224]{2,1,0:T(8,128)(2,1)} %bitcast.80, bf16[2,10,384,512]{3,2,1,0:T(8,128)(2,1)} %bitcast.84, bf16[2,10,384,512]{3,2,1,0:T(8,128)(2,1)} %bitcast.85, ...), custom_call_target="tpu_custom_call" | custom-call | tf_op jit(solution)/shard_map/pallas_call | solution.py:1144
  743.9 1.8 slice_bitcast_fusion.2
  745.7 2.3 slice_bitcast_fusion
  749.5 1.5 collective-permute-start.2
  752.5 1.6 slice_reduce_fusion
  754.1 2.9 maximum_select_fusion
  757.0 1.6 collective-permute-done.2
  758.6 1.0 maximum_select_fusion.1
  759.6 2.0 copy.63
  761.6 1.5 copy-done.4
  763.2 2.0 copy.64
  765.2 1.5 copy-done.3
  766.7 1.9 copy.65
  (66 shorter events, 13.0 us)
Async XLA Ops:
  7.2 7.6 copy-start
  7.2 7.7 copy-start.15
  7.2 8.5 %copy-start.10 = (bf16[2,1,128,1536]{3,2,1,0:T(8,128)(2,1)S(1)}, bf16[2,1,128,1536]{3,2,1,0:T(8,128)(2,1)}, u32[]{:S(2)}) copy-start(bf16[2,1,128,1536]{3,2,1,0:T(8,128)(2,1)} %param.16) | copy-start | bytes 2359300
  7.2 8.5 %copy-start.11 = (bf16[2,1,128,1536]{3,2,1,0:T(8,128)(2,1)S(1)}, bf16[2,1,128,1536]{3,2,1,0:T(8,128)(2,1)}, u32[]{:S(2)}) copy-start(bf16[2,1,128,1536]{3,2,1,0:T(8,128)(2,1)} %param.15) | copy-start | bytes 2359300
  7.2 267.6 %all-gather.2.cloned.1.call-start = ((), (), s32[]{:S(2)}) async-start(), calls=%async_computation.1 | async-start | bytes 13787136 | tf_op jit(solution)/shard_map/all_gather | solution.py:1435
  11.8 115.8 %collective-permute-start = (bf16[96,4224]{1,0:T(8,128)(2,1)}, bf16[96,4224]{1,0:T(8,128)(2,1)S(1)}, u32[]{:S(2)}, u32[]{:S(2)}) collective-permute-start(bf16[96,4224]{1,0:T(8,128)(2,1)} %concatenate.31.w_ref), channel_id=1, source_target_pairs={{16,0},{17,1},{18,2},{19,3},{20,4},{21,5},{22,6},{23,7},{24,8},{25... | collective-permute-start | bytes 2433032 | tf_op jit(solution)/shard_map/ppermute | solution.py:1408
  262.1 1.9 copy-start.7
  288.9 108.3 %copy-start.12 = (s32[1,2,1,128,8]{3,4,2,1,0:T(8,128)S(1)}, s32[1,2,1,128,8]{3,4,2,1,0:T(8,128)}, u32[]{:S(2)}) copy-start(s32[1,2,1,128,8]{3,4,2,1,0:T(8,128)} %param.19) | copy-start | bytes 24580
  288.9 108.3 %copy-start.14 = (s32[8,128]{1,0:T(8,128)S(1)}, s32[8,128]{1,0:T(8,128)}, u32[]{:S(2)}) copy-start(s32[8,128]{1,0:T(8,128)} %get-tuple-element.78) | copy-start | bytes 12292
  395.7 124.2 %collective-permute-start.1 = (bf16[4,128,1536]{2,1,0:T(8,128)(2,1)}, bf16[4,128,1536]{2,1,0:T(8,128)(2,1)S(1)}, u32[]{:S(2)}, u32[]{:S(2)}) collective-permute-start(bf16[4,128,1536]{2,1,0:T(8,128)(2,1)} %get-tuple-element.86), channel_id=1, source_target_pairs={{16,0},{17,1},{18,2},{19,3},{20,4},{21,5},{22,6},{23,7},{24,8},{25... | collective-permute-start | bytes 4718600 | tf_op jit(solution)/shard_map/ppermute | solution.py:1442
  425.5 94.4 %copy-start.9 = (bf16[4,128,1536]{2,1,0:T(8,128)(2,1)S(1)}, bf16[4,128,1536]{2,1,0:T(8,128)(2,1)}, u32[]{:S(2)}) copy-start(bf16[4,128,1536]{2,1,0:T(8,128)(2,1)} %get-tuple-element.89) | copy-start | bytes 4718596
  521.2 12.8 %copy-start.13 = (f32[4,8,128]{2,1,0:T(8,128)S(1)}, f32[4,8,128]{2,1,0:T(8,128)}, u32[]{:S(2)}) copy-start(f32[4,8,128]{2,1,0:T(8,128)} %get-tuple-element.94) | copy-start | bytes 49156
  521.2 226.8 %all-to-all-start = ((bf16[4,128,1536]{2,1,0:T(8,128)(2,1)}), bf16[4,128,1536]{2,1,0:T(8,128)(2,1)S(1)}, u32[]{:S(2)}, u32[]{:S(2)}) async-start(bf16[4,128,1536]{2,1,0:T(8,128)(2,1)} %broadcast_select_fusion), calls=%async_computation | async-start | bytes 3145728 | tf_op jit(solution)/shard_map/all_to_all | solution.py:1453
  534.6 24.5 %copy-start.8 = (f32[128,1536]{1,0:T(8,128)S(1)}, f32[128,1536]{1,0:T(8,128)}, u32[]{:S(2)}) copy-start(f32[128,1536]{1,0:T(8,128)} %get-tuple-element.79) | copy-start | bytes 2359300
  561.3 192.8 %collective-permute-start.3 = (f32[128,1536]{1,0:T(8,128)}, f32[128,1536]{1,0:T(8,128)}, u32[]{:S(2)}, u32[]{:S(2)}) collective-permute-start(f32[128,1536]{1,0:T(8,128)} %get-tuple-element.155), channel_id=1, source_target_pairs={{0,16},{16,0},{1,17},{17,1},{2,18},{18,2},{3,19},{19,3},{4,20},{20... | collective-permute-start | bytes 2359304 | tf_op jit(solution)/shard_map/ppermute | solution.py:1370
  748.0 1.0 copy-start.2
  748.0 1.3 copy-start.6
  749.5 9.1 %collective-permute-start.2 = (bf16[128,1536]{1,0:T(8,128)(2,1)S(1)}, bf16[128,1536]{1,0:T(8,128)(2,1)S(1)}, u32[]{:S(2)}, u32[]{:S(2)}) collective-permute-start(bf16[128,1536]{1,0:T(8,128)(2,1)S(1)} %broadcast_select_fusion.3), channel_id=1, source_target_pairs={{0,16},{16,0},{1,17},{17,1},{2,18},{18,2},{3,19},{19,3},{4,20},{20... | collective-permute-start | bytes 1179656 | tf_op jit(solution)/shard_map/ppermute | solution.py:1370
  754.1 5.5 copy-start.5
  759.6 3.5 copy-start.4
  763.2 3.5 copy-start.3
  766.7 1.9 copy-start.1
Sparse Core Ops, SparseCore 0:
  128.8 145.9 all-gather.1

commit v5 on v4

--- a/solution.py
+++ b/solution.py
@@ -65,8 +65,36 @@
     return jnp.where(masks[half], z, jnp.zeros_like(z))
 
 
-def attn_fwd_kernel(x_ref, w_ref, cos_ref, sin_ref, meta_ref, segr_ref, qkv_ref, p_ref, o_ref, h_ref, b_ref, wrt_ref):
+def weight_pieces(d, order):
+    aux = [(pl.ds(0, d), pl.ds(QKV + QW, LANES))]
+    qkv = [(pl.ds(0, d), pl.ds(n * TILE, TILE)) for n in range(QKV // TILE)]
+    out = [(pl.ds(n * TILE, TILE), pl.ds(QKV, QW)) for n in range(d // TILE)]
+    down = [(pl.ds(0, d), pl.ds(QKV + n * TILE, TILE)) for n in range(QW // TILE)]
+    rows = [(pl.ds(n * TILE, TILE), pl.ds(0, QKV)) for n in range(d // TILE)]
+    return aux + qkv + out if order == "forward" else down + rows
+
+
+def arriving(w_hbm, w_ref, sem, order):
+    copies = [
+        pltpu.make_async_copy(w_hbm.at[rows, cols], w_ref.at[rows, cols], sem.at[i])
+        for i, (rows, cols) in enumerate(weight_pieces(w_ref.shape[0], order))
+    ]
+    for c in copies:
+        c.start()
+    return copies
+
+
+def attn_fwd_kernel(
+    below_ref, back_ref, w_hbm, cos_ref, sin_ref, meta_ref, segr_ref,
+    qkv_ref, p_ref, o_ref, h_ref, b_ref, wrt_ref, x_ref, w_ref, w_sem,
+):
     t, d = x_ref.shape
+    pieces = arriving(w_hbm, w_ref, w_sem, "forward")
+    entering = below_ref[...].astype(F32)
+    for z in range(back_ref.shape[0]):
+        entering = entering + back_ref[z].astype(F32)
+    x_ref[...] = entering.astype(BF)
+    pieces.pop(0).wait()
     aux = jnp.transpose(w_ref[:, QKV + QW :].astype(F32))
     wrt_ref[...] = aux.astype(BF)
     gain_attn = aux[GAIN_ATTN_ROW : GAIN_ATTN_ROW + 1]
@@ -77,6 +105,7 @@
     cos, sin = cos_ref[...], sin_ref[...]
     for n in range(QKV // TILE):
         cols = slice(n * TILE, (n + 1) * TILE)
+        pieces.pop(0).wait()
         y = dot(a, w_ref[:, cols])
         if n * TILE < QW + KW:
             y = rope(y, cos, sin, 1.0)
@@ -98,7 +127,7 @@
             s = dot(q, ks if swap else kp, 1, 1) * HEAD_SIZE ** (-0.5)
             s = jnp.where(allowed, s, NEG_FILL)
             e = jnp.exp(s - jnp.max(s, axis=1, keepdims=True))
-            p = e / jnp.sum(e, axis=1, keepdims=True)
+            p = e * (1.0 / jnp.sum(e, axis=1, keepdims=True))
             p_ref[m * 2 * TILES_PER_PAIR + 2 * r + half] = p
             part = dot(p.astype(BF), pick(vs if swap else vp, half, masks))
             parts[half] = part
@@ -110,6 +139,7 @@
     o = o_ref[...]
     for n in range(d // TILE):
         rows = slice(n * TILE, (n + 1) * TILE)
+        pieces.pop(0).wait()
         h_ref[:, rows] = x_ref[:, rows].astype(F32) + dot(o, w_ref[rows, QKV : QKV + QW], 1, 1)
     h = h_ref[...]
     r2 = lax.rsqrt(jnp.mean(h * h, axis=1, keepdims=True) + EPS)
@@ -120,8 +150,8 @@
     return [pl.BlockSpec(memory_space=pltpu.VMEM)] * n
 
 
-def attn_fwd(x, w, cos, sin, meta, segr):
-    t, d = x.shape
+def attn_fwd(below, back, w, cos, sin, meta, segr):
+    t, d = below.shape
     sds = jax.ShapeDtypeStruct
     return pl.pallas_call(
         attn_fwd_kernel,
@@ -132,12 +162,14 @@
             sds((t, d), F32),
             sds((t, d), BF),
             sds((LANES, d), BF),
+            sds((t, d), BF),
         ),
-        in_specs=vmem(6),
-        out_specs=tuple(vmem(6)),
+        in_specs=vmem(2) + [any_spec()] + vmem(4),
+        out_specs=tuple(vmem(7)),
+        scratch_shapes=[pltpu.VMEM(w.shape, BF), pltpu.SemaphoreType.DMA((1 + QKV // TILE + d // TILE,))],
         compiler_params=pltpu.CompilerParams(vmem_limit_bytes=VMEM_LIMIT),
         cost_estimate=pl.CostEstimate(flops=2 * t * d * 4096, bytes_accessed=w.size * 2, transcendentals=QUERY_HEADS * t * t),
-    )(x, w, cos, sin, meta, segr)
+    )(below, back, w, cos, sin, meta, segr)
 
 
 def gates_of(rt, wrt, b, e_pad):
@@ -152,10 +184,22 @@
 
 
 def attn_bwd_kernel(
-    e_pad, gy_ref, h_ref, x_ref, w_ref, qkv_ref, p_ref, o_ref, b_ref, wrt_ref, back_ref, dg_ref, rt_ref, cos_ref, sin_ref,
-    dx_ref, dd_ref, do_ref, dqkv_ref, dh_ref, lt_ref,
+    now, e_pad, gy_ref, h_ref, x_ref, w_hbm, qkv_ref, p_ref, o_ref, b_ref, wrt_ref, back_ref, dg_ref, rt_ref, cos_ref, sin_ref,
+    dx_ref, dxb_ref, *rest,
 ):
     t, d = x_ref.shape
+    if now:
+        dd_hbm, do_ref, dqkv_ref, dh_ref, w_ref, w_sem, lt_ref, dd_ref, dd_sem = rest
+    else:
+        dqkv_ref, at_ref, dht_ref, daux_ref, do_ref, dh_ref, w_ref, w_sem = rest
+    pieces = arriving(w_hbm, w_ref, w_sem, "backward")
+    leaving = []
+
+    def leave(first, width):
+        cols = pl.ds(first, width)
+        leaving.append(pltpu.make_async_copy(dd_ref.at[:, cols], dd_hbm.at[:, cols], dd_sem.at[len(leaving)]))
+        leaving[-1].start()
+
     gain_attn = wrt_ref[GAIN_ATTN_ROW - 7 :, :].astype(F32)[7:8]
     gain_moe = wrt_ref[GAIN_ATTN_ROW - 7 :, :].astype(F32)[6:7]
     b = b_ref[...]
@@ -175,6 +219,7 @@
     dhb = dh.astype(BF)
     for n in range(QW // TILE):
         cols = slice(n * TILE, (n + 1) * TILE)
+        pieces.pop(0).wait()
         do_ref[:, cols] = dot(dhb, w_ref[:, QKV + n * TILE : QKV + (n + 1) * TILE]).astype(BF)
     masks = lane_masks(t)
     cos, sin = cos_ref[...], sin_ref[...]
@@ -216,41 +261,61 @@
     dqkv = dqkv_ref[...]
     for n in range(d // TILE):
         rows = slice(n * TILE, (n + 1) * TILE)
+        pieces.pop(0).wait()
         dx_ref[:, rows] = dot(dqkv, w_ref[rows, 0:QKV], 1, 1)
     da = dx_ref[...]
     grad_attn = jnp.sum(da * x * r1, axis=0, keepdims=True)
     dag = da * gain_attn
-    dx_ref[...] = dh_ref[...] + r1 * dag - x * (r1 * r1 * r1) * jnp.mean(dag * x, axis=1, keepdims=True)
+    dx = dh_ref[...] + r1 * dag - x * (r1 * r1 * r1) * jnp.mean(dag * x, axis=1, keepdims=True)
+    dx_ref[...] = dx
+    dxb_ref[...] = dx.astype(BF)
+    row = iota((LANES, d), 0)
+    grads = jnp.where(row == GAIN_MOE_ROW, grad_moe, jnp.where(row == GAIN_ATTN_ROW, grad_attn, 0.0))
+    dl_full = jnp.concatenate([dl, jnp.zeros((LANES - e_pad, t), F32)], axis=0)
+    dl_rows = jnp.transpose(dl_full).astype(BF)
+    bt = jnp.transpose(b_ref[...].astype(F32)).astype(BF)
+    daux = (dot(bt, dl_rows) + jnp.transpose(grads)).astype(BF)
+    if not now:
+        at_ref[...] = jnp.transpose(x * r1 * gain_attn).astype(BF)
+        dht_ref[...] = jnp.transpose(dh_ref[...]).astype(BF)
+        daux_ref[...] = daux
+        return
     lt_ref[...] = jnp.transpose(x * r1 * gain_attn).astype(BF)
     for n in range(QKV // TILE):
         cols = slice(n * TILE, (n + 1) * TILE)
         dd_ref[:, cols] = dot(lt_ref[...], dqkv_ref[:, cols]).astype(BF)
+        leave(n * TILE, TILE)
     lt_ref[...] = jnp.transpose(dh_ref[...]).astype(BF)
     for n in range(QW // TILE):
         cols = slice(n * TILE, (n + 1) * TILE)
         dd_ref[:, QKV + n * TILE : QKV + (n + 1) * TILE] = dot(lt_ref[...], o_ref[:, cols]).astype(BF)
-    lt_ref[...] = jnp.transpose(b_ref[...].astype(F32)).astype(BF)
-    row = iota((LANES, d), 0)
-    grads = jnp.where(row == GAIN_MOE_ROW, grad_moe, jnp.where(row == GAIN_ATTN_ROW, grad_attn, 0.0))
-    dl_full = jnp.concatenate([dl, jnp.zeros((LANES - e_pad, t), F32)], axis=0)
-    dl_rows = jnp.transpose(dl_full).astype(BF)
-    dd_ref[:, QKV + QW :] = (dot(lt_ref[...], dl_rows) + jnp.transpose(grads)).astype(BF)
-
-
-def attn_bwd(gy, h, x, w, qkv, p, o, b, wrt, back, dg, rt, cos, sin):
+        leave(QKV + n * TILE, TILE)
+    dd_ref[:, QKV + QW :] = daux
+    leave(QKV + QW, LANES)
+    for c in leaving:
+        c.wait()
+
+
+def attn_bwd(now, gy, h, x, w, qkv, p, o, b, wrt, back, dg, rt, cos, sin):
     t, d = x.shape
     sds = jax.ShapeDtypeStruct
+    dma = pltpu.SemaphoreType.DMA
+    outs = [sds((t, d), F32), sds((t, d), BF)]
+    scratch = [pltpu.VMEM((t, QW), BF)]
+    if now:
+        outs.append(sds(w.shape, BF))
+        scratch.append(pltpu.VMEM((t, QKV), BF))
+    else:
+        outs += [sds((t, QKV), BF), sds((d, t), BF), sds((d, t), BF), sds((d, LANES), BF)]
+    scratch += [pltpu.VMEM((t, d), F32), pltpu.VMEM(w.shape, BF), dma((QW // TILE + d // TILE,))]
+    if now:
+        scratch += [pltpu.VMEM((d, t), BF), pltpu.VMEM(w.shape, BF), dma((1 + QKV // TILE + QW // TILE,))]
     return pl.pallas_call(
-        functools.partial(attn_bwd_kernel, dg.shape[0]),
-        out_shape=(sds((t, d), F32), sds(w.shape, BF)),
-        in_specs=vmem(14),
-        out_specs=tuple(vmem(2)),
-        scratch_shapes=[
-            pltpu.VMEM((t, QW), BF),
-            pltpu.VMEM((t, QKV), BF),
-            pltpu.VMEM((t, d), F32),
-            pltpu.VMEM((d, t), BF),
-        ],
+        functools.partial(attn_bwd_kernel, now, dg.shape[0]),
+        out_shape=tuple(outs),
+        in_specs=vmem(3) + [any_spec()] + vmem(10),
+        out_specs=tuple(vmem(2) + [any_spec()] if now else vmem(6)),
+        scratch_shapes=scratch,
         compiler_params=pltpu.CompilerParams(vmem_limit_bytes=VMEM_LIMIT),
         cost_estimate=pl.CostEstimate(flops=4 * t * d * 4096, bytes_accessed=w.size * 4, transcendentals=0),
     )(gy, h, x, w, qkv, p, o, b, wrt, back, dg, rt, cos, sin)
@@ -401,16 +466,14 @@
         finished(slot)
 
 
-def meet(n, with_cross):
-    s, z = lax.axis_index("section"), lax.axis_index("expert")
+def meet(n, bits):
+    s, g, z = lax.axis_index("section"), lax.axis_index("group"), lax.axis_index("expert")
     barrier = pltpu.get_barrier_semaphore()
-    for k in range(1, n):
-        pl.semaphore_signal(barrier, inc=1, device_id={"expert": lax.rem(z + k, n)}, device_id_type=MESH)
-    for k in range(n if with_cross else 1):
-        pl.semaphore_signal(
-            barrier, inc=1, device_id={"section": 1 - s, "expert": lax.rem(z + k, n)}, device_id_type=MESH
-        )
-    pl.semaphore_wait(barrier, 2 * n - 1 if with_cross else n)
+    peers = [{"section": 1 - s}] + [{"expert": lax.rem(z + k, n)} for k in range(1, n)]
+    peers += [{"group": lax.bitwise_xor(g, 1 << b)} for b in range(bits)]
+    for peer in peers:
+        pl.semaphore_signal(barrier, inc=1, device_id=peer, device_id_type=MESH)
+    pl.semaphore_wait(barrier, len(peers))
 
 
 def moe_kernel(layer, mode, n, e_pad, cap, names, *refs):
@@ -421,21 +484,53 @@
     count = 2 * n
     per, rows, d = r.y_scr.shape
     first = z * per
-    chunk = 256
+    chunk = n * cap
     remote = functools.partial(pltpu.make_async_remote_copy, device_id_type=MESH)
     other = {"section": 1 - s}
-    meet(n, False)
+    g = lax.axis_index("group")
+    riding = forward and not backward
+    groups = r.dense_out.shape[0] // n if riding else 1
+    bits = top_bit(groups)
+    meet(n, bits)
     r.blk[s, z] = r.own[...]
 
-    def weights(j, slot):
+    def over(q, b, zz):
+        at = q | (1 << b)
+        shard = r.dense_out.at[lax.bitwise_xor(g, q) * n + zz]
+        return remote(
+            src_ref=shard, dst_ref=shard, send_sem=r.s_over.at[at, zz], recv_sem=r.r_over.at[at, zz],
+            device_id={"group": lax.bitwise_xor(g, 1 << b)},
+        )
+
+    def ride():
+        for b in reversed(range(bits)):
+            for zz in range(n):
+                over(0, b, zz).start()
+
+    def ride_on():
+        for q in sorted(range(1, groups), key=lambda q: -low_bit(q)):
+            for zz in range(n):
+                over(q & (q - 1), low_bit(q), zz).wait_recv()
+                for b in reversed(range(low_bit(q))):
+                    over(q, b, zz).start()
+
+    if riding:
+        ride()
+
+    def half(i):
+        section = jnp.where(i < per, layer, 1 - layer)
+        return lax.rem(i, per), section, pl.ds(pl.multiple_of(section * chunk, chunk), chunk)
+
+    def weights(i, slot):
+        j, _, at = half(i)
         both = [
             pltpu.make_async_copy(r.wg.at[j], r.wg_buf.at[slot], r.w_sem.at[slot, 0]),
             pltpu.make_async_copy(r.wu.at[j], r.wu_buf.at[slot], r.w_sem.at[slot, 1]),
             pltpu.make_async_copy(r.wd.at[j], r.wd_buf.at[slot], r.w_sem.at[slot, 2]),
         ]
         if mode == "bwd":
-            both.append(pltpu.make_async_copy(r.gp.at[j], r.gp_buf.at[slot], r.gp_sem.at[slot, 0]))
-            both.append(pltpu.make_async_copy(r.up.at[j], r.gp_buf.at[2 + slot], r.gp_sem.at[slot, 1]))
+            both.append(pltpu.make_async_copy(r.gp.at[j, at], r.gp_buf.at[slot], r.gp_sem.at[slot, 0]))
+            both.append(pltpu.make_async_copy(r.up.at[j, at], r.gp_buf.at[2 + slot], r.gp_sem.at[slot, 1]))
         return both
 
     def chain(to, zz, t, ssem, rsem):
@@ -474,10 +569,57 @@
         for c in weights(0, 0):
             c.start()
 
-    @pl.loop(0, n + 1)
+    def prepare_at(section, t):
+        def candidate(m, carry):
+            zz = jnp.where(m == 0, z - t, z + t)
+
+            @pl.when((zz >= 0) & (zz < n) & ((m == 0) | (t > 0)))
+            def _():
+                prepare(section, zz)
+
+            return carry
+
+        lax.fori_loop(0, 2, candidate, 0)
+
+    def dense_tiles():
+        tiles = []
+        for first_row in range(0, d, rows):
+            for left, right, col, width in ((r.at, r.dqkv, 0, QW), (r.at, r.dqkv, QW, 2 * KW), (r.dht, r.o, QKV, QW)):
+                source = right if left is r.dht else right.at[:, pl.ds(col, width)]
+                tiles.append((left.at[pl.ds(first_row, rows)], source, first_row, col, width))
+        return tiles
+
+    def dense_copy(i, tile):
+        _, _, row, col, width = tile
+        return pltpu.make_async_copy(
+            r.x_scr.at[i % per, :, pl.ds(0, width)], r.dd.at[pl.ds(row, rows), pl.ds(col, width)], r.dd_sem.at[i]
+        )
+
+    def aux_copy():
+        return pltpu.make_async_copy(r.daux, r.dd.at[:, pl.ds(QKV + QW, LANES)], r.daux_sem)
+
+    def dense_start(step):
+        if step == 0:
+            aux_copy().start()
+        tiles = dense_tiles()
+        share = len(tiles) // 3
+        for i, tile in list(enumerate(tiles))[step * share : (step + 1) * share]:
+            if i >= per:
+                dense_copy(i - per, tiles[i - per]).wait()
+            left, right, _, _, width = tile
+            r.x_scr[i % per, :, 0:width] = dot(left[...], right[...]).astype(BF)
+            dense_copy(i, tile).start()
+
+    def dense_wait():
+        aux_copy().wait()
+        tiles = dense_tiles()
+        for i in range(max(0, len(tiles) - per), len(tiles)):
+            dense_copy(i, tiles[i]).wait()
+
+    @pl.loop(0, n)
     def _(t):
-        from_left = (t < n) & (z >= t)
-        from_right = (t < n) & (z + t < n)
+        from_left = z >= t
+        from_right = z + t < n
 
         @pl.when(from_left & (t > 0))
         def _():
@@ -502,6 +644,14 @@
         @pl.when(from_right & (t > 0) & jnp.logical_not(here))
         def _():
             cross(z + t).start()
+
+        if mode == "bwd":
+
+            for step in range(3):
+
+                @pl.when(t == step)
+                def _(step=step):
+                    dense_start(step)
 
         @pl.when(here)
         def _():
@@ -515,29 +665,33 @@
 
                     gather_from(count, per, cap, r.pos, r.gy, r.y_scr, r.row_buf, r.row_sem)
 
-            u = t - 1
-
-            @pl.when((u >= 0) & (z >= u))
-            def _():
-                cross(z - u).wait_recv()
-
-            @pl.when((u > 0) & (z + u < n))
-            def _():
-                cross(z + u).wait_recv()
-
-            def candidate(m, carry):
-                on_left = lax.rem(m, 2) == 0
-                far = t - m // 2
-                zz = jnp.where(on_left, z - far, z + far)
-                valid = (far >= 0) & (far < n) & (zz >= 0) & (zz < n) & (on_left | (far > 0))
-
-                @pl.when(valid)
-                def _():
-                    prepare(jnp.where(m >= 2, 1 - layer, layer), zz)
-
-                return carry
-
-            lax.fori_loop(0, 4, candidate, 0)
+            prepare_at(layer, t)
+
+    def late_blocks():
+        @pl.loop(0, n)
+        def _(t):
+            @pl.when(z >= t)
+            def _():
+                cross(z - t).wait_recv()
+
+            @pl.when((t > 0) & (z + t < n))
+            def _():
+                cross(z + t).wait_recv()
+
+            prepare_at(1 - layer, t)
+
+    def over_part(zz):
+        return remote(
+            src_ref=r.part.at[zz], dst_ref=r.part_out.at[zz], send_sem=r.s_part.at[zz], recv_sem=r.r_part.at[zz], device_id=other
+        )
+
+    if mode == "bwd":
+        dense_wait()
+
+        @pl.when(jnp.logical_not(here))
+        def _():
+            for zz in range(n):
+                over_part(zz).start()
 
     srcs = (r.pbuf, r.dg) if backward else (r.pbuf,)
     outs = (r.back, r.dgate) if backward else (r.back,)
@@ -565,57 +719,55 @@
     def keep(a, source):
         return pltpu.make_async_copy(source, outs[a].at[z], r.keep_sem.at[a])
 
-    def saved(j, slot):
+    def saved(i, slot):
+        j, _, at = half(i)
         return [
-            pltpu.make_async_copy(r.gp_buf.at[slot], r.gp.at[j], r.gp_sem.at[slot, 0]),
-            pltpu.make_async_copy(r.gp_buf.at[2 + slot], r.up.at[j], r.gp_sem.at[slot, 1]),
+            pltpu.make_async_copy(r.gp_buf.at[slot], r.gp.at[j, at], r.gp_sem.at[slot, 0]),
+            pltpu.make_async_copy(r.gp_buf.at[2 + slot], r.up.at[j, at], r.gp_sem.at[slot, 1]),
         ]
 
-    def expert(j, slot):
+    def expert(i, slot):
+        j, section, at = half(i)
+
+        @pl.when(i == per)
+        def _():
+            late_blocks()
+
         if mode == "fwd":
 
-            @pl.when(j >= 2)
-            def _():
-                for c in saved(j - 2, slot):
+            @pl.when(i >= 2)
+            def _():
+                for c in saved(i - 2, slot):
                     c.wait()
 
-        def part(c, carry):
-            at = pl.ds(pl.multiple_of(c * chunk, chunk), chunk)
-            if forward:
-                x = r.x_scr[j, at, :]
-                gp = dot(x, r.wg_buf[slot])
-                up = dot(x, r.wu_buf[slot])
-            else:
-                gp, up = r.gp_buf[slot, at, :].astype(F32), r.gp_buf[2 + slot, at, :].astype(F32)
-            sg = 1.0 / (1.0 + jnp.exp(-gp))
-            silu = gp * sg
-            hid = silu * up
-            hots, gate = chunk_gates(c, j, chunk, cap, r.pos, r.gate)
-            if not backward:
-                r.gp_buf[slot, at, :] = gp.astype(BF)
-                r.gp_buf[2 + slot, at, :] = up.astype(BF)
-                r.y_scr[j, at, :] = (dot(hid.astype(BF), r.wd_buf[slot]) * gate).astype(BF)
-                return carry
-            raw = dot(r.y_scr[j, at, :], r.wd_buf[slot], 1, 1)
-            dgate = jnp.sum(hid.astype(BF).astype(F32) * raw, axis=1, keepdims=True)
-            for bb in range(chunk // cap):
-                b = c * (chunk // cap) + bb
-                r.dg[b // n, lax.rem(b, n), pl.ds(j, 1), :] = jnp.sum(
-                    hots[bb] * dgate[bb * cap : (bb + 1) * cap], axis=0, keepdims=True
-                )
-            dh = raw * gate
-            dgp = (dh * up * sg * (1.0 + gp * (1.0 - sg))).astype(BF)
-            dup = (dh * silu).astype(BF)
-            r.act[0, j, at, :] = dgp
-            r.act[1, j, at, :] = dup
-            r.act[2, j, at, :] = (hid * gate).astype(BF)
-            r.y_scr[j, at, :] = (dot(dgp, r.wg_buf[slot], 1, 1) + dot(dup, r.wu_buf[slot], 1, 1)).astype(BF)
-            return carry
-
-        lax.fori_loop(0, rows // chunk, part, 0)
-        if mode == "fwd":
-            for c in saved(j, slot):
+        if forward:
+            x = r.x_scr[j, at, :]
+            gp = dot(x, r.wg_buf[slot])
+            up = dot(x, r.wu_buf[slot])
+        else:
+            gp, up = r.gp_buf[slot].astype(F32), r.gp_buf[2 + slot].astype(F32)
+        sg = 1.0 / (1.0 + jnp.exp(-gp))
+        silu = gp * sg
+        hid = silu * up
+        hots, gate = chunk_gates(section, j, chunk, cap, r.pos, r.gate)
+        if not backward:
+            r.gp_buf[slot] = gp.astype(BF)
+            r.gp_buf[2 + slot] = up.astype(BF)
+            r.y_scr[j, at, :] = (dot(hid.astype(BF), r.wd_buf[slot]) * gate).astype(BF)
+            for c in saved(i, slot):
                 c.start()
+            return
+        raw = dot(r.y_scr[j, at, :], r.wd_buf[slot], 1, 1)
+        dgate = jnp.sum(hid.astype(BF).astype(F32) * raw, axis=1, keepdims=True)
+        for bb in range(n):
+            r.dg[section, bb, pl.ds(j, 1), :] = jnp.sum(hots[bb] * dgate[bb * cap : (bb + 1) * cap], axis=0, keepdims=True)
+        dh = raw * gate
+        dgp = (dh * up * sg * (1.0 + gp * (1.0 - sg))).astype(BF)
+        dup = (dh * silu).astype(BF)
+        r.act[0, j, at, :] = dgp
+        r.act[1, j, at, :] = dup
+        r.act[2, j, at, :] = (hid * gate).astype(BF)
+        r.y_scr[j, at, :] = (dot(dgp, r.wg_buf[slot], 1, 1) + dot(dup, r.wu_buf[slot], 1, 1)).astype(BF)
 
     def summed(b, source):
         at = pl.ds(pl.multiple_of(b * cap, cap), cap)
@@ -628,8 +780,9 @@
             r.dg[...] = jnp.zeros_like(r.dg)
         if mode == "fwd":
             keep_blocks = pltpu.make_async_copy(r.blk, r.blocks, r.row_sem.at[0])
+        streamed(2 * per, weights, expert, primed=True)
+        if mode == "fwd":
             keep_blocks.start()
-        streamed(per, weights, expert, primed=True)
 
         def emit(i, carry):
             to = lax.rem(z + i + 1, n)
@@ -652,8 +805,8 @@
         for a in arrays:
             keep(a, srcs[a].at[layer, z]).start()
         if mode == "fwd":
-            for j in (per - 2, per - 1):
-                for c in saved(j, j % 2):
+            for i in (2 * per - 2, 2 * per - 1):
+                for c in saved(i, i % 2):
                     c.wait()
             keep_blocks.wait()
         if mode == "bwd":
@@ -669,7 +822,7 @@
             weight_grads(r, per)
         if mode == "both":
             def output(j, slot):
-                @pl.loop(0, rows // chunk)
+                @pl.loop(0, 2)
                 def _(c):
                     at = pl.ds(pl.multiple_of(c * chunk, chunk), chunk)
                     r.x_scr[j, at, :] = dot(r.act[2, j, at, :], r.wd_buf[slot]).astype(BF)
@@ -699,6 +852,23 @@
         for zz in range(n):
             cross(zz).wait_send()
 
+    if mode == "bwd":
+
+        @pl.when(here)
+        def _():
+            for zz in range(n):
+                over_part(zz).wait_recv()
+
+        @pl.when(jnp.logical_not(here))
+        def _():
+            for zz in range(n):
+                over_part(zz).wait_send()
+
+    if riding:
+        ride_on()
+        for q in range(1, groups):
+            for zz in range(n):
+                over(q & (q - 1), low_bit(q), zz).wait_send()
     for a in arrays:
         keep(a, relays[a].at[z]).wait()
         for k in range(1, n):
@@ -724,7 +894,7 @@
     sds = jax.ShapeDtypeStruct
     dma = pltpu.SemaphoreType.DMA
     vm, hbm = pl.BlockSpec(memory_space=pltpu.VMEM), any_spec()
-    on_chip = ("own", "rt", "wrt", "pos", "gate")
+    on_chip = ("own", "rt", "wrt", "pos", "gate", "dqkv", "at", "dht", "daux", "o")
     ins = dict(own=own, wg=wg, wu=wu, wd=wd, **given)
     outs = dict(back=sds((n, t, d), BF))
     scratch = dict(
@@ -748,7 +918,7 @@
         scratch["s_" + name] = dma((2, n))
         scratch["r_" + name] = dma((2, n))
     if mode != "both":
-        scratch["gp_buf"] = pltpu.VMEM((4, rows, f), BF)
+        scratch["gp_buf"] = pltpu.VMEM((4, n * cap, f), BF)
         scratch["gp_sem"] = dma((2, 2))
     if mode != "bwd":
         scratch["gates"] = pltpu.VMEM((e_pad, t), F32)
@@ -756,6 +926,8 @@
         del scratch["row_buf"]
         outs.update(pos=sds((count, 8, t), jnp.int32), gate=sds((count, 8, t), F32))
         outs.update(gp=sds((per, rows, f), BF), up=sds((per, rows, f), BF), blocks=sds((2, n, t, d), BF))
+        outs["dense_out"] = sds(given["dense"].shape, BF)
+        scratch.update(s_over=dma((groups, n)), r_over=dma((groups, n)))
     else:
         outs["dgate"] = sds((n, 8, t), F32)
         outs["even"] = outs["odd"] = sds((groups // 2, 2, per, piece, f), BF)
@@ -769,6 +941,11 @@
             gu_sem=dma((2, 2)),
             dn_sem=dma((2, 2)),
         )
+    if mode == "bwd":
+        outs["dd"] = sds((d, QKV + QW + LANES), BF)
+        outs["part_out"] = sds((n, t, d), BF)
+        scratch.update(s_part=dma((n,)), r_part=dma((n,)))
+        scratch.update(dd_sem=dma((3 * d // rows,)), daux_sem=dma)
     if mode == "both":
         outs["part0"] = outs["part1"] = sds((n, t, d), BF)
         scratch.update(pos=pltpu.VMEM((count, 8, t), jnp.int32), gate=pltpu.VMEM((count, 8, t), F32))
@@ -779,6 +956,7 @@
         in_specs=[vm if name in on_chip else hbm for name in ins],
         out_specs=tuple(vm if name in on_chip else hbm for name in outs),
         scratch_shapes=list(scratch.values()),
+        input_output_aliases={list(ins).index("dense"): list(outs).index("dense_out")} if mode == "fwd" else {},
         compiler_params=pltpu.CompilerParams(collective_id=cid, has_side_effects=True, vmem_limit_bytes=VMEM_LIMIT),
     )(*ins.values())
     return types.SimpleNamespace(**dict(zip(outs, results)))
@@ -1179,7 +1357,7 @@
 
 
 def open_kernel(
-    n, groups, pieces, w_ref, cot_ref, rt_ref, w_out, gy_out, rt_out, rt_side,
+    n, groups, pieces, w_ref, cot_ref, rt_ref, w0_out, w1_out, gy_out, rt_out, rt_side,
     s_right, r_right, s_left, r_left, s_group, r_group, s_y, r_y, s_cross, r_cross, s_rt, r_rt, s_side, r_side, local_sem,
 ):
     s, g, z = lax.axis_index("section"), lax.axis_index("group"), lax.axis_index("expert")
@@ -1205,7 +1383,9 @@
                 make().start()
 
     def part(q, zz, c):
-        return w_out.at[lax.bitwise_xor(g, q) * n + zz, pl.ds(c * rows, rows)] if c < pieces else gy_out.at[s, zz]
+        if c == 2 * pieces:
+            return gy_out.at[s, zz]
+        return (w0_out, w1_out)[c // pieces].at[lax.bitwise_xor(g, q) * n + zz, pl.ds(c % pieces * rows, rows)]
 
     def chain(to, zz, t, c, ssem, rsem):
         return remote(src_ref=part(0, zz, c), dst_ref=part(0, zz, c), send_sem=ssem.at[t, c], recv_sem=rsem.at[t, c], device_id={"expert": to})
@@ -1223,11 +1403,16 @@
             device_id={"group": lax.bitwise_xor(g, 1 << b)},
         )
 
-    def hop(c):
+    def hop(c, to=w0_out):
         at = pl.ds(c * rows, rows)
-        return remote(
-            src_ref=w_ref.at[at], dst_ref=w_out.at[g * n + z, at], send_sem=s_y.at[c], recv_sem=r_y.at[c], device_id=other
-        )
+        return remote(src_ref=w_ref.at[at], dst_ref=to.at[g * n + z, at], send_sem=s_y.at[c], recv_sem=r_y.at[c], device_id=other)
+
+    def by_layer(action):
+        for layer, to in enumerate((w0_out, w1_out)):
+
+            @pl.when(s == layer)
+            def _(to=to):
+                action(to)
 
     def cross(zz):
         return remote(src_ref=gy_out.at[0, zz], dst_ref=gy_out.at[0, zz], send_sem=s_cross.at[zz], recv_sem=r_cross.at[zz], device_id=other)
@@ -1241,47 +1426,42 @@
     def side():
         return remote(src_ref=rt_ref.at[1 - s], dst_ref=rt_side, send_sem=s_side, recv_sem=r_side, device_id=other)
 
-    launch(s == 0, functools.partial(hop, 0))
+    by_layer(lambda to: hop(0, to).start())
     launch(None, side)
     own = [pltpu.make_async_copy(cot_ref, gy_out.at[s, z], local_sem.at[0])]
     own += [pltpu.make_async_copy(rt_ref.at[m], rt_out.at[m, z], local_sem.at[1 + m]) for m in range(2)]
 
-    def keep():
-        return pltpu.make_async_copy(w_ref, w_out.at[g * n + z], local_sem.at[3])
+    def keep(to=w0_out):
+        return pltpu.make_async_copy(w_ref, to.at[g * n + z], local_sem.at[3])
 
     for copy in own:
         copy.start()
 
-    @pl.when(s == 0)
-    def _():
-        keep().start()
-        keep().wait()
+    by_layer(lambda to: keep(to).start())
+    keep().wait()
 
     def spread_out(cond, zz, c):
         if c < pieces:
             for b in reversed(range(bits)):
                 launch(cond, functools.partial(over, 0, b, zz, c))
-        else:
+        elif c == 2 * pieces:
             launch((s == 0) if cond is None else ((s == 0) & cond), functools.partial(cross, zz))
 
     def pass_along(t, c):
         if t == 0:
-            if c < pieces:
-
-                @pl.when(s != 0)
+            if c < 2 * pieces:
+
+                @pl.when(s != c // pieces)
                 def _():
-                    hop(c).wait_recv()
+                    hop(c % pieces).wait_recv()
             else:
                 own[0].wait()
             launch(z < n - 1, functools.partial(right, t, c))
             launch(z > 0, functools.partial(left, t, c))
             spread_out(None, z, c)
             if c + 1 < pieces:
-
-                @pl.when(s == 0)
-                def _():
-                    hop(c).wait_send()
-                    hop(c + 1).start()
+                hop(c).wait_send()
+                by_layer(lambda to: hop(c + 1, to).start())
         else:
             from_left, from_right = z >= t, z + t < n
 
@@ -1315,8 +1495,11 @@
                     launch(None, functools.partial(route, m, k))
     pending = [(q, k) for q in sorted(range(1, groups), key=lambda q: -low_bit(q)) for k in range(n)]
     for t in range(n):
-        pass_along(t, pieces)
+        pass_along(t, 2 * pieces)
         forward(*pending.pop(0))
+    for t in range(n):
+        for c in range(pieces, 2 * pieces):
+            pass_along(t, c)
     for q, k in pending:
         forward(q, k)
 
@@ -1330,12 +1513,8 @@
         own[1 + m].wait()
         for k in range(1, n):
             route(m, k).wait_recv()
-    @pl.when(s == 0)
-    def _():
-        if pieces > 1:
-            hop(pieces - 1).wait_send()
-
-    for cond, make in sent[(1 if pieces > 1 else 0) :]:
+    hop(pieces - 1).wait_send()
+    for cond, make in sent:
         if cond is None:
             make().wait_send()
         else:
@@ -1355,15 +1534,15 @@
     def both(shape):
         return [dma(shape), dma(shape)]
 
-    w, gy, rt_all, rt_side = pl.pallas_call(
+    w0, w1, gy, rt_all, rt_side = pl.pallas_call(
         functools.partial(open_kernel, n, groups, pieces),
-        out_shape=(sds((groups * n,) + packed.shape, BF), sds((2, n) + cot.shape, BF), sds((2, n) + rt.shape[1:], rt.dtype), sds(rt.shape[1:], rt.dtype)),
+        out_shape=(sds((groups * n,) + packed.shape, BF),) * 2 + (sds((2, n) + cot.shape, BF), sds((2, n) + rt.shape[1:], rt.dtype), sds(rt.shape[1:], rt.dtype)),
         in_specs=vmem(3),
-        out_specs=(any_spec(), any_spec(), any_spec(), any_spec()),
-        scratch_shapes=both((n, pieces + 1)) + both((n, pieces + 1)) + both((groups, n, pieces)) + both((pieces,)) + both((n,)) + both((2, n)) + [dma, dma] + [dma((4,))],
+        out_specs=tuple([any_spec()] * 5),
+        scratch_shapes=both((n, 2 * pieces + 1)) + both((n, 2 * pieces + 1)) + both((groups, n, pieces)) + both((pieces,)) + both((n,)) + both((2, n)) + [dma, dma] + [dma((4,))],
         compiler_params=pltpu.CompilerParams(collective_id=cid, has_side_effects=True),
     )(packed, cot, rt)
-    return w.reshape(groups * n * sh, -1), gy, rt_all, rt_side
+    return w0.reshape(groups * n * sh, -1), w1, gy, rt_all, rt_side
 
 
 def swap_sections(value):
@@ -1405,9 +1584,6 @@
         axis=1,
     )
     packed = jnp.concatenate([w_query[0], key_weight[0], value_weight[0], w_out[0].T, aux], axis=1)
-    other = lax.ppermute(packed, "section", [(1, 0)])
-    second_shard = jnp.where(at_zero, other, packed)
-
     x0 = lax.dynamic_index_in_dim(inputs[:, 0], s, 0, keepdims=False)
     cot = lax.dynamic_index_in_dim(cotangent[:, 0], s, 0, keepdims=False)
     seg = lax.dynamic_index_in_dim(segment_ids[:, 0], s, 0, keepdims=False)
@@ -1426,33 +1602,31 @@
     def paired(z):
         return z.reshape((2, n) + z.shape[1:])
 
-    first_weights, gy1, rt_all, rt_theirs = open_up(1, packed, cot, rt)
+    first_weights, second_weights, gy1, rt_all, rt_theirs = open_up(1, packed, cot, rt)
     rt_tokens = (jnp.where(at_zero, rt_mine, rt_theirs), jnp.where(at_zero, rt_theirs, rt_mine))
     gy1, rt_all = flat(gy1), flat(rt_all)
 
-    qkv0, p0, o0, h0, b0, wrt0 = attn_fwd(x0, first_weights, cos, sin, meta, segr)
-    second_shard, b0 = lax.optimization_barrier((second_shard, b0))
-    second_weights = lax.all_gather(second_shard, ("group", "expert"), axis=0, tiled=True)
-    m0 = moe(0, "fwd", 2, e_pad, cap, b0, wg, wu, wd, rt=rt_all, wrt=wrt0)
-    x1 = (h0 + jnp.sum(m0.back.astype(F32), axis=0)).astype(BF)
-
-    qkv1, p1, o1, h1, b1, wrt1 = attn_fwd(x1, second_weights, cos, sin, meta, segr)
+    none = jnp.zeros((1, t, d), BF)
+    qkv0, p0, o0, h0, b0, wrt0, x0 = attn_fwd(x0, none, first_weights, cos, sin, meta, segr)
+    m0 = moe(0, "fwd", 2, e_pad, cap, b0, wg, wu, wd, rt=rt_all, wrt=wrt0, dense=second_weights)
+    second_weights = m0.dense_out.reshape(first_weights.shape)
+
+    qkv1, p1, o1, h1, b1, wrt1, x1 = attn_fwd(h0, m0.back, second_weights, cos, sin, meta, segr)
     m1 = moe(1, "both", 3, e_pad, cap, b1, wg, wu, wd, rt=rt_all, wrt=wrt1, gy=gy1)
-
-    crossed = lax.ppermute(m1.part0, "section", [(1, 0)])
 
     def gates_back(dg):
         dg = dg[:, :per].reshape(experts, t)
         return jnp.pad(dg, ((0, e_pad - experts), (0, 0)))
 
-    dx1, dd1 = attn_bwd(cot, h1, x1, second_weights, qkv1, p1, o1, b1, wrt1, m1.back, gates_back(m1.dgate), rt_tokens[1], cos, sin)
-    gy0 = dx1.astype(BF)
-
-    n0 = moe(0, "bwd", 4, e_pad, cap, gy0, wg, wu, wd, pos=m0.pos, gate=m0.gate, gp=m0.gp, up=m0.up, blocks=flat(m0.blocks))
-    dback0, crossed, straight = lax.optimization_barrier((n0.back, crossed, m1.part1))
-    back1 = lax.all_to_all(jnp.where(at_zero, crossed, straight), "expert", split_axis=0, concat_axis=0, tiled=True)
+    dx1, gy0, dqkv1, at1, dht1, daux1 = attn_bwd(False, cot, h1, x1, second_weights, qkv1, p1, o1, b1, wrt1, m1.back, gates_back(m1.dgate), rt_tokens[1], cos, sin)
+
+    n0 = moe(0, "bwd", 4, e_pad, cap, gy0, wg, wu, wd, pos=m0.pos, gate=m0.gate, gp=m0.gp, up=m0.up, blocks=flat(m0.blocks),
+             dqkv=dqkv1, at=at1, dht=dht1, daux=daux1, o=o1, part=m1.part0)
+    dd1 = n0.dd
+    dback0 = n0.back
+    back1 = lax.all_to_all(jnp.where(at_zero, n0.part_out, m1.part1), "expert", split_axis=0, concat_axis=0, tiled=True)
     y1 = (h1 + jnp.sum(back1.astype(F32), axis=0)).astype(BF)
-    dx0, dd0 = attn_bwd(gy0, h0, x0, first_weights, qkv0, p0, o0, b0, wrt0, dback0, gates_back(n0.dgate), rt_tokens[0], cos, sin)
+    dx0, _, dd0 = attn_bwd(True, gy0, h0, x0, first_weights, qkv0, p0, o0, b0, wrt0, dback0, gates_back(n0.dgate), rt_tokens[0], cos, sin)
 
     dense, gate_grad, up_grad, down = finish(5, dd0, dd1, (n0.even, n0.odd, n0.even_dn, n0.odd_dn), (m1.even, m1.odd, m1.even_dn, m1.odd_dn))
 

time: 784 us -> 726 us (0.926)
  Pallas kernels: 683 us -> 659 us
  between operations: 14.5 us -> 1.09 us
  starting transfers between devices: 24.9 us -> 13.8 us
  waiting for transfers between devices: 11.5 us -> 1.34 us
    pallas_call x3, Pallas kernels: 335 us -> 279 us  [moe(): pl.pallas_call(functools.partial(moe_kernel, layer, mode, n, e_pad, cap,...]
    pallas_call x1, Pallas kernels: 96.4 us -> 143 us  [open_up(): pl.pallas_call(functools.partial(open_kernel, n, groups, pieces), out_sha...]
    pallas_call x2, Pallas kernels: 48.9 us -> 36.5 us  [attn_bwd(): pl.pallas_call(functools.partial(attn_bwd_kernel, now, dg.shape[0]), out_...]
    all_gather x1 -> x0, waiting for transfers between devices: 9.92 us -> none  [local(): lax.all_gather(second_shard, ('group', 'expert'), axis=0, tiled=True)]
    all_to_all x1, starting transfers between devices: 12.7 us -> 4.69 us  [local(): lax.all_to_all(jnp.where(at_zero, n0.part_out, m1.part1), 'expert', split...]
  transfers between devices with their start and end apart: 6 -> 3, of which waited for: 2 -> 1; matrix products, arithmetic and copies ran while one was open for 3% -> 2% of each run, Pallas kernels for 72% -> 27%
where the time goes in v5:
time: 726 us; the launch traced here: 714 us
  Pallas kernels  659 us (91%)
  local copies, waits for them, and re-layouts  29.2 us (4%)
  starting transfers between devices  13.8 us (2%)
  other arithmetic  10 us (1%)
    pallas_call x3, Pallas kernels, moe(): pl.pallas_call(functools.partial(moe_kernel, layer, mode, n, e_pad, cap,...  279 us
    pallas_call x1, Pallas kernels, finish(): pl.pallas_call(functools.partial(finish_kernel, n), out_shape=(sds((rows,...  172 us
    pallas_call x1, Pallas kernels, open_up(): pl.pallas_call(functools.partial(open_kernel, n, groups, pieces), out_sha...  143 us
    pallas_call x2, Pallas kernels, attn_bwd(): pl.pallas_call(functools.partial(attn_bwd_kernel, now, dg.shape[0]), out_...  36.5 us
    pallas_call x2, Pallas kernels, attn_fwd(): pl.pallas_call(attn_fwd_kernel, out_shape=(sds((t, QKV), BF), sds((QUERY_...  28.1 us
  transfers between devices with their start and end apart: 3, of which 1 were waited for; matrix products, arithmetic and copies ran while one was open for 2% of the time, Pallas kernels for 27%

profile of v5, /device:TPU:0, one launch (start us, length us, event | category | flops | bytes accessed | tf_op | source)
XLA Modules:
  0.0 714.0 jit_solution(8295573226581249265)
XLA Ops:
  1.5 0.8 copy.50
  2.3 0.8 copy.49
  3.1 0.8 copy.48
  6.3 2.0 dynamic-slice_bitcast_fusion
  8.3 2.1 concatenate.31.w_ref
  10.4 142.9 %shard_map.238 = (bf16[16,96,4224]{2,1,0:T(8,128)(2,1)}, bf16[16,96,4224]{2,1,0:T(8,128)(2,1)}, bf16[2,4,128,1536]{3,2,1,0:T(8,128)(2,1)}, s32[2,4,8,128]{3,2,1,0:T(8,128)}, s32[8,128]{1,0:T(8,128)}) custom-call(bf16[96,4224]{1,0:T(8,128)(2,1)} %concatenate.31.w_ref, bf16[128,1536]{1,0:T(8,128)(2,1)} %get-tuple-element.172.cot_ref.gy_ref, s32[2,8,128]{2,1,0:T(8,128)} %bitcast.104), custom_call_target="tpu_custom_call" | custom-call | tf_op jit(solution)/shard_map/pallas_call | solution.py:1537
  153.9 0.8 broadcast_in_dim.45.back_ref
  154.6 13.8 %shard_map.239 = (bf16[128,2560]{1,0:T(8,128)(2,1)}, f32[24,128,128]{2,1,0:T(8,128)}, bf16[128,1536]{1,0:T(8,128)(2,1)}, f32[128,1536]{1,0:T(8,128)}, bf16[128,1...) custom-call(bf16[128,1536]{1,0:T(8,128)(2,1)} %get-tuple-element.173.below_ref, ...), custom_call_target="tpu_custom_call" | custom-call | flops 1610612736 | bytes 12976128 | tf_op jit(solution)/shard_map/pallas_call | solution.py:156
  168.5 93.3 %shard_map.240 = (bf16[4,128,1536]{2,1,0:T(8,128)(2,1)}, s32[8,8,128]{2,1,0:T(8,128)}, f32[8,8,128]{2,1,0:T(8,128)}, bf16[5,512,512]{2,1,0:T(8,128)(2,1)}, bf16[...) custom-call(bf16[128,1536]{1,0:T(8,128)(2,1)} %get-tuple-element.68., ...), custom_call_target="tpu_custom_call", output_to_operand_aliasing={{6}: (6, {})} | custom-call | tf_op jit(solution)/shard_map/pallas_call | solution.py:953
  261.8 14.3 %shard_map.241 = (bf16[128,2560]{1,0:T(8,128)(2,1)}, f32[24,128,128]{2,1,0:T(8,128)}, bf16[128,1536]{1,0:T(8,128)(2,1)}, f32[128,1536]{1,0:T(8,128)}, bf16[128,1...) custom-call(f32[128,1536]{1,0:T(8,128)} %get-tuple-element.67.below_ref.h_ref, ...), custom_call_target="tpu_custom_call" | custom-call | flops 1610612736 | bytes 12976128 | tf_op jit(solution)/shard_map/pallas_call | solution.py:156
  276.1 97.2 %shard_map.242 = (bf16[4,128,1536]{2,1,0:T(8,128)(2,1)}, f32[4,8,128]{2,1,0:T(8,128)}, bf16[2,2,5,384,512]{4,3,2,1,0:T(8,128)(2,1)}, bf16[2,2,5,384,512]{4,3,2,1...) custom-call(bf16[128,1536]{1,0:T(8,128)(2,1)} %get-tuple-element.79., ...), custom_call_target="tpu_custom_call" | custom-call | tf_op jit(solution)/shard_map/pallas_call | solution.py:953
  375.2 15.8 %shard_map.243 = (f32[128,1536]{1,0:T(8,128)}, bf16[128,1536]{1,0:T(8,128)(2,1)}, bf16[128,2560]{1,0:T(8,128)(2,1)}, bf16[1536,128]{1,0:T(8,128)(2,1)}, bf16[153...) custom-call(bf16[128,1536]{1,0:T(8,128)(2,1)} %get-tuple-element.172.cot_ref.gy_ref, f32[128,1536]{1,0:T(8,128)} %get-tuple-element.75.h_ref, ...), custom_call_target="tpu_custom_call" | custom-call | flops 3221225472 | bytes 25952256 | tf_op jit(solution)/shard_map/pallas_call | solution.py:313
  391.0 89.0 %shard_map.244 = (bf16[4,128,1536]{2,1,0:T(8,128)(2,1)}, f32[4,8,128]{2,1,0:T(8,128)}, bf16[2,2,5,384,512]{4,3,2,1,0:T(8,128)(2,1)}, bf16[2,2,5,384,512]{4,3,2,1...) custom-call(bf16[128,1536]{1,0:T(8,128)(2,1)} %get-tuple-element.85., ...), custom_call_target="tpu_custom_call" | custom-call | tf_op jit(solution)/shard_map/pallas_call | solution.py:953
  480.1 2.8 broadcast_select_fusion
  482.9 4.7 all-to-all-start
  488.2 20.7 %shard_map.245 = (f32[128,1536]{1,0:T(8,128)}, bf16[128,1536]{1,0:T(8,128)(2,1)}, bf16[1536,4224]{1,0:T(8,128)(2,1)}) custom-call(bf16[128,1536]{1,0:T(8,128)(2,1)} %get-tuple-element.85.refs_0_.gy_ref, f32[128,1536]{1,0:T(8,128)} %get-tuple-element.67.below_ref.h_ref, bf16[128,1536]{1,0:T(8,128)(2,1)} %get-tuple-element.98.x_ref, ...), custom_call_target="tpu_custom_call" | custom-call | flops 3221225472 | bytes 25952256 | tf_op jit(solution)/shard_map/pallas_call | solution.py:313
  508.9 2.2 select_bitcast_fusion
  511.1 7.1 collective-permute-start.1
  518.2 171.6 %shard_map.246 = (f32[96,4224]{1,0:T(8,128)}, f32[5,384,512]{2,1,0:T(8,128)}, f32[5,384,512]{2,1,0:T(8,128)}, f32[5,512,384]{2,1,0:T(8,128)}) custom-call(bf16[16,96,4224]{2,1,0:T(8,128)(2,1)} %bitcast.84, bf16[16,96,4224]{2,1,0:T(8,128)(2,1)} %bitcast.83, bf16[2,10,384,512]{3,2,1,0:T(8,128)(2,1)} %bitcast.87, bf16[2,10,384,512]{3,2,1,0:T(8,128)(2,1)} %bitcast.88, ...), custom_call_target="tpu_custom_call" | custom-call | tf_op jit(solution)/shard_map/pallas_call | solution.py:1322
  689.8 1.9 slice_bitcast_fusion.2
  691.6 2.3 slice_bitcast_fusion
  694.4 2.1 collective-permute-start
  696.5 0.8 slice_bitcast_fusion.4
  698.0 1.7 slice_reduce_fusion
  699.7 2.8 maximum_select_fusion
  702.5 1.3 collective-permute-done
  703.9 1.0 maximum_select_fusion.1
  704.9 2.0 copy.65
  706.9 1.5 copy-done.3
  708.4 2.0 copy.66
  710.4 1.5 copy-done.2
  711.9 1.9 copy.67
  (48 shorter events, 7.5 us)
Async XLA Ops:
  276.1 97.9 %copy-start.9 = (s32[1,2,1,128,8]{3,4,2,1,0:T(8,128)S(1)}, s32[1,2,1,128,8]{3,4,2,1,0:T(8,128)}, u32[]{:S(2)}) copy-start(s32[1,2,1,128,8]{3,4,2,1,0:T(8,128)} %param.19) | copy-start | bytes 24580
  276.1 97.9 %copy-start.11 = (s32[8,128]{1,0:T(8,128)S(1)}, s32[8,128]{1,0:T(8,128)}, u32[]{:S(2)}) copy-start(s32[8,128]{1,0:T(8,128)} %get-tuple-element.84) | copy-start | bytes 12292
  391.0 89.0 %copy-start.7 = (bf16[4,128,1536]{2,1,0:T(8,128)(2,1)S(1)}, bf16[4,128,1536]{2,1,0:T(8,128)(2,1)}, u32[]{:S(2)}) copy-start(bf16[4,128,1536]{2,1,0:T(8,128)(2,1)} %get-tuple-element.97) | copy-start | bytes 4718596
  482.9 4.7 copy-start.10
  482.9 211.1 %all-to-all-start = ((bf16[4,128,1536]{2,1,0:T(8,128)(2,1)}), bf16[4,128,1536]{2,1,0:T(8,128)(2,1)S(1)}, u32[]{:S(2)}, u32[]{:S(2)}) async-start(bf16[4,128,1536]{2,1,0:T(8,128)(2,1)} %broadcast_select_fusion), calls=%async_computation | async-start | bytes 3145728 | tf_op jit(solution)/shard_map/all_to_all | solution.py:1627
  488.2 20.7 %copy-start.8 = (f32[128,1536]{1,0:T(8,128)S(1)}, f32[128,1536]{1,0:T(8,128)}, u32[]{:S(2)}) copy-start(f32[128,1536]{1,0:T(8,128)} %get-tuple-element.105) | copy-start | bytes 2359300
  511.1 188.6 %collective-permute-start.1 = (f32[128,1536]{1,0:T(8,128)}, f32[128,1536]{1,0:T(8,128)}, u32[]{:S(2)}, u32[]{:S(2)}) collective-permute-start(f32[128,1536]{1,0:T(8,128)} %get-tuple-element.165), channel_id=1, source_target_pairs={{0,16},{16,0},{1,17},{17,1},{2,18},{18,2},{3,19},{19,3},{4,20},{20... | collective-permute-start | bytes 2359304 | tf_op jit(solution)/shard_map/ppermute | solution.py:1549
  689.7 4.5 copy-start.5
  689.7 4.5 copy-start.6
  694.4 9.4 %collective-permute-start = (bf16[128,1536]{1,0:T(8,128)(2,1)S(1)}, bf16[128,1536]{1,0:T(8,128)(2,1)S(1)}, u32[]{:S(2)}, u32[]{:S(2)}) collective-permute-start(bf16[128,1536]{1,0:T(8,128)(2,1)S(1)} %broadcast_select_fusion.2), channel_id=1, source_target_pairs={{0,16},{16,0},{1,17},{17,1},{2,18},{18,2},{3,19},{19,3},{4,20},{20... | collective-permute-start | bytes 1179656 | tf_op jit(solution)/shard_map/ppermute | solution.py:1549
  698.0 6.8 copy-start.4
  704.9 3.5 copy-start.3
  708.4 3.5 copy-start.2
  708.4 5.5 copy-start.1
  (1 other events, 0.0 us)

commit v6 on v5

--- a/solution.py
+++ b/solution.py
@@ -3,6 +3,7 @@
 
 import jax
 import jax.numpy as jnp
+import numpy as np
 from jax import lax
 from jax.experimental import pallas as pl
 from jax.experimental.pallas import tpu as pltpu
@@ -85,12 +86,13 @@
 
 
 def attn_fwd_kernel(
-    below_ref, back_ref, w_hbm, cos_ref, sin_ref, meta_ref, segr_ref,
+    below_ref, back_ref, w_hbm, cos_ref, sin_ref, seg_ref, live_ref,
     qkv_ref, p_ref, o_ref, h_ref, b_ref, wrt_ref, x_ref, w_ref, w_sem,
 ):
     t, d = x_ref.shape
     pieces = arriving(w_hbm, w_ref, w_sem, "forward")
-    entering = below_ref[...].astype(F32)
+    mine = lax.axis_index("section")
+    entering = (below_ref[mine] if len(below_ref.shape) == 3 else below_ref[...]).astype(F32)
     for z in range(back_ref.shape[0]):
         entering = entering + back_ref[z].astype(F32)
     x_ref[...] = entering.astype(BF)
@@ -111,7 +113,11 @@
             y = rope(y, cos, sin, 1.0)
         qkv_ref[:, cols] = y.astype(BF)
     i, j = iota((t, t), 0), iota((t, t), 1)
-    allowed = (j <= i) & (meta_ref[:, 0:1] == segr_ref[0:1, :]) & (j // BLK >= meta_ref[:, 1:2])
+    segments = jnp.broadcast_to(seg_ref[pl.ds(mine, 1), :].astype(F32), (t, t))
+    first_block = jnp.zeros((t, t), jnp.int32)
+    for block in range(t // BLK):
+        first_block = jnp.where(i // BLK == block, live_ref[mine, block], first_block)
+    allowed = (j <= i) & (jnp.transpose(segments) == segments) & (j // BLK >= first_block)
     masks = lane_masks(t)
 
     def pair(m, carry):
@@ -150,8 +156,8 @@
     return [pl.BlockSpec(memory_space=pltpu.VMEM)] * n
 
 
-def attn_fwd(below, back, w, cos, sin, meta, segr):
-    t, d = below.shape
+def attn_fwd(below, back, w, cos, sin, seg, live):
+    t, d = below.shape[-2:]
     sds = jax.ShapeDtypeStruct
     return pl.pallas_call(
         attn_fwd_kernel,
@@ -164,12 +170,12 @@
             sds((LANES, d), BF),
             sds((t, d), BF),
         ),
-        in_specs=vmem(2) + [any_spec()] + vmem(4),
+        in_specs=vmem(2) + [any_spec()] + vmem(3) + [pl.BlockSpec(memory_space=pltpu.SMEM)],
         out_specs=tuple(vmem(7)),
         scratch_shapes=[pltpu.VMEM(w.shape, BF), pltpu.SemaphoreType.DMA((1 + QKV // TILE + d // TILE,))],
         compiler_params=pltpu.CompilerParams(vmem_limit_bytes=VMEM_LIMIT),
         cost_estimate=pl.CostEstimate(flops=2 * t * d * 4096, bytes_accessed=w.size * 2, transcendentals=QUERY_HEADS * t * t),
-    )(below, back, w, cos, sin, meta, segr)
+    )(below, back, w, cos, sin, seg, live)
 
 
 def gates_of(rt, wrt, b, e_pad):
@@ -214,7 +220,8 @@
     r2 = lax.rsqrt(jnp.mean(h * h, axis=1, keepdims=True) + EPS)
     grad_moe = jnp.sum(db * h * r2, axis=0, keepdims=True)
     dn = db * gain_moe
-    dh = gy_ref[...].astype(F32) + r2 * dn - h * (r2 * r2 * r2) * jnp.mean(dn * h, axis=1, keepdims=True)
+    gy = gy_ref[lax.axis_index("section")] if len(gy_ref.shape) == 3 else gy_ref[...]
+    dh = gy.astype(F32) + r2 * dn - h * (r2 * r2 * r2) * jnp.mean(dn * h, axis=1, keepdims=True)
     dh_ref[...] = dh
     dhb = dh.astype(BF)
     for n in range(QW // TILE):
@@ -967,11 +974,11 @@
 
 
 def finish_kernel(
-    n, dd0, dd1, egu0, ogu0, ed0, od0, egu1, ogu1, ed1, od1,
-    dense_out, gate_out, up_out, down_out,
-    core_gu, core_dn, hop_gu, hop_dn, core_dd, hop_y, hop_z, hop_x, dd_buf, gu_buf, dn_buf, gu_f32, dn_f32,
+    n, dd0, dd1, dx0, dx1, egu0, ogu0, ed0, od0, egu1, ogu1, ed1, od1,
+    dense_out, dx_out, gate_out, up_out, down_out,
+    core_gu, core_dn, hop_gu, hop_dn, core_dd, hop_y, hop_z, hop_x, dd_buf, gu_buf, dn_buf, gu_res, dn_res,
     s_core_gu, r_core_gu, s_core_dn, r_core_dn, s_hop_gu, r_hop_gu, s_hop_dn, r_hop_dn,
-    s_core_dd, r_core_dd, s_y, r_y, s_z, r_z, s_x, r_x, l_dd, l_gu, l_dn, o_gu, o_dn,
+    s_core_dd, r_core_dd, s_y, r_y, s_z, r_z, s_x, r_x, l_dd, l_gu, l_dn, o_gu, o_dn, s_dx, r_dx,
 ):
     s, g, z = lax.axis_index("section"), lax.axis_index("group"), lax.axis_index("expert")
     pairs, cgu = core_gu.shape[:2]
@@ -1064,6 +1071,9 @@
 
     by_section(send_all)
 
+    def dx_copy(source):
+        return remote(src_ref=source, dst_ref=dx_out, send_sem=s_dx, recv_sem=r_dx, device_id=other)
+
     def load(buf, sem, slot, source):
         return pltpu.make_async_copy(source, buf.at[slot], sem.at[slot])
 
@@ -1181,11 +1191,19 @@
 
         stepped(steps, start, body)
 
+    @pl.when(s == 0)
+    def _():
+        dx_copy(dx1).start()
+
+    @pl.when(s != 0)
+    def _():
+        dx_copy(dx0).start()
+
     def gu_out_copy(c, slot, to=gate_out):
-        return pltpu.make_async_copy(gu_f32.at[slot], to.at[lax.rem(c, cgu // 2)], o_gu.at[slot])
+        return pltpu.make_async_copy(gu_res.at[slot], to.at[lax.rem(c, cgu // 2)], o_gu.at[slot])
 
     def dn_out_copy(c, slot):
-        return pltpu.make_async_copy(dn_f32.at[slot], down_out.at[c], o_dn.at[slot])
+        return pltpu.make_async_copy(dn_res.at[slot], down_out.at[c], o_dn.at[slot])
 
     def dense_sum(q):
         i = (pairs - 1 - q) * n + n - 1
@@ -1203,6 +1221,22 @@
         core_dd[1, i] = total.astype(BF)
         x_copy(top_bit(q), q, i).start()
 
+    def core_sent():
+        @pl.loop(0, units)
+        def _(i):
+            core_dd_copy(0, i, dd0).wait_send()
+            core_dd_copy(1, i, dd0).wait_send()
+
+        for q in range(pairs):
+
+            @pl.loop(0, cgu)
+            def _(c):
+                core_gu_copy(ogu0, q, c).wait_send()
+
+            @pl.loop(0, cdn)
+            def _(c):
+                core_dn_copy(od0, q, c).wait_send()
+
     steps = max(units, cgu, cdn)
 
     def start(i, slot):
@@ -1235,13 +1269,17 @@
             def _():
                 pass_on(q)
 
+        @pl.when(i == units - 2)
+        def _():
+            core_sent()
+
         @pl.when(i < cgu)
         def _():
             @pl.when(i >= 2)
             def _():
                 gu_out_copy(i - 2, slot).wait()
 
-            gu_f32[slot] = gu_sum(slot, 0, i)
+            gu_res[slot] = gu_sum(slot, 0, i).astype(BF)
 
             @pl.when(i < cgu // 2)
             def _():
@@ -1257,7 +1295,7 @@
             def _():
                 dn_out_copy(i - 2, slot).wait()
 
-            dn_f32[slot] = dn_sum(slot, 0, i)
+            dn_res[slot] = dn_sum(slot, 0, i).astype(BF)
             dn_out_copy(i, slot).start()
 
     stepped(steps, start, body)
@@ -1268,10 +1306,10 @@
     for c in (cdn - 2, cdn - 1):
         dn_out_copy(c, c % 2).wait()
 
+    dx_copy(dx0).wait()
+
     @pl.loop(0, units)
     def _(i):
-        core_dd_copy(0, i, dd0).wait_send()
-        core_dd_copy(1, i, dd0).wait_send()
         y_copy(i).wait_send()
         q, _ = unit(i)
         k = lax.rem(i, n) + 1
@@ -1280,24 +1318,19 @@
         def _():
             z_copy(q, k, i).wait_send()
 
-    for q in range(pairs):
-        if q:
-            x_copy(top_bit(q), q, (pairs - 1 - q) * n + n - 1).wait_send()
+    for q in range(1, pairs):
+        x_copy(top_bit(q), q, (pairs - 1 - q) * n + n - 1).wait_send()
 
         @pl.loop(0, cgu)
         def _(c):
-            core_gu_copy(ogu0, q, c).wait_send()
-            if q:
-                gu_hop(top_bit(q), q, c).wait_send()
+            gu_hop(top_bit(q), q, c).wait_send()
 
         @pl.loop(0, cdn)
         def _(c):
-            core_dn_copy(od0, q, c).wait_send()
-            if q:
-                dn_hop(top_bit(q), q, c).wait_send()
-
-
-def finish(cid, dd0, dd1, experts0, experts1):
+            dn_hop(top_bit(q), q, c).wait_send()
+
+
+def finish(cid, dd0, dd1, dx0, dx1, experts0, experts1):
     n, groups = lax.axis_size("expert"), lax.axis_size("group")
     pairs, levels = groups // 2, top_bit(groups // 2)
     width = dd0.shape[1]
@@ -1321,9 +1354,15 @@
 
     return pl.pallas_call(
         functools.partial(finish_kernel, n),
-        out_shape=(sds((rows, width), F32), sds((gu[0] // 2,) + gu[1:], F32), sds((gu[0] // 2,) + gu[1:], F32), sds(dn, F32)),
-        in_specs=[any_spec()] * 10,
-        out_specs=(pl.BlockSpec(memory_space=pltpu.VMEM), any_spec(), any_spec(), any_spec()),
+        out_shape=(
+            sds((rows, width), F32),
+            sds(dx0.shape, F32),
+            sds((gu[0] // 2,) + gu[1:], BF),
+            sds((gu[0] // 2,) + gu[1:], BF),
+            sds(dn, BF),
+        ),
+        in_specs=[any_spec()] * 12,
+        out_specs=tuple(vmem(1) + [any_spec()] * 4),
         scratch_shapes=[
             pltpu.VMEM((pairs,) + gu, BF),
             pltpu.VMEM((pairs,) + dn, BF),
@@ -1336,8 +1375,8 @@
             pltpu.VMEM((2, rows, width), BF),
             pltpu.VMEM((2,) + gu[1:], BF),
             pltpu.VMEM((2,) + dn[1:], BF),
-            pltpu.VMEM((2,) + gu[1:], F32),
-            pltpu.VMEM((2,) + dn[1:], F32),
+            pltpu.VMEM((2,) + gu[1:], BF),
+            pltpu.VMEM((2,) + dn[1:], BF),
         ]
         + both((pairs, gu[0]))
         + both((pairs, dn[0]))
@@ -1347,9 +1386,56 @@
         + both((units,))
         + both((n - 1, pairs))
         + both((levels, half))
-        + [dma((2,))] * 5,
+        + [dma((2,))] * 5
+        + [dma, dma],
         compiler_params=pltpu.CompilerParams(collective_id=cid, has_side_effects=True, vmem_limit_bytes=VMEM_LIMIT),
-    )(dd0, dd1, *experts0, *experts1)
+    )(dd0, dd1, dx0, dx1, *experts0, *experts1)
+
+
+def last_kernel(
+    experts, dense_ref, dx0_ref, dx1_ref, got_ref, gate_ref, up_ref, down_ref,
+    gate_out, up_out, down_out, q_out, k_out, v_out, o_out, router_out, attn_out, moe_out, dx_out,
+):
+    gate_out[...] = gate_ref[...].astype(F32)
+    up_out[...] = up_ref[...].astype(F32)
+    down_out[...] = down_ref[...].astype(F32)
+
+    @pl.when(pl.program_id(0) == 0)
+    def _():
+        s = lax.axis_index("section")
+        q_out[...] = dense_ref[:, 0:QW]
+        k_out[...] = dense_ref[:, QW : QW + KW]
+        v_out[...] = dense_ref[:, QW + KW : QKV]
+        o_out[...] = jnp.transpose(dense_ref[:, QKV : QKV + QW])
+        aux = dense_ref[:, QKV + QW :]
+        router_out[...] = aux[:, 0:experts]
+        aux_rows = jnp.transpose(aux)
+        moe_out[...] = aux_rows[GAIN_MOE_ROW : GAIN_MOE_ROW + 1]
+        attn_out[...] = aux_rows[GAIN_ATTN_ROW : GAIN_ATTN_ROW + 1]
+        dx_out[s] = jnp.where(s == 0, dx0_ref[...], dx1_ref[...])
+        dx_out[1 - s] = got_ref[...]
+
+
+def last(experts, dense, dx0, dx1, got, gate, up, down):
+    sh = dense.shape[0]
+    t, d = dx0.shape
+    per, piece, f = gate.shape
+    sds = jax.ShapeDtypeStruct
+
+    def whole(shape):
+        return pl.BlockSpec(shape, lambda j: (0,) * len(shape))
+
+    wide = pl.BlockSpec((1, piece, f), lambda j: (j, 0, 0))
+    tall = pl.BlockSpec((1, f, piece), lambda j: (j, 0, 0))
+    small = [(sh, QW), (sh, KW), (sh, KW), (QW, sh), (sh, experts), (1, sh), (1, sh), (2, t, d)]
+    return pl.pallas_call(
+        functools.partial(last_kernel, experts),
+        grid=(per,),
+        out_shape=tuple(sds(v.shape, F32) for v in (gate, up, down)) + tuple(sds(shape, F32) for shape in small),
+        in_specs=[whole(v.shape) for v in (dense, dx0, dx1, got)] + [wide, wide, tall],
+        out_specs=tuple([wide, wide, tall] + [whole(shape) for shape in small]),
+        compiler_params=pltpu.CompilerParams(vmem_limit_bytes=VMEM_LIMIT),
+    )(dense, dx0, dx1, got, gate, up, down)
 
 
 def low_bit(q):
@@ -1428,7 +1514,7 @@
 
     by_layer(lambda to: hop(0, to).start())
     launch(None, side)
-    own = [pltpu.make_async_copy(cot_ref, gy_out.at[s, z], local_sem.at[0])]
+    own = [pltpu.make_async_copy(cot_ref.at[s], gy_out.at[s, z], local_sem.at[0])]
     own += [pltpu.make_async_copy(rt_ref.at[m], rt_out.at[m, z], local_sem.at[1 + m]) for m in range(2)]
 
     def keep(to=w0_out):
@@ -1536,7 +1622,7 @@
 
     w0, w1, gy, rt_all, rt_side = pl.pallas_call(
         functools.partial(open_kernel, n, groups, pieces),
-        out_shape=(sds((groups * n,) + packed.shape, BF),) * 2 + (sds((2, n) + cot.shape, BF), sds((2, n) + rt.shape[1:], rt.dtype), sds(rt.shape[1:], rt.dtype)),
+        out_shape=(sds((groups * n,) + packed.shape, BF),) * 2 + (sds((2, n) + cot.shape[1:], BF), sds((2, n) + rt.shape[1:], rt.dtype), sds(rt.shape[1:], rt.dtype)),
         in_specs=vmem(3),
         out_specs=tuple([any_spec()] * 5),
         scratch_shapes=both((n, 2 * pieces + 1)) + both((n, 2 * pieces + 1)) + both((groups, n, pieces)) + both((pieces,)) + both((n,)) + both((2, n)) + [dma, dma] + [dma((4,))],
@@ -1551,10 +1637,10 @@
 
 def rope_tables(t):
     half = HEAD_SIZE // 2
-    frequency = THETA ** (-jnp.arange(half, dtype=F32) * 2.0 / HEAD_SIZE)
-    angles = jnp.arange(t, dtype=F32)[:, None] * frequency[None, :]
+    frequency = THETA ** (-np.arange(half) * 2.0 / HEAD_SIZE)
+    angles = np.arange(t)[:, None] * frequency[None, :]
     reps = LANES // half
-    return jnp.tile(jnp.cos(angles), (1, reps)), jnp.tile(jnp.sin(angles), (1, reps))
+    return (jnp.asarray(np.tile(f(angles), (1, reps)).astype(np.float32)) for f in (np.cos, np.sin))
 
 
 def local(
@@ -1584,13 +1670,7 @@
         axis=1,
     )
     packed = jnp.concatenate([w_query[0], key_weight[0], value_weight[0], w_out[0].T, aux], axis=1)
-    x0 = lax.dynamic_index_in_dim(inputs[:, 0], s, 0, keepdims=False)
-    cot = lax.dynamic_index_in_dim(cotangent[:, 0], s, 0, keepdims=False)
-    seg = lax.dynamic_index_in_dim(segment_ids[:, 0], s, 0, keepdims=False)
-    live = lax.dynamic_index_in_dim(live_first[:, 0], s, 0, keepdims=False)
-    meta = jnp.stack([seg, jnp.repeat(live, BLK)], axis=1)
-    meta = jnp.pad(meta, ((0, 0), (0, LANES - 2)))
-    segr = jnp.broadcast_to(seg[None, :], (8, t))
+    seg, live, cot = segment_ids[:, 0], live_first[:, 0], cotangent[:, 0]
     cos, sin = rope_tables(t)
 
     rt = jnp.swapaxes(routes[0, :, 0], 1, 2)
@@ -1607,11 +1687,11 @@
     gy1, rt_all = flat(gy1), flat(rt_all)
 
     none = jnp.zeros((1, t, d), BF)
-    qkv0, p0, o0, h0, b0, wrt0, x0 = attn_fwd(x0, none, first_weights, cos, sin, meta, segr)
+    qkv0, p0, o0, h0, b0, wrt0, x0 = attn_fwd(inputs[:, 0], none, first_weights, cos, sin, seg, live)
     m0 = moe(0, "fwd", 2, e_pad, cap, b0, wg, wu, wd, rt=rt_all, wrt=wrt0, dense=second_weights)
     second_weights = m0.dense_out.reshape(first_weights.shape)
 
-    qkv1, p1, o1, h1, b1, wrt1, x1 = attn_fwd(h0, m0.back, second_weights, cos, sin, meta, segr)
+    qkv1, p1, o1, h1, b1, wrt1, x1 = attn_fwd(h0, m0.back, second_weights, cos, sin, seg, live)
     m1 = moe(1, "both", 3, e_pad, cap, b1, wg, wu, wd, rt=rt_all, wrt=wrt1, gy=gy1)
 
     def gates_back(dg):
@@ -1625,31 +1705,28 @@
     dd1 = n0.dd
     dback0 = n0.back
     back1 = lax.all_to_all(jnp.where(at_zero, n0.part_out, m1.part1), "expert", split_axis=0, concat_axis=0, tiled=True)
-    y1 = (h1 + jnp.sum(back1.astype(F32), axis=0)).astype(BF)
     dx0, _, dd0 = attn_bwd(True, gy0, h0, x0, first_weights, qkv0, p0, o0, b0, wrt0, dback0, gates_back(n0.dgate), rt_tokens[0], cos, sin)
 
-    dense, gate_grad, up_grad, down = finish(5, dd0, dd1, (n0.even, n0.odd, n0.even_dn, n0.odd_dn), (m1.even, m1.odd, m1.even_dn, m1.odd_dn))
+    dense, got, *sums = finish(5, dd0, dd1, dx0, dx1, (n0.even, n0.odd, n0.even_dn, n0.odd_dn), (m1.even, m1.odd, m1.even_dn, m1.odd_dn))
+    dense, late = lax.optimization_barrier((dense, h1))
+    y1 = (late + jnp.sum(back1.astype(F32), axis=0)).astype(BF)
 
     kept_out = jnp.where(at_zero, x1, y1)
     swapped_out = swap_sections(jnp.where(at_zero, y1, x1))
     layer_out = jnp.where(at_zero, jnp.stack([kept_out, swapped_out]), jnp.stack([swapped_out, kept_out]))
-    kept_in = jnp.where(at_zero, dx0, dx1)
-    swapped_in = swap_sections(jnp.where(at_zero, dx1, dx0))
-    input_grad = jnp.where(at_zero, jnp.stack([kept_in, swapped_in]), jnp.stack([swapped_in, kept_in]))
-
+    gate_grad, up_grad, down_grad, *dense_grads, router_grad, attn_grad, moe_grad, input_grad = last(
+        experts, dense, dx0, dx1, got, *sums
+    )
     return (
         layer_out[None, :, None],
         input_grad[None, :, None],
-        dense[:, QKV + QW + GAIN_ATTN_ROW][None],
-        dense[:, QKV + QW + GAIN_MOE_ROW][None],
-        dense[None, :, 0:QW],
-        dense[None, :, QW : QW + KW],
-        dense[None, :, QW + KW : QKV],
-        dense[:, QKV : QKV + QW].T[None],
-        dense[None, :, QKV + QW : QKV + QW + experts],
+        attn_grad,
+        moe_grad,
+        *(v[None] for v in dense_grads),
+        router_grad[None],
         gate_grad[None],
         up_grad[None],
-        down[None],
+        down_grad[None],
     )
 
 

time: 726 us -> 701 us (0.966)
  local copies, waits for them, and re-layouts: 29.2 us -> 10.9 us
  Pallas kernels: 659 us -> 673 us
  starting transfers between devices: 13.8 us -> 4.63 us
    pallas_call x0 -> x1, Pallas kernels: none -> 10.3 us  [last(): pl.pallas_call(functools.partial(last_kernel, experts), grid=(per,), out_...]
    ppermute x2 -> x1, starting transfers between devices: 9.14 us -> 0.07 us  [swap_sections(): return lax.ppermute(value, 'section', [(0, 1), (1, 0)])]
  transfers between devices with their start and end apart: 3 -> 2, of which waited for: 1 -> 0; matrix products, arithmetic and copies ran while one was open for 2% -> 1% of each run, Pallas kernels for 27% -> 30%
where the time goes in v6:
time: 701 us; the launch traced here: 694 us
  Pallas kernels  673 us (96%)
  local copies, waits for them, and re-layouts  10.9 us (2%)
    pallas_call x3, Pallas kernels, moe(): pl.pallas_call(functools.partial(moe_kernel, layer, mode, n, e_pad, cap,...  281 us
    pallas_call x1, Pallas kernels, finish(): pl.pallas_call(functools.partial(finish_kernel, n), out_shape=(sds((rows,...  175 us
    pallas_call x1, Pallas kernels, open_up(): pl.pallas_call(functools.partial(open_kernel, n, groups, pieces), out_sha...  141 us
    pallas_call x2, Pallas kernels, attn_bwd(): pl.pallas_call(functools.partial(attn_bwd_kernel, now, dg.shape[0]), out_...  36.8 us
    pallas_call x2, Pallas kernels, attn_fwd(): pl.pallas_call(attn_fwd_kernel, out_shape=(sds((t, QKV), BF), sds((QUERY_...  28.3 us
  transfers between devices with their start and end apart: 2, of which 0 were waited for; matrix products, arithmetic and copies ran while one was open for 1% of the time, Pallas kernels for 30%

profile of v6, /device:TPU:0, one launch (start us, length us, event | category | flops | bytes accessed | tf_op | source)
XLA Modules:
  0.0 694.4 jit_solution(10913443644893710739)
XLA Ops:
  0.6 0.8 copy.38
  1.4 0.8 copy.37
  2.2 0.8 copy.36
  3.0 2.1 concatenate.17.w_ref
  5.1 141.3 %shard_map.256 = (bf16[16,96,4224]{2,1,0:T(8,128)(2,1)}, bf16[16,96,4224]{2,1,0:T(8,128)(2,1)}, bf16[2,4,128,1536]{3,2,1,0:T(8,128)(2,1)}, s32[2,4,8,128]{3,2,1,0:T(8,128)}, s32[8,128]{1,0:T(8,128)}) custom-call(bf16[96,4224]{1,0:T(8,128)(2,1)} %concatenate.17.w_ref, bf16[2,128,1536]{2,1,0:T(8,128)(2,1)} %bitcast.72, s32[2,8,128]{2,1,0:T(8,128)} %bitcast.87), custom_call_target="tpu_custom_call" | custom-call | tf_op jit(solution)/shard_map/pallas_call | solution.py:1623
  146.3 0.8 broadcast_in_dim.34.back_ref
  147.1 14.0 %shard_map.257 = (bf16[128,2560]{1,0:T(8,128)(2,1)}, f32[24,128,128]{2,1,0:T(8,128)}, bf16[128,1536]{1,0:T(8,128)(2,1)}, f32[128,1536]{1,0:T(8,128)}, bf16[128,1...) custom-call(bf16[2,128,1536]{2,1,0:T(8,128)(2,1)} %bitcast.77, ...), custom_call_target="tpu_custom_call" | custom-call | flops 1610612736 | bytes 12976128 | tf_op jit(solution)/shard_map/pallas_call | solution.py:162
  161.1 94.4 %shard_map.258 = (bf16[4,128,1536]{2,1,0:T(8,128)(2,1)}, s32[8,8,128]{2,1,0:T(8,128)}, f32[8,8,128]{2,1,0:T(8,128)}, bf16[5,512,512]{2,1,0:T(8,128)(2,1)}, bf16[...) custom-call(bf16[128,1536]{1,0:T(8,128)(2,1)} %get-tuple-element.82., ...), custom_call_target="tpu_custom_call", output_to_operand_aliasing={{6}: (6, {})} | custom-call | tf_op jit(solution)/shard_map/pallas_call | solution.py:960
  255.6 14.3 %shard_map.259 = (bf16[128,2560]{1,0:T(8,128)(2,1)}, f32[24,128,128]{2,1,0:T(8,128)}, bf16[128,1536]{1,0:T(8,128)(2,1)}, f32[128,1536]{1,0:T(8,128)}, bf16[128,1...) custom-call(f32[128,1536]{1,0:T(8,128)} %get-tuple-element.81.below_ref.h_ref, ...), custom_call_target="tpu_custom_call" | custom-call | flops 1610612736 | bytes 12976128 | tf_op jit(solution)/shard_map/pallas_call | solution.py:162
  269.9 0.0 copy-start.3
  269.9 97.7 %shard_map.260 = (bf16[4,128,1536]{2,1,0:T(8,128)(2,1)}, f32[4,8,128]{2,1,0:T(8,128)}, bf16[2,2,5,384,512]{4,3,2,1,0:T(8,128)(2,1)}, bf16[2,2,5,384,512]{4,3,2,1...) custom-call(bf16[128,1536]{1,0:T(8,128)(2,1)} %get-tuple-element.93., ...), custom_call_target="tpu_custom_call" | custom-call | tf_op jit(solution)/shard_map/pallas_call | solution.py:960
  367.6 0.7 reshape.129
  368.3 0.6 pad.7.dg_ref
  369.0 0.0 copy-done.5
  369.0 0.6 bitcast_select_fusion
  369.6 16.0 %shard_map.261 = (f32[128,1536]{1,0:T(8,128)}, bf16[128,1536]{1,0:T(8,128)(2,1)}, bf16[128,2560]{1,0:T(8,128)(2,1)}, bf16[1536,128]{1,0:T(8,128)(2,1)}, bf16[153...) custom-call(bf16[2,128,1536]{2,1,0:T(8,128)(2,1)} %bitcast.73, f32[128,1536]{1,0:T(8,128)} %get-tuple-element.129.h_ref, ...), custom_call_target="tpu_custom_call" | custom-call | flops 3221225472 | bytes 25952256 | tf_op jit(solution)/shard_map/pallas_call | solution.py:320
  385.6 88.8 %shard_map.262 = (bf16[4,128,1536]{2,1,0:T(8,128)(2,1)}, f32[4,8,128]{2,1,0:T(8,128)}, bf16[2,2,5,384,512]{4,3,2,1,0:T(8,128)(2,1)}, bf16[2,2,5,384,512]{4,3,2,1...) custom-call(bf16[128,1536]{1,0:T(8,128)(2,1)} %get-tuple-element.99., ...), custom_call_target="tpu_custom_call" | custom-call | tf_op jit(solution)/shard_map/pallas_call | solution.py:960
  474.5 2.7 broadcast_select_fusion
  477.2 4.6 all-to-all-start
  481.8 0.6 pad.8.dg_ref
  482.4 20.7 %shard_map.263 = (f32[128,1536]{1,0:T(8,128)}, bf16[128,1536]{1,0:T(8,128)(2,1)}, bf16[1536,4224]{1,0:T(8,128)(2,1)}) custom-call(bf16[128,1536]{1,0:T(8,128)(2,1)} %get-tuple-element.99.refs_0_.gy_ref, f32[128,1536]{1,0:T(8,128)} %get-tuple-element.81.below_ref.h_ref, bf16[128,1536]{1,0:T(8,128)(2,1)} %get-tuple-element.100.x_ref, ...), custom_call_target="tpu_custom_call" | custom-call | flops 3221225472 | bytes 25952256 | tf_op jit(solution)/shard_map/pallas_call | solution.py:320
  503.1 0.0 copy-start.1
  503.2 175.5 %shard_map.264 = (f32[96,4224]{1,0:T(8,128)}, f32[128,1536]{1,0:T(8,128)}, bf16[5,384,512]{2,1,0:T(8,128)(2,1)}, bf16[5,384,512]{2,1,0:T(8,128)(2,1)}, bf16[5,512,384]{2,1,0:T(8,128)(2,1)}) custom-call(bf16[16,96,4224]{2,1,0:T(8,128)(2,1)} %bitcast.67, bf16[16,96,4224]{2,1,0:T(8,128)(2,1)} %bitcast.66, f32[128,1536]{1,0:T(8,128)} %get-tuple-element.118.dx0.dx0_ref, ...), custom_call_target="tpu_custom_call" | custom-call | tf_op jit(solution)/shard_map/pallas_call | solution.py:1355
  678.7 0.0 all-to-all-done
  678.7 0.2 convert_reduce_fusion
  678.9 0.2 select_bitcast_fusion
  679.1 0.1 collective-permute-start
  679.2 10.3 %shard_map.265 = (f32[5,384,512]{2,1,0:T(8,128)}, f32[5,384,512]{2,1,0:T(8,128)}, f32[5,512,384]{2,1,0:T(8,128)}, f32[96,1536]{1,0:T(8,128)}, f32[96,512]{1,0:T(...) custom-call(f32[96,4224]{1,0:T(8,128)} %get-tuple-element.132.dense_, ...), custom_call_target="tpu_custom_call" | custom-call | tf_op jit(solution)/shard_map/pallas_call | solution.py:1431
  689.5 1.5 copy.41
  691.0 2.2 copy.40
  693.2 0.0 collective-permute-done
  693.2 1.0 maximum_select_fusion
  (12 shorter events, 0.1 us)
Async XLA Ops:
  269.9 99.1 %copy-start.3 = (s32[1,2,1,128,8]{3,4,2,1,0:T(8,128)S(1)}, s32[1,2,1,128,8]{3,4,2,1,0:T(8,128)}, u32[]{:S(2)}) copy-start(s32[1,2,1,128,8]{3,4,2,1,0:T(8,128)} %param.21) | copy-start | bytes 24580
  269.9 99.1 %copy-start.5 = (s32[8,128]{1,0:T(8,128)S(1)}, s32[8,128]{1,0:T(8,128)}, u32[]{:S(2)}) copy-start(s32[8,128]{1,0:T(8,128)} %get-tuple-element.98) | copy-start | bytes 12292
  385.6 88.8 %copy-start.2 = (bf16[4,128,1536]{2,1,0:T(8,128)(2,1)S(1)}, bf16[4,128,1536]{2,1,0:T(8,128)(2,1)}, u32[]{:S(2)}) copy-start(bf16[4,128,1536]{2,1,0:T(8,128)(2,1)} %get-tuple-element.131) | copy-start | bytes 4718596
  474.5 7.3 %copy-start.4 = (f32[4,8,128]{2,1,0:T(8,128)S(1)}, f32[4,8,128]{2,1,0:T(8,128)}, u32[]{:S(2)}) copy-start(f32[4,8,128]{2,1,0:T(8,128)} %get-tuple-element.115) | copy-start | bytes 49156
  477.2 201.5 %all-to-all-start = ((bf16[4,128,1536]{2,1,0:T(8,128)(2,1)}), bf16[4,128,1536]{2,1,0:T(8,128)(2,1)S(1)}, u32[]{:S(2)}, u32[]{:S(2)}) async-start(bf16[4,128,1536]{2,1,0:T(8,128)(2,1)} %broadcast_select_fusion), calls=%async_computation | async-start | bytes 3145728 | tf_op jit(solution)/shard_map/all_to_all | solution.py:1707
  503.1 175.8 %copy-start = (bf16[128,1536]{1,0:T(8,128)(2,1)S(1)}, bf16[128,1536]{1,0:T(8,128)(2,1)}, u32[]{:S(2)}) copy-start(bf16[128,1536]{1,0:T(8,128)(2,1)} %get-tuple-element.88.x_ref) | copy-start | bytes 1179652
  503.1 175.8 %copy-start.1 = (f32[128,1536]{1,0:T(8,128)S(1)}, f32[128,1536]{1,0:T(8,128)}, u32[]{:S(2)}) copy-start(f32[128,1536]{1,0:T(8,128)} %get-tuple-element.129.h_ref) | copy-start | bytes 2359300
  679.1 14.1 %collective-permute-start = (bf16[128,1536]{1,0:T(8,128)(2,1)S(1)}, bf16[128,1536]{1,0:T(8,128)(2,1)S(1)}, u32[]{:S(2)}, u32[]{:S(2)}) collective-permute-start(bf16[128,1536]{1,0:T(8,128)(2,1)S(1)} %broadcast_select_fusion.1), channel_id=1, source_target_pairs={{0,16},{16,0},{1,17},{17,1},{2,18},{18,2},{3,19},{19,3},{4,20},{20... | collective-permute-start | bytes 1179656 | tf_op jit(solution)/shard_map/ppermute | solution.py:1635

commit v7 on v6

--- a/solution.py
+++ b/solution.py
@@ -86,14 +86,18 @@
 
 
 def attn_fwd_kernel(
-    below_ref, back_ref, w_hbm, cos_ref, sin_ref, seg_ref, live_ref,
-    qkv_ref, p_ref, o_ref, h_ref, b_ref, wrt_ref, x_ref, w_ref, w_sem,
+    blocks, below_ref, *refs,
 ):
+    back_ref = refs[0] if blocks else None
+    (
+        w_hbm, cos_ref, sin_ref, seg_ref, live_ref,
+        qkv_ref, p_ref, o_ref, h_ref, b_ref, wrt_ref, x_ref, w_ref, w_sem,
+    ) = refs[1 if blocks else 0 :]
     t, d = x_ref.shape
     pieces = arriving(w_hbm, w_ref, w_sem, "forward")
     mine = lax.axis_index("section")
     entering = (below_ref[mine] if len(below_ref.shape) == 3 else below_ref[...]).astype(F32)
-    for z in range(back_ref.shape[0]):
+    for z in range(blocks):
         entering = entering + back_ref[z].astype(F32)
     x_ref[...] = entering.astype(BF)
     pieces.pop(0).wait()
@@ -127,18 +131,21 @@
         kp = qkv_ref[:, lanes(QW + m * LANES)]
         vp = qkv_ref[:, lanes(QW + KW + m * LANES)]
         ks, vs = swapped(kp), swapped(vp)
-        parts = {}
-        for r, half, swap in head_plan():
+        plan = head_plan()
+        scores = []
+        for r, half, swap in plan:
             q = pick(qkv_ref[:, lanes((m * TILES_PER_PAIR + r) * LANES)], half, masks)
             s = dot(q, ks if swap else kp, 1, 1) * HEAD_SIZE ** (-0.5)
-            s = jnp.where(allowed, s, NEG_FILL)
-            e = jnp.exp(s - jnp.max(s, axis=1, keepdims=True))
-            p = e * (1.0 / jnp.sum(e, axis=1, keepdims=True))
+            scores.append(jnp.where(allowed, s, NEG_FILL))
+        tops = [jnp.max(s, axis=1, keepdims=True) for s in scores]
+        exps = [jnp.exp(s - top) for s, top in zip(scores, tops)]
+        sums = [1.0 / jnp.sum(e, axis=1, keepdims=True) for e in exps]
+        probs = [e * u for e, u in zip(exps, sums)]
+        for (r, half, swap), p in zip(plan, probs):
             p_ref[m * 2 * TILES_PER_PAIR + 2 * r + half] = p
-            part = dot(p.astype(BF), pick(vs if swap else vp, half, masks))
-            parts[half] = part
-            if half == 1:
-                o_ref[:, lanes((m * TILES_PER_PAIR + r) * LANES)] = (parts[0] + parts[1]).astype(BF)
+        parts = [dot(p.astype(BF), pick(vs if swap else vp, half, masks)) for (r, half, swap), p in zip(plan, probs)]
+        for r in range(TILES_PER_PAIR):
+            o_ref[:, lanes((m * TILES_PER_PAIR + r) * LANES)] = (parts[2 * r] + parts[2 * r + 1]).astype(BF)
         return carry
 
     lax.fori_loop(0, HEAD_PAIRS, pair, 0)
@@ -160,7 +167,7 @@
     t, d = below.shape[-2:]
     sds = jax.ShapeDtypeStruct
     return pl.pallas_call(
-        attn_fwd_kernel,
+        functools.partial(attn_fwd_kernel, len(back)),
         out_shape=(
             sds((t, QKV), BF),
             sds((QUERY_HEADS, t, t), F32),
@@ -170,12 +177,12 @@
             sds((LANES, d), BF),
             sds((t, d), BF),
         ),
-        in_specs=vmem(2) + [any_spec()] + vmem(3) + [pl.BlockSpec(memory_space=pltpu.SMEM)],
+        in_specs=vmem(2 if len(back) else 1) + [any_spec()] + vmem(3) + [pl.BlockSpec(memory_space=pltpu.SMEM)],
         out_specs=tuple(vmem(7)),
         scratch_shapes=[pltpu.VMEM(w.shape, BF), pltpu.SemaphoreType.DMA((1 + QKV // TILE + d // TILE,))],
         compiler_params=pltpu.CompilerParams(vmem_limit_bytes=VMEM_LIMIT),
         cost_estimate=pl.CostEstimate(flops=2 * t * d * 4096, bytes_accessed=w.size * 2, transcendentals=QUERY_HEADS * t * t),
-    )(below, back, w, cos, sin, seg, live)
+    )(below, *((back,) if len(back) else ()), w, cos, sin, seg, live)
 
 
 def gates_of(rt, wrt, b, e_pad):
@@ -190,7 +197,7 @@
 
 
 def attn_bwd_kernel(
-    now, e_pad, gy_ref, h_ref, x_ref, w_hbm, qkv_ref, p_ref, o_ref, b_ref, wrt_ref, back_ref, dg_ref, rt_ref, cos_ref, sin_ref,
+    layer, now, e_pad, e_real, gy_ref, h_ref, x_ref, w_hbm, qkv_ref, p_ref, o_ref, b_ref, wrt_ref, back_ref, dg_ref, rt_ref, side_ref, cos_ref, sin_ref,
     dx_ref, dxb_ref, *rest,
 ):
     t, d = x_ref.shape
@@ -209,8 +216,13 @@
     gain_attn = wrt_ref[GAIN_ATTN_ROW - 7 :, :].astype(F32)[7:8]
     gain_moe = wrt_ref[GAIN_ATTN_ROW - 7 :, :].astype(F32)[6:7]
     b = b_ref[...]
-    gates = gates_of(rt_ref[...], wrt_ref, b, e_pad)
-    dg = dg_ref[...]
+    mine = lax.axis_index("section")
+    gates = gates_of(jnp.where(mine == layer, rt_ref[mine], side_ref[...]), wrt_ref, b, e_pad)
+    per = e_real // dg_ref.shape[0]
+    dg = [dg_ref[z][0:per] for z in range(dg_ref.shape[0])]
+    if e_pad > e_real:
+        dg.append(jnp.zeros((e_pad - e_real, t), F32))
+    dg = jnp.concatenate(dg, axis=0)
     dl = (gates * (dg - jnp.sum(gates * dg, axis=0, keepdims=True)))
     dlb = dl.astype(BF)
     db = dot(dlb, wrt_ref[0:e_pad, :], 0, 0)
@@ -238,24 +250,23 @@
         kp = qkv_ref[:, lanes(QW + m * LANES)]
         vp = qkv_ref[:, lanes(QW + KW + m * LANES)]
         ks, vs = swapped(kp), swapped(vp)
-        zero = jnp.zeros((t, LANES), F32)
-        dk = {False: zero, True: zero}
-        dv = {False: zero, True: zero}
-        dq = zero
-        for r, half, swap in head_plan():
-            tile = lanes((m * TILES_PER_PAIR + r) * LANES)
-            q = pick(qkv_ref[:, tile], half, masks)
-            do = pick(do_ref[:, tile], half, masks)
-            p = p_ref[m * 2 * TILES_PER_PAIR + 2 * r + half]
-            dp = dot(do, vs if swap else vp, 1, 1)
-            dv[swap] = dv[swap] + dot(p.astype(BF), do, 0, 0)
-            dt = p * (dp - jnp.sum(p * dp, axis=1, keepdims=True)) * HEAD_SIZE ** (-0.5)
-            dt = dt.astype(BF)
-            dk[swap] = dk[swap] + dot(dt, q, 0, 0)
-            part = dot(dt, pick(ks if swap else kp, half, masks))
-            dq = part if half == 0 else dq + part
-            if half == 1:
-                dqkv_ref[:, tile] = rope(dq, cos, sin, -1.0).astype(BF)
+        plan = head_plan()
+        tiles = [lanes((m * TILES_PER_PAIR + r) * LANES) for r in range(TILES_PER_PAIR)]
+        qs = [pick(qkv_ref[:, tiles[r]], half, masks) for r, half, _ in plan]
+        dos = [pick(do_ref[:, tiles[r]], half, masks) for r, half, _ in plan]
+        ps = [p_ref[m * 2 * TILES_PER_PAIR + 2 * r + half] for r, half, _ in plan]
+        dps = [dot(do, vs if swap else vp, 1, 1) for do, (_, _, swap) in zip(dos, plan)]
+        dvs = [dot(p.astype(BF), do, 0, 0) for p, do in zip(ps, dos)]
+        sums = [jnp.sum(p * dp, axis=1, keepdims=True) for p, dp in zip(ps, dps)]
+        dts = [(p * (dp - total) * HEAD_SIZE ** (-0.5)).astype(BF) for p, dp, total in zip(ps, dps, sums)]
+        dks = [dot(dt, q, 0, 0) for dt, q in zip(dts, qs)]
+        dqs = [dot(dt, pick(ks if swap else kp, half, masks)) for dt, (_, half, swap) in zip(dts, plan)]
+        for r in range(TILES_PER_PAIR):
+            dqkv_ref[:, tiles[r]] = rope(dqs[2 * r] + dqs[2 * r + 1], cos, sin, -1.0).astype(BF)
+        dk, dv = (
+            {way: functools.reduce(jnp.add, [v for v, (_, _, swap) in zip(vals, plan) if swap == way]) for way in (False, True)}
+            for vals in (dks, dvs)
+        )
         dk_all = dk[False] + pltpu.roll(dk[True], HEAD_SIZE, 1)
         dv_all = dv[False] + pltpu.roll(dv[True], HEAD_SIZE, 1)
         dqkv_ref[:, lanes(QW + m * LANES)] = rope(dk_all, cos, sin, -1.0).astype(BF)
@@ -303,7 +314,7 @@
         c.wait()
 
 
-def attn_bwd(now, gy, h, x, w, qkv, p, o, b, wrt, back, dg, rt, cos, sin):
+def attn_bwd(layer, now, experts, gy, h, x, w, qkv, p, o, b, wrt, back, dg, rt, side, cos, sin):
     t, d = x.shape
     sds = jax.ShapeDtypeStruct
     dma = pltpu.SemaphoreType.DMA
@@ -318,14 +329,14 @@
     if now:
         scratch += [pltpu.VMEM((d, t), BF), pltpu.VMEM(w.shape, BF), dma((1 + QKV // TILE + QW // TILE,))]
     return pl.pallas_call(
-        functools.partial(attn_bwd_kernel, now, dg.shape[0]),
+        functools.partial(attn_bwd_kernel, layer, now, -(-experts // 16) * 16, experts),
         out_shape=tuple(outs),
-        in_specs=vmem(3) + [any_spec()] + vmem(10),
+        in_specs=vmem(3) + [any_spec()] + vmem(11),
         out_specs=tuple(vmem(2) + [any_spec()] if now else vmem(6)),
         scratch_shapes=scratch,
         compiler_params=pltpu.CompilerParams(vmem_limit_bytes=VMEM_LIMIT),
         cost_estimate=pl.CostEstimate(flops=4 * t * d * 4096, bytes_accessed=w.size * 4, transcendentals=0),
-    )(gy, h, x, w, qkv, p, o, b, wrt, back, dg, rt, cos, sin)
+    )(gy, h, x, w, qkv, p, o, b, wrt, back, dg, rt, side, cos, sin)
 
 
 def one_hot(pos_row, cap):
@@ -509,8 +520,8 @@
             device_id={"group": lax.bitwise_xor(g, 1 << b)},
         )
 
-    def ride():
-        for b in reversed(range(bits)):
+    def ride(bs):
+        for b in bs:
             for zz in range(n):
                 over(0, b, zz).start()
 
@@ -522,7 +533,7 @@
                     over(q, b, zz).start()
 
     if riding:
-        ride()
+        ride(reversed(range(1, bits)))
 
     def half(i):
         section = jnp.where(i < per, layer, 1 - layer)
@@ -686,6 +697,9 @@
                 cross(z + t).wait_recv()
 
             prepare_at(1 - layer, t)
+
+    if riding:
+        ride((0,))
 
     def over_part(zz):
         return remote(
@@ -1356,7 +1370,7 @@
         functools.partial(finish_kernel, n),
         out_shape=(
             sds((rows, width), F32),
-            sds(dx0.shape, F32),
+            sds(dx0.shape, dx0.dtype),
             sds((gu[0] // 2,) + gu[1:], BF),
             sds((gu[0] // 2,) + gu[1:], BF),
             sds(dn, BF),
@@ -1406,14 +1420,13 @@
         q_out[...] = dense_ref[:, 0:QW]
         k_out[...] = dense_ref[:, QW : QW + KW]
         v_out[...] = dense_ref[:, QW + KW : QKV]
-        o_out[...] = jnp.transpose(dense_ref[:, QKV : QKV + QW])
-        aux = dense_ref[:, QKV + QW :]
-        router_out[...] = aux[:, 0:experts]
-        aux_rows = jnp.transpose(aux)
+        o_out[...] = dense_ref[:, QKV : QKV + QW]
+        aux_rows = jnp.transpose(dense_ref[:, QKV + QW :])
+        router_out[...] = aux_rows[0:experts]
         moe_out[...] = aux_rows[GAIN_MOE_ROW : GAIN_MOE_ROW + 1]
         attn_out[...] = aux_rows[GAIN_ATTN_ROW : GAIN_ATTN_ROW + 1]
         dx_out[s] = jnp.where(s == 0, dx0_ref[...], dx1_ref[...])
-        dx_out[1 - s] = got_ref[...]
+        dx_out[1 - s] = got_ref[...].astype(F32)
 
 
 def last(experts, dense, dx0, dx1, got, gate, up, down):
@@ -1427,7 +1440,7 @@
 
     wide = pl.BlockSpec((1, piece, f), lambda j: (j, 0, 0))
     tall = pl.BlockSpec((1, f, piece), lambda j: (j, 0, 0))
-    small = [(sh, QW), (sh, KW), (sh, KW), (QW, sh), (sh, experts), (1, sh), (1, sh), (2, t, d)]
+    small = [(sh, QW), (sh, KW), (sh, KW), (sh, QW), (experts, sh), (1, sh), (1, sh), (2, t, d)]
     return pl.pallas_call(
         functools.partial(last_kernel, experts),
         grid=(per,),
@@ -1443,14 +1456,22 @@
 
 
 def open_kernel(
-    n, groups, pieces, w_ref, cot_ref, rt_ref, w0_out, w1_out, gy_out, rt_out, rt_side,
-    s_right, r_right, s_left, r_left, s_group, r_group, s_y, r_y, s_cross, r_cross, s_rt, r_rt, s_side, r_side, local_sem,
+    n, groups, pieces, wq_ref, wk_ref, wv_ref, wo_ref, wr_ref, ga_ref, gm_ref, cot_ref, rt_ref, w0_out, w1_out, gy_out, rt_out, rt_side,
+    w_ref, s_right, r_right, s_left, r_left, s_group, r_group, s_y, r_y, s_cross, r_cross, s_rt, r_rt, s_side, r_side, local_sem,
 ):
     s, g, z = lax.axis_index("section"), lax.axis_index("group"), lax.axis_index("expert")
     remote = functools.partial(pltpu.make_async_remote_copy, device_id_type=MESH)
     rows = w_ref.shape[0] // pieces
     bits = top_bit(groups)
     other = {"section": 1 - s}
+    w_ref[:, 0:QW] = wq_ref[...]
+    w_ref[:, QW : QW + KW] = wk_ref[...]
+    w_ref[:, QW + KW : QKV] = wv_ref[...]
+    w_ref[:, QKV : QKV + QW] = wo_ref[...]
+    experts, sh = wr_ref.shape
+    gap = jnp.zeros((GAIN_MOE_ROW - experts, sh), F32)
+    aux = jnp.concatenate([wr_ref[...].astype(F32), gap, gm_ref[...].astype(F32), ga_ref[...].astype(F32)], axis=0)
+    w_ref[:, QKV + QW :] = jnp.transpose(aux).astype(BF)
     barrier = pltpu.get_barrier_semaphore()
     peers = [other] + [{"group": lax.bitwise_xor(g, 1 << b)} for b in range(bits)] + [{"expert": lax.rem(z + k, n)} for k in range(1, n)]
     for peer in peers:
@@ -1610,9 +1631,10 @@
                 make().wait_send()
 
 
-def open_up(cid, packed, cot, rt):
+def open_up(cid, weights, cot, rt):
     n, groups = lax.axis_size("expert"), lax.axis_size("group")
-    sh = packed.shape[0]
+    sh = weights[0].shape[0]
+    packed = (sh, QKV + QW + LANES)
     pieces = 3 if sh % 48 == 0 else 1
     dma = pltpu.SemaphoreType.DMA
     sds = jax.ShapeDtypeStruct
@@ -1622,12 +1644,12 @@
 
     w0, w1, gy, rt_all, rt_side = pl.pallas_call(
         functools.partial(open_kernel, n, groups, pieces),
-        out_shape=(sds((groups * n,) + packed.shape, BF),) * 2 + (sds((2, n) + cot.shape[1:], BF), sds((2, n) + rt.shape[1:], rt.dtype), sds(rt.shape[1:], rt.dtype)),
-        in_specs=vmem(3),
+        out_shape=(sds((groups * n,) + packed, BF),) * 2 + (sds((2, n) + cot.shape[1:], BF), sds((2, n) + rt.shape[1:], rt.dtype), sds(rt.shape[1:], rt.dtype)),
+        in_specs=vmem(9),
         out_specs=tuple([any_spec()] * 5),
-        scratch_shapes=both((n, 2 * pieces + 1)) + both((n, 2 * pieces + 1)) + both((groups, n, pieces)) + both((pieces,)) + both((n,)) + both((2, n)) + [dma, dma] + [dma((4,))],
+        scratch_shapes=[pltpu.VMEM(packed, BF)] + both((n, 2 * pieces + 1)) + both((n, 2 * pieces + 1)) + both((groups, n, pieces)) + both((pieces,)) + both((n,)) + both((2, n)) + [dma, dma] + [dma((4,))],
         compiler_params=pltpu.CompilerParams(collective_id=cid, has_side_effects=True),
-    )(packed, cot, rt)
+    )(*weights, cot, rt)
     return w0.reshape(groups * n * sh, -1), w1, gy, rt_all, rt_side
 
 
@@ -1659,22 +1681,12 @@
     wg, wu, wd = w_gate[0], w_up[0], w_down[0]
     at_zero = s == 0
 
-    shard = w_query.shape[1]
-    aux = jnp.concatenate(
-        [
-            w_router[0],
-            jnp.zeros((shard, GAIN_MOE_ROW - experts), BF),
-            gain_moe[0][:, None],
-            gain_attn[0][:, None],
-        ],
-        axis=1,
-    )
-    packed = jnp.concatenate([w_query[0], key_weight[0], value_weight[0], w_out[0].T, aux], axis=1)
+    dense_shards = (w_query[0], key_weight[0], value_weight[0], w_out[0].T, w_router[0].T, gain_attn, gain_moe)
+
     seg, live, cot = segment_ids[:, 0], live_first[:, 0], cotangent[:, 0]
     cos, sin = rope_tables(t)
 
     rt = jnp.swapaxes(routes[0, :, 0], 1, 2)
-    rt_mine = lax.dynamic_index_in_dim(rt, s, 0, keepdims=False)
 
     def flat(z):
         return z.reshape((2 * n,) + z.shape[2:])
@@ -1682,39 +1694,33 @@
     def paired(z):
         return z.reshape((2, n) + z.shape[1:])
 
-    first_weights, second_weights, gy1, rt_all, rt_theirs = open_up(1, packed, cot, rt)
-    rt_tokens = (jnp.where(at_zero, rt_mine, rt_theirs), jnp.where(at_zero, rt_theirs, rt_mine))
+    first_weights, second_weights, gy1, rt_all, rt_theirs = open_up(1, dense_shards, cot, rt)
     gy1, rt_all = flat(gy1), flat(rt_all)
 
-    none = jnp.zeros((1, t, d), BF)
-    qkv0, p0, o0, h0, b0, wrt0, x0 = attn_fwd(inputs[:, 0], none, first_weights, cos, sin, seg, live)
+    qkv0, p0, o0, h0, b0, wrt0, x0 = attn_fwd(inputs[:, 0], (), first_weights, cos, sin, seg, live)
     m0 = moe(0, "fwd", 2, e_pad, cap, b0, wg, wu, wd, rt=rt_all, wrt=wrt0, dense=second_weights)
     second_weights = m0.dense_out.reshape(first_weights.shape)
 
     qkv1, p1, o1, h1, b1, wrt1, x1 = attn_fwd(h0, m0.back, second_weights, cos, sin, seg, live)
     m1 = moe(1, "both", 3, e_pad, cap, b1, wg, wu, wd, rt=rt_all, wrt=wrt1, gy=gy1)
 
-    def gates_back(dg):
-        dg = dg[:, :per].reshape(experts, t)
-        return jnp.pad(dg, ((0, e_pad - experts), (0, 0)))
-
-    dx1, gy0, dqkv1, at1, dht1, daux1 = attn_bwd(False, cot, h1, x1, second_weights, qkv1, p1, o1, b1, wrt1, m1.back, gates_back(m1.dgate), rt_tokens[1], cos, sin)
+    dx1, gy0, dqkv1, at1, dht1, daux1 = attn_bwd(1, False, experts, cot, h1, x1, second_weights, qkv1, p1, o1, b1, wrt1, m1.back, m1.dgate, rt, rt_theirs, cos, sin)
 
     n0 = moe(0, "bwd", 4, e_pad, cap, gy0, wg, wu, wd, pos=m0.pos, gate=m0.gate, gp=m0.gp, up=m0.up, blocks=flat(m0.blocks),
              dqkv=dqkv1, at=at1, dht=dht1, daux=daux1, o=o1, part=m1.part0)
     dd1 = n0.dd
     dback0 = n0.back
     back1 = lax.all_to_all(jnp.where(at_zero, n0.part_out, m1.part1), "expert", split_axis=0, concat_axis=0, tiled=True)
-    dx0, _, dd0 = attn_bwd(True, gy0, h0, x0, first_weights, qkv0, p0, o0, b0, wrt0, dback0, gates_back(n0.dgate), rt_tokens[0], cos, sin)
-
-    dense, got, *sums = finish(5, dd0, dd1, dx0, dx1, (n0.even, n0.odd, n0.even_dn, n0.odd_dn), (m1.even, m1.odd, m1.even_dn, m1.odd_dn))
+    dx0, low0, dd0 = attn_bwd(0, True, experts, gy0, h0, x0, first_weights, qkv0, p0, o0, b0, wrt0, dback0, n0.dgate, rt, rt_theirs, cos, sin)
+
+    dense, got, *sums = finish(5, dd0, dd1, low0, gy0, (n0.even, n0.odd, n0.even_dn, n0.odd_dn), (m1.even, m1.odd, m1.even_dn, m1.odd_dn))
     dense, late = lax.optimization_barrier((dense, h1))
     y1 = (late + jnp.sum(back1.astype(F32), axis=0)).astype(BF)
 
     kept_out = jnp.where(at_zero, x1, y1)
     swapped_out = swap_sections(jnp.where(at_zero, y1, x1))
     layer_out = jnp.where(at_zero, jnp.stack([kept_out, swapped_out]), jnp.stack([swapped_out, kept_out]))
-    gate_grad, up_grad, down_grad, *dense_grads, router_grad, attn_grad, moe_grad, input_grad = last(
+    gate_grad, up_grad, down_grad, *dense_grads, out_grad, router_grad, attn_grad, moe_grad, input_grad = last(
         experts, dense, dx0, dx1, got, *sums
     )
     return (
@@ -1723,7 +1729,8 @@
         attn_grad,
         moe_grad,
         *(v[None] for v in dense_grads),
-        router_grad[None],
+        out_grad.T[None],
+        router_grad.T[None],
         gate_grad[None],
         up_grad[None],
         down_grad[None],

time: 701 us -> 682 us (0.973)
  local copies, waits for them, and re-layouts: 10.9 us -> 1.33 us
  Pallas kernels: 673 us -> 664 us
    pallas_call x4, Pallas kernels: 65.1 us -> 56.7 us  [the longest x2 33.3 us: attn_bwd(): pl.pallas_call(functools.partial(attn_bwd_kernel, layer, now, -(-experts...]
  transfers between devices with their start and end apart: 2 -> 2, of which waited for: 0 -> 0; matrix products, arithmetic and copies ran while one was open for 1% -> 0% of each run, Pallas kernels for 30% -> 30%
where the time goes in v7:
time: 682 us; the launch traced here: 676 us
  Pallas kernels  664 us (97%)
    pallas_call x3, Pallas kernels, moe(): pl.pallas_call(functools.partial(moe_kernel, layer, mode, n, e_pad, cap,...  281 us
    pallas_call x1, Pallas kernels, finish(): pl.pallas_call(functools.partial(finish_kernel, n), out_shape=(sds((rows,...  176 us
    pallas_call x1, Pallas kernels, open_up(): pl.pallas_call(functools.partial(open_kernel, n, groups, pieces), out_sha...  141 us
    pallas_call x2, Pallas kernels, attn_bwd(): pl.pallas_call(functools.partial(attn_bwd_kernel, layer, now, -(-experts...  33.3 us
    pallas_call x2, Pallas kernels, attn_fwd(): pl.pallas_call(functools.partial(attn_fwd_kernel, len(back)), out_shape=(...  23.4 us
  transfers between devices with their start and end apart: 2, of which 0 were waited for; matrix products, arithmetic and copies ran while one was open for 0% of the time, Pallas kernels for 30%

profile of v7, /device:TPU:0, one launch (start us, length us, event | category | flops | bytes accessed | tf_op | source)
XLA Modules:
  0.0 675.6 jit_solution(15870106026592325931)
XLA Ops:
  0.7 141.5 %shard_map.256 = (bf16[16,96,4224]{2,1,0:T(8,128)(2,1)}, bf16[16,96,4224]{2,1,0:T(8,128)(2,1)}, bf16[2,4,128,1536]{3,2,1,0:T(8,128)(2,1)}, s32[2,4,8,128]{3,2,1,0:T(8,128)}, s32[8,128]{1,0:T(8,128)}) custom-call(bf16[96,1536]{1,0:T(8,128)(2,1)} %bitcast.73, bf16[96,512]{1,0:T(8,128)(2,1)} %bitcast.77, bf16[96,512]{1,0:T(8,128)(2,1)} %bitcast.78, ...), custom_call_target="tpu_custom_call" | custom-call | tf_op jit(solution)/shard_map/pallas_call | solution.py:1645
  142.1 11.5 %shard_map.257 = (bf16[128,2560]{1,0:T(8,128)(2,1)}, f32[24,128,128]{2,1,0:T(8,128)}, bf16[128,1536]{1,0:T(8,128)(2,1)}, f32[128,1536]{1,0:T(8,128)}, bf16[128,1...) custom-call(bf16[2,128,1536]{2,1,0:T(8,128)(2,1)} %bitcast.71, bf16[1536,4224]{1,0:T(8,128)(2,1)} %bitcast.59, ...), custom_call_target="tpu_custom_call" | custom-call | flops 1610612736 | bytes 12976128 | tf_op jit(solution)/shard_map/pallas_call | solution.py:169
  153.6 94.4 %shard_map.258 = (bf16[4,128,1536]{2,1,0:T(8,128)(2,1)}, s32[8,8,128]{2,1,0:T(8,128)}, f32[8,8,128]{2,1,0:T(8,128)}, bf16[5,512,512]{2,1,0:T(8,128)(2,1)}, bf16[...) custom-call(bf16[128,1536]{1,0:T(8,128)(2,1)} %get-tuple-element.83., ...), custom_call_target="tpu_custom_call", output_to_operand_aliasing={{6}: (6, {})} | custom-call | tf_op jit(solution)/shard_map/pallas_call | solution.py:974
  248.0 11.9 %shard_map.259 = (bf16[128,2560]{1,0:T(8,128)(2,1)}, f32[24,128,128]{2,1,0:T(8,128)}, bf16[128,1536]{1,0:T(8,128)(2,1)}, f32[128,1536]{1,0:T(8,128)}, bf16[128,1...) custom-call(f32[128,1536]{1,0:T(8,128)} %get-tuple-element.82.below_ref.h_ref, ...), custom_call_target="tpu_custom_call" | custom-call | flops 1610612736 | bytes 12976128 | tf_op jit(solution)/shard_map/pallas_call | solution.py:169
  259.9 97.7 %shard_map.260 = (bf16[4,128,1536]{2,1,0:T(8,128)(2,1)}, f32[4,8,128]{2,1,0:T(8,128)}, bf16[2,2,5,384,512]{4,3,2,1,0:T(8,128)(2,1)}, bf16[2,2,5,384,512]{4,3,2,1...) custom-call(bf16[128,1536]{1,0:T(8,128)(2,1)} %get-tuple-element.94., ...), custom_call_target="tpu_custom_call" | custom-call | tf_op jit(solution)/shard_map/pallas_call | solution.py:974
  357.6 14.3 %shard_map.261 = (f32[128,1536]{1,0:T(8,128)}, bf16[128,1536]{1,0:T(8,128)(2,1)}, bf16[128,2560]{1,0:T(8,128)(2,1)}, bf16[1536,128]{1,0:T(8,128)(2,1)}, bf16[153...) custom-call(bf16[2,128,1536]{2,1,0:T(8,128)(2,1)} %bitcast.68, f32[128,1536]{1,0:T(8,128)} %get-tuple-element.129.h_ref, ...), custom_call_target="tpu_custom_call" | custom-call | flops 3221225472 | bytes 25952256 | tf_op jit(solution)/shard_map/pallas_call | solution.py:331
  371.9 0.0 copy-start.2
  371.9 88.8 %shard_map.262 = (bf16[4,128,1536]{2,1,0:T(8,128)(2,1)}, f32[4,8,128]{2,1,0:T(8,128)}, bf16[2,2,5,384,512]{4,3,2,1,0:T(8,128)(2,1)}, bf16[2,2,5,384,512]{4,3,2,1...) custom-call(bf16[128,1536]{1,0:T(8,128)(2,1)} %get-tuple-element.100, ...), custom_call_target="tpu_custom_call" | custom-call | tf_op jit(solution)/shard_map/pallas_call | solution.py:974
  460.8 0.0 copy-done.2
  460.8 2.7 broadcast_select_fusion
  463.5 4.5 all-to-all-start
  468.0 19.0 %shard_map.263 = (f32[128,1536]{1,0:T(8,128)}, bf16[128,1536]{1,0:T(8,128)(2,1)}, bf16[1536,4224]{1,0:T(8,128)(2,1)}) custom-call(bf16[128,1536]{1,0:T(8,128)(2,1)} %get-tuple-element.100.refs_0_.gy_ref.dx1, f32[128,1536]{1,0:T(8,128)} %get-tuple-element.82.below_ref.h_ref, bf16[128,1536]{1,0:T(8,128)(2,1)} %get-tuple-element.101.x_ref, ...), custom_call_target="tpu_custom_call" | custom-call | flops 3221225472 | bytes 25952256 | tf_op jit(solution)/shard_map/pallas_call | solution.py:331
  487.0 0.0 copy-start
  487.0 0.0 copy-start.1
  487.0 175.5 %shard_map.264 = (f32[96,4224]{1,0:T(8,128)}, bf16[128,1536]{1,0:T(8,128)(2,1)}, bf16[5,384,512]{2,1,0:T(8,128)(2,1)}, bf16[5,384,512]{2,1,0:T(8,128)(2,1)}, bf16[5,512,384]{2,1,0:T(8,128)(2,1)}) custom-call(bf16[16,96,4224]{2,1,0:T(8,128)(2,1)} %bitcast.62, bf16[16,96,4224]{2,1,0:T(8,128)(2,1)} %bitcast.61, bf16[128,1536]{1,0:T(8,128)(2,1)} %get-tuple-element.119.dx0, ...), custom_call_target="tpu_custom_call" | custom-call | tf_op jit(solution)/shard_map/pallas_call | solution.py:1369
  662.6 0.0 all-to-all-done
  662.6 0.2 convert_reduce_fusion
  662.8 0.0 copy-done
  662.8 0.0 copy-done.1
  662.8 0.2 select_bitcast_fusion
  663.0 0.1 collective-permute-start
  663.1 9.9 %shard_map.265 = (f32[5,384,512]{2,1,0:T(8,128)}, f32[5,384,512]{2,1,0:T(8,128)}, f32[5,512,384]{2,1,0:T(8,128)}, f32[96,1536]{1,0:T(8,128)}, f32[96,512]{1,0:T(...) custom-call(f32[96,4224]{1,0:T(8,128)} %get-tuple-element.132.dense_, ...), custom_call_target="tpu_custom_call" | custom-call | tf_op jit(solution)/shard_map/pallas_call | solution.py:1444
  673.0 1.3 copy.31
  674.4 0.0 collective-permute-done
  674.4 1.0 maximum_select_fusion
  (1 shorter events, 0.0 us)
Async XLA Ops:
  371.9 88.9 %copy-start.2 = (bf16[4,128,1536]{2,1,0:T(8,128)(2,1)S(1)}, bf16[4,128,1536]{2,1,0:T(8,128)(2,1)}, u32[]{:S(2)}) copy-start(bf16[4,128,1536]{2,1,0:T(8,128)(2,1)} %get-tuple-element.131) | copy-start | bytes 4718596
  463.5 199.1 %all-to-all-start = ((bf16[4,128,1536]{2,1,0:T(8,128)(2,1)}), bf16[4,128,1536]{2,1,0:T(8,128)(2,1)S(1)}, u32[]{:S(2)}, u32[]{:S(2)}) async-start(bf16[4,128,1536]{2,1,0:T(8,128)(2,1)} %broadcast_select_fusion), calls=%async_computation | async-start | bytes 3145728 | tf_op jit(solution)/shard_map/all_to_all | solution.py:1713
  487.0 175.8 %copy-start = (bf16[128,1536]{1,0:T(8,128)(2,1)S(1)}, bf16[128,1536]{1,0:T(8,128)(2,1)}, u32[]{:S(2)}) copy-start(bf16[128,1536]{1,0:T(8,128)(2,1)} %get-tuple-element.89.x_ref) | copy-start | bytes 1179652
  487.0 175.8 %copy-start.1 = (f32[128,1536]{1,0:T(8,128)S(1)}, f32[128,1536]{1,0:T(8,128)}, u32[]{:S(2)}) copy-start(f32[128,1536]{1,0:T(8,128)} %get-tuple-element.129.h_ref) | copy-start | bytes 2359300
  663.0 11.3 %collective-permute-start = (bf16[128,1536]{1,0:T(8,128)(2,1)S(1)}, bf16[128,1536]{1,0:T(8,128)(2,1)S(1)}, u32[]{:S(2)}, u32[]{:S(2)}) collective-permute-start(bf16[128,1536]{1,0:T(8,128)(2,1)S(1)} %broadcast_select_fusion.1), channel_id=1, source_target_pairs={{0,16},{16,0},{1,17},{17,1},{2,18},{18,2},{3,19},{19,3},{4,20},{20... | collective-permute-start | bytes 1179656 | tf_op jit(solution)/shard_map/ppermute | solution.py:1657

commit v8 on v7

--- a/solution.py
+++ b/solution.py
@@ -148,7 +148,7 @@
             o_ref[:, lanes((m * TILES_PER_PAIR + r) * LANES)] = (parts[2 * r] + parts[2 * r + 1]).astype(BF)
         return carry
 
-    lax.fori_loop(0, HEAD_PAIRS, pair, 0)
+    lax.fori_loop(0, HEAD_PAIRS, pair, 0, unroll=True)
     o = o_ref[...]
     for n in range(d // TILE):
         rows = slice(n * TILE, (n + 1) * TILE)
@@ -273,7 +273,7 @@
         dqkv_ref[:, lanes(QW + KW + m * LANES)] = dv_all.astype(BF)
         return carry
 
-    lax.fori_loop(0, HEAD_PAIRS, pair, 0)
+    lax.fori_loop(0, HEAD_PAIRS, pair, 0, unroll=True)
     x = x_ref[...].astype(F32)
     r1 = lax.rsqrt(jnp.mean(x * x, axis=1, keepdims=True) + EPS)
     dqkv = dqkv_ref[...]
@@ -599,40 +599,39 @@
 
         lax.fori_loop(0, 2, candidate, 0)
 
-    def dense_tiles():
-        tiles = []
-        for first_row in range(0, d, rows):
-            for left, right, col, width in ((r.at, r.dqkv, 0, QW), (r.at, r.dqkv, QW, 2 * KW), (r.dht, r.o, QKV, QW)):
-                source = right if left is r.dht else right.at[:, pl.ds(col, width)]
-                tiles.append((left.at[pl.ds(first_row, rows)], source, first_row, col, width))
-        return tiles
-
-    def dense_copy(i, tile):
-        _, _, row, col, width = tile
+    tiles = (("at", "dqkv", 0, QW), ("at", "dqkv", QW, 2 * KW), ("dht", "o", QKV, QW))
+
+    def dense_copy(block, m):
+        _, _, col, width = tiles[m]
+        at = pl.ds(pl.multiple_of(block * rows, rows), rows)
         return pltpu.make_async_copy(
-            r.x_scr.at[i % per, :, pl.ds(0, width)], r.dd.at[pl.ds(row, rows), pl.ds(col, width)], r.dd_sem.at[i]
+            r.x_scr.at[m, :, pl.ds(0, width)], r.dd.at[at, pl.ds(col, width)], r.dd_sem.at[m]
         )
 
     def aux_copy():
         return pltpu.make_async_copy(r.daux, r.dd.at[:, pl.ds(QKV + QW, LANES)], r.daux_sem)
 
-    def dense_start(step):
-        if step == 0:
+    def dense_start(block):
+        @pl.when(block == 0)
+        def _():
             aux_copy().start()
-        tiles = dense_tiles()
-        share = len(tiles) // 3
-        for i, tile in list(enumerate(tiles))[step * share : (step + 1) * share]:
-            if i >= per:
-                dense_copy(i - per, tiles[i - per]).wait()
-            left, right, _, _, width = tile
-            r.x_scr[i % per, :, 0:width] = dot(left[...], right[...]).astype(BF)
-            dense_copy(i, tile).start()
+
+        at = pl.ds(pl.multiple_of(block * rows, rows), rows)
+        for m, (left, right, col, width) in enumerate(tiles):
+
+            @pl.when(block > 0)
+            def _():
+                dense_copy(block - 1, m).wait()
+
+            source = getattr(r, right)
+            source = source[:, col : col + width] if right == "dqkv" else source[...]
+            r.x_scr[m, :, 0:width] = dot(getattr(r, left)[at, :], source).astype(BF)
+            dense_copy(block, m).start()
 
     def dense_wait():
         aux_copy().wait()
-        tiles = dense_tiles()
-        for i in range(max(0, len(tiles) - per), len(tiles)):
-            dense_copy(i, tiles[i]).wait()
+        for m in range(len(tiles)):
+            dense_copy(d // rows - 1, m).wait()
 
     @pl.loop(0, n)
     def _(t):
@@ -665,11 +664,9 @@
 
         if mode == "bwd":
 
-            for step in range(3):
-
-                @pl.when(t == step)
-                def _(step=step):
-                    dense_start(step)
+            @pl.when(t < d // rows)
+            def _():
+                dense_start(t)
 
         @pl.when(here)
         def _():
@@ -685,14 +682,19 @@
 
             prepare_at(layer, t)
 
+            @pl.when(t == min(2, n - 1))
+            def _():
+                cross(z).wait_recv()
+                prepare(1 - layer, z)
+
     def late_blocks():
-        @pl.loop(0, n)
+        @pl.loop(1, n)
         def _(t):
             @pl.when(z >= t)
             def _():
                 cross(z - t).wait_recv()
 
-            @pl.when((t > 0) & (z + t < n))
+            @pl.when(z + t < n)
             def _():
                 cross(z + t).wait_recv()
 
@@ -713,6 +715,10 @@
         def _():
             for zz in range(n):
                 over_part(zz).start()
+            pltpu.make_async_copy(r.part_own, r.pbuf.at[layer], r.part_sem.at[0]).start()
+
+    def part_home():
+        return pltpu.make_async_copy(r.pbuf.at[layer], r.part_out, r.part_sem.at[1])
 
     srcs = (r.pbuf, r.dg) if backward else (r.pbuf,)
     outs = (r.back, r.dgate) if backward else (r.back,)
@@ -882,6 +888,9 @@
 
         @pl.when(jnp.logical_not(here))
         def _():
+            pltpu.make_async_copy(r.part_own, r.pbuf.at[layer], r.part_sem.at[0]).wait()
+            part_home().start()
+            part_home().wait()
             for zz in range(n):
                 over_part(zz).wait_send()
 
@@ -965,8 +974,8 @@
     if mode == "bwd":
         outs["dd"] = sds((d, QKV + QW + LANES), BF)
         outs["part_out"] = sds((n, t, d), BF)
-        scratch.update(s_part=dma((n,)), r_part=dma((n,)))
-        scratch.update(dd_sem=dma((3 * d // rows,)), daux_sem=dma)
+        scratch.update(s_part=dma((n,)), r_part=dma((n,)), part_sem=dma((2,)))
+        scratch.update(dd_sem=dma((3,)), daux_sem=dma)
     if mode == "both":
         outs["part0"] = outs["part1"] = sds((n, t, d), BF)
         scratch.update(pos=pltpu.VMEM((count, 8, t), jnp.int32), gate=pltpu.VMEM((count, 8, t), F32))
@@ -1050,7 +1059,7 @@
     def core_dn_copy(source, q, c):
         return core_chunk(source, core_dn, s_core_dn, r_core_dn, q, c)
 
-    def send_all(own, away, egu, ogu, ed, od):
+    def send_first(own, away, egu, ogu, ed, od):
         @pl.loop(0, units)
         def _(i):
             core_dd_copy(0, i, away).start()
@@ -1069,6 +1078,7 @@
             if i < cdn:
                 core_dn_copy(od, pairs - 1, i).start()
 
+    def send_rest(own, away, egu, ogu, ed, od):
         @pl.loop(0, units)
         def _(i):
             core_dd_copy(1, i, own).start()
@@ -1083,7 +1093,7 @@
             def _(c):
                 core_dn_copy(od, q, c).start()
 
-    by_section(send_all)
+    by_section(send_first)
 
     def dx_copy(source):
         return remote(src_ref=source, dst_ref=dx_out, send_sem=s_dx, recv_sem=r_dx, device_id=other)
@@ -1169,6 +1179,8 @@
 
     for q in reversed(range(1, pairs)):
         dense_too = q == pairs - 1
+        if not dense_too and q == pairs - 2:
+            by_section(send_rest)
         steps = max(units, cgu, cdn) if dense_too else max(cgu, cdn)
 
         def start(i, slot):
@@ -1204,6 +1216,9 @@
                 dn_hop(top_bit(q), q, i).start()
 
         stepped(steps, start, body)
+
+    if pairs == 2:
+        by_section(send_rest)
 
     @pl.when(s == 0)
     def _():
@@ -1422,7 +1437,8 @@
         v_out[...] = dense_ref[:, QW + KW : QKV]
         o_out[...] = dense_ref[:, QKV : QKV + QW]
         aux_rows = jnp.transpose(dense_ref[:, QKV + QW :])
-        router_out[...] = aux_rows[0:experts]
+        for e in range(experts):
+            router_out[e] = aux_rows[e : e + 1]
         moe_out[...] = aux_rows[GAIN_MOE_ROW : GAIN_MOE_ROW + 1]
         attn_out[...] = aux_rows[GAIN_ATTN_ROW : GAIN_ATTN_ROW + 1]
         dx_out[s] = jnp.where(s == 0, dx0_ref[...], dx1_ref[...])
@@ -1440,7 +1456,7 @@
 
     wide = pl.BlockSpec((1, piece, f), lambda j: (j, 0, 0))
     tall = pl.BlockSpec((1, f, piece), lambda j: (j, 0, 0))
-    small = [(sh, QW), (sh, KW), (sh, KW), (sh, QW), (experts, sh), (1, sh), (1, sh), (2, t, d)]
+    small = [(sh, QW), (sh, KW), (sh, KW), (sh, QW), (experts, 1, sh), (1, sh), (1, sh), (2, t, d)]
     return pl.pallas_call(
         functools.partial(last_kernel, experts),
         grid=(per,),
@@ -1707,10 +1723,10 @@
     dx1, gy0, dqkv1, at1, dht1, daux1 = attn_bwd(1, False, experts, cot, h1, x1, second_weights, qkv1, p1, o1, b1, wrt1, m1.back, m1.dgate, rt, rt_theirs, cos, sin)
 
     n0 = moe(0, "bwd", 4, e_pad, cap, gy0, wg, wu, wd, pos=m0.pos, gate=m0.gate, gp=m0.gp, up=m0.up, blocks=flat(m0.blocks),
-             dqkv=dqkv1, at=at1, dht=dht1, daux=daux1, o=o1, part=m1.part0)
+             dqkv=dqkv1, at=at1, dht=dht1, daux=daux1, o=o1, part=m1.part0, part_own=m1.part1)
     dd1 = n0.dd
     dback0 = n0.back
-    back1 = lax.all_to_all(jnp.where(at_zero, n0.part_out, m1.part1), "expert", split_axis=0, concat_axis=0, tiled=True)
+    back1 = lax.all_to_all(n0.part_out, "expert", split_axis=0, concat_axis=0, tiled=True)
     dx0, low0, dd0 = attn_bwd(0, True, experts, gy0, h0, x0, first_weights, qkv0, p0, o0, b0, wrt0, dback0, n0.dgate, rt, rt_theirs, cos, sin)
 
     dense, got, *sums = finish(5, dd0, dd1, low0, gy0, (n0.even, n0.odd, n0.even_dn, n0.odd_dn), (m1.even, m1.odd, m1.even_dn, m1.odd_dn))
@@ -1730,7 +1746,7 @@
         moe_grad,
         *(v[None] for v in dense_grads),
         out_grad.T[None],
-        router_grad.T[None],
+        jnp.transpose(router_grad, (1, 2, 0)),
         gate_grad[None],
         up_grad[None],
         down_grad[None],

time: 682 us -> 678 us (level)
  transfers between devices with their start and end apart: 2 -> 2, of which waited for: 0 -> 1; matrix products, arithmetic and copies ran while one was open for 0% -> 0% of each run, Pallas kernels for 30% -> 30%
where the time goes in v8:
time: 678 us; the launch traced here: 670 us
  Pallas kernels  661 us (97%)
    pallas_call x3, Pallas kernels, moe(): pl.pallas_call(functools.partial(moe_kernel, layer, mode, n, e_pad, cap,...  279 us
    pallas_call x1, Pallas kernels, finish(): pl.pallas_call(functools.partial(finish_kernel, n), out_shape=(sds((rows,...  176 us
    pallas_call x1, Pallas kernels, open_up(): pl.pallas_call(functools.partial(open_kernel, n, groups, pieces), out_sha...  141 us
    pallas_call x2, Pallas kernels, attn_bwd(): pl.pallas_call(functools.partial(attn_bwd_kernel, layer, now, -(-experts...  31.7 us
    pallas_call x2, Pallas kernels, attn_fwd(): pl.pallas_call(functools.partial(attn_fwd_kernel, len(back)), out_shape=(...  22.3 us
  transfers between devices with their start and end apart: 2, of which 1 were waited for; matrix products, arithmetic and copies ran while one was open for 0% of the time, Pallas kernels for 30%

profile of v8, /device:TPU:0, one launch (start us, length us, event | category | flops | bytes accessed | tf_op | source)
XLA Modules:
  0.0 669.7 jit_solution(6333080701684360482)
XLA Ops:
  0.6 141.4 %shard_map.256 = (bf16[16,96,4224]{2,1,0:T(8,128)(2,1)}, bf16[16,96,4224]{2,1,0:T(8,128)(2,1)}, bf16[2,4,128,1536]{3,2,1,0:T(8,128)(2,1)}, s32[2,4,8,128]{3,2,1,0:T(8,128)}, s32[8,128]{1,0:T(8,128)}) custom-call(bf16[96,1536]{1,0:T(8,128)(2,1)} %bitcast.71, bf16[96,512]{1,0:T(8,128)(2,1)} %bitcast.75, bf16[96,512]{1,0:T(8,128)(2,1)} %bitcast.76, ...), custom_call_target="tpu_custom_call" | custom-call | tf_op jit(solution)/shard_map/pallas_call | solution.py:1661
  142.1 10.9 %shard_map.257 = (bf16[128,2560]{1,0:T(8,128)(2,1)}, f32[24,128,128]{2,1,0:T(8,128)}, bf16[128,1536]{1,0:T(8,128)(2,1)}, f32[128,1536]{1,0:T(8,128)}, bf16[128,1...) custom-call(bf16[2,128,1536]{2,1,0:T(8,128)(2,1)} %bitcast.69, bf16[1536,4224]{1,0:T(8,128)(2,1)} %bitcast.57, ...), custom_call_target="tpu_custom_call" | custom-call | flops 1610612736 | bytes 12976128 | tf_op jit(solution)/shard_map/pallas_call | solution.py:169
  153.1 94.8 %shard_map.258 = (bf16[4,128,1536]{2,1,0:T(8,128)(2,1)}, s32[8,8,128]{2,1,0:T(8,128)}, f32[8,8,128]{2,1,0:T(8,128)}, bf16[5,512,512]{2,1,0:T(8,128)(2,1)}, bf16[...) custom-call(bf16[128,1536]{1,0:T(8,128)(2,1)} %get-tuple-element.83., ...), custom_call_target="tpu_custom_call", output_to_operand_aliasing={{6}: (6, {})} | custom-call | tf_op jit(solution)/shard_map/pallas_call | solution.py:983
  247.8 11.4 %shard_map.259 = (bf16[128,2560]{1,0:T(8,128)(2,1)}, f32[24,128,128]{2,1,0:T(8,128)}, bf16[128,1536]{1,0:T(8,128)(2,1)}, f32[128,1536]{1,0:T(8,128)}, bf16[128,1...) custom-call(f32[128,1536]{1,0:T(8,128)} %get-tuple-element.82.below_ref.h_ref, ...), custom_call_target="tpu_custom_call" | custom-call | flops 1610612736 | bytes 12976128 | tf_op jit(solution)/shard_map/pallas_call | solution.py:169
  259.2 96.8 %shard_map.260 = (bf16[4,128,1536]{2,1,0:T(8,128)(2,1)}, f32[4,8,128]{2,1,0:T(8,128)}, bf16[2,2,5,384,512]{4,3,2,1,0:T(8,128)(2,1)}, bf16[2,2,5,384,512]{4,3,2,1...) custom-call(bf16[128,1536]{1,0:T(8,128)(2,1)} %get-tuple-element.94., ...), custom_call_target="tpu_custom_call" | custom-call | tf_op jit(solution)/shard_map/pallas_call | solution.py:983
  356.1 13.5 %shard_map.261 = (f32[128,1536]{1,0:T(8,128)}, bf16[128,1536]{1,0:T(8,128)(2,1)}, bf16[128,2560]{1,0:T(8,128)(2,1)}, bf16[1536,128]{1,0:T(8,128)(2,1)}, bf16[153...) custom-call(bf16[2,128,1536]{2,1,0:T(8,128)(2,1)} %bitcast.66, f32[128,1536]{1,0:T(8,128)} %get-tuple-element.130.h_ref, ...), custom_call_target="tpu_custom_call" | custom-call | flops 3221225472 | bytes 25952256 | tf_op jit(solution)/shard_map/pallas_call | solution.py:331
  369.6 87.9 %shard_map.262 = (bf16[4,128,1536]{2,1,0:T(8,128)(2,1)}, f32[4,8,128]{2,1,0:T(8,128)}, bf16[2,2,5,384,512]{4,3,2,1,0:T(8,128)(2,1)}, bf16[2,2,5,384,512]{4,3,2,1...) custom-call(bf16[128,1536]{1,0:T(8,128)(2,1)} %get-tuple-element.100, ...), custom_call_target="tpu_custom_call" | custom-call | tf_op jit(solution)/shard_map/pallas_call | solution.py:983
  457.5 4.8 all-to-all-start
  462.3 18.2 %shard_map.263 = (f32[128,1536]{1,0:T(8,128)}, bf16[128,1536]{1,0:T(8,128)(2,1)}, bf16[1536,4224]{1,0:T(8,128)(2,1)}) custom-call(bf16[128,1536]{1,0:T(8,128)(2,1)} %get-tuple-element.100.refs_0_.gy_ref.dx1, f32[128,1536]{1,0:T(8,128)} %get-tuple-element.82.below_ref.h_ref, bf16[128,1536]{1,0:T(8,128)(2,1)} %get-tuple-element.101.x_ref, ...), custom_call_target="tpu_custom_call" | custom-call | flops 3221225472 | bytes 25952256 | tf_op jit(solution)/shard_map/pallas_call | solution.py:331
  480.5 0.0 copy-start
  480.5 0.0 copy-start.1
  480.5 175.7 %shard_map.264 = (f32[96,4224]{1,0:T(8,128)}, bf16[128,1536]{1,0:T(8,128)(2,1)}, bf16[5,384,512]{2,1,0:T(8,128)(2,1)}, bf16[5,384,512]{2,1,0:T(8,128)(2,1)}, bf16[5,512,384]{2,1,0:T(8,128)(2,1)}) custom-call(bf16[16,96,4224]{2,1,0:T(8,128)(2,1)} %bitcast.60, bf16[16,96,4224]{2,1,0:T(8,128)(2,1)} %bitcast.59, bf16[128,1536]{1,0:T(8,128)(2,1)} %get-tuple-element.120.dx0, ...), custom_call_target="tpu_custom_call" | custom-call | tf_op jit(solution)/shard_map/pallas_call | solution.py:1384
  656.3 0.0 all-to-all-done
  656.3 0.2 convert_reduce_fusion
  656.5 0.0 copy-done
  656.5 0.0 copy-done.1
  656.5 0.2 select_bitcast_fusion
  656.7 0.1 collective-permute-start
  656.8 9.9 %shard_map.265 = (f32[5,384,512]{2,1,0:T(8,128)}, f32[5,384,512]{2,1,0:T(8,128)}, f32[5,512,384]{2,1,0:T(8,128)}, f32[96,1536]{1,0:T(8,128)}, f32[96,512]{1,0:T(...) custom-call(f32[96,4224]{1,0:T(8,128)} %get-tuple-element.132.dense_, ...), custom_call_target="tpu_custom_call" | custom-call | tf_op jit(solution)/shard_map/pallas_call | solution.py:1460
  666.8 1.4 collective-permute-done
  668.1 1.0 maximum_select_fusion
  (1 shorter events, 0.0 us)
Async XLA Ops:
  457.5 198.7 %all-to-all-start = ((bf16[4,128,1536]{2,1,0:T(8,128)(2,1)}), bf16[4,128,1536]{2,1,0:T(8,128)(2,1)S(1)}, u32[]{:S(2)}, u32[]{:S(2)}) async-start(bf16[4,128,1536]{2,1,0:T(8,128)(2,1)} %get-tuple-element.131), calls=%async_computation | async-start | bytes 3145728 | tf_op jit(solution)/shard_map/all_to_all | solution.py:1729
  480.5 176.0 %copy-start = (bf16[128,1536]{1,0:T(8,128)(2,1)S(1)}, bf16[128,1536]{1,0:T(8,128)(2,1)}, u32[]{:S(2)}) copy-start(bf16[128,1536]{1,0:T(8,128)(2,1)} %get-tuple-element.89.x_ref) | copy-start | bytes 1179652
  480.5 176.0 %copy-start.1 = (f32[128,1536]{1,0:T(8,128)S(1)}, f32[128,1536]{1,0:T(8,128)}, u32[]{:S(2)}) copy-start(f32[128,1536]{1,0:T(8,128)} %get-tuple-element.130.h_ref) | copy-start | bytes 2359300
  656.7 11.4 %collective-permute-start = (bf16[128,1536]{1,0:T(8,128)(2,1)S(1)}, bf16[128,1536]{1,0:T(8,128)(2,1)S(1)}, u32[]{:S(2)}, u32[]{:S(2)}) collective-permute-start(bf16[128,1536]{1,0:T(8,128)(2,1)S(1)} %broadcast_select_fusion), channel_id=1, source_target_pairs={{0,16},{16,0},{1,17},{17,1},{2,18},{18,2},{3,19},{19,3},{4,20},{20... | collective-permute-start | bytes 1179656 | tf_op jit(solution)/shard_map/ppermute | solution.py:1673

commit v9 on v8

--- a/solution.py
+++ b/solution.py
@@ -206,12 +206,11 @@
     else:
         dqkv_ref, at_ref, dht_ref, daux_ref, do_ref, dh_ref, w_ref, w_sem = rest
     pieces = arriving(w_hbm, w_ref, w_sem, "backward")
-    leaving = []
-
-    def leave(first, width):
-        cols = pl.ds(first, width)
-        leaving.append(pltpu.make_async_copy(dd_ref.at[:, cols], dd_hbm.at[:, cols], dd_sem.at[len(leaving)]))
-        leaving[-1].start()
+    last_tile = (QKV + QW) // TILE
+
+    def leave(n, width):
+        cols = pl.ds(pl.multiple_of(n * TILE, LANES), width)
+        return pltpu.make_async_copy(dd_ref.at[:, cols], dd_hbm.at[:, cols], dd_sem.at[n])
 
     gain_attn = wrt_ref[GAIN_ATTN_ROW - 7 :, :].astype(F32)[7:8]
     gain_moe = wrt_ref[GAIN_ATTN_ROW - 7 :, :].astype(F32)[6:7]
@@ -299,19 +298,29 @@
         daux_ref[...] = daux
         return
     lt_ref[...] = jnp.transpose(x * r1 * gain_attn).astype(BF)
-    for n in range(QKV // TILE):
-        cols = slice(n * TILE, (n + 1) * TILE)
+
+    @pl.loop(0, QKV // TILE)
+    def _(n):
+        cols = pl.ds(pl.multiple_of(n * TILE, LANES), TILE)
         dd_ref[:, cols] = dot(lt_ref[...], dqkv_ref[:, cols]).astype(BF)
-        leave(n * TILE, TILE)
+        leave(n, TILE).start()
+
     lt_ref[...] = jnp.transpose(dh_ref[...]).astype(BF)
-    for n in range(QW // TILE):
-        cols = slice(n * TILE, (n + 1) * TILE)
-        dd_ref[:, QKV + n * TILE : QKV + (n + 1) * TILE] = dot(lt_ref[...], o_ref[:, cols]).astype(BF)
-        leave(QKV + n * TILE, TILE)
+
+    @pl.loop(0, QW // TILE)
+    def _(n):
+        cols = pl.ds(pl.multiple_of(n * TILE, LANES), TILE)
+        dd_ref[:, pl.ds(pl.multiple_of(QKV + n * TILE, LANES), TILE)] = dot(lt_ref[...], o_ref[:, cols]).astype(BF)
+        leave(QKV // TILE + n, TILE).start()
+
     dd_ref[:, QKV + QW :] = daux
-    leave(QKV + QW, LANES)
-    for c in leaving:
-        c.wait()
+    leave(last_tile, LANES).start()
+
+    @pl.loop(0, last_tile)
+    def _(n):
+        leave(n, TILE).wait()
+
+    leave(last_tile, LANES).wait()
 
 
 def attn_bwd(layer, now, experts, gy, h, x, w, qkv, p, o, b, wrt, back, dg, rt, side, cos, sin):
@@ -456,30 +465,27 @@
         for c in outgoing(0, 0, slot):
             c.wait()
 
-    def body(j, carry):
-        for q in range(parts):
-            slot = q % 2
-            if q >= 2:
-                finished(slot)
-            else:
-
-                @pl.when(j > 0)
-                def _():
-                    finished(slot)
-
-            cols = slice(2 * q * piece, 2 * (q + 1) * piece)
-            for m in range(2):
-                full = dot(r.x_scr[j, :, cols], r.act[m, j], 0, 0).astype(BF)
-                r.gu_buf[slot, parity, m] = full[:piece]
-                r.gu_buf[slot, 1 - parity, m] = full[piece:]
-            full = dot(r.act[2, j], r.y_scr[j, :, cols], 0, 0).astype(BF)
-            r.dn_buf[slot, parity] = full[:, :piece]
-            r.dn_buf[slot, 1 - parity] = full[:, piece:]
-            for c in outgoing(j, lax.bitwise_xor(place, q), slot):
-                c.start()
+    def body(i, carry):
+        j, q = i // parts, lax.rem(i, parts)
+        slot = lax.rem(i, 2)
+
+        @pl.when(i >= 2)
+        def _():
+            finished(slot)
+
+        cols = pl.ds(pl.multiple_of(2 * q * piece, LANES), 2 * piece)
+        for m in range(2):
+            full = dot(r.x_scr[j, :, cols], r.act[m, j], 0, 0).astype(BF)
+            r.gu_buf[slot, parity, m] = full[:piece]
+            r.gu_buf[slot, 1 - parity, m] = full[piece:]
+        full = dot(r.act[2, j], r.y_scr[j, :, cols], 0, 0).astype(BF)
+        r.dn_buf[slot, parity] = full[:, :piece]
+        r.dn_buf[slot, 1 - parity] = full[:, piece:]
+        for c in outgoing(j, lax.bitwise_xor(place, q), slot):
+            c.start()
         return carry
 
-    lax.fori_loop(0, per, body, 0)
+    lax.fori_loop(0, per * parts, body, 0)
     for slot in range(2):
         finished(slot)
 

time: 678 us -> 678 us (level)
  transfers between devices with their start and end apart: 2 -> 2, of which waited for: 1 -> 1; matrix products, arithmetic and copies ran while one was open for 0% -> 0% of each run, Pallas kernels for 30% -> 31%
where the time goes in v9:
time: 678 us; the launch traced here: 670 us
  Pallas kernels  661 us (97%)
    pallas_call x3, Pallas kernels, moe(): pl.pallas_call(functools.partial(moe_kernel, layer, mode, n, e_pad, cap,...  279 us
    pallas_call x1, Pallas kernels, finish(): pl.pallas_call(functools.partial(finish_kernel, n), out_shape=(sds((rows,...  176 us
    pallas_call x1, Pallas kernels, open_up(): pl.pallas_call(functools.partial(open_kernel, n, groups, pieces), out_sha...  141 us
    pallas_call x2, Pallas kernels, attn_bwd(): pl.pallas_call(functools.partial(attn_bwd_kernel, layer, now, -(-experts...  32.6 us
    pallas_call x2, Pallas kernels, attn_fwd(): pl.pallas_call(functools.partial(attn_fwd_kernel, len(back)), out_shape=(...  22.3 us
  transfers between devices with their start and end apart: 2, of which 1 were waited for; matrix products, arithmetic and copies ran while one was open for 0% of the time, Pallas kernels for 31%

profile of v9, /device:TPU:0, one launch (start us, length us, event | category | flops | bytes accessed | tf_op | source)
XLA Modules:
  0.0 669.6 jit_solution(12086985387746501485)
XLA Ops:
  0.6 141.4 %shard_map.256 = (bf16[16,96,4224]{2,1,0:T(8,128)(2,1)}, bf16[16,96,4224]{2,1,0:T(8,128)(2,1)}, bf16[2,4,128,1536]{3,2,1,0:T(8,128)(2,1)}, s32[2,4,8,128]{3,2,1,0:T(8,128)}, s32[8,128]{1,0:T(8,128)}) custom-call(bf16[96,1536]{1,0:T(8,128)(2,1)} %bitcast.71, bf16[96,512]{1,0:T(8,128)(2,1)} %bitcast.75, bf16[96,512]{1,0:T(8,128)(2,1)} %bitcast.76, ...), custom_call_target="tpu_custom_call" | custom-call | tf_op jit(solution)/shard_map/pallas_call | solution.py:1667
  142.1 11.0 %shard_map.257 = (bf16[128,2560]{1,0:T(8,128)(2,1)}, f32[24,128,128]{2,1,0:T(8,128)}, bf16[128,1536]{1,0:T(8,128)(2,1)}, f32[128,1536]{1,0:T(8,128)}, bf16[128,1...) custom-call(bf16[2,128,1536]{2,1,0:T(8,128)(2,1)} %bitcast.69, bf16[1536,4224]{1,0:T(8,128)(2,1)} %bitcast.57, ...), custom_call_target="tpu_custom_call" | custom-call | flops 1610612736 | bytes 12976128 | tf_op jit(solution)/shard_map/pallas_call | solution.py:169
  153.1 94.5 %shard_map.258 = (bf16[4,128,1536]{2,1,0:T(8,128)(2,1)}, s32[8,8,128]{2,1,0:T(8,128)}, f32[8,8,128]{2,1,0:T(8,128)}, bf16[5,512,512]{2,1,0:T(8,128)(2,1)}, bf16[...) custom-call(bf16[128,1536]{1,0:T(8,128)(2,1)} %get-tuple-element.83., ...), custom_call_target="tpu_custom_call", output_to_operand_aliasing={{6}: (6, {})} | custom-call | tf_op jit(solution)/shard_map/pallas_call | solution.py:989
  247.6 11.4 %shard_map.259 = (bf16[128,2560]{1,0:T(8,128)(2,1)}, f32[24,128,128]{2,1,0:T(8,128)}, bf16[128,1536]{1,0:T(8,128)(2,1)}, f32[128,1536]{1,0:T(8,128)}, bf16[128,1...) custom-call(f32[128,1536]{1,0:T(8,128)} %get-tuple-element.82.below_ref.h_ref, ...), custom_call_target="tpu_custom_call" | custom-call | flops 1610612736 | bytes 12976128 | tf_op jit(solution)/shard_map/pallas_call | solution.py:169
  259.0 96.9 %shard_map.260 = (bf16[4,128,1536]{2,1,0:T(8,128)(2,1)}, f32[4,8,128]{2,1,0:T(8,128)}, bf16[2,2,5,384,512]{4,3,2,1,0:T(8,128)(2,1)}, bf16[2,2,5,384,512]{4,3,2,1...) custom-call(bf16[128,1536]{1,0:T(8,128)(2,1)} %get-tuple-element.94., ...), custom_call_target="tpu_custom_call" | custom-call | tf_op jit(solution)/shard_map/pallas_call | solution.py:989
  355.9 13.5 %shard_map.261 = (f32[128,1536]{1,0:T(8,128)}, bf16[128,1536]{1,0:T(8,128)(2,1)}, bf16[128,2560]{1,0:T(8,128)(2,1)}, bf16[1536,128]{1,0:T(8,128)(2,1)}, bf16[153...) custom-call(bf16[2,128,1536]{2,1,0:T(8,128)(2,1)} %bitcast.66, f32[128,1536]{1,0:T(8,128)} %get-tuple-element.130.h_ref, ...), custom_call_target="tpu_custom_call" | custom-call | flops 3221225472 | bytes 25952256 | tf_op jit(solution)/shard_map/pallas_call | solution.py:340
  369.4 88.0 %shard_map.262 = (bf16[4,128,1536]{2,1,0:T(8,128)(2,1)}, f32[4,8,128]{2,1,0:T(8,128)}, bf16[2,2,5,384,512]{4,3,2,1,0:T(8,128)(2,1)}, bf16[2,2,5,384,512]{4,3,2,1...) custom-call(bf16[128,1536]{1,0:T(8,128)(2,1)} %get-tuple-element.100, ...), custom_call_target="tpu_custom_call" | custom-call | tf_op jit(solution)/shard_map/pallas_call | solution.py:989
  457.4 4.1 all-to-all-start
  461.6 19.0 %shard_map.263 = (f32[128,1536]{1,0:T(8,128)}, bf16[128,1536]{1,0:T(8,128)(2,1)}, bf16[1536,4224]{1,0:T(8,128)(2,1)}) custom-call(bf16[128,1536]{1,0:T(8,128)(2,1)} %get-tuple-element.100.refs_0_.gy_ref.dx1, f32[128,1536]{1,0:T(8,128)} %get-tuple-element.82.below_ref.h_ref, bf16[128,1536]{1,0:T(8,128)(2,1)} %get-tuple-element.101.x_ref, ...), custom_call_target="tpu_custom_call" | custom-call | flops 3221225472 | bytes 25952256 | tf_op jit(solution)/shard_map/pallas_call | solution.py:340
  480.6 0.0 copy-start
  480.6 0.0 copy-start.1
  480.6 175.8 %shard_map.264 = (f32[96,4224]{1,0:T(8,128)}, bf16[128,1536]{1,0:T(8,128)(2,1)}, bf16[5,384,512]{2,1,0:T(8,128)(2,1)}, bf16[5,384,512]{2,1,0:T(8,128)(2,1)}, bf16[5,512,384]{2,1,0:T(8,128)(2,1)}) custom-call(bf16[16,96,4224]{2,1,0:T(8,128)(2,1)} %bitcast.60, bf16[16,96,4224]{2,1,0:T(8,128)(2,1)} %bitcast.59, bf16[128,1536]{1,0:T(8,128)(2,1)} %get-tuple-element.120.dx0, ...), custom_call_target="tpu_custom_call" | custom-call | tf_op jit(solution)/shard_map/pallas_call | solution.py:1390
  656.4 0.0 all-to-all-done
  656.5 0.2 convert_reduce_fusion
  656.7 0.0 copy-done
  656.7 0.0 copy-done.1
  656.7 0.2 select_bitcast_fusion
  656.9 0.3 collective-permute-start
  657.2 9.9 %shard_map.265 = (f32[5,384,512]{2,1,0:T(8,128)}, f32[5,384,512]{2,1,0:T(8,128)}, f32[5,512,384]{2,1,0:T(8,128)}, f32[96,1536]{1,0:T(8,128)}, f32[96,512]{1,0:T(...) custom-call(f32[96,4224]{1,0:T(8,128)} %get-tuple-element.132.dense_, ...), custom_call_target="tpu_custom_call" | custom-call | tf_op jit(solution)/shard_map/pallas_call | solution.py:1466
  667.1 1.2 collective-permute-done
  668.3 1.0 maximum_select_fusion
  (1 shorter events, 0.0 us)
Async XLA Ops:
  457.4 199.0 %all-to-all-start = ((bf16[4,128,1536]{2,1,0:T(8,128)(2,1)}), bf16[4,128,1536]{2,1,0:T(8,128)(2,1)S(1)}, u32[]{:S(2)}, u32[]{:S(2)}) async-start(bf16[4,128,1536]{2,1,0:T(8,128)(2,1)} %get-tuple-element.131), calls=%async_computation | async-start | bytes 3145728 | tf_op jit(solution)/shard_map/all_to_all | solution.py:1735
  480.6 176.1 %copy-start = (bf16[128,1536]{1,0:T(8,128)(2,1)S(1)}, bf16[128,1536]{1,0:T(8,128)(2,1)}, u32[]{:S(2)}) copy-start(bf16[128,1536]{1,0:T(8,128)(2,1)} %get-tuple-element.89.x_ref) | copy-start | bytes 1179652
  480.6 176.1 %copy-start.1 = (f32[128,1536]{1,0:T(8,128)S(1)}, f32[128,1536]{1,0:T(8,128)}, u32[]{:S(2)}) copy-start(f32[128,1536]{1,0:T(8,128)} %get-tuple-element.130.h_ref) | copy-start | bytes 2359300
  656.9 11.4 %collective-permute-start = (bf16[128,1536]{1,0:T(8,128)(2,1)S(1)}, bf16[128,1536]{1,0:T(8,128)(2,1)S(1)}, u32[]{:S(2)}, u32[]{:S(2)}) collective-permute-start(bf16[128,1536]{1,0:T(8,128)(2,1)S(1)} %broadcast_select_fusion), channel_id=1, source_target_pairs={{0,16},{16,0},{1,17},{17,1},{2,18},{18,2},{3,19},{19,3},{4,20},{20... | collective-permute-start | bytes 1179656 | tf_op jit(solution)/shard_map/ppermute | solution.py:1679

commit v10 on v9

--- a/solution.py
+++ b/solution.py
@@ -1300,7 +1300,7 @@
 
         for q in range(1, pairs):
 
-            @pl.when(i == (pairs - q) * n + min(2, n - 1))
+            @pl.when(i == (pairs - q) * n)
             def _():
                 pass_on(q)
 

time: 678 us -> 679 us (level)
  transfers between devices with their start and end apart: 2 -> 2, of which waited for: 1 -> 0; matrix products, arithmetic and copies ran while one was open for 0% -> 0% of each run, Pallas kernels for 31% -> 31%
where the time goes in v10:
time: 679 us; the launch traced here: 671 us
  Pallas kernels  661 us (97%)
    pallas_call x3, Pallas kernels, moe(): pl.pallas_call(functools.partial(moe_kernel, layer, mode, n, e_pad, cap,...  279 us
    pallas_call x1, Pallas kernels, finish(): pl.pallas_call(functools.partial(finish_kernel, n), out_shape=(sds((rows,...  176 us
    pallas_call x1, Pallas kernels, open_up(): pl.pallas_call(functools.partial(open_kernel, n, groups, pieces), out_sha...  141 us
    pallas_call x2, Pallas kernels, attn_bwd(): pl.pallas_call(functools.partial(attn_bwd_kernel, layer, now, -(-experts...  32.6 us
    pallas_call x2, Pallas kernels, attn_fwd(): pl.pallas_call(functools.partial(attn_fwd_kernel, len(back)), out_shape=(...  22.3 us
  transfers between devices with their start and end apart: 2, of which 0 were waited for; matrix products, arithmetic and copies ran while one was open for 0% of the time, Pallas kernels for 31%

profile of v10, /device:TPU:0, one launch (start us, length us, event | category | flops | bytes accessed | tf_op | source)
XLA Modules:
  0.0 670.7 jit_solution(14558842861573582993)
XLA Ops:
  0.6 141.4 %shard_map.256 = (bf16[16,96,4224]{2,1,0:T(8,128)(2,1)}, bf16[16,96,4224]{2,1,0:T(8,128)(2,1)}, bf16[2,4,128,1536]{3,2,1,0:T(8,128)(2,1)}, s32[2,4,8,128]{3,2,1,0:T(8,128)}, s32[8,128]{1,0:T(8,128)}) custom-call(bf16[96,1536]{1,0:T(8,128)(2,1)} %bitcast.71, bf16[96,512]{1,0:T(8,128)(2,1)} %bitcast.75, bf16[96,512]{1,0:T(8,128)(2,1)} %bitcast.76, ...), custom_call_target="tpu_custom_call" | custom-call | tf_op jit(solution)/shard_map/pallas_call | solution.py:1667
  142.1 11.0 %shard_map.257 = (bf16[128,2560]{1,0:T(8,128)(2,1)}, f32[24,128,128]{2,1,0:T(8,128)}, bf16[128,1536]{1,0:T(8,128)(2,1)}, f32[128,1536]{1,0:T(8,128)}, bf16[128,1...) custom-call(bf16[2,128,1536]{2,1,0:T(8,128)(2,1)} %bitcast.69, bf16[1536,4224]{1,0:T(8,128)(2,1)} %bitcast.57, ...), custom_call_target="tpu_custom_call" | custom-call | flops 1610612736 | bytes 12976128 | tf_op jit(solution)/shard_map/pallas_call | solution.py:169
  153.1 94.5 %shard_map.258 = (bf16[4,128,1536]{2,1,0:T(8,128)(2,1)}, s32[8,8,128]{2,1,0:T(8,128)}, f32[8,8,128]{2,1,0:T(8,128)}, bf16[5,512,512]{2,1,0:T(8,128)(2,1)}, bf16[...) custom-call(bf16[128,1536]{1,0:T(8,128)(2,1)} %get-tuple-element.83., ...), custom_call_target="tpu_custom_call", output_to_operand_aliasing={{6}: (6, {})} | custom-call | tf_op jit(solution)/shard_map/pallas_call | solution.py:989
  247.6 11.4 %shard_map.259 = (bf16[128,2560]{1,0:T(8,128)(2,1)}, f32[24,128,128]{2,1,0:T(8,128)}, bf16[128,1536]{1,0:T(8,128)(2,1)}, f32[128,1536]{1,0:T(8,128)}, bf16[128,1...) custom-call(f32[128,1536]{1,0:T(8,128)} %get-tuple-element.82.below_ref.h_ref, ...), custom_call_target="tpu_custom_call" | custom-call | flops 1610612736 | bytes 12976128 | tf_op jit(solution)/shard_map/pallas_call | solution.py:169
  259.0 96.9 %shard_map.260 = (bf16[4,128,1536]{2,1,0:T(8,128)(2,1)}, f32[4,8,128]{2,1,0:T(8,128)}, bf16[2,2,5,384,512]{4,3,2,1,0:T(8,128)(2,1)}, bf16[2,2,5,384,512]{4,3,2,1...) custom-call(bf16[128,1536]{1,0:T(8,128)(2,1)} %get-tuple-element.94., ...), custom_call_target="tpu_custom_call" | custom-call | tf_op jit(solution)/shard_map/pallas_call | solution.py:989
  355.9 13.5 %shard_map.261 = (f32[128,1536]{1,0:T(8,128)}, bf16[128,1536]{1,0:T(8,128)(2,1)}, bf16[128,2560]{1,0:T(8,128)(2,1)}, bf16[1536,128]{1,0:T(8,128)(2,1)}, bf16[153...) custom-call(bf16[2,128,1536]{2,1,0:T(8,128)(2,1)} %bitcast.66, f32[128,1536]{1,0:T(8,128)} %get-tuple-element.130.h_ref, ...), custom_call_target="tpu_custom_call" | custom-call | flops 3221225472 | bytes 25952256 | tf_op jit(solution)/shard_map/pallas_call | solution.py:340
  369.4 88.0 %shard_map.262 = (bf16[4,128,1536]{2,1,0:T(8,128)(2,1)}, f32[4,8,128]{2,1,0:T(8,128)}, bf16[2,2,5,384,512]{4,3,2,1,0:T(8,128)(2,1)}, bf16[2,2,5,384,512]{4,3,2,1...) custom-call(bf16[128,1536]{1,0:T(8,128)(2,1)} %get-tuple-element.100, ...), custom_call_target="tpu_custom_call" | custom-call | tf_op jit(solution)/shard_map/pallas_call | solution.py:989
  457.4 4.1 all-to-all-start
  461.6 19.0 %shard_map.263 = (f32[128,1536]{1,0:T(8,128)}, bf16[128,1536]{1,0:T(8,128)(2,1)}, bf16[1536,4224]{1,0:T(8,128)(2,1)}) custom-call(bf16[128,1536]{1,0:T(8,128)(2,1)} %get-tuple-element.100.refs_0_.gy_ref.dx1, f32[128,1536]{1,0:T(8,128)} %get-tuple-element.82.below_ref.h_ref, bf16[128,1536]{1,0:T(8,128)(2,1)} %get-tuple-element.101.x_ref, ...), custom_call_target="tpu_custom_call" | custom-call | flops 3221225472 | bytes 25952256 | tf_op jit(solution)/shard_map/pallas_call | solution.py:340
  480.6 0.0 copy-start
  480.6 0.0 copy-start.1
  480.6 175.8 %shard_map.264 = (f32[96,4224]{1,0:T(8,128)}, bf16[128,1536]{1,0:T(8,128)(2,1)}, bf16[5,384,512]{2,1,0:T(8,128)(2,1)}, bf16[5,384,512]{2,1,0:T(8,128)(2,1)}, bf16[5,512,384]{2,1,0:T(8,128)(2,1)}) custom-call(bf16[16,96,4224]{2,1,0:T(8,128)(2,1)} %bitcast.60, bf16[16,96,4224]{2,1,0:T(8,128)(2,1)} %bitcast.59, bf16[128,1536]{1,0:T(8,128)(2,1)} %get-tuple-element.120.dx0, ...), custom_call_target="tpu_custom_call" | custom-call | tf_op jit(solution)/shard_map/pallas_call | solution.py:1390
  656.4 0.0 all-to-all-done
  656.5 0.2 convert_reduce_fusion
  656.7 0.0 copy-done
  656.7 0.0 copy-done.1
  656.7 0.2 select_bitcast_fusion
  656.9 2.6 collective-permute-start
  659.6 9.9 %shard_map.265 = (f32[5,384,512]{2,1,0:T(8,128)}, f32[5,384,512]{2,1,0:T(8,128)}, f32[5,512,384]{2,1,0:T(8,128)}, f32[96,1536]{1,0:T(8,128)}, f32[96,512]{1,0:T(...) custom-call(f32[96,4224]{1,0:T(8,128)} %get-tuple-element.132.dense_, ...), custom_call_target="tpu_custom_call" | custom-call | tf_op jit(solution)/shard_map/pallas_call | solution.py:1466
  669.5 0.0 collective-permute-done
  669.5 1.0 maximum_select_fusion
  (1 shorter events, 0.0 us)
Async XLA Ops:
  457.4 199.0 %all-to-all-start = ((bf16[4,128,1536]{2,1,0:T(8,128)(2,1)}), bf16[4,128,1536]{2,1,0:T(8,128)(2,1)S(1)}, u32[]{:S(2)}, u32[]{:S(2)}) async-start(bf16[4,128,1536]{2,1,0:T(8,128)(2,1)} %get-tuple-element.131), calls=%async_computation | async-start | bytes 3145728 | tf_op jit(solution)/shard_map/all_to_all | solution.py:1735
  480.6 176.1 %copy-start = (bf16[128,1536]{1,0:T(8,128)(2,1)S(1)}, bf16[128,1536]{1,0:T(8,128)(2,1)}, u32[]{:S(2)}) copy-start(bf16[128,1536]{1,0:T(8,128)(2,1)} %get-tuple-element.89.x_ref) | copy-start | bytes 1179652
  480.6 176.1 %copy-start.1 = (f32[128,1536]{1,0:T(8,128)S(1)}, f32[128,1536]{1,0:T(8,128)}, u32[]{:S(2)}) copy-start(f32[128,1536]{1,0:T(8,128)} %get-tuple-element.130.h_ref) | copy-start | bytes 2359300
  656.9 12.6 %collective-permute-start = (bf16[128,1536]{1,0:T(8,128)(2,1)S(1)}, bf16[128,1536]{1,0:T(8,128)(2,1)S(1)}, u32[]{:S(2)}, u32[]{:S(2)}) collective-permute-start(bf16[128,1536]{1,0:T(8,128)(2,1)S(1)} %broadcast_select_fusion), channel_id=1, source_target_pairs={{0,16},{16,0},{1,17},{17,1},{2,18},{18,2},{3,19},{19,3},{4,20},{20... | collective-permute-start | bytes 1179656 | tf_op jit(solution)/shard_map/ppermute | solution.py:1679
